TPU v7x, 32 devices: a whole 2x2x4 slice. The times are simulated.
32 devices in a mesh: dp: 16 (over z, y, x), mp: 2 (over core).
Axes of the slice: x: 2, y: 2, z: 4, core: 2. Of those that a mesh axis runs over, the one named last changes fastest.
Arguments:
- context: bfloat16 [16384, 4096], P('dp'), may hold values from -6 to 6
- counts: int32 [16, 2], P('dp'), may hold values from 256 to 768, as said below
- routes: int32 [2048, 1], P('dp'), may hold values from 0 to 15; in each aligned block of 128 rows (0 to 127, 128 to 255, ...) at most 16 rows name the same one
- w_query: bfloat16 [4096, 1536], P(None, 'mp'), may hold values from -0.09375 to 0.09375
- w_key: bfloat16 [4096, 384], P(None, 'mp'), may hold values from -0.09375 to 0.09375
- w_value: bfloat16 [4096, 384], P(None, 'mp'), may hold values from -0.09375 to 0.09375
- w_out: bfloat16 [1536, 4096], P('mp'), may hold values from -2 to 2
- latents: bfloat16 [64, 4096], replicated, may hold values from -9 to 9
- gain_ctx: float32 [4096], replicated, may hold values from 0.25 to 1.75
- gain_lat: float32 [4096], replicated, may hold values from 0.25 to 1.75
- gain_out: float32 [4096], replicated, may hold values from 0.25 to 1.75
- cotangent: bfloat16 [4096, 4096], P('dp', 'mp'), may hold values from -9 to 9
Outputs:
- routed: bfloat16 [4096, 4096], P('dp', 'mp')
- ctx_grad: bfloat16 [16384, 4096], P('dp', 'mp')
- grad_w_query: float32 [4096, 1536], P('dp', 'mp')
- grad_w_key: float32 [4096, 384], P('dp', 'mp')
- grad_w_value: float32 [4096, 384], P('dp', 'mp')
- grad_w_out: float32 [1536, 4096], P('mp', 'dp')
- grad_latents: float32 [64, 4096], P(None, ('dp', 'mp'))
- grad_gain_ctx: float32 [4096], P(('dp', 'mp'))
- grad_gain_lat: float32 [4096], P(('dp', 'mp'))
- grad_gain_out: float32 [4096], P(('dp', 'mp'))
Inputs may be any that keep to these rules, and one draw needn't show every extreme that they name: `counts`: in every block the 2 images hold together at most 1024 patches, exactly 1024 in at least two blocks; each image has 256 or more patches and one has 768. `routes`: within the rows of one dp index no decoder shard is named by more than 16 rows.
All inputs are finite; a program needn't handle non-finite values.
Results may differ from a plain program's by a relative error of at most 0.01.
Values may be sent and summed in bfloat16 or wider, within the bound.
No kernel may reach another device: no remote copies, remote signals or barrier semaphores. Data moves between devices by JAX's collectives and lax.ppermute only.
A program may use at most 192 MiB of HBM per device.

v0:
```python
import functools

import jax
import jax.numpy as jnp
from jax import lax
from jax.experimental import pallas as pl
from jax.experimental.pallas import tpu as pltpu
from jax.sharding import PartitionSpec as P

HD = 96
EPSILON = 1e-06
NEGATIVE = -1e30
BF16 = jnp.bfloat16
F32 = jnp.float32
VMEM_LIMIT = 63 << 20


def dot_general(left, right, left_dim, right_dim):
    return lax.dot_general(
        left, right, (((left_dim,), (right_dim,)), ((), ())), preferred_element_type=F32
    )


def norm_parts(values_in):
    inverse = lax.rsqrt(jnp.mean(values_in * values_in, axis=-1, keepdims=True) + EPSILON)
    return (values_in * inverse, inverse)


def swap_cores(array):
    return lax.ppermute(array, "mp", [(0, 1), (1, 0)])


def swap_bit(array, bit, dp_count):
    return lax.ppermute(array, "dp", [(i, i ^ (1 << bit)) for i in range(dp_count)])


def halve(array, axis, bit, dp_count):
    mine = (lax.axis_index("dp") >> bit) & 1
    going = lax.dynamic_index_in_dim(array, 1 - mine, axis, keepdims=False)
    kept = lax.dynamic_index_in_dim(array, mine, axis, keepdims=False)
    return kept.astype(F32) + swap_bit(going.astype(BF16), bit, dp_count).astype(F32)


def scatter_sum(array, bits, dp_count):
    rows, owners, columns = array.shape
    left = sorted(bits, reverse=True)
    array = array.reshape((rows,) + (2,) * len(left) + (columns,))
    for bit in bits:
        axis = left.index(bit)
        array = halve(array, 1 + axis, bit, dp_count)
        left.pop(axis)
    return array


def forward_kernel(
    counts_ref,
    x_ref,
    wk_ref,
    wv_ref,
    wq_ref,
    lat_ref,
    gain_ctx_ref,
    gain_lat_ref,
    attn_ref,
    k_ref,
    v_ref,
    inv_row_ref,
    q_ref,
    lk_ref,
    lv_ref,
    lat_proj_ref,
    p_ref,
    pl_ref,
    lat_normed_ref,
    query_acc,
    gained_ref,
):
    step = pl.program_id(0)
    steps = pl.num_programs(0)
    rows, width = x_ref.shape
    slab = wq_ref.shape[0]
    groups, patch_rows, _ = k_ref.shape
    latent_rows = lat_ref.shape[0]
    key_width = wk_ref.shape[0]
    query_width = wq_ref.shape[1]
    per_group = query_width // key_width

    @pl.when(step == 0)
    def _():
        lat = lat_ref[...].astype(F32)
        inverse = lax.rsqrt(jnp.mean(lat * lat, axis=-1, keepdims=True) + EPSILON)
        lat_normed_ref[...] = (lat * inverse * gain_lat_ref[...]).astype(BF16)
        for i, ref in enumerate((wk_ref, wv_ref)):
            projected = dot_general(lat_normed_ref[...], ref[...], 1, 1)
            at = query_width + i * key_width
            lat_proj_ref[:, at : at + key_width] = projected
            for g in range(groups):
                (lk_ref, lv_ref)[i][g] = projected[:, g * HD : (g + 1) * HD].astype(BF16)
            gained_ref[i * key_width : (i + 1) * key_width, :] = (
                ref[...].astype(F32) * gain_ctx_ref[...]
            ).astype(BF16)
        query_acc[...] = jnp.zeros_like(query_acc)

    squares = jnp.zeros((rows, 128), F32)
    for c in range(width // 128):
        part = x_ref[:, c * 128 : (c + 1) * 128].astype(F32)
        squares = squares + part * part
    inverse = lax.rsqrt(jnp.sum(squares, axis=-1, keepdims=True) / width + EPSILON)
    pair = (dot_general(x_ref[...], gained_ref[...], 1, 1) * inverse).astype(BF16)
    at = pl.ds(pl.multiple_of(step * rows, rows), rows)
    inv_row_ref[:, at] = jnp.transpose(jnp.broadcast_to(inverse, (rows, 128)))[:8]
    for g in range(groups):
        k_ref[g, at, :] = pair[:, g * HD : (g + 1) * HD]
        v_ref[g, at, :] = pair[:, key_width + g * HD : key_width + (g + 1) * HD]
    query_acc[...] += jnp.dot(
        lat_normed_ref[:, pl.ds(pl.multiple_of(step * slab, slab), slab)],
        wq_ref[...],
        preferred_element_type=F32,
    )

    @pl.when(step == steps - 1)
    def _():
        query = query_acc[...] * HD ** (-0.5)
        lat_proj_ref[:, :query_width] = query
        stacked = per_group * latent_rows
        first_count = counts_ref[0, 0]
        both_count = first_count + counts_ref[0, 1]
        position = lax.broadcasted_iota(jnp.int32, (1, patch_rows), 1)
        in_first = position < first_count
        in_second = jnp.logical_and(position >= first_count, position < both_count)
        rows_at = lax.broadcasted_iota(jnp.int32, (patch_rows, HD), 0)
        row_first = rows_at < first_count
        row_second = jnp.logical_and(rows_at >= first_count, rows_at < both_count)
        for g in range(groups):
            for h in range(per_group):
                head = g * per_group + h
                q_ref[g, h * latent_rows : (h + 1) * latent_rows, :] = query[
                    :, head * HD : (head + 1) * HD
                ].astype(BF16)
            q = q_ref[g]
            scores = dot_general(q, k_ref[g], 1, 1)
            lat_scores = dot_general(q, lk_ref[g], 1, 1)
            lat_max = jnp.max(lat_scores, axis=-1, keepdims=True)
            max_first = jnp.maximum(
                jnp.max(jnp.where(in_first, scores, NEGATIVE), axis=-1, keepdims=True), lat_max
            )
            max_second = jnp.maximum(
                jnp.max(jnp.where(in_second, scores, NEGATIVE), axis=-1, keepdims=True), lat_max
            )
            masked = jnp.where(
                in_first, scores - max_first, jnp.where(in_second, scores - max_second, NEGATIVE)
            )
            exponent = jnp.exp(masked)
            lat_first = jnp.exp(lat_scores - max_first)
            lat_second = jnp.exp(lat_scores - max_second)
            sum_first = jnp.sum(
                jnp.where(in_first, exponent, 0.0), axis=-1, keepdims=True
            ) + jnp.sum(lat_first, axis=-1, keepdims=True)
            sum_second = jnp.sum(
                jnp.where(in_second, exponent, 0.0), axis=-1, keepdims=True
            ) + jnp.sum(lat_second, axis=-1, keepdims=True)
            per_first = 1.0 / sum_first
            per_second = 1.0 / sum_second
            p = (exponent * jnp.where(in_first, per_first, per_second)).astype(BF16)
            p_ref[g] = p
            lat_p_first = (lat_first * per_first).astype(BF16)
            lat_p_second = (lat_second * per_second).astype(BF16)
            pl_ref[g, 0] = lat_p_first
            pl_ref[g, 1] = lat_p_second
            v = v_ref[g]
            zero = jnp.zeros_like(v)
            lv = lv_ref[g]
            for j, (row_mask, lat_p) in enumerate(
                ((row_first, lat_p_first), (row_second, lat_p_second))
            ):
                mixed = jnp.dot(
                    p, jnp.where(row_mask, v, zero), preferred_element_type=F32
                ) + jnp.dot(lat_p, lv, preferred_element_type=F32)
                mixed = mixed.astype(BF16)
                for h in range(per_group):
                    head = g * per_group + h
                    attn_ref[
                        j * latent_rows : (j + 1) * latent_rows, head * HD : (head + 1) * HD
                    ] = mixed[h * latent_rows : (h + 1) * latent_rows]


def whole(shape):
    return pl.BlockSpec(shape, lambda *_: (0,) * len(shape))


def held(shape):
    return pl.BlockSpec(shape, lambda *_: (0,) * len(shape), pipeline_mode=pl.Buffered(1))


def forward_call(context, counts, w_query, w_key, w_value, latents, gain_ctx, gain_lat):
    patch_rows, width = context.shape
    steps = 4
    rows = patch_rows // steps
    slab = width // steps
    key_width = w_key.shape[0]
    query_width = w_query.shape[1]
    groups = key_width // HD
    latent_rows = latents.shape[0]
    stacked = query_width // key_width * latent_rows
    out = [
        ((2 * latent_rows, query_width), BF16),
        ((groups, patch_rows, HD), BF16),
        ((groups, patch_rows, HD), BF16),
        ((8, patch_rows), F32),
        ((groups, stacked, HD), BF16),
        ((groups, latent_rows, HD), BF16),
        ((groups, latent_rows, HD), BF16),
        ((latent_rows, query_width + 2 * key_width), F32),
        ((groups, stacked, patch_rows), BF16),
        ((groups, 2, stacked, latent_rows), BF16),
    ]
    return pl.pallas_call(
        forward_kernel,
        name="forward_attention",
        grid=(steps,),
        in_specs=[
            pl.BlockSpec(memory_space=pltpu.SMEM),
            pl.BlockSpec((rows, width), lambda i: (i, 0)),
            held(w_key.shape),
            held(w_value.shape),
            pl.BlockSpec((slab, query_width), lambda i: (i, 0)),
            held(latents.shape),
            held((1, width)),
            held((1, width)),
        ],
        out_specs=[held(shape) for shape, _ in out],
        out_shape=[jax.ShapeDtypeStruct(shape, dtype) for shape, dtype in out],
        scratch_shapes=[
            pltpu.VMEM((latent_rows, width), BF16),
            pltpu.VMEM((latent_rows, query_width), F32),
            pltpu.VMEM((2 * key_width, width), BF16),
        ],
        cost_estimate=pl.CostEstimate(
            flops=5_000_000_000, bytes_accessed=24_000_000, transcendentals=600_000
        ),
        compiler_params=pltpu.CompilerParams(vmem_limit_bytes=VMEM_LIMIT),
    )(
        counts,
        context,
        w_key,
        w_value,
        w_query,
        latents,
        gain_ctx.reshape(1, width),
        gain_lat.reshape(1, width),
    )


def slots_of(routes_ref, slot_count, as_row):
    rows = routes_ref.shape[1]
    turned = jnp.broadcast_to(routes_ref[...].astype(F32), (rows, rows))
    shard = jnp.transpose(turned)
    down = lax.broadcasted_iota(jnp.int32, (rows, rows), 0)
    across = lax.broadcasted_iota(jnp.int32, (rows, rows), 1)
    same = shard == turned
    if as_row:
        rank = jnp.sum(jnp.where(same & (down < across), 1.0, 0.0), axis=0, keepdims=True)
        return (turned[:1] * slot_count + rank).astype(jnp.int32)
    rank = jnp.sum(jnp.where(same & (across < down), 1.0, 0.0), axis=1, keepdims=True)
    return (shard[:, :1] * slot_count + rank).astype(jnp.int32)


def branch_kernel(
    slot_count,
    mp_ref,
    own_ref,
    other_ref,
    w_own_ref,
    w_other_ref,
    lat_ref,
    gain_ref,
    routes_ref,
    hat_ref,
    inv_ref,
    out_ref,
    square_acc,
):
    step = pl.program_id(0)
    steps = pl.num_programs(0)
    columns = w_own_ref.shape[1]
    half = out_ref.shape[1]
    slots = out_ref.shape[0]
    rows = own_ref.shape[0]

    @pl.when(step == 0)
    def _():
        square_acc[...] = jnp.zeros_like(square_acc)

    lat = lat_ref[...].astype(F32)
    resid = (
        jnp.concatenate([lat, lat], axis=0)
        + jnp.dot(own_ref[...], w_own_ref[...], preferred_element_type=F32)
        + jnp.dot(other_ref[...], w_other_ref[...], preferred_element_type=F32)
    )
    hat_ref[:, pl.ds(pl.multiple_of(step * columns, columns), columns)] = resid
    square_acc[...] += jnp.sum(resid * resid, axis=-1, keepdims=True)

    @pl.when(step == steps - 1)
    def _():
        width = hat_ref.shape[1]
        inverse = lax.rsqrt(square_acc[...] / width + EPSILON)
        inv_ref[...] = inverse
        hat_ref[...] = hat_ref[...] * inverse
        place = slots_of(routes_ref, slot_count, True)
        table = jnp.where(
            lax.broadcasted_iota(jnp.int32, (slots, rows), 0) == place, 1.0, 0.0
        ).astype(BF16)
        at = pl.ds(pl.multiple_of(mp_ref[0] * half, half), half)
        final = (hat_ref[:, at] * gain_ref[:, at]).astype(BF16)
        out_ref[...] = jnp.dot(table, final, preferred_element_type=F32).astype(BF16)


def branch_call(mp_index, own, other, w_own, w_other, latents, gain_out, routes, slots, slot_count):
    width = w_own.shape[1]
    rows, heads = own.shape
    steps = 8
    columns = width // steps
    half = width // 2
    return pl.pallas_call(
        functools.partial(branch_kernel, slot_count),
        name="branch_norm",
        grid_spec=pltpu.PrefetchScalarGridSpec(
            num_scalar_prefetch=1,
            grid=(steps,),
            in_specs=[
                held((rows, heads)),
                held((rows, heads)),
                pl.BlockSpec((heads, columns), lambda i, *_: (0, i)),
                pl.BlockSpec((heads, columns), lambda i, *_: (0, i)),
                pl.BlockSpec((latents.shape[0], columns), lambda i, *_: (0, i)),
                held((1, width)),
                held((1, rows)),
            ],
            out_specs=[held((rows, width)), held((rows, 1)), held((slots, half))],
            scratch_shapes=[pltpu.VMEM((rows, 1), F32)],
        ),
        out_shape=[
            jax.ShapeDtypeStruct((rows, width), F32),
            jax.ShapeDtypeStruct((rows, 1), F32),
            jax.ShapeDtypeStruct((slots, half), BF16),
        ],
        cost_estimate=pl.CostEstimate(
            flops=2 * 2 * rows * heads * width, bytes_accessed=16_000_000, transcendentals=0
        ),
        compiler_params=pltpu.CompilerParams(vmem_limit_bytes=VMEM_LIMIT),
    )(mp_index, own, other, w_own, w_other, latents, gain_out.reshape(1, width), routes)


def attention_backward(
    counts_ref,
    d_attn,
    k_ref,
    v_ref,
    q_ref,
    lk_ref,
    lv_ref,
    p_ref,
    pl_ref,
    inv_row_ref,
    pair_ref,
    scaled_ref,
    lat_ref,
):
    groups, patch_rows, _ = k_ref.shape
    latent_rows = lk_ref.shape[1]
    stacked = q_ref.shape[1]
    per_group = stacked // latent_rows
    key_width = groups * HD
    query_width = groups * per_group * HD
    first_count = counts_ref[0, 0]
    both_count = first_count + counts_ref[0, 1]
    position = lax.broadcasted_iota(jnp.int32, (1, patch_rows), 1)
    in_first = position < first_count
    rows_at = lax.broadcasted_iota(jnp.int32, (patch_rows, HD), 0)
    row_first = rows_at < first_count
    row_second = jnp.logical_and(rows_at >= first_count, rows_at < both_count)
    scale_row = inv_row_ref[:1]
    row_dot = jnp.zeros((1, patch_rows), F32)
    for g in range(groups):
        d_first = jnp.concatenate(
            [
                d_attn[:latent_rows, head * HD : (head + 1) * HD]
                for head in range(g * per_group, (g + 1) * per_group)
            ],
            axis=0,
        )
        d_second = jnp.concatenate(
            [
                d_attn[latent_rows:, head * HD : (head + 1) * HD]
                for head in range(g * per_group, (g + 1) * per_group)
            ],
            axis=0,
        )
        q = q_ref[g]
        k = k_ref[g]
        v = v_ref[g]
        lk = lk_ref[g]
        lv = lv_ref[g]
        p_low = p_ref[g]
        p = p_low.astype(F32)
        zero = jnp.zeros_like(v)
        d_p = dot_general(d_first, jnp.where(row_first, v, zero), 1, 1) + dot_general(
            d_second, jnp.where(row_second, v, zero), 1, 1
        )
        product = p * d_p
        lat_first = pl_ref[g, 0]
        lat_second = pl_ref[g, 1]
        d_lat_first = dot_general(d_first, lv, 1, 1)
        d_lat_second = dot_general(d_second, lv, 1, 1)
        lat_product_first = lat_first.astype(F32) * d_lat_first
        lat_product_second = lat_second.astype(F32) * d_lat_second
        whole_sum = jnp.sum(product, axis=-1, keepdims=True)
        first_sum = jnp.sum(jnp.where(in_first, product, 0.0), axis=-1, keepdims=True)
        delta_first = first_sum + jnp.sum(lat_product_first, axis=-1, keepdims=True)
        delta_second = (whole_sum - first_sum) + jnp.sum(
            lat_product_second, axis=-1, keepdims=True
        )
        ds = product - p * jnp.where(in_first, delta_first, delta_second)
        ds_low = ds.astype(BF16)
        dsl = (
            lat_product_first
            - lat_first.astype(F32) * delta_first
            + lat_product_second
            - lat_second.astype(F32) * delta_second
        ).astype(BF16)
        scores = dot_general(q, k, 1, 1)
        row_dot = row_dot + jnp.sum(ds * scores + product, axis=0, keepdims=True)
        d_q = (
            jnp.dot(ds_low, k, preferred_element_type=F32)
            + jnp.dot(dsl, lk, preferred_element_type=F32)
        ).astype(BF16)
        for h in range(per_group):
            head = g * per_group + h
            lat_ref[:latent_rows, head * HD : (head + 1) * HD] = d_q[
                h * latent_rows : (h + 1) * latent_rows
            ]
        d_k = dot_general(q, ds_low, 0, 0)
        nothing = jnp.zeros_like(p_low)
        d_v = dot_general(d_first, jnp.where(in_first, p_low, nothing), 0, 0) + dot_general(
            d_second, jnp.where(in_first, nothing, p_low), 0, 0
        )
        k_at = slice(g * HD, (g + 1) * HD)
        v_at = slice(key_width + g * HD, key_width + (g + 1) * HD)
        pair_ref[k_at, :] = d_k.astype(BF16)
        pair_ref[v_at, :] = d_v.astype(BF16)
        scaled_ref[k_at, :] = (d_k * scale_row).astype(BF16)
        scaled_ref[v_at, :] = (d_v * scale_row).astype(BF16)
        d_lk = dot_general(dsl, q, 0, 0)
        d_lv = dot_general(lat_first, d_first, 0, 0) + dot_general(lat_second, d_second, 0, 0)
        lat_ref[:latent_rows, query_width + g * HD : query_width + (g + 1) * HD] = d_lk.astype(BF16)
        at = query_width + key_width + g * HD
        lat_ref[:latent_rows, at : at + HD] = d_lv.astype(BF16)
    high = row_dot.astype(BF16)
    low = (row_dot - high.astype(F32)).astype(BF16)
    rest = pair_ref.shape[0] - 2 * key_width - 2
    pair_ref[2 * key_width :, :] = jnp.concatenate(
        [high.astype(F32), low.astype(F32), jnp.zeros((rest, patch_rows), F32)], axis=0
    ).astype(BF16)


def backward_kernel(
    slot_count,
    where_ref,
    counts_ref,
    got_own_ref,
    got_other_ref,
    hat_ref,
    inv_out_ref,
    gain_ref,
    routes_ref,
    w_out_ref,
    k_ref,
    v_ref,
    q_ref,
    lk_ref,
    lv_ref,
    p_ref,
    pl_ref,
    inv_row_ref,
    x_ref,
    line_own_ref,
    line_low_ref,
    line_high_ref,
    line_both_ref,
    pair_ref,
    lat_ref,
    value_going_ref,
    value_kept_ref,
    key_going_ref,
    key_kept_ref,
    d_final_ref,
    branch_ref,
    attn_acc,
    scaled_ref,
):
    step = pl.program_id(0)
    steps = pl.num_programs(0) // 2
    rows, width = hat_ref.shape
    half = width // 2
    columns = w_out_ref.shape[1]
    slots = got_own_ref.shape[0]
    latent_rows = lk_ref.shape[1]
    key_width = value_going_ref.shape[1]

    @pl.when(step == 0)
    def _():
        place = slots_of(routes_ref, slot_count, False)
        table = jnp.where(
            lax.broadcasted_iota(jnp.int32, (rows, slots), 1) == place, 1.0, 0.0
        ).astype(BF16)
        total = jnp.zeros((rows, 1), F32)
        chunk = 512
        for got_ref, which in ((got_own_ref, where_ref[1]), (got_other_ref, 1 - where_ref[1])):
            for c in range(half // chunk):
                at = pl.ds(pl.multiple_of(which * half + c * chunk, chunk), chunk)
                d_final = jnp.dot(
                    table, got_ref[:, c * chunk : (c + 1) * chunk], preferred_element_type=F32
                )
                product = d_final * hat_ref[:, at]
                total = total + jnp.sum(product * gain_ref[:, at], axis=-1, keepdims=True)
                d_final_ref[:, at] = d_final
        total = total / width
        lat_ref[latent_rows:, :] = jnp.zeros_like(lat_ref[latent_rows:, :])
        highs, lows = [], []
        part = width // 4
        for c in range(width // chunk):
            at = slice(c * chunk, (c + 1) * chunk)
            d_final = d_final_ref[:, at]
            hat = hat_ref[:, at]
            term = jnp.sum(d_final * hat, axis=0, keepdims=True)
            high = term.astype(BF16).astype(F32)
            highs.append(high)
            lows.append(term - high)
            branch_ref[:, at] = (
                inv_out_ref[...] * (d_final * gain_ref[:, at] - hat * total)
            ).astype(BF16)
        per_row = part // chunk
        lines = [
            jnp.concatenate(group[i * per_row : (i + 1) * per_row], axis=1)
            for group in (highs, lows)
            for i in range(4)
        ]
        lat_ref[latent_rows : latent_rows + 16, :part] = jnp.concatenate(
            lines + [jnp.zeros((8, part), F32)], axis=0
        ).astype(BF16)
        attn_acc[...] = jnp.zeros_like(attn_acc)
        z = where_ref[0] >> 2
        some = pl.ds(pl.multiple_of(where_ref[1] * (rows // 2), rows // 2), rows // 2)
        line_own_ref[...] = branch_ref[:, pl.ds(pl.multiple_of(z * part, part), part)]
        for turn, ref in ((1, line_low_ref), (2, line_high_ref), (3, line_both_ref)):
            ref[...] = branch_ref[some, pl.ds(pl.multiple_of((z ^ turn) * part, part), part)]

    @pl.when(step < steps)
    def _():
        at = pl.ds(pl.multiple_of(step * columns, columns), columns)
        attn_acc[...] += dot_general(branch_ref[:, at], w_out_ref[...], 1, 1)

    @pl.when(step == steps - 1)
    def _():
        attention_backward(
            counts_ref,
            attn_acc[...].astype(BF16),
            k_ref,
            v_ref,
            q_ref,
            lk_ref,
            lv_ref,
            p_ref,
            pl_ref,
            inv_row_ref,
            pair_ref,
            scaled_ref,
            lat_ref,
        )

    @pl.when(step >= steps)
    def _():
        own = x_ref.shape[1] // 2
        odd = where_ref[0] & 1
        far = x_ref[:, pl.ds(pl.multiple_of((1 - odd) * own, own), own)]
        near = x_ref[:, pl.ds(pl.multiple_of(odd * own, own), own)]
        far_grad = jnp.dot(scaled_ref[...], far, preferred_element_type=F32).astype(BF16)
        near_grad = jnp.dot(scaled_ref[...], near, preferred_element_type=F32).astype(BF16)
        value_going_ref[0] = far_grad[key_width:]
        value_kept_ref[0] = near_grad[key_width:]

        @pl.when(step < steps + steps // 2)
        def _():
            key_going_ref[0, 0] = far_grad[:key_width]
            key_going_ref[1, 0] = near_grad[:key_width]

        @pl.when(step >= steps + steps // 2)
        def _():
            key_kept_ref[0, 0] = far_grad[:key_width]
            key_kept_ref[1, 0] = near_grad[:key_width]


def backward_call(
    where, counts, got_own, got_other, hat, inv_out, gain_out, routes, w_out, kept, context, slot_count
):
    k, v, q, lk, lv, p, lat_p, inv_row = kept
    rows, width = hat.shape
    patch_rows = context.shape[0]
    heads = w_out.shape[0]
    groups = k.shape[0]
    key_width = groups * HD
    latent_rows = lk.shape[1]
    steps = 8
    columns = width // steps
    own = width // 16

    def x_block(i, where_ref):
        j = jnp.maximum(i - steps, 0)
        me = where_ref[0]
        y = ((me >> 1) & 1) ^ (1 - (j >> 2))
        low = 1 - ((j >> 1) & 1)
        high = 1 - (j & 1)
        z = (me >> 2) ^ (low + 2 * high)
        return (0, 2 * z + y)

    def turn(i):
        return jnp.maximum(i - steps, 0)

    lat_width = heads + 2 * key_width
    return pl.pallas_call(
        functools.partial(backward_kernel, slot_count),
        name="attention_backward",
        grid_spec=pltpu.PrefetchScalarGridSpec(
            num_scalar_prefetch=1,
            grid=(2 * steps,),
            in_specs=[
                pl.BlockSpec(memory_space=pltpu.SMEM),
                held(got_own.shape),
                held(got_other.shape),
                held(hat.shape),
                held(inv_out.shape),
                held((1, width)),
                held(routes.shape),
                pl.BlockSpec((heads, columns), lambda i, *_: (0, jnp.minimum(i, steps - 1))),
                held(k.shape),
                held(v.shape),
                held(q.shape),
                held(lk.shape),
                held(lv.shape),
                held(p.shape),
                held(lat_p.shape),
                held(inv_row.shape),
                pl.BlockSpec((patch_rows, 2 * own), x_block),
            ],
            out_specs=[
                held((rows, width // 4)),
                held((rows // 2, width // 4)),
                held((rows // 2, width // 4)),
                held((rows // 2, width // 4)),
                held((2 * key_width + 16, patch_rows)),
                held((latent_rows + 16, lat_width)),
                pl.BlockSpec((1, key_width, own), lambda i, *_: (turn(i), 0, 0)),
                pl.BlockSpec((1, key_width, own), lambda i, *_: (turn(i), 0, 0)),
                pl.BlockSpec(
                    (2, 1, key_width, own), lambda i, *_: (0, jnp.minimum(turn(i), 3), 0, 0)
                ),
                pl.BlockSpec(
                    (2, 1, key_width, own), lambda i, *_: (0, jnp.maximum(turn(i) - 4, 0), 0, 0)
                ),
            ],
            scratch_shapes=[
                pltpu.VMEM((rows, width), F32),
                pltpu.VMEM((rows, width), BF16),
                pltpu.VMEM((rows, heads), F32),
                pltpu.VMEM((2 * key_width, patch_rows), BF16),
            ],
        ),
        out_shape=[
            jax.ShapeDtypeStruct((rows, width // 4), BF16),
            jax.ShapeDtypeStruct((rows // 2, width // 4), BF16),
            jax.ShapeDtypeStruct((rows // 2, width // 4), BF16),
            jax.ShapeDtypeStruct((rows // 2, width // 4), BF16),
            jax.ShapeDtypeStruct((2 * key_width + 16, patch_rows), BF16),
            jax.ShapeDtypeStruct((latent_rows + 16, lat_width), BF16),
            jax.ShapeDtypeStruct((8, key_width, own), BF16),
            jax.ShapeDtypeStruct((8, key_width, own), BF16),
            jax.ShapeDtypeStruct((2, 4, key_width, own), BF16),
            jax.ShapeDtypeStruct((2, 4, key_width, own), BF16),
        ],
        cost_estimate=pl.CostEstimate(
            flops=5_000_000_000, bytes_accessed=26_000_000, transcendentals=0
        ),
        compiler_params=pltpu.CompilerParams(vmem_limit_bytes=VMEM_LIMIT),
    )(
        where,
        counts,
        got_own,
        got_other,
        hat,
        inv_out,
        gain_out.reshape(1, width),
        routes,
        w_out,
        k,
        v,
        q,
        lk,
        lv,
        p,
        lat_p,
        inv_row,
        context,
    )


def patch_kernel(
    width,
    mp_ref,
    own_ref,
    other_ref,
    wk_ref,
    wv_ref,
    wk_other_ref,
    wv_other_ref,
    x_ref,
    inv_row_ref,
    gain_ref,
    out_ref,
    turned_ref,
    inv_ref,
    dot_ref,
    w_ref,
):
    step = pl.program_id(0)
    key_width = wk_ref.shape[0]
    patch_rows = turned_ref.shape[0]
    pair = 2 * key_width

    @pl.when(step == 0)
    def _():
        row_dot = jnp.zeros((patch_rows, 1), F32)
        for i, ref in enumerate((own_ref, other_ref)):
            turned = jnp.transpose(ref[...])
            turned_ref[:, i * pair : (i + 1) * pair] = turned[:, :pair]
            row_dot = row_dot + turned[:, pair : pair + 1].astype(F32)
            row_dot = row_dot + turned[:, pair + 1 : pair + 2].astype(F32)
        inverse = jnp.transpose(jnp.broadcast_to(inv_row_ref[:1], (128, patch_rows)))[:, :1]
        inv_ref[...] = inverse
        dot_ref[...] = row_dot * (inverse * inverse / width)
        for i, ref in enumerate((wk_ref, wv_ref, wk_other_ref, wv_other_ref)):
            w_ref[i * key_width : (i + 1) * key_width, :] = ref[...]

    rows = x_ref.shape[0]
    at = pl.ds(pl.multiple_of(step * rows, rows), rows)
    d_in = jnp.dot(turned_ref[at, :], w_ref[...], preferred_element_type=F32)
    out_ref[...] = (
        d_in * gain_ref[...] * inv_ref[at, :] - x_ref[...].astype(F32) * dot_ref[at, :]
    ).astype(BF16)


def patch_call(mp_index, own, other, wk, wv, wk_other, wv_other, context, inv_row, gain_ctx):
    patch_rows, width = context.shape
    half = width // 2
    steps = 4
    rows = patch_rows // steps
    key_width = wk.shape[0]
    once = pl.Buffered(1)
    w_spec = pl.BlockSpec((key_width, half), lambda i, mp: (0, mp[0]), pipeline_mode=once)
    return pl.pallas_call(
        functools.partial(patch_kernel, width),
        name="patch_gradient",
        grid_spec=pltpu.PrefetchScalarGridSpec(
            num_scalar_prefetch=1,
            grid=(steps,),
            in_specs=[
                held(own.shape),
                held(other.shape),
                w_spec,
                w_spec,
                w_spec,
                w_spec,
                pl.BlockSpec((rows, half), lambda i, mp: (i, mp[0])),
                held(inv_row.shape),
                pl.BlockSpec((1, half), lambda i, mp: (0, mp[0])),
            ],
            out_specs=pl.BlockSpec((rows, half), lambda i, mp: (i, 0)),
            scratch_shapes=[
                pltpu.VMEM((patch_rows, 4 * key_width), BF16),
                pltpu.VMEM((patch_rows, 1), F32),
                pltpu.VMEM((patch_rows, 1), F32),
                pltpu.VMEM((4 * key_width, half), BF16),
            ],
        ),
        out_shape=jax.ShapeDtypeStruct((patch_rows, half), BF16),
        cost_estimate=pl.CostEstimate(
            flops=3_300_000_000, bytes_accessed=14_000_000, transcendentals=0
        ),
        compiler_params=pltpu.CompilerParams(vmem_limit_bytes=VMEM_LIMIT),
    )(mp_index, own, other, wk, wv, wk_other, wv_other, context, inv_row, gain_ctx.reshape(1, width))


def out_kernel(
    where_ref,
    a0_ref,
    a1_ref,
    a2_ref,
    a3_ref,
    d0_ref,
    d1_ref,
    d2_ref,
    d3_ref,
    e1_ref,
    e2_ref,
    e3_ref,
    first_going_ref,
    first_kept_ref,
    second_going_ref,
    second_kept_ref,
    attn_ref,
    line_ref,
    resid_ref,
):
    rows, heads = a0_ref.shape
    columns = line_ref.shape[1]
    own = columns // 4
    latent_rows = rows // 2
    mine = where_ref[1]
    for i, ref in enumerate((a0_ref, a1_ref, a2_ref, a3_ref)):
        attn_ref[i * rows : (i + 1) * rows, :] = ref[...]
    line_ref[:rows, :] = d0_ref[...]
    half = rows // 2
    for i, (ref, other) in enumerate(((d1_ref, e1_ref), (d2_ref, e2_ref), (d3_ref, e3_ref))):
        at = (i + 1) * rows
        line_ref[pl.ds(pl.multiple_of(at + mine * half, half), half), :] = ref[...]
        line_ref[pl.ds(pl.multiple_of(at + (1 - mine) * half, half), half), :] = other[...]
    resid = jnp.zeros((latent_rows, columns), F32)
    for i in range(8):
        resid = resid + line_ref[i * latent_rows : (i + 1) * latent_rows, :].astype(F32)
    resid_ref[...] = resid
    odd = where_ref[0] & 1
    upper = (where_ref[0] >> 1) & 1
    cut = heads // 2
    share = own // 2
    for turn in range(4):
        x_differs, y_differs = 1 - (turn & 1), 1 - (turn >> 1)
        owner = 2 * (upper ^ y_differs) + (odd ^ x_differs)
        at = pl.ds(pl.multiple_of(owner * own, own), own)
        grad = dot_general(attn_ref[...], line_ref[:, at], 0, 0).astype(BF16)
        mine_at = pl.ds(pl.multiple_of(owner * own + mine * share, share), share)
        part = resid_ref[:, mine_at]
        part = jnp.concatenate([part[: latent_rows // 2], part[latent_rows // 2 :]], axis=1)
        ref = first_going_ref if x_differs else first_kept_ref
        ref[1 - y_differs, :cut, :] = grad[:cut]
        ref[1 - y_differs, cut:, :] = part.astype(BF16)
        ref = second_going_ref if y_differs else second_kept_ref
        ref[1 - x_differs] = grad[cut:]


def out_call(where, attn, line, line_other):
    rows, heads = attn[0].shape
    columns = line[0].shape[1]
    own = columns // 4
    first = (2, heads // 2 + rows // 4, own)
    second = (2, heads // 2, own)
    shapes = [first, first, second, second]
    return pl.pallas_call(
        out_kernel,
        name="output_projection_gradient",
        grid_spec=pltpu.PrefetchScalarGridSpec(
            num_scalar_prefetch=1,
            grid=(1,),
            in_specs=[held(a.shape) for a in (*attn, *line, *line_other)],
            out_specs=[held(shape) for shape in shapes],
            scratch_shapes=[
                pltpu.VMEM((4 * rows, heads), BF16),
                pltpu.VMEM((4 * rows, columns), BF16),
                pltpu.VMEM((rows // 2, columns), F32),
            ],
        ),
        out_shape=[jax.ShapeDtypeStruct(shape, BF16) for shape in shapes],
        cost_estimate=pl.CostEstimate(
            flops=8 * rows * heads * columns, bytes_accessed=4_000_000, transcendentals=0
        ),
        compiler_params=pltpu.CompilerParams(vmem_limit_bytes=VMEM_LIMIT),
    )(where, *attn, *line, *line_other)


def latent_kernel(
    where_ref,
    sum_ref,
    got_ref,
    proj_ref,
    lat_ref,
    gain_ref,
    wq_ref,
    wk_ref,
    wv_ref,
    query_ref,
    pair_ref,
    message_ref,
    gain_out_ref,
    total_ref,
):
    latent_rows, width = lat_ref.shape
    own, query_width = wq_ref.shape
    key_width = wk_ref.shape[0]
    scaling = HD ** (-0.5)
    total_ref[...] = sum_ref[...] + got_ref[...].astype(F32)
    total = total_ref[:latent_rows, :]
    low = total.astype(BF16)
    at = pl.ds(pl.multiple_of(where_ref[0] * own, own), own)
    lat = lat_ref[...].astype(F32)
    inverse = lax.rsqrt(jnp.mean(lat * lat, axis=-1, keepdims=True) + EPSILON)
    gain = gain_ref[:, at]
    normed = (lat_ref[:, at].astype(F32) * inverse * gain).astype(BF16)
    query = dot_general(normed, low[:, :query_width], 0, 0) * scaling
    query_ref[...] = query
    pair = dot_general(low[:, query_width:], normed, 0, 0)
    pair_ref[...] = pair
    wq = wq_ref[...]
    wk = wk_ref[...]
    wv = wv_ref[...]
    gain_term = jnp.transpose(
        jnp.broadcast_to(jnp.sum(wq.astype(F32) * query, axis=1, keepdims=True), (own, 128))
    )[:1]
    gain_term = gain_term + jnp.sum(wk.astype(F32) * pair[:key_width], axis=0, keepdims=True)
    gain_term = gain_term + jnp.sum(wv.astype(F32) * pair[key_width:], axis=0, keepdims=True)
    scaled = (total[:, :query_width] * scaling).astype(BF16)
    d_lat = dot_general(scaled, wq, 1, 1)
    d_lat = d_lat + jnp.dot(
        low[:, query_width : query_width + key_width], wk, preferred_element_type=F32
    )
    d_lat = d_lat + jnp.dot(low[:, query_width + key_width :], wv, preferred_element_type=F32)
    message_ref[:latent_rows, :own] = d_lat
    message_ref[:latent_rows, own:] = jnp.broadcast_to(
        jnp.sum(total * proj_ref[...], axis=-1, keepdims=True), (latent_rows, 128)
    )
    message_ref[latent_rows:, :own] = jnp.broadcast_to(gain_term / gain, (8, own))
    message_ref[latent_rows:, own:] = jnp.zeros((8, 128), F32)
    part = width // 4
    share = own // 2
    first = where_ref[0] * own + where_ref[1] * share
    line = first // part
    mine = pl.ds(pl.multiple_of(first % part, share), share)
    gain_out_ref[...] = jnp.sum(
        jnp.where(
            lax.broadcasted_iota(jnp.int32, (8, share), 0) % 4 == line,
            total_ref[latent_rows : latent_rows + 8, mine],
            0.0,
        ),
        axis=0,
        keepdims=True,
    )


def latent_call(where, sums, got, proj, latents, gain_lat, w_query, wk, wv, own):
    latent_rows, width = latents.shape
    query_width = w_query.shape[1]
    key_width = wk.shape[0]
    return pl.pallas_call(
        latent_kernel,
        name="latent_gradients",
        grid_spec=pltpu.PrefetchScalarGridSpec(
            num_scalar_prefetch=1,
            grid=(1,),
            in_specs=[
                held(sums.shape),
                held(got.shape),
                held(proj.shape),
                held(latents.shape),
                held((1, width)),
                pl.BlockSpec((own, query_width), lambda i, w: (w[0], 0)),
                pl.BlockSpec((key_width, own), lambda i, w: (0, w[0])),
                pl.BlockSpec((key_width, own), lambda i, w: (0, w[0])),
            ],
            out_specs=[
                held((own, query_width)),
                held((2 * key_width, own)),
                held((latent_rows + 8, own + 128)),
                held((1, own // 2)),
            ],
            scratch_shapes=[pltpu.VMEM(sums.shape, F32)],
        ),
        out_shape=[
            jax.ShapeDtypeStruct((own, query_width), F32),
            jax.ShapeDtypeStruct((2 * key_width, own), F32),
            jax.ShapeDtypeStruct((latent_rows + 8, own + 128), F32),
            jax.ShapeDtypeStruct((1, own // 2), F32),
        ],
        cost_estimate=pl.CostEstimate(
            flops=100_000_000, bytes_accessed=3_000_000, transcendentals=0
        ),
        compiler_params=pltpu.CompilerParams(vmem_limit_bytes=VMEM_LIMIT),
    )(where, sums, got, proj, latents, gain_lat.reshape(1, width), w_query, wk, wv)


def plane_kernel(
    value_ref,
    value_got_ref,
    key_ref,
    key_got_ref,
    both_ref,
    low_ref,
    high_ref,
    kept_ref,
):
    key_width = value_ref.shape[1]
    for i, ref in enumerate((both_ref, low_ref, high_ref, kept_ref)):
        ref[:key_width, :] = (key_ref[i] + key_got_ref[i].astype(F32)).astype(ref.dtype)
        ref[key_width:, :] = (value_ref[i] + value_got_ref[i].astype(F32)).astype(ref.dtype)


def plane_call(value, value_got, key, key_got):
    _, key_width, own = value.shape
    shape = (2 * key_width, own)
    return pl.pallas_call(
        plane_kernel,
        name="plane_sum",
        out_shape=[jax.ShapeDtypeStruct(shape, BF16)] * 3 + [jax.ShapeDtypeStruct(shape, F32)],
        cost_estimate=pl.CostEstimate(flops=1_000_000, bytes_accessed=5_000_000, transcendentals=0),
        compiler_params=pltpu.CompilerParams(vmem_limit_bytes=VMEM_LIMIT),
    )(value, value_got, key, key_got)


def halve_kernel(kept_ref, got_ref, going_ref, rest_ref):
    half = going_ref.shape[0]
    going_ref[...] = (kept_ref[:half].astype(F32) + got_ref[:half].astype(F32)).astype(BF16)
    rest_ref[...] = kept_ref[half:].astype(F32) + got_ref[half:].astype(F32)


def halve_call(kept, got):
    shape = (kept.shape[0] // 2,) + kept.shape[1:]
    return pl.pallas_call(
        halve_kernel,
        name="halve_sum",
        out_shape=[jax.ShapeDtypeStruct(shape, BF16), jax.ShapeDtypeStruct(shape, F32)],
        cost_estimate=pl.CostEstimate(flops=1_000_000, bytes_accessed=4_000_000, transcendentals=0),
        compiler_params=pltpu.CompilerParams(vmem_limit_bytes=VMEM_LIMIT),
    )(kept, got)


def final_kernel(
    where_ref,
    kept_ref,
    both_ref,
    low_ref,
    high_ref,
    gain_ref,
    pair_ref,
    wk_ref,
    wv_ref,
    key_grad_ref,
    value_grad_ref,
    gain_term_ref,
):
    key_width = wk_ref.shape[0]
    total = (
        kept_ref[...]
        + both_ref[...].astype(F32)
        + low_ref[...].astype(F32)
        + high_ref[...].astype(F32)
    )
    term = jnp.sum(wk_ref[...].astype(F32) * total[:key_width], axis=0, keepdims=True)
    term = term + jnp.sum(wv_ref[...].astype(F32) * total[key_width:], axis=0, keepdims=True)
    gain_term_ref[...] = jnp.broadcast_to(term, gain_term_ref.shape)
    total = total * gain_ref[...] + pair_ref[...]
    key_grad_ref[...] = total[:key_width]
    value_grad_ref[...] = total[key_width:]


def final_call(where, kept, both, low, high, gain_ctx, pair, wk, wv):
    rows, own = kept.shape
    width = gain_ctx.shape[0]
    key_width = rows // 2
    w_spec = pl.BlockSpec((key_width, own), lambda i, w: (0, w[0]))
    return pl.pallas_call(
        final_kernel,
        name="key_value_gradients",
        grid_spec=pltpu.PrefetchScalarGridSpec(
            num_scalar_prefetch=1,
            grid=(1,),
            in_specs=[held(kept.shape)] * 4
            + [pl.BlockSpec((1, own), lambda i, w: (0, w[0])), held(pair.shape), w_spec, w_spec],
            out_specs=[held((key_width, own)), held((key_width, own)), held((8, own))],
        ),
        out_shape=[
            jax.ShapeDtypeStruct((key_width, own), F32),
            jax.ShapeDtypeStruct((key_width, own), F32),
            jax.ShapeDtypeStruct((8, own), F32),
        ],
        cost_estimate=pl.CostEstimate(flops=1_000_000, bytes_accessed=3_000_000, transcendentals=0),
        compiler_params=pltpu.CompilerParams(vmem_limit_bytes=VMEM_LIMIT),
    )(where, kept, both, low, high, gain_ctx.reshape(1, width), pair, wk, wv)


def local(
    context,
    counts,
    routes,
    w_query,
    w_key,
    w_value,
    w_out,
    latents,
    gain_ctx,
    gain_lat,
    gain_out,
    cotangent,
):
    dp_count = lax.axis_size("dp")
    mp_index = lax.axis_index("mp")
    dp_index = lax.axis_index("dp")
    patch_rows, width = context.shape
    half_width = width // 2
    own_width = width // dp_count
    latent_rows = latents.shape[0]
    slot_count = cotangent.shape[0] // dp_count
    slots = dp_count * slot_count
    query_width = w_query.shape[1]

    def swap(array, turn):
        return lax.ppermute(array, "dp", [(i, i ^ turn) for i in range(dp_count)])

    def exchange(array):
        blocks = array.reshape(dp_count, slot_count, half_width)
        return lax.all_to_all(blocks, "dp", split_axis=0, concat_axis=0, tiled=True).reshape(
            slots, half_width
        )

    wk = w_key.T
    wv = w_value.T
    turned_routes = routes.reshape(1, -1)
    mp_scalar = mp_index.reshape(1)
    where = jnp.stack([dp_index, mp_index])

    returned = exchange(cotangent)
    w_out_other = swap_cores(w_out)
    wk_other = swap_cores(wk)
    wv_other = swap_cores(wv)

    (attn_rows, k, v, inv_row, q, lat_k, lat_v, lat_proj, p, lat_p) = forward_call(
        context, counts, w_query, wk, wv, latents, gain_ctx, gain_lat
    )
    attn_other = swap_cores(attn_rows)
    attn_high = swap(attn_rows, 8)
    attn_low = swap(attn_rows, 4)
    attn_both = swap(attn_high, 4)
    out_hat, out_inv, outgoing = branch_call(
        mp_scalar,
        attn_rows,
        attn_other,
        w_out,
        w_out_other,
        latents,
        gain_out,
        turned_routes,
        slots,
        slot_count,
    )
    routed = exchange(outgoing)

    returned, out_inv = lax.optimization_barrier((returned, out_inv))
    returned_other = swap_cores(returned)
    (
        line_own,
        line_low,
        line_high,
        line_both,
        pair,
        lat_terms,
        value_going,
        value_kept,
        key_going,
        key_kept,
    ) = backward_call(
        where,
        counts,
        returned,
        returned_other,
        out_hat,
        out_inv,
        gain_out,
        turned_routes,
        w_out,
        (k, v, q, lat_k, lat_v, p, lat_p, inv_row),
        context,
        slot_count,
    )

    value_got = swap(value_going, 1)
    key_got = swap(key_going, 2)

    pair_other = swap_cores(pair)
    ctx_grad = patch_call(
        mp_scalar, pair, pair_other, wk, wv, wk_other, wv_other, context, inv_row, gain_ctx
    )

    got_low = swap(line_low, 4)
    got_high = swap(line_high, 8)
    got_both = swap(line_both, 12)

    lat_sum = lat_terms.astype(F32)
    for turn in (4, 8, 1):
        lat_sum = lat_sum + swap(lat_sum.astype(BF16), turn).astype(F32)
    lat_got = swap(lat_sum.astype(BF16), 2)

    value_going, value_kept = halve_call(value_kept, value_got)
    value_got = swap(value_going, 2)
    key_going, key_kept = halve_call(
        key_kept.reshape((8,) + key_kept.shape[2:]), key_got.reshape((8,) + key_got.shape[2:])
    )
    key_got = swap(key_going, 1)

    first_going, first_kept, second_going, second_kept = out_call(
        where,
        (attn_rows, attn_low, attn_high, attn_both),
        (line_own, got_low, got_high, got_both),
        (swap_cores(got_low), swap_cores(got_high), swap_cores(got_both)),
    )

    both, low, high, kept = plane_call(value_kept, value_got, key_kept, key_got)
    both = swap(both, 12)
    low = swap(low, 4)
    high = swap(high, 8)

    first_going, first_kept = halve_call(first_kept, swap(first_going, 1))
    second_going, second_kept = halve_call(second_kept, swap(second_going, 2))
    first = first_kept[0] + swap(first_going[0], 2).astype(F32)
    second = second_kept[0] + swap(second_going[0], 1).astype(F32)
    cut = query_width // 2
    grad_w_out = jnp.concatenate([first[:cut], second], axis=0)
    share = own_width // 2
    resid_sum = jnp.concatenate([first[cut:, :share], first[cut:, share:]], axis=0)

    grad_w_query, pair_lat, message, grad_gain_out = latent_call(
        where, lat_sum, lat_got, lat_proj, latents, gain_lat, w_query, wk, wv, own_width
    )
    message = message + swap_cores(message)

    grad_key, grad_value, gain_term = final_call(
        where, kept, both, low, high, gain_ctx, pair_lat, wk, wv
    )
    gain_term = gain_term + swap_cores(gain_term)

    def mine_of(array, axis):
        return lax.dynamic_slice_in_dim(
            array, dp_index * own_width + mp_index * share, share, axis
        )

    lat_hat, lat_inv = norm_parts(latents.astype(F32))
    mine = lax.dynamic_slice_in_dim(message, mp_index * share, share, 1)
    lat_dot = message[:latent_rows, own_width : own_width + 1] / width
    grad_latents = resid_sum + lat_inv * (
        mine_of(gain_lat, 0) * mine[:latent_rows] - mine_of(lat_hat, 1) * lat_dot
    )
    return (
        routed,
        ctx_grad,
        grad_w_query,
        grad_key.T,
        grad_value.T,
        grad_w_out,
        grad_latents,
        lax.dynamic_slice_in_dim(gain_term, mp_index * share, share, 1)[0],
        mine[latent_rows],
        grad_gain_out[0],
    )


def local_general(
    context,
    counts,
    routes,
    w_query,
    w_key,
    w_value,
    w_out,
    latents,
    gain_ctx,
    gain_lat,
    gain_out,
    cotangent,
):
    dp_count = lax.axis_size("dp")
    mp_count = lax.axis_size("mp")
    mp_index = lax.axis_index("mp")
    dp_index = lax.axis_index("dp")
    bits = dp_count.bit_length() - 1
    gather_bits = [bits - 1, bits - 2]
    scatter_bits = list(range(bits - 2))
    order_one = list(range(bits))
    order_two = [1, 0] + order_one[2:]
    patch_rows, width = context.shape
    half_width = width // mp_count
    own_width = width // dp_count
    head_local = w_query.shape[1] // HD
    group_local = w_key.shape[1] // HD
    per_group = head_local // group_local
    latent_rows = latents.shape[0]
    image_slots = counts.shape[1]
    out_rows = image_slots * latent_rows
    slot_count = cotangent.shape[0] // dp_count
    key_width = w_key.shape[1]
    query_width = w_query.shape[1]
    scaling = HD ** (-0.5)

    returned = lax.all_to_all(
        cotangent.reshape(dp_count, slot_count, half_width),
        "dp",
        split_axis=0,
        concat_axis=0,
        tiled=True,
    ).reshape(dp_count * slot_count, half_width)
    returned_other = swap_cores(returned)
    w_out_other = swap_cores(w_out)
    w_pair = jnp.concatenate([w_key, w_value], axis=1)
    w_pair_half = lax.dynamic_slice_in_dim(w_pair, mp_index * half_width, half_width, 0)
    w_pair_other = swap_cores(
        lax.dynamic_slice_in_dim(w_pair, (1 - mp_index) * half_width, half_width, 0)
    )

    patch_hat, patch_inv = norm_parts(context.astype(F32))
    normed_ctx = (patch_hat * gain_ctx).astype(BF16)
    key_f32 = jnp.dot(normed_ctx, w_key, preferred_element_type=F32)
    value_f32 = jnp.dot(normed_ctx, w_value, preferred_element_type=F32)
    key_rows = key_f32.astype(BF16)
    value_rows = value_f32.astype(BF16)
    lat_float = latents.astype(F32)
    lat_hat, lat_inv = norm_parts(lat_float)
    normed_lat = (lat_hat * gain_lat).astype(BF16)
    lat_key_f32 = jnp.dot(normed_lat, w_key, preferred_element_type=F32)
    lat_value_f32 = jnp.dot(normed_lat, w_value, preferred_element_type=F32)
    lat_keys = lat_key_f32.astype(BF16)
    lat_values = lat_value_f32.astype(BF16)
    query_f32 = jnp.dot(normed_lat, w_query, preferred_element_type=F32) * scaling
    query_rows = query_f32.astype(BF16)
    query_heads = query_rows.reshape(latent_rows, group_local, per_group, HD)
    key_heads = key_rows.reshape(patch_rows, group_local, HD)
    value_heads = value_rows.reshape(patch_rows, group_local, HD)
    lat_key_heads = lat_keys.reshape(latent_rows, group_local, HD)
    lat_value_heads = lat_values.reshape(latent_rows, group_local, HD)
    scores = jnp.einsum(
        "rkgd,tkd->kgrt", query_heads, key_heads, preferred_element_type=jnp.float32
    )
    lat_scores = jnp.einsum(
        "rkgd,skd->kgrs", query_heads, lat_key_heads, preferred_element_type=jnp.float32
    )
    position = jnp.arange(patch_rows, dtype=jnp.int32)
    image_count = counts[0]
    image_start = jnp.cumsum(image_count) - image_count
    member = (position[None, :] >= image_start[:, None]) & (
        position[None, :] < (image_start + image_count)[:, None]
    )
    member_wide = member[:, None, None, None, :]
    masked = jnp.where(member_wide, scores[None], NEGATIVE)
    row_max = jnp.maximum(
        jnp.max(masked, axis=-1, keepdims=True), jnp.max(lat_scores, axis=-1, keepdims=True)[None]
    )
    exponent = jnp.where(member_wide, jnp.exp(masked - row_max), 0.0)
    lat_exponent = jnp.exp(lat_scores[None] - row_max)
    total = jnp.sum(exponent, axis=-1, keepdims=True) + jnp.sum(
        lat_exponent, axis=-1, keepdims=True
    )
    attention = exponent / total
    lat_attention = lat_exponent / total
    attention_low = attention.astype(BF16)
    lat_attention_low = lat_attention.astype(BF16)
    mixed = jnp.einsum(
        "ikgrt,tkd->irkgd", attention_low, value_heads, preferred_element_type=jnp.float32
    )
    mixed = mixed + jnp.einsum(
        "ikgrs,skd->irkgd", lat_attention_low, lat_value_heads, preferred_element_type=jnp.float32
    )
    attn_rows = mixed.reshape(out_rows, query_width).astype(BF16)
    attn_other = swap_cores(attn_rows)
    branch = jnp.dot(attn_rows, w_out, preferred_element_type=F32) + jnp.dot(
        attn_other, w_out_other, preferred_element_type=F32
    )
    resid = jnp.tile(lat_float, (image_slots, 1)) + branch
    out_hat, out_inv = norm_parts(resid)
    final_rows = (out_hat * gain_out).astype(BF16)
    shard_of = routes[:, 0]
    shard_hot = (shard_of[:, None] == jnp.arange(dp_count, dtype=jnp.int32)[None, :]).astype(
        jnp.int32
    )
    rank = jnp.sum((jnp.cumsum(shard_hot, axis=0) - shard_hot) * shard_hot, axis=1)
    place = shard_of * slot_count + rank
    scatter_table = (
        jnp.arange(dp_count * slot_count, dtype=jnp.int32)[:, None] == place[None, :]
    ).astype(BF16)
    final_half = lax.dynamic_slice_in_dim(final_rows, mp_index * half_width, half_width, 1)
    outgoing = jnp.dot(scatter_table, final_half, preferred_element_type=F32).astype(BF16)
    routed = lax.all_to_all(
        outgoing.reshape(dp_count, slot_count, half_width),
        "dp",
        split_axis=0,
        concat_axis=0,
        tiled=True,
    ).reshape(dp_count * slot_count, half_width)

    attn_line = attn_rows
    for bit in gather_bits:
        attn_line = jnp.concatenate([attn_line, swap_bit(attn_line, bit, dp_count)], axis=0)

    first = jnp.where(mp_index == 0, returned, returned_other)
    second = jnp.where(mp_index == 0, returned_other, returned)
    d_final = jnp.concatenate(
        [dot_general(scatter_table, first, 0, 0), dot_general(scatter_table, second, 0, 0)], axis=1
    )
    d_hat = d_final * gain_out
    d_resid = out_inv * (d_hat - out_hat * jnp.mean(d_hat * out_hat, axis=1, keepdims=True))
    gain_out_term = jnp.sum(d_final * out_hat, axis=0)
    d_branch = d_resid.astype(BF16)
    d_attn = dot_general(d_branch, w_out, 1, 1).astype(BF16)

    d_attn_heads = d_attn.reshape(image_slots, latent_rows, group_local, per_group, HD)
    d_probs = jnp.einsum(
        "irkgd,tkd->ikgrt", d_attn_heads, value_heads, preferred_element_type=jnp.float32
    )
    d_lat_probs = jnp.einsum(
        "irkgd,skd->ikgrs", d_attn_heads, lat_value_heads, preferred_element_type=jnp.float32
    )
    row_delta = jnp.sum(attention * d_probs, axis=-1, keepdims=True) + jnp.sum(
        lat_attention * d_lat_probs, axis=-1, keepdims=True
    )
    d_scores = jnp.sum(attention * (d_probs - row_delta), axis=0).astype(BF16)
    d_lat_scores = jnp.sum(lat_attention * (d_lat_probs - row_delta), axis=0).astype(BF16)
    d_query = jnp.einsum("kgrt,tkd->rkgd", d_scores, key_heads, preferred_element_type=jnp.float32)
    d_query = d_query + jnp.einsum(
        "kgrs,skd->rkgd", d_lat_scores, lat_key_heads, preferred_element_type=jnp.float32
    )
    d_query = d_query.reshape(latent_rows, query_width).astype(BF16)
    d_keys = jnp.einsum("kgrt,rkgd->tkd", d_scores, query_heads, preferred_element_type=jnp.float32)
    d_keys = d_keys.reshape(patch_rows, key_width).astype(BF16)
    d_values = jnp.einsum(
        "ikgrt,irkgd->tkd", attention_low, d_attn_heads, preferred_element_type=jnp.float32
    )
    d_values = d_values.reshape(patch_rows, key_width).astype(BF16)
    d_lat_keys = jnp.einsum(
        "kgrs,rkgd->skd", d_lat_scores, query_heads, preferred_element_type=jnp.float32
    )
    d_lat_keys = d_lat_keys.reshape(latent_rows, key_width).astype(BF16)
    d_lat_values = jnp.einsum(
        "ikgrs,irkgd->skd", lat_attention_low, d_attn_heads, preferred_element_type=jnp.float32
    )
    d_lat_values = d_lat_values.reshape(latent_rows, key_width).astype(BF16)
    d_pair = jnp.concatenate([d_keys, d_values], axis=1)

    value_grad = dot_general(d_values, normed_ctx, 0, 0).reshape(key_width, dp_count, own_width)
    key_grad = dot_general(d_keys, normed_ctx, 0, 0).reshape(key_width, dp_count, own_width)
    value_block = scatter_sum(value_grad, order_one, dp_count)
    key_block = scatter_sum(key_grad, order_two, dp_count)

    row_dot = jnp.sum(d_keys.astype(F32) * key_f32, axis=1) + jnp.sum(
        d_values.astype(F32) * value_f32, axis=1
    )
    row_dot = (row_dot + swap_cores(row_dot)) / width
    d_pair_other = swap_cores(d_pair)
    d_ctx_in = dot_general(d_pair, w_pair_half, 1, 1) + dot_general(
        d_pair_other, w_pair_other, 1, 1
    )
    gain_ctx_half = lax.dynamic_slice_in_dim(gain_ctx, mp_index * half_width, half_width, 0)
    hat_half = lax.dynamic_slice_in_dim(patch_hat, mp_index * half_width, half_width, 1)
    ctx_grad = (patch_inv * (d_ctx_in * gain_ctx_half - hat_half * row_dot[:, None])).astype(BF16)

    high = gain_out_term.astype(BF16)
    low = (gain_out_term - high.astype(F32)).astype(BF16)
    lat_sum = jnp.concatenate(
        [
            d_query,
            d_lat_keys,
            d_lat_values,
            high.reshape(latent_rows, width // latent_rows),
            low.reshape(latent_rows, width // latent_rows),
        ],
        axis=1,
    ).astype(F32)
    for bit in gather_bits + scatter_bits:
        lat_sum = lat_sum + swap_bit(lat_sum.astype(BF16), bit, dp_count).astype(F32)
    pair_sum = lat_sum[:, query_width : query_width + 2 * key_width]
    query_sum = lat_sum[:, :query_width]
    gains_at = query_width + 2 * key_width
    gain_step = width // latent_rows
    gain_out_full = (
        lat_sum[:, gains_at : gains_at + gain_step]
        + lat_sum[:, gains_at + gain_step : gains_at + 2 * gain_step]
    ).reshape(width)

    plane = dp_count // 4
    row_half = out_rows // mp_count
    d_block = lax.dynamic_slice_in_dim(d_branch, mp_index * row_half, row_half, 0)
    d_line = d_block.reshape(1, row_half, 2, 2, plane * own_width)
    for step, bit in enumerate(gather_bits):
        mine = (dp_index >> bit) & 1
        going = lax.dynamic_index_in_dim(d_line, 1 - mine, 2, keepdims=False)
        kept = lax.dynamic_index_in_dim(d_line, mine, 2, keepdims=False)
        d_line = jnp.concatenate([kept, swap_bit(going, bit, dp_count)], axis=0)
    d_line_other = swap_cores(d_line)
    d_line = jnp.concatenate(
        [
            jnp.where(mp_index == 0, d_line, d_line_other),
            jnp.where(mp_index == 0, d_line_other, d_line),
        ],
        axis=1,
    )
    out_part = dot_general(attn_line, d_line.reshape(4 * out_rows, plane * own_width), 0, 0)
    resid_part = jnp.sum(
        d_line.astype(F32).reshape(4 * image_slots, latent_rows, plane * own_width), axis=0
    )
    resid_part = lax.dynamic_index_in_dim(
        resid_part.reshape(2, latent_rows // 2, plane, mp_count, own_width // mp_count),
        mp_index,
        3,
        keepdims=False,
    )
    resid_part = jnp.transpose(resid_part, (1, 2, 0, 3)).reshape(
        latent_rows // 2, plane, own_width
    )
    out_part = jnp.concatenate([out_part.reshape(query_width, plane, own_width), resid_part], axis=0)
    cut = out_part.shape[0] // 2
    out_block = jnp.concatenate(
        [
            scatter_sum(out_part[:cut], scatter_bits, dp_count),
            scatter_sum(out_part[cut:], [1, 0] + scatter_bits[2:], dp_count),
        ],
        axis=0,
    )
    grad_w_out = out_block[:query_width]
    resid_sum = (
        out_block[query_width:]
        .reshape(latent_rows // 2, 2, own_width // mp_count)
        .transpose(1, 0, 2)
        .reshape(latent_rows, own_width // mp_count)
    )

    def own(array, axis):
        return lax.dynamic_slice_in_dim(array, dp_index * own_width, own_width, axis)

    lat_own = own(normed_lat, 1)
    pair_ctx = jnp.concatenate([key_block, value_block], axis=0).T
    query_grad = dot_general(lat_own, query_sum.astype(BF16), 0, 0) * scaling
    pair_lat = dot_general(lat_own, pair_sum.astype(BF16), 0, 0)
    pair_all = pair_ctx + pair_lat
    wq_own = own(w_query, 0)
    pair_own = own(w_pair, 0)
    gain_ctx_part = jnp.sum(pair_own.astype(F32) * pair_ctx, axis=1) / own(gain_ctx, 0)
    gain_lat_part = (
        jnp.sum(wq_own.astype(F32) * query_grad, axis=1)
        + jnp.sum(pair_own.astype(F32) * pair_lat, axis=1)
    ) / own(gain_lat, 0)
    d_lat_part = dot_general(
        (query_sum * scaling).astype(BF16), wq_own, 1, 1
    ) + dot_general(pair_sum.astype(BF16), pair_own, 1, 1)
    lat_dot_part = (
        jnp.sum(query_sum * query_f32, axis=1)
        + jnp.sum(pair_sum[:, :key_width] * lat_key_f32, axis=1)
        + jnp.sum(pair_sum[:, key_width:] * lat_value_f32, axis=1)
    )
    small = jnp.concatenate(
        [
            d_lat_part,
            jnp.broadcast_to(lat_dot_part[:, None], (latent_rows, own_width)),
            jnp.broadcast_to(gain_ctx_part[None, :], (8, own_width)),
            jnp.broadcast_to(gain_lat_part[None, :], (8, own_width)),
        ],
        axis=0,
    )
    small = small + swap_cores(small)
    share = own_width // mp_count
    small = lax.dynamic_slice_in_dim(small, mp_index * share, share, 1)
    d_lat_in = small[:latent_rows]
    lat_dot = small[latent_rows : 2 * latent_rows] / width

    def mine_of(array, axis):
        return lax.dynamic_slice_in_dim(
            array, dp_index * own_width + mp_index * share, share, axis
        )

    grad_latents = resid_sum + lat_inv * (
        mine_of(gain_lat, 0) * d_lat_in - mine_of(lat_hat, 1) * lat_dot
    )
    return (
        routed,
        ctx_grad,
        query_grad,
        pair_all[:, :key_width],
        pair_all[:, key_width:],
        grad_w_out,
        grad_latents,
        small[2 * latent_rows],
        small[2 * latent_rows + 8],
        mine_of(gain_out_full, 0),
    )


def solution(mesh):
    placed = (
        P("dp", None),
        P("dp", None),
        P("dp", None),
        P(None, "mp"),
        P(None, "mp"),
        P(None, "mp"),
        P("mp", None),
        P(),
        P(),
        P(),
        P(),
        P("dp", "mp"),
    )
    return jax.shard_map(
        local if mesh.shape["dp"] == 16 else local_general,
        mesh=mesh,
        in_specs=placed,
        out_specs=(
            P("dp", "mp"),
            P("dp", "mp"),
            P("dp", "mp"),
            P("dp", "mp"),
            P("dp", "mp"),
            P("mp", "dp"),
            P(None, ("dp", "mp")),
            P(("dp", "mp")),
            P(("dp", "mp")),
            P(("dp", "mp")),
        ),
        check_vma=False,
    )
```

profile of v0, /device:TPU:0, one launch (start us, length us, event | category | flops | bytes accessed | tf_op | source)
XLA Modules:
  0.0 205.6 jit_solution(15545845039489096944)
XLA Ops:
  1.2 7.9 %all-to-all-start.1 = ((bf16[16,16,2048]{2,1,0:T(8,128)(2,1)}), bf16[16,16,2048]{2,1,0:T(8,128)(2,1)}, u32[]{:S(2)}, u32[]{:S(2)}) async-start(bf16[16,16,2048]{2,1,0:T(8,128)(2,1)} %bitcast.37), calls=%async_computation.1 | async-start | bytes 2097152 | tf_op jit(solution)/shard_map/all_to_all | solution.py:1126
  9.1 17.3 %forward_attention.1 = (bf16[128,768]{1,0:T(8,128)(2,1)}, bf16[2,1024,96]{2,1,0:T(8,128)(2,1)}, bf16[2,1024,96]{2,1,0:T(8,128)(2,1)}, f32[8,1024]{1,0:T(8,128)},...) custom-call(s32[1,2]{1,0:T(1,128)} %counts_ref.3, ...), custom_call_target="tpu_custom_call" | custom-call | flops 5000000000 | bytes 24000000 | tf_op jit(solution)/shard_map/forward_attention/pallas_call | solution.py:217
  28.8 11.0 %branch_norm.1 = (f32[128,4096]{1,0:T(8,128)}, f32[128,1]{1,0:T(8,128)}, bf16[256,2048]{1,0:T(8,128)(2,1)}) custom-call(s32[1]{0:T(128)} %bitcast.mp_ref, bf16[128,768]{1,0:T(8,128)(2,1)} %get-tuple-element.58.own_ref.a0_ref, bf16[128,768]{1,0:T(8,128)(2,1)} %copy-done.5, bf16[768,4096]{1,0:T(8,128)(2,1)} %w_out_ref.1, ...), custom_call_target="tpu_custom_call" | custom-call | flops 1610612736 | bytes 16000000 | tf_op jit(solution)/shard_map/branch_norm/pallas_call | solution.py:324
  42.8 24.3 %attention_backward.1 = (bf16[128,1024]{1,0:T(8,128)(2,1)}, bf16[64,1024]{1,0:T(8,128)(2,1)}, bf16[64,1024]{1,0:T(8,128)(2,1)}, bf16[64,1024]{1,0:T(8,128)(2,1)}...) custom-call(s32[2]{0:T(128)} %pad_add_fusion.where_ref, ...), custom_call_target="tpu_custom_call" | custom-call | flops 5000000000 | bytes 26000000 | tf_op jit(solution)/shard_map/attention_backward/pallas_call | solution.py:630
  69.0 2.4 %collective-permute-start.18 = (bf16[128,768]{1,0:T(8,128)(2,1)}, bf16[128,768]{1,0:T(8,128)(2,1)S(1)}, u32[]{:S(2)}, u32[]{:S(2)}) collective-permute-start(bf16[128,768]{1,0:T(8,128)(2,1)} %get-tuple-element.58.own_ref.a0_ref), channel_id=1, source_target_pairs={{0,16},{2,18},{4,20},{6,22},{8,24},{10,26},{12,28},{14,30},{16,0},... | collective-permute-start | bytes 589832 | tf_op jit(solution)/shard_map/ppermute | solution.py:1122
  71.4 6.5 %collective-permute-done.6 = bf16[80,1152]{1,0:T(8,128)(2,1)S(1)} collective-permute-done((bf16[80,1152]{1,0:T(8,128)(2,1)}, bf16[80,1152]{1,0:T(8,128)(2,1)S(1)}, u32[]{:S(2)}, u32[]{:S(2)}) %collective-permute-start.6) | collective-permute-done | bytes 184352 | tf_op jit(solution)/shard_map/ppermute | solution.py:1122
  79.8 2.4 %collective-permute-start.20 = (bf16[64,1024]{1,0:T(8,128)(2,1)}, bf16[64,1024]{1,0:T(8,128)(2,1)S(1)}, u32[]{:S(2)}, u32[]{:S(2)}) collective-permute-start(bf16[64,1024]{1,0:T(8,128)(2,1)} %get-tuple-element.92), channel_id=1, source_target_pairs={{0,8},{2,10},{4,12},{6,14},{8,0},{10,2},{12,4},{14,6},{16,24},{18,... | collective-permute-start | bytes 393224 | tf_op jit(solution)/shard_map/ppermute | solution.py:1122
  87.7 2.4 %collective-permute-start.19 = (bf16[128,768]{1,0:T(8,128)(2,1)S(1)}, bf16[128,768]{1,0:T(8,128)(2,1)S(1)}, u32[]{:S(2)}, u32[]{:S(2)}) collective-permute-start(bf16[128,768]{1,0:T(8,128)(2,1)S(1)} %collective-permute-done.18.a2_ref), channel_id=1, source_target_pairs={{0,8},{2,10},{4,12},{6,14},{8,0},{10,2},{12,4},{14,6},{16,24},{18,... | collective-permute-start | bytes 589832 | tf_op jit(solution)/shard_map/ppermute | solution.py:1122
  90.1 8.1 %collective-permute-done.21.d2_ref = bf16[64,1024]{1,0:T(8,128)(2,1)S(1)} collective-permute-done((bf16[64,1024]{1,0:T(8,128)(2,1)}, bf16[64,1024]{1,0:T(8,128)(2,1)S(1)}, u32[]{:S(2)}, u32[]{:S(2)}) %collective-permute-start.21) | collective-permute-done | bytes 131104 | tf_op jit(solution)/shard_map/ppermute | solution.py:1122
  105.3 4.6 %output_projection_gradient.1 = (bf16[2,416,256]{2,1,0:T(8,128)(2,1)}, bf16[2,416,256]{2,1,0:T(8,128)(2,1)}, bf16[2,384,256]{2,1,0:T(8,128)(2,1)}, bf16[2,384,256]{2,1,0:T(8,128)(2,1)}) custom-call(s32[2]{0:T(128)} %pad_add_fusion.where_ref, bf16[128,768]{1,0:T(8,128)(2,1)} %get-tuple-element.58.own_ref.a0_ref, bf16[128,768]{1,0:T(8,128)(2,1)} %copy-done.9, ...), custom_call_target="tpu_custom_call" | custom-call | flops 805306368 | bytes 4000000 | tf_op jit(solution)/shard_map/output_projection_gradient/pallas_call | solution.py:866
  115.3 8.4 %collective-permute-done.28.got_ref = bf16[2,384,256]{2,1,0:T(8,128)(2,1)} collective-permute-done((bf16[2,384,256]{2,1,0:T(8,128)(2,1)}, bf16[2,384,256]{2,1,0:T(8,128)(2,1)}, u32[]{:S(2)}, u32[]{:S(2)}) %collective-permute-start.28) | collective-permute-done | bytes 393248 | tf_op jit(solution)/shard_map/ppermute | solution.py:1122
  129.1 4.9 %all-to-all-start = ((bf16[16,16,2048]{2,1,0:T(8,128)(2,1)}), bf16[16,16,2048]{2,1,0:T(8,128)(2,1)}, u32[]{:S(2)}, u32[]{:S(2)}) async-start(bf16[16,16,2048]{2,1,0:T(8,128)(2,1)} %bitcast.38), calls=%async_computation | async-start | bytes 2097152 | tf_op jit(solution)/shard_map/all_to_all | solution.py:1126
  138.2 3.7 %latent_gradients.1 = (f32[256,768]{1,0:T(8,128)}, f32[384,256]{1,0:T(8,128)}, f32[72,384]{1,0:T(8,128)}, f32[1,128]{1,0:T(1,128)}) custom-call(s32[2]{0:T(128)} %pad_add_fusion.where_ref, f32[80,1152]{1,0:T(8,128)} %get-tuple-element.107.sum_ref, bf16[80,1152]{1,0:T(8,128)(2,1)} %copy-done.6, f32[64,1152]{1,0:T(8,128)} %get-tuple-element.74.proj_ref, ...), custom_call_target="tpu_custom_call" | custom-call | flops 100000000 | bytes 3000000 | tf_op jit(solution)/shard_map/latent_gradients/pallas_call | solution.py:960
  141.9 8.8 %collective-permute-done.12 = bf16[2,4,192,256]{3,2,1,0:T(8,128)(2,1)} collective-permute-done((bf16[2,4,192,256]{3,2,1,0:T(8,128)(2,1)}, bf16[2,4,192,256]{3,2,1,0:T(8,128)(2,1)}, u32[]{:S(2)}, u32[]{:S(2)}) %collective-permute-start.12) | collective-permute-done | bytes 786464 | tf_op jit(solution)/shard_map/ppermute | solution.py:1122
  150.8 2.6 %halve_sum.5 = (bf16[4,192,256]{2,1,0:T(8,128)(2,1)}, f32[4,192,256]{2,1,0:T(8,128)}) custom-call(bf16[8,192,256]{2,1,0:T(8,128)(2,1)} %bitcast.39, bf16[8,192,256]{2,1,0:T(8,128)(2,1)} %bitcast.13.got_ref), custom_call_target="tpu_custom_call" | custom-call | flops 1000000 | bytes 4000000 | tf_op jit(solution)/shard_map/halve_sum/pallas_call | solution.py:1033
  153.4 2.6 %collective-permute-start.27 = (bf16[416,256]{1,0:T(8,128)(2,1)}, bf16[416,256]{1,0:T(8,128)(2,1)}, u32[]{:S(2)}, u32[]{:S(2)}) collective-permute-start(bf16[416,256]{1,0:T(8,128)(2,1)} %bitcast.17), channel_id=1, source_target_pairs={{0,4},{2,6},{4,0},{6,2},{8,12},{10,14},{12,8},{14,10},{16,20},{18,... | collective-permute-start | bytes 638984 | tf_op jit(solution)/shard_map/ppermute | solution.py:1122
  156.0 2.5 %halve_sum.4 = (bf16[4,192,256]{2,1,0:T(8,128)(2,1)}, f32[4,192,256]{2,1,0:T(8,128)}) custom-call(bf16[8,192,256]{2,1,0:T(8,128)(2,1)} %get-tuple-element.76.kept_ref, bf16[8,192,256]{2,1,0:T(8,128)(2,1)} %collective-permute-done.10.got_ref), custom_call_target="tpu_custom_call" | custom-call | flops 1000000 | bytes 4000000 | tf_op jit(solution)/shard_map/halve_sum/pallas_call | solution.py:1033
  160.6 9.6 %patch_gradient.1 = bf16[1024,2048]{1,0:T(8,128)(2,1)} custom-call(s32[1]{0:T(128)} %bitcast.mp_ref, bf16[400,1024]{1,0:T(8,128)(2,1)} %get-tuple-element.72.own_ref, bf16[400,1024]{1,0:T(8,128)(2,1)} %collective-permute-done.3.other_ref, bf16[192,4096]{1,0:T(8,128)(2,1)} %bitcast.30, bf16[192,4096]{1,0:T(8,128)(2,1)} %bitcast.35, ...), custom_call_target="tpu_custom_call" | custom-call | flops 3300000000 | bytes 14000000 | tf_op jit(solution)/shard_map/patch_gradient/pallas_call | solution.py:769
  174.6 2.6 %plane_sum.1 = (bf16[384,256]{1,0:T(8,128)(2,1)}, bf16[384,256]{1,0:T(8,128)(2,1)}, bf16[384,256]{1,0:T(8,128)(2,1)}, f32[384,256]{1,0:T(8,128)}) custom-call(f32[4,192,256]{2,1,0:T(8,128)} %get-tuple-element.78.value_ref, bf16[4,192,256]{2,1,0:T(8,128)(2,1)} %collective-permute-done.11.value_got_ref, f32[4,192,256]{2,1,0:T(8,128)} %get-tuple-element.82.key_ref, ...), custom_call_target="tpu_custom_call" | custom-call | flops 1000000 | bytes 5000000 | tf_op jit(solution)/shard_map/plane_sum/pallas_call | solution.py:1016
  183.0 4.1 %collective-permute-done.14.both_ref = bf16[384,256]{1,0:T(8,128)(2,1)} collective-permute-done((bf16[384,256]{1,0:T(8,128)(2,1)}, bf16[384,256]{1,0:T(8,128)(2,1)}, u32[]{:S(2)}, u32[]{:S(2)}) %collective-permute-start.14) | collective-permute-done | bytes 196640 | tf_op jit(solution)/shard_map/ppermute | solution.py:1122
  187.1 3.5 %collective-permute-done.15.low_ref = bf16[384,256]{1,0:T(8,128)(2,1)} collective-permute-done((bf16[384,256]{1,0:T(8,128)(2,1)}, bf16[384,256]{1,0:T(8,128)(2,1)}, u32[]{:S(2)}, u32[]{:S(2)}) %collective-permute-start.15) | collective-permute-done | bytes 196640 | tf_op jit(solution)/shard_map/ppermute | solution.py:1122
  190.6 7.2 %collective-permute-done.16.high_ref = bf16[384,256]{1,0:T(8,128)(2,1)} collective-permute-done((bf16[384,256]{1,0:T(8,128)(2,1)}, bf16[384,256]{1,0:T(8,128)(2,1)}, u32[]{:S(2)}, u32[]{:S(2)}) %collective-permute-start.16) | collective-permute-done | bytes 196640 | tf_op jit(solution)/shard_map/ppermute | solution.py:1122
  197.8 2.9 %key_value_gradients.1 = (f32[192,256]{1,0:T(8,128)}, f32[192,256]{1,0:T(8,128)}, f32[8,256]{1,0:T(8,128)}) custom-call(s32[2]{0:T(128)} %pad_add_fusion.where_ref, f32[384,256]{1,0:T(8,128)} %get-tuple-element.84.kept_ref, bf16[384,256]{1,0:T(8,128)(2,1)} %collective-permute-done.14.both_ref, bf16[384,256]{1,0:T(8,128)(2,1)} %collective-permute-done.15.low_ref, ...), custom_call_target="tpu_custom_call" | custom-call | flops 1000000 | bytes 3000000 | tf_op jit(solution)/shard_map/key_value_gradients/pallas_call | solution.py:1076
  203.3 2.3 %copy.23 = bf16[256,2048]{1,0:T(8,128)(2,1)} copy(bf16[256,2048]{1,0:T(8,128)(2,1)} %bitcast.8) | data formatting | bytes 2097152
  (110 shorter events, 52.4 us)
Async XLA Ops:
  0.6 27.5 %collective-permute-start.1 = (bf16[768,4096]{1,0:T(8,128)(2,1)}, bf16[768,4096]{1,0:T(8,128)(2,1)}, u32[]{:S(2)}, u32[]{:S(2)}) collective-permute-start(bf16[768,4096]{1,0:T(8,128)(2,1)} %w_out_ref.1), channel_id=1, source_target_pairs={{0,1},{1,0},{2,3},{3,2},{4,5},{5,4},{6,7},{7,6},{8,9},{9,8},{10,11... | collective-permute-start | bytes 18874376 | tf_op jit(solution)/shard_map/ppermute | solution.py:30
  1.2 38.6 %all-to-all-start.1 = ((bf16[16,16,2048]{2,1,0:T(8,128)(2,1)}), bf16[16,16,2048]{2,1,0:T(8,128)(2,1)}, u32[]{:S(2)}, u32[]{:S(2)}) async-start(bf16[16,16,2048]{2,1,0:T(8,128)(2,1)} %bitcast.37), calls=%async_computation.1 | async-start | bytes 2097152 | tf_op jit(solution)/shard_map/all_to_all | solution.py:1126
  69.0 15.5 %collective-permute-start.18 = (bf16[128,768]{1,0:T(8,128)(2,1)}, bf16[128,768]{1,0:T(8,128)(2,1)S(1)}, u32[]{:S(2)}, u32[]{:S(2)}) collective-permute-start(bf16[128,768]{1,0:T(8,128)(2,1)} %get-tuple-element.58.own_ref.a0_ref), channel_id=1, source_target_pairs={{0,16},{2,18},{4,20},{6,22},{8,24},{10,26},{12,28},{14,30},{16,0},... | collective-permute-start | bytes 589832 | tf_op jit(solution)/shard_map/ppermute | solution.py:1122
  78.8 19.9 %collective-permute-start.7 = (bf16[80,1152]{1,0:T(8,128)(2,1)S(1)}, bf16[80,1152]{1,0:T(8,128)(2,1)S(1)}, u32[]{:S(2)}, u32[]{:S(2)}) collective-permute-start(bf16[80,1152]{1,0:T(8,128)(2,1)S(1)} %fusion), channel_id=1, source_target_pairs={{0,16},{2,18},{4,20},{6,22},{8,24},{10,26},{12,28},{14,30},{16,0},... | collective-permute-start | bytes 552968 | tf_op jit(solution)/shard_map/ppermute | solution.py:1122
  82.2 16.0 %collective-permute-start.21 = (bf16[64,1024]{1,0:T(8,128)(2,1)}, bf16[64,1024]{1,0:T(8,128)(2,1)S(1)}, u32[]{:S(2)}, u32[]{:S(2)}) collective-permute-start(bf16[64,1024]{1,0:T(8,128)(2,1)} %get-tuple-element.93), channel_id=1, source_target_pairs={{0,16},{2,18},{4,20},{6,22},{8,24},{10,26},{12,28},{14,30},{16,0},... | collective-permute-start | bytes 393224 | tf_op jit(solution)/shard_map/ppermute | solution.py:1122
  82.2 16.0 %collective-permute-start.22 = (bf16[64,1024]{1,0:T(8,128)(2,1)}, bf16[64,1024]{1,0:T(8,128)(2,1)S(1)}, u32[]{:S(2)}, u32[]{:S(2)}) collective-permute-start(bf16[64,1024]{1,0:T(8,128)(2,1)} %get-tuple-element.94), channel_id=1, source_target_pairs={{0,24},{2,26},{4,28},{6,30},{8,16},{10,18},{12,20},{14,22},{16,8},... | collective-permute-start | bytes 393224 | tf_op jit(solution)/shard_map/ppermute | solution.py:1122
  84.5 16.6 %collective-permute-start.17 = (bf16[128,768]{1,0:T(8,128)(2,1)}, bf16[128,768]{1,0:T(8,128)(2,1)S(1)}, u32[]{:S(2)}, u32[]{:S(2)}) collective-permute-start(bf16[128,768]{1,0:T(8,128)(2,1)} %get-tuple-element.58.own_ref.a0_ref), channel_id=1, source_target_pairs={{0,8},{2,10},{4,12},{6,14},{8,0},{10,2},{12,4},{14,6},{16,24},{18,... | collective-permute-start | bytes 589832 | tf_op jit(solution)/shard_map/ppermute | solution.py:1122
  87.7 15.5 %collective-permute-start.19 = (bf16[128,768]{1,0:T(8,128)(2,1)S(1)}, bf16[128,768]{1,0:T(8,128)(2,1)S(1)}, u32[]{:S(2)}, u32[]{:S(2)}) collective-permute-start(bf16[128,768]{1,0:T(8,128)(2,1)S(1)} %collective-permute-done.18.a2_ref), channel_id=1, source_target_pairs={{0,8},{2,10},{4,12},{6,14},{8,0},{10,2},{12,4},{14,6},{16,24},{18,... | collective-permute-start | bytes 589832 | tf_op jit(solution)/shard_map/ppermute | solution.py:1122
  103.2 55.3 %collective-permute-start.4 = (bf16[192,4096]{1,0:T(8,128)(2,1)}, bf16[192,4096]{1,0:T(8,128)(2,1)}, u32[]{:S(2)}, u32[]{:S(2)}) collective-permute-start(bf16[192,4096]{1,0:T(8,128)(2,1)} %bitcast.28), channel_id=1, source_target_pairs={{0,1},{1,0},{2,3},{3,2},{4,5},{5,4},{6,7},{7,6},{8,9},{9,8},{10,11... | collective-permute-start | bytes 4718600 | tf_op jit(solution)/shard_map/ppermute | solution.py:30
  103.9 54.6 %collective-permute-start.5 = (bf16[192,4096]{1,0:T(8,128)(2,1)}, bf16[192,4096]{1,0:T(8,128)(2,1)}, u32[]{:S(2)}, u32[]{:S(2)}) collective-permute-start(bf16[192,4096]{1,0:T(8,128)(2,1)} %bitcast.33), channel_id=1, source_target_pairs={{0,1},{1,0},{2,3},{3,2},{4,5},{5,4},{6,7},{7,6},{8,9},{9,8},{10,11... | collective-permute-start | bytes 4718600 | tf_op jit(solution)/shard_map/ppermute | solution.py:30
  109.9 13.8 %collective-permute-start.26 = (bf16[2,416,256]{2,1,0:T(8,128)(2,1)}, bf16[2,416,256]{2,1,0:T(8,128)(2,1)}, u32[]{:S(2)}, u32[]{:S(2)}) collective-permute-start(bf16[2,416,256]{2,1,0:T(8,128)(2,1)} %get-tuple-element.96), channel_id=1, source_target_pairs={{0,2},{2,0},{4,6},{6,4},{8,10},{10,8},{12,14},{14,12},{16,18},{18,... | collective-permute-start | bytes 1277960 | tf_op jit(solution)/shard_map/ppermute | solution.py:1122
  111.4 12.3 %collective-permute-start.28 = (bf16[2,384,256]{2,1,0:T(8,128)(2,1)}, bf16[2,384,256]{2,1,0:T(8,128)(2,1)}, u32[]{:S(2)}, u32[]{:S(2)}) collective-permute-start(bf16[2,384,256]{2,1,0:T(8,128)(2,1)} %get-tuple-element.100), channel_id=1, source_target_pairs={{0,4},{2,6},{4,0},{6,2},{8,12},{10,14},{12,8},{14,10},{16,20},{18,... | collective-permute-start | bytes 1179656 | tf_op jit(solution)/shard_map/ppermute | solution.py:1122
  114.7 12.1 %collective-permute-start.9 = (bf16[80,1152]{1,0:T(8,128)(2,1)S(1)}, bf16[80,1152]{1,0:T(8,128)(2,1)S(1)}, u32[]{:S(2)}, u32[]{:S(2)}) collective-permute-start(bf16[80,1152]{1,0:T(8,128)(2,1)S(1)} %get-tuple-element.106), channel_id=1, source_target_pairs={{0,4},{2,6},{4,0},{6,2},{8,12},{10,14},{12,8},{14,10},{16,20},{18,... | collective-permute-start | bytes 552968 | tf_op jit(solution)/shard_map/ppermute | solution.py:1122
  123.6 36.9 %collective-permute-start.3 = (bf16[400,1024]{1,0:T(8,128)(2,1)}, bf16[400,1024]{1,0:T(8,128)(2,1)}, u32[]{:S(2)}, u32[]{:S(2)}) collective-permute-start(bf16[400,1024]{1,0:T(8,128)(2,1)} %get-tuple-element.72.own_ref), channel_id=1, source_target_pairs={{0,1},{1,0},{2,3},{3,2},{4,5},{5,4},{6,7},{7,6},{8,9},{9,8},{10,11... | collective-permute-start | bytes 2457608 | tf_op jit(solution)/shard_map/ppermute | solution.py:30
  123.6 27.1 %collective-permute-start.12 = (bf16[2,4,192,256]{3,2,1,0:T(8,128)(2,1)}, bf16[2,4,192,256]{3,2,1,0:T(8,128)(2,1)}, u32[]{:S(2)}, u32[]{:S(2)}) collective-permute-start(bf16[2,4,192,256]{3,2,1,0:T(8,128)(2,1)} %get-tuple-element.81), channel_id=1, source_target_pairs={{0,4},{2,6},{4,0},{6,2},{8,12},{10,14},{12,8},{14,10},{16,20},{18,... | collective-permute-start | bytes 2359304 | tf_op jit(solution)/shard_map/ppermute | solution.py:1122
  126.7 26.7 %collective-permute-start.10 = (bf16[8,192,256]{2,1,0:T(8,128)(2,1)}, bf16[8,192,256]{2,1,0:T(8,128)(2,1)}, u32[]{:S(2)}, u32[]{:S(2)}) collective-permute-start(bf16[8,192,256]{2,1,0:T(8,128)(2,1)} %get-tuple-element.77), channel_id=1, source_target_pairs={{0,2},{2,0},{4,6},{6,4},{8,10},{10,8},{12,14},{14,12},{16,18},{18,... | collective-permute-start | bytes 2359304 | tf_op jit(solution)/shard_map/ppermute | solution.py:1122
  129.1 72.6 %all-to-all-start = ((bf16[16,16,2048]{2,1,0:T(8,128)(2,1)}), bf16[16,16,2048]{2,1,0:T(8,128)(2,1)}, u32[]{:S(2)}, u32[]{:S(2)}) async-start(bf16[16,16,2048]{2,1,0:T(8,128)(2,1)} %bitcast.38), calls=%async_computation | async-start | bytes 2097152 | tf_op jit(solution)/shard_map/all_to_all | solution.py:1126
  150.8 21.0 %collective-permute-start.29 = (bf16[384,256]{1,0:T(8,128)(2,1)}, bf16[384,256]{1,0:T(8,128)(2,1)S(1)}, u32[]{:S(2)}, u32[]{:S(2)}) collective-permute-start(bf16[384,256]{1,0:T(8,128)(2,1)} %bitcast.19), channel_id=1, source_target_pairs={{0,2},{2,0},{4,6},{6,4},{8,10},{10,8},{12,14},{14,12},{16,18},{18,... | collective-permute-start | bytes 589832 | tf_op jit(solution)/shard_map/ppermute | solution.py:1122
  153.4 20.1 %collective-permute-start.27 = (bf16[416,256]{1,0:T(8,128)(2,1)}, bf16[416,256]{1,0:T(8,128)(2,1)}, u32[]{:S(2)}, u32[]{:S(2)}) collective-permute-start(bf16[416,256]{1,0:T(8,128)(2,1)} %bitcast.17), channel_id=1, source_target_pairs={{0,4},{2,6},{4,0},{6,2},{8,12},{10,14},{12,8},{14,10},{16,20},{18,... | collective-permute-start | bytes 638984 | tf_op jit(solution)/shard_map/ppermute | solution.py:1122
  158.5 11.7 %collective-permute-start.30 = (f32[72,384]{1,0:T(8,128)}, f32[72,384]{1,0:T(8,128)}, u32[]{:S(2)}, u32[]{:S(2)}) collective-permute-start(f32[72,384]{1,0:T(8,128)} %get-tuple-element.103), channel_id=1, source_target_pairs={{0,1},{1,0},{2,3},{3,2},{4,5},{5,4},{6,7},{7,6},{8,9},{9,8},{10,11... | collective-permute-start | bytes 331784 | tf_op jit(solution)/shard_map/ppermute | solution.py:30
  158.5 16.1 %collective-permute-start.13 = (bf16[4,192,256]{2,1,0:T(8,128)(2,1)}, bf16[4,192,256]{2,1,0:T(8,128)(2,1)}, u32[]{:S(2)}, u32[]{:S(2)}) collective-permute-start(bf16[4,192,256]{2,1,0:T(8,128)(2,1)} %get-tuple-element.83), channel_id=1, source_target_pairs={{0,2},{2,0},{4,6},{6,4},{8,10},{10,8},{12,14},{14,12},{16,18},{18,... | collective-permute-start | bytes 1179656 | tf_op jit(solution)/shard_map/ppermute | solution.py:1122
  160.6 14.0 %collective-permute-start.11 = (bf16[4,192,256]{2,1,0:T(8,128)(2,1)}, bf16[4,192,256]{2,1,0:T(8,128)(2,1)}, u32[]{:S(2)}, u32[]{:S(2)}) collective-permute-start(bf16[4,192,256]{2,1,0:T(8,128)(2,1)} %get-tuple-element.79), channel_id=1, source_target_pairs={{0,4},{2,6},{4,0},{6,2},{8,12},{10,14},{12,8},{14,10},{16,20},{18,... | collective-permute-start | bytes 1179656 | tf_op jit(solution)/shard_map/ppermute | solution.py:1122
  178.5 12.1 %collective-permute-start.15 = (bf16[384,256]{1,0:T(8,128)(2,1)}, bf16[384,256]{1,0:T(8,128)(2,1)}, u32[]{:S(2)}, u32[]{:S(2)}) collective-permute-start(bf16[384,256]{1,0:T(8,128)(2,1)} %get-tuple-element.86), channel_id=1, source_target_pairs={{0,8},{2,10},{4,12},{6,14},{8,0},{10,2},{12,4},{14,6},{16,24},{18,... | collective-permute-start | bytes 589832 | tf_op jit(solution)/shard_map/ppermute | solution.py:1122
  180.2 17.6 %collective-permute-start.16 = (bf16[384,256]{1,0:T(8,128)(2,1)}, bf16[384,256]{1,0:T(8,128)(2,1)}, u32[]{:S(2)}, u32[]{:S(2)}) collective-permute-start(bf16[384,256]{1,0:T(8,128)(2,1)} %get-tuple-element.87), channel_id=1, source_target_pairs={{0,16},{2,18},{4,20},{6,22},{8,24},{10,26},{12,28},{14,30},{16,0},... | collective-permute-start | bytes 589832 | tf_op jit(solution)/shard_map/ppermute | solution.py:1122
  (27 other events, 254.4 us)
where the time goes:
time: 207 us; the launch traced here: 206 us
  Pallas kernels  85 us (41%)
  waiting for transfers between devices  55.1 us (27%)
  starting transfers between devices  44 us (21%)
  other arithmetic  12.5 us (6%)
  local copies, waits for them, and re-layouts  8.09 us (4%)
    ppermute x21, waiting for transfers between devices, swap(): return lax.ppermute(array, 'dp', [(i, i ^ turn) for i in range(dp_count)])  51 us
    ppermute x21, starting transfers between devices, swap(): return lax.ppermute(array, 'dp', [(i, i ^ turn) for i in range(dp_count)])  29.6 us
    pallas_call x1, Pallas kernels, backward_call(): pl.pallas_call(functools.partial(backward_kernel, slot_count), name='atte...  24.3 us
    pallas_call x1, Pallas kernels, forward_call(): pl.pallas_call(forward_kernel, name='forward_attention', grid=(steps,), i...  17.3 us
    all_to_all x2, starting transfers between devices, exchange(): lax.all_to_all(blocks, 'dp', split_axis=0, concat_axis=0, tiled=True)  12.8 us
    pallas_call x1, Pallas kernels, branch_call(): pl.pallas_call(functools.partial(branch_kernel, slot_count), name='branch...  11 us
    pallas_call x1, Pallas kernels, patch_call(): pl.pallas_call(functools.partial(patch_kernel, width), name='patch_gradie...  9.62 us
    pallas_call x4, Pallas kernels, halve_call(): pl.pallas_call(halve_kernel, name='halve_sum', out_shape=[jax.ShapeDtypeS...  9.04 us
  transfers between devices with their start and end apart: 34, of which 14 were waited for; matrix products, arithmetic and copies ran while one was open for 6% of the time, Pallas kernels for 30%

commit v1 on v0

--- a/solution.py
+++ b/solution.py
@@ -54,13 +54,28 @@
 
 def forward_kernel(
     counts_ref,
-    x_ref,
+    gain_ctx_ref,
+    gain_lat_ref,
+    lat_hbm,
+    wk_hbm,
+    wv_hbm,
+    x_hbm,
+    wq_hbm,
+    attn_hbm,
+    k_hbm,
+    v_hbm,
+    inv_row_hbm,
+    q_hbm,
+    lk_hbm,
+    lv_hbm,
+    lat_proj_hbm,
+    p_hbm,
+    pl_hbm,
+    lat_ref,
     wk_ref,
     wv_ref,
+    x_ref,
     wq_ref,
-    lat_ref,
-    gain_ctx_ref,
-    gain_lat_ref,
     attn_ref,
     k_ref,
     v_ref,
@@ -72,116 +87,163 @@
     p_ref,
     pl_ref,
     lat_normed_ref,
-    query_acc,
+    last_ref,
     gained_ref,
+    sems,
+    out_sems,
 ):
-    step = pl.program_id(0)
-    steps = pl.num_programs(0)
-    rows, width = x_ref.shape
-    slab = wq_ref.shape[0]
-    groups, patch_rows, _ = k_ref.shape
+    patch_rows, width = x_ref.shape
+    chunks = sems.shape[0] - 4
+    rows = patch_rows // chunks
+    groups = k_ref.shape[0]
     latent_rows = lat_ref.shape[0]
     key_width = wk_ref.shape[0]
     query_width = wq_ref.shape[1]
     per_group = query_width // key_width
 
-    @pl.when(step == 0)
-    def _():
-        lat = lat_ref[...].astype(F32)
-        inverse = lax.rsqrt(jnp.mean(lat * lat, axis=-1, keepdims=True) + EPSILON)
-        lat_normed_ref[...] = (lat * inverse * gain_lat_ref[...]).astype(BF16)
-        for i, ref in enumerate((wk_ref, wv_ref)):
-            projected = dot_general(lat_normed_ref[...], ref[...], 1, 1)
-            at = query_width + i * key_width
-            lat_proj_ref[:, at : at + key_width] = projected
-            for g in range(groups):
-                (lk_ref, lv_ref)[i][g] = projected[:, g * HD : (g + 1) * HD].astype(BF16)
-            gained_ref[i * key_width : (i + 1) * key_width, :] = (
-                ref[...].astype(F32) * gain_ctx_ref[...]
-            ).astype(BF16)
-        query_acc[...] = jnp.zeros_like(query_acc)
-
-    squares = jnp.zeros((rows, 128), F32)
-    for c in range(width // 128):
-        part = x_ref[:, c * 128 : (c + 1) * 128].astype(F32)
-        squares = squares + part * part
-    inverse = lax.rsqrt(jnp.sum(squares, axis=-1, keepdims=True) / width + EPSILON)
-    pair = (dot_general(x_ref[...], gained_ref[...], 1, 1) * inverse).astype(BF16)
-    at = pl.ds(pl.multiple_of(step * rows, rows), rows)
-    inv_row_ref[:, at] = jnp.transpose(jnp.broadcast_to(inverse, (rows, 128)))[:8]
+    def fetch(source, target, i):
+        return pltpu.make_async_copy(source, target, sems.at[i])
+
+    def fetch_rows(i):
+        at = pl.ds(i * rows, rows)
+        return fetch(x_hbm.at[at], x_ref.at[at], i)
+
+    weights = [
+        fetch(source, target, chunks + i)
+        for i, (source, target) in enumerate(
+            ((lat_hbm, lat_ref), (wk_hbm, wk_ref), (wv_hbm, wv_ref), (wq_hbm, wq_ref))
+        )
+    ]
+    for copy in weights[:3]:
+        copy.start()
+    blocks = [fetch_rows(i) for i in range(chunks)]
+    for copy in blocks + weights[3:]:
+        copy.start()
+    results = {}
+    for i, (name, source, target) in enumerate(
+        (
+            ("attn", attn_ref, attn_hbm),
+            ("k", k_ref, k_hbm),
+            ("v", v_ref, v_hbm),
+            ("inv_row", inv_row_ref, inv_row_hbm),
+            ("q", q_ref, q_hbm),
+            ("lk", lk_ref, lk_hbm),
+            ("lv", lv_ref, lv_hbm),
+            ("lat_proj", lat_proj_ref, lat_proj_hbm),
+            ("p0", p_ref.at[0], p_hbm.at[0]),
+            ("p1", p_ref.at[1], p_hbm.at[1]),
+            ("pl", pl_ref, pl_hbm),
+        )
+    ):
+        results[name] = pltpu.make_async_copy(source, target, out_sems.at[i])
+
+    weights[0].wait()
+    lat = lat_ref[...].astype(F32)
+    lat_inverse = lax.rsqrt(jnp.mean(lat * lat, axis=-1, keepdims=True) + EPSILON)
+    lat_normed = lat * lat_inverse * gain_lat_ref[...]
+    lat_normed_ref[...] = lat_normed.astype(BF16)
+    last_ref[rows:, :] = (lat_normed / gain_ctx_ref[...]).astype(BF16)
+    for i, ref in enumerate((wk_ref, wv_ref)):
+        weights[1 + i].wait()
+        gained_ref[i * key_width : (i + 1) * key_width, :] = (
+            ref[...].astype(F32) * gain_ctx_ref[...]
+        ).astype(BF16)
+    for i in range(chunks):
+        blocks[i].wait()
+        at = slice(i * rows, (i + 1) * rows)
+        squares = jnp.zeros((rows, 128), F32)
+        for c in range(width // 128):
+            part = x_ref[at, c * 128 : (c + 1) * 128].astype(F32)
+            squares = squares + part * part
+        inverse = lax.rsqrt(jnp.sum(squares, axis=-1, keepdims=True) / width + EPSILON)
+        if i < chunks - 1:
+            pair = dot_general(x_ref[at, :], gained_ref[...], 1, 1)
+        else:
+            last_ref[:rows, :] = x_ref[at, :]
+            pair = dot_general(last_ref[...], gained_ref[...], 1, 1)
+            projected = pair[rows:]
+        pair = (pair[:rows] * inverse).astype(BF16)
+        inv_row_ref[:, at] = jnp.transpose(jnp.broadcast_to(inverse, (rows, 128)))[:8]
+        for g in range(groups):
+            k_ref[g, at, :HD] = pair[:, g * HD : (g + 1) * HD]
+            v_ref[g, at, :HD] = pair[:, key_width + g * HD : key_width + (g + 1) * HD]
+    lat_proj_ref[:, query_width:] = projected
+    for i, ref in enumerate((lk_ref, lv_ref)):
+        for g in range(groups):
+            at = i * key_width + g * HD
+            ref[g, :, :HD] = projected[:, at : at + HD].astype(BF16)
+    for name in ("k", "v", "inv_row", "lk", "lv"):
+        results[name].start()
+    weights[3].wait()
+    query = jnp.dot(lat_normed_ref[...], wq_ref[...], preferred_element_type=F32) * HD ** (-0.5)
+    lat_proj_ref[:, :query_width] = query
+    first_count = counts_ref[0, 0]
+    both_count = first_count + counts_ref[0, 1]
+    position = lax.broadcasted_iota(jnp.int32, (1, patch_rows), 1)
+    in_first = position < first_count
+    in_second = jnp.logical_and(position >= first_count, position < both_count)
+    rows_at = lax.broadcasted_iota(jnp.int32, (patch_rows, HD), 0)
+    row_first = rows_at < first_count
+    row_second = jnp.logical_and(rows_at >= first_count, rows_at < both_count)
     for g in range(groups):
-        k_ref[g, at, :] = pair[:, g * HD : (g + 1) * HD]
-        v_ref[g, at, :] = pair[:, key_width + g * HD : key_width + (g + 1) * HD]
-    query_acc[...] += jnp.dot(
-        lat_normed_ref[:, pl.ds(pl.multiple_of(step * slab, slab), slab)],
-        wq_ref[...],
-        preferred_element_type=F32,
-    )
-
-    @pl.when(step == steps - 1)
-    def _():
-        query = query_acc[...] * HD ** (-0.5)
-        lat_proj_ref[:, :query_width] = query
-        stacked = per_group * latent_rows
-        first_count = counts_ref[0, 0]
-        both_count = first_count + counts_ref[0, 1]
-        position = lax.broadcasted_iota(jnp.int32, (1, patch_rows), 1)
-        in_first = position < first_count
-        in_second = jnp.logical_and(position >= first_count, position < both_count)
-        rows_at = lax.broadcasted_iota(jnp.int32, (patch_rows, HD), 0)
-        row_first = rows_at < first_count
-        row_second = jnp.logical_and(rows_at >= first_count, rows_at < both_count)
-        for g in range(groups):
+        for h in range(per_group):
+            head = g * per_group + h
+            q_ref[g, h * latent_rows : (h + 1) * latent_rows, :HD] = query[
+                :, head * HD : (head + 1) * HD
+            ].astype(BF16)
+    results["lat_proj"].start()
+    results["q"].start()
+    for g in range(groups):
+        q = q_ref[g, :, :HD]
+        scores = dot_general(q, k_ref[g, :, :HD], 1, 1)
+        lat_scores = dot_general(q, lk_ref[g, :, :HD], 1, 1)
+        lat_max = jnp.max(lat_scores, axis=-1, keepdims=True)
+        max_first = jnp.maximum(
+            jnp.max(jnp.where(in_first, scores, NEGATIVE), axis=-1, keepdims=True), lat_max
+        )
+        max_second = jnp.maximum(
+            jnp.max(jnp.where(in_second, scores, NEGATIVE), axis=-1, keepdims=True), lat_max
+        )
+        masked = jnp.where(
+            in_first, scores - max_first, jnp.where(in_second, scores - max_second, NEGATIVE)
+        )
+        exponent = jnp.exp(masked)
+        lat_first = jnp.exp(lat_scores - max_first)
+        lat_second = jnp.exp(lat_scores - max_second)
+        sum_first = jnp.sum(
+            jnp.where(in_first, exponent, 0.0), axis=-1, keepdims=True
+        ) + jnp.sum(lat_first, axis=-1, keepdims=True)
+        sum_second = jnp.sum(
+            jnp.where(in_second, exponent, 0.0), axis=-1, keepdims=True
+        ) + jnp.sum(lat_second, axis=-1, keepdims=True)
+        per_first = 1.0 / sum_first
+        per_second = 1.0 / sum_second
+        p = (exponent * jnp.where(in_first, per_first, per_second)).astype(BF16)
+        p_ref[g] = p
+        results[f"p{g}"].start()
+        lat_p_first = (lat_first * per_first).astype(BF16)
+        lat_p_second = (lat_second * per_second).astype(BF16)
+        pl_ref[g, :, :latent_rows] = lat_p_first
+        pl_ref[g, :, latent_rows:] = lat_p_second
+        v = v_ref[g, :, :HD]
+        zero = jnp.zeros_like(v)
+        lv = lv_ref[g, :, :HD]
+        for j, (row_mask, lat_p) in enumerate(
+            ((row_first, lat_p_first), (row_second, lat_p_second))
+        ):
+            mixed = jnp.dot(
+                p, jnp.where(row_mask, v, zero), preferred_element_type=F32
+            ) + jnp.dot(lat_p, lv, preferred_element_type=F32)
+            mixed = mixed.astype(BF16)
             for h in range(per_group):
                 head = g * per_group + h
-                q_ref[g, h * latent_rows : (h + 1) * latent_rows, :] = query[
-                    :, head * HD : (head + 1) * HD
-                ].astype(BF16)
-            q = q_ref[g]
-            scores = dot_general(q, k_ref[g], 1, 1)
-            lat_scores = dot_general(q, lk_ref[g], 1, 1)
-            lat_max = jnp.max(lat_scores, axis=-1, keepdims=True)
-            max_first = jnp.maximum(
-                jnp.max(jnp.where(in_first, scores, NEGATIVE), axis=-1, keepdims=True), lat_max
-            )
-            max_second = jnp.maximum(
-                jnp.max(jnp.where(in_second, scores, NEGATIVE), axis=-1, keepdims=True), lat_max
-            )
-            masked = jnp.where(
-                in_first, scores - max_first, jnp.where(in_second, scores - max_second, NEGATIVE)
-            )
-            exponent = jnp.exp(masked)
-            lat_first = jnp.exp(lat_scores - max_first)
-            lat_second = jnp.exp(lat_scores - max_second)
-            sum_first = jnp.sum(
-                jnp.where(in_first, exponent, 0.0), axis=-1, keepdims=True
-            ) + jnp.sum(lat_first, axis=-1, keepdims=True)
-            sum_second = jnp.sum(
-                jnp.where(in_second, exponent, 0.0), axis=-1, keepdims=True
-            ) + jnp.sum(lat_second, axis=-1, keepdims=True)
-            per_first = 1.0 / sum_first
-            per_second = 1.0 / sum_second
-            p = (exponent * jnp.where(in_first, per_first, per_second)).astype(BF16)
-            p_ref[g] = p
-            lat_p_first = (lat_first * per_first).astype(BF16)
-            lat_p_second = (lat_second * per_second).astype(BF16)
-            pl_ref[g, 0] = lat_p_first
-            pl_ref[g, 1] = lat_p_second
-            v = v_ref[g]
-            zero = jnp.zeros_like(v)
-            lv = lv_ref[g]
-            for j, (row_mask, lat_p) in enumerate(
-                ((row_first, lat_p_first), (row_second, lat_p_second))
-            ):
-                mixed = jnp.dot(
-                    p, jnp.where(row_mask, v, zero), preferred_element_type=F32
-                ) + jnp.dot(lat_p, lv, preferred_element_type=F32)
-                mixed = mixed.astype(BF16)
-                for h in range(per_group):
-                    head = g * per_group + h
-                    attn_ref[
-                        j * latent_rows : (j + 1) * latent_rows, head * HD : (head + 1) * HD
-                    ] = mixed[h * latent_rows : (h + 1) * latent_rows]
+                attn_ref[
+                    j * latent_rows : (j + 1) * latent_rows, head * HD : (head + 1) * HD
+                ] = mixed[h * latent_rows : (h + 1) * latent_rows]
+    for name in ("attn", "pl"):
+        results[name].start()
+    for copy in results.values():
+        copy.wait()
 
 
 def whole(shape):
@@ -194,61 +256,50 @@
 
 def forward_call(context, counts, w_query, w_key, w_value, latents, gain_ctx, gain_lat):
     patch_rows, width = context.shape
-    steps = 4
-    rows = patch_rows // steps
-    slab = width // steps
+    chunks = 4
     key_width = w_key.shape[0]
     query_width = w_query.shape[1]
     groups = key_width // HD
     latent_rows = latents.shape[0]
     stacked = query_width // key_width * latent_rows
+    large = (latents, w_key, w_value, context, w_query)
     out = [
         ((2 * latent_rows, query_width), BF16),
-        ((groups, patch_rows, HD), BF16),
-        ((groups, patch_rows, HD), BF16),
+        ((groups, patch_rows, 128), BF16),
+        ((groups, patch_rows, 128), BF16),
         ((8, patch_rows), F32),
-        ((groups, stacked, HD), BF16),
-        ((groups, latent_rows, HD), BF16),
-        ((groups, latent_rows, HD), BF16),
+        ((groups, stacked, 128), BF16),
+        ((groups, latent_rows, 128), BF16),
+        ((groups, latent_rows, 128), BF16),
         ((latent_rows, query_width + 2 * key_width), F32),
         ((groups, stacked, patch_rows), BF16),
-        ((groups, 2, stacked, latent_rows), BF16),
+        ((groups, stacked, 2 * latent_rows), BF16),
     ]
     return pl.pallas_call(
         forward_kernel,
         name="forward_attention",
-        grid=(steps,),
         in_specs=[
             pl.BlockSpec(memory_space=pltpu.SMEM),
-            pl.BlockSpec((rows, width), lambda i: (i, 0)),
-            held(w_key.shape),
-            held(w_value.shape),
-            pl.BlockSpec((slab, query_width), lambda i: (i, 0)),
-            held(latents.shape),
-            held((1, width)),
-            held((1, width)),
-        ],
-        out_specs=[held(shape) for shape, _ in out],
+            pl.BlockSpec(memory_space=pltpu.VMEM),
+            pl.BlockSpec(memory_space=pltpu.VMEM),
+        ]
+        + [pl.BlockSpec(memory_space=pl.ANY)] * len(large),
+        out_specs=[pl.BlockSpec(memory_space=pl.ANY)] * len(out),
         out_shape=[jax.ShapeDtypeStruct(shape, dtype) for shape, dtype in out],
-        scratch_shapes=[
+        scratch_shapes=[pltpu.VMEM(a.shape, a.dtype) for a in large]
+        + [pltpu.VMEM(shape, dtype) for shape, dtype in out]
+        + [
             pltpu.VMEM((latent_rows, width), BF16),
-            pltpu.VMEM((latent_rows, query_width), F32),
+            pltpu.VMEM((patch_rows // chunks + latent_rows, width), BF16),
             pltpu.VMEM((2 * key_width, width), BF16),
+            pltpu.SemaphoreType.DMA((chunks + 4,)),
+            pltpu.SemaphoreType.DMA((len(out) + 1,)),
         ],
         cost_estimate=pl.CostEstimate(
             flops=5_000_000_000, bytes_accessed=24_000_000, transcendentals=600_000
         ),
         compiler_params=pltpu.CompilerParams(vmem_limit_bytes=VMEM_LIMIT),
-    )(
-        counts,
-        context,
-        w_key,
-        w_value,
-        w_query,
-        latents,
-        gain_ctx.reshape(1, width),
-        gain_lat.reshape(1, width),
-    )
+    )(counts, gain_ctx.reshape(1, width), gain_lat.reshape(1, width), *large)
 
 
 def slots_of(routes_ref, slot_count, as_row):
@@ -270,85 +321,107 @@
     mp_ref,
     own_ref,
     other_ref,
-    w_own_ref,
-    w_other_ref,
     lat_ref,
     gain_ref,
     routes_ref,
-    hat_ref,
+    w_own_hbm,
+    w_other_hbm,
+    hat_hbm,
     inv_ref,
     out_ref,
-    square_acc,
+    w_own_ref,
+    w_other_ref,
+    hat_ref,
+    sems,
+    hat_sem,
 ):
-    step = pl.program_id(0)
-    steps = pl.num_programs(0)
-    columns = w_own_ref.shape[1]
-    half = out_ref.shape[1]
-    slots = out_ref.shape[0]
-    rows = own_ref.shape[0]
-
-    @pl.when(step == 0)
-    def _():
-        square_acc[...] = jnp.zeros_like(square_acc)
-
-    lat = lat_ref[...].astype(F32)
-    resid = (
-        jnp.concatenate([lat, lat], axis=0)
-        + jnp.dot(own_ref[...], w_own_ref[...], preferred_element_type=F32)
-        + jnp.dot(other_ref[...], w_other_ref[...], preferred_element_type=F32)
-    )
-    hat_ref[:, pl.ds(pl.multiple_of(step * columns, columns), columns)] = resid
-    square_acc[...] += jnp.sum(resid * resid, axis=-1, keepdims=True)
-
-    @pl.when(step == steps - 1)
-    def _():
-        width = hat_ref.shape[1]
-        inverse = lax.rsqrt(square_acc[...] / width + EPSILON)
-        inv_ref[...] = inverse
-        hat_ref[...] = hat_ref[...] * inverse
-        place = slots_of(routes_ref, slot_count, True)
-        table = jnp.where(
-            lax.broadcasted_iota(jnp.int32, (slots, rows), 0) == place, 1.0, 0.0
-        ).astype(BF16)
-        at = pl.ds(pl.multiple_of(mp_ref[0] * half, half), half)
-        final = (hat_ref[:, at] * gain_ref[:, at]).astype(BF16)
-        out_ref[...] = jnp.dot(table, final, preferred_element_type=F32).astype(BF16)
+    rows, width = hat_ref.shape
+    slots, half = out_ref.shape
+    parts = sems.shape[1]
+    size = width // parts
+    copies = []
+    for part in range(parts):
+        at = pl.ds(part * size, size)
+        for i, (source, target) in enumerate(
+            ((w_own_hbm, w_own_ref), (w_other_hbm, w_other_ref))
+        ):
+            copies.append(
+                pltpu.make_async_copy(source.at[:, at], target.at[:, at], sems.at[i, part])
+            )
+    for copy in copies:
+        copy.start()
+    place = slots_of(routes_ref, slot_count, True)
+    table = jnp.where(
+        lax.broadcasted_iota(jnp.int32, (slots, rows), 0) == place, 1.0, 0.0
+    ).astype(BF16)
+    squares = jnp.zeros((rows, 128), F32)
+    for part in range(parts):
+        at = slice(part * size, (part + 1) * size)
+        copies[2 * part].wait()
+        copies[2 * part + 1].wait()
+        lat = lat_ref[:, at].astype(F32)
+        resid = (
+            jnp.concatenate([lat, lat], axis=0)
+            + jnp.dot(own_ref[...], w_own_ref[:, at], preferred_element_type=F32)
+            + jnp.dot(other_ref[...], w_other_ref[:, at], preferred_element_type=F32)
+        )
+        hat_ref[:, at] = resid
+        for c in range(size // 128):
+            piece = resid[:, c * 128 : (c + 1) * 128]
+            squares = squares + piece * piece
+    inverse = lax.rsqrt(jnp.sum(squares, axis=-1, keepdims=True) / width + EPSILON)
+    inv_ref[...] = inverse
+    hat_ref[...] = hat_ref[...] * inverse
+    hat_copy = pltpu.make_async_copy(hat_ref, hat_hbm, hat_sem)
+    hat_copy.start()
+    at = pl.ds(pl.multiple_of(mp_ref[0] * half, half), half)
+    final = (hat_ref[:, at] * gain_ref[:, at]).astype(BF16)
+    out_ref[...] = jnp.dot(table, final, preferred_element_type=F32).astype(BF16)
+    hat_copy.wait()
 
 
 def branch_call(mp_index, own, other, w_own, w_other, latents, gain_out, routes, slots, slot_count):
     width = w_own.shape[1]
     rows, heads = own.shape
-    steps = 8
-    columns = width // steps
-    half = width // 2
+    parts = 4
     return pl.pallas_call(
         functools.partial(branch_kernel, slot_count),
         name="branch_norm",
         grid_spec=pltpu.PrefetchScalarGridSpec(
             num_scalar_prefetch=1,
-            grid=(steps,),
+            grid=(1,),
             in_specs=[
                 held((rows, heads)),
                 held((rows, heads)),
-                pl.BlockSpec((heads, columns), lambda i, *_: (0, i)),
-                pl.BlockSpec((heads, columns), lambda i, *_: (0, i)),
-                pl.BlockSpec((latents.shape[0], columns), lambda i, *_: (0, i)),
+                held(latents.shape),
                 held((1, width)),
                 held((1, rows)),
+                pl.BlockSpec(memory_space=pl.ANY),
+                pl.BlockSpec(memory_space=pl.ANY),
             ],
-            out_specs=[held((rows, width)), held((rows, 1)), held((slots, half))],
-            scratch_shapes=[pltpu.VMEM((rows, 1), F32)],
+            out_specs=[
+                pl.BlockSpec(memory_space=pl.ANY),
+                held((rows, 1)),
+                held((slots, width // 2)),
+            ],
+            scratch_shapes=[
+                pltpu.VMEM(w_own.shape, BF16),
+                pltpu.VMEM(w_other.shape, BF16),
+                pltpu.VMEM((rows, width), F32),
+                pltpu.SemaphoreType.DMA((2, parts)),
+                pltpu.SemaphoreType.DMA,
+            ],
         ),
         out_shape=[
             jax.ShapeDtypeStruct((rows, width), F32),
             jax.ShapeDtypeStruct((rows, 1), F32),
-            jax.ShapeDtypeStruct((slots, half), BF16),
+            jax.ShapeDtypeStruct((slots, width // 2), BF16),
         ],
         cost_estimate=pl.CostEstimate(
             flops=2 * 2 * rows * heads * width, bytes_accessed=16_000_000, transcendentals=0
         ),
         compiler_params=pltpu.CompilerParams(vmem_limit_bytes=VMEM_LIMIT),
-    )(mp_index, own, other, w_own, w_other, latents, gain_out.reshape(1, width), routes)
+    )(mp_index, own, other, latents, gain_out.reshape(1, width), routes, w_own, w_other)
 
 
 def attention_backward(
@@ -396,11 +469,11 @@
             ],
             axis=0,
         )
-        q = q_ref[g]
-        k = k_ref[g]
-        v = v_ref[g]
-        lk = lk_ref[g]
-        lv = lv_ref[g]
+        q = q_ref[g, :, :HD]
+        k = k_ref[g, :, :HD]
+        v = v_ref[g, :, :HD]
+        lk = lk_ref[g, :, :HD]
+        lv = lv_ref[g, :, :HD]
         p_low = p_ref[g]
         p = p_low.astype(F32)
         zero = jnp.zeros_like(v)
@@ -408,8 +481,8 @@
             d_second, jnp.where(row_second, v, zero), 1, 1
         )
         product = p * d_p
-        lat_first = pl_ref[g, 0]
-        lat_second = pl_ref[g, 1]
+        lat_first = pl_ref[g, :, :latent_rows]
+        lat_second = pl_ref[g, :, latent_rows:]
         d_lat_first = dot_general(d_first, lv, 1, 1)
         d_lat_second = dot_general(d_second, lv, 1, 1)
         lat_product_first = lat_first.astype(F32) * d_lat_first
@@ -467,12 +540,35 @@
     slot_count,
     where_ref,
     counts_ref,
+    inv_out_ref,
+    gain_ref,
+    routes_ref,
+    inv_row_ref,
+    got_own_hbm,
+    got_other_hbm,
+    hat_hbm,
+    w_out_hbm,
+    k_hbm,
+    v_hbm,
+    q_hbm,
+    lk_hbm,
+    lv_hbm,
+    p_hbm,
+    pl_hbm,
+    x_hbm,
+    line_own_hbm,
+    line_low_hbm,
+    line_high_hbm,
+    line_both_hbm,
+    pair_hbm,
+    lat_hbm,
+    value_going_hbm,
+    value_kept_hbm,
+    key_going_hbm,
+    key_kept_hbm,
     got_own_ref,
     got_other_ref,
     hat_ref,
-    inv_out_ref,
-    gain_ref,
-    routes_ref,
     w_out_ref,
     k_ref,
     v_ref,
@@ -481,123 +577,179 @@
     lv_ref,
     p_ref,
     pl_ref,
-    inv_row_ref,
     x_ref,
+    d_final_ref,
+    branch_ref,
+    scaled_ref,
     line_own_ref,
     line_low_ref,
     line_high_ref,
     line_both_ref,
     pair_ref,
     lat_ref,
-    value_going_ref,
-    value_kept_ref,
-    key_going_ref,
-    key_kept_ref,
-    d_final_ref,
-    branch_ref,
-    attn_acc,
-    scaled_ref,
+    value_ref,
+    key_ref,
+    sems,
+    out_sems,
+    value_sems,
+    key_sems,
 ):
-    step = pl.program_id(0)
-    steps = pl.num_programs(0) // 2
+    sources = (
+        got_own_hbm,
+        got_other_hbm,
+        hat_hbm,
+        w_out_hbm,
+        k_hbm,
+        v_hbm,
+        q_hbm,
+        lk_hbm,
+        lv_hbm,
+        p_hbm,
+        pl_hbm,
+        x_hbm,
+    )
+    targets = (
+        got_own_ref,
+        got_other_ref,
+        hat_ref,
+        w_out_ref,
+        k_ref,
+        v_ref,
+        q_ref,
+        lk_ref,
+        lv_ref,
+        p_ref,
+        pl_ref,
+        x_ref,
+    )
+    copies = [
+        pltpu.make_async_copy(source, target, sems.at[i])
+        for i, (source, target) in enumerate(zip(sources, targets))
+    ]
+    for copy in copies[:4]:
+        copy.start()
     rows, width = hat_ref.shape
     half = width // 2
-    columns = w_out_ref.shape[1]
     slots = got_own_ref.shape[0]
     latent_rows = lk_ref.shape[1]
-    key_width = value_going_ref.shape[1]
-
-    @pl.when(step == 0)
-    def _():
-        place = slots_of(routes_ref, slot_count, False)
-        table = jnp.where(
-            lax.broadcasted_iota(jnp.int32, (rows, slots), 1) == place, 1.0, 0.0
+    key_width, own = value_ref.shape[2:]
+
+    place = slots_of(routes_ref, slot_count, False)
+    table = jnp.where(
+        lax.broadcasted_iota(jnp.int32, (rows, slots), 1) == place, 1.0, 0.0
+    ).astype(BF16)
+    total = jnp.zeros((rows, 1), F32)
+    chunk = 512
+    for copy in copies[:3]:
+        copy.wait()
+    for copy in copies[4:]:
+        copy.start()
+    for got_ref, which in ((got_own_ref, where_ref[1]), (got_other_ref, 1 - where_ref[1])):
+        for c in range(half // chunk):
+            at = pl.ds(pl.multiple_of(which * half + c * chunk, chunk), chunk)
+            d_final = jnp.dot(
+                table, got_ref[:, c * chunk : (c + 1) * chunk], preferred_element_type=F32
+            )
+            product = d_final * hat_ref[:, at]
+            total = total + jnp.sum(product * gain_ref[:, at], axis=-1, keepdims=True)
+            d_final_ref[:, at] = d_final
+    total = total / width
+    lat_ref[latent_rows:, :] = jnp.zeros_like(lat_ref[latent_rows:, :])
+    highs, lows = [], []
+    part = width // 4
+    for c in range(width // chunk):
+        at = slice(c * chunk, (c + 1) * chunk)
+        d_final = d_final_ref[:, at]
+        hat = hat_ref[:, at]
+        term = jnp.sum(d_final * hat, axis=0, keepdims=True)
+        high = term.astype(BF16).astype(F32)
+        highs.append(high)
+        lows.append(term - high)
+        branch_ref[:, at] = (
+            inv_out_ref[...] * (d_final * gain_ref[:, at] - hat * total)
         ).astype(BF16)
-        total = jnp.zeros((rows, 1), F32)
-        chunk = 512
-        for got_ref, which in ((got_own_ref, where_ref[1]), (got_other_ref, 1 - where_ref[1])):
-            for c in range(half // chunk):
-                at = pl.ds(pl.multiple_of(which * half + c * chunk, chunk), chunk)
-                d_final = jnp.dot(
-                    table, got_ref[:, c * chunk : (c + 1) * chunk], preferred_element_type=F32
-                )
-                product = d_final * hat_ref[:, at]
-                total = total + jnp.sum(product * gain_ref[:, at], axis=-1, keepdims=True)
-                d_final_ref[:, at] = d_final
-        total = total / width
-        lat_ref[latent_rows:, :] = jnp.zeros_like(lat_ref[latent_rows:, :])
-        highs, lows = [], []
-        part = width // 4
-        for c in range(width // chunk):
-            at = slice(c * chunk, (c + 1) * chunk)
-            d_final = d_final_ref[:, at]
-            hat = hat_ref[:, at]
-            term = jnp.sum(d_final * hat, axis=0, keepdims=True)
-            high = term.astype(BF16).astype(F32)
-            highs.append(high)
-            lows.append(term - high)
-            branch_ref[:, at] = (
-                inv_out_ref[...] * (d_final * gain_ref[:, at] - hat * total)
-            ).astype(BF16)
-        per_row = part // chunk
-        lines = [
-            jnp.concatenate(group[i * per_row : (i + 1) * per_row], axis=1)
-            for group in (highs, lows)
-            for i in range(4)
-        ]
-        lat_ref[latent_rows : latent_rows + 16, :part] = jnp.concatenate(
-            lines + [jnp.zeros((8, part), F32)], axis=0
+    per_row = part // chunk
+    lines = [
+        jnp.concatenate(group[i * per_row : (i + 1) * per_row], axis=1)
+        for group in (highs, lows)
+        for i in range(4)
+    ]
+    lat_ref[latent_rows : latent_rows + 16, :part] = jnp.concatenate(
+        lines + [jnp.zeros((8, part), F32)], axis=0
+    ).astype(BF16)
+    z = where_ref[0] >> 2
+    some = pl.ds(pl.multiple_of(where_ref[1] * (rows // 2), rows // 2), rows // 2)
+    line_own_ref[...] = branch_ref[:, pl.ds(pl.multiple_of(z * part, part), part)]
+    for turn, ref in ((1, line_low_ref), (2, line_high_ref), (3, line_both_ref)):
+        ref[...] = branch_ref[some, pl.ds(pl.multiple_of((z ^ turn) * part, part), part)]
+    results = [
+        pltpu.make_async_copy(source, target, out_sems.at[i])
+        for i, (source, target) in enumerate(
+            (
+                (line_low_ref, line_low_hbm),
+                (line_high_ref, line_high_hbm),
+                (line_both_ref, line_both_hbm),
+                (line_own_ref, line_own_hbm),
+                (pair_ref, pair_hbm),
+                (lat_ref, lat_hbm),
+            )
+        )
+    ]
+    for copy in results[:4]:
+        copy.start()
+
+    copies[3].wait()
+    d_attn = dot_general(branch_ref[...], w_out_ref[...], 1, 1).astype(BF16)
+    for copy in copies[4:11]:
+        copy.wait()
+    attention_backward(
+        counts_ref,
+        d_attn,
+        k_ref,
+        v_ref,
+        q_ref,
+        lk_ref,
+        lv_ref,
+        p_ref,
+        pl_ref,
+        inv_row_ref,
+        pair_ref,
+        scaled_ref,
+        lat_ref,
+    )
+    for copy in results[4:]:
+        copy.start()
+    copies[11].wait()
+
+    me = where_ref[0]
+    odd = me & 1
+    for j in range(8):
+        y = ((me >> 1) & 1) ^ (1 - (j >> 2))
+        z = (me >> 2) ^ ((1 - ((j >> 1) & 1)) + 2 * (1 - (j & 1)))
+        first = 4 * z + 2 * y
+        line = j & 3
+        key_hbm = key_kept_hbm if j >> 2 else key_going_hbm
+        grad = jnp.dot(
+            scaled_ref[...],
+            x_ref[:, pl.ds(pl.multiple_of(first * own, 2 * own), 2 * own)],
+            preferred_element_type=F32,
         ).astype(BF16)
-        attn_acc[...] = jnp.zeros_like(attn_acc)
-        z = where_ref[0] >> 2
-        some = pl.ds(pl.multiple_of(where_ref[1] * (rows // 2), rows // 2), rows // 2)
-        line_own_ref[...] = branch_ref[:, pl.ds(pl.multiple_of(z * part, part), part)]
-        for turn, ref in ((1, line_low_ref), (2, line_high_ref), (3, line_both_ref)):
-            ref[...] = branch_ref[some, pl.ds(pl.multiple_of((z ^ turn) * part, part), part)]
-
-    @pl.when(step < steps)
-    def _():
-        at = pl.ds(pl.multiple_of(step * columns, columns), columns)
-        attn_acc[...] += dot_general(branch_ref[:, at], w_out_ref[...], 1, 1)
-
-    @pl.when(step == steps - 1)
-    def _():
-        attention_backward(
-            counts_ref,
-            attn_acc[...].astype(BF16),
-            k_ref,
-            v_ref,
-            q_ref,
-            lk_ref,
-            lv_ref,
-            p_ref,
-            pl_ref,
-            inv_row_ref,
-            pair_ref,
-            scaled_ref,
-            lat_ref,
-        )
-
-    @pl.when(step >= steps)
-    def _():
-        own = x_ref.shape[1] // 2
-        odd = where_ref[0] & 1
-        far = x_ref[:, pl.ds(pl.multiple_of((1 - odd) * own, own), own)]
-        near = x_ref[:, pl.ds(pl.multiple_of(odd * own, own), own)]
-        far_grad = jnp.dot(scaled_ref[...], far, preferred_element_type=F32).astype(BF16)
-        near_grad = jnp.dot(scaled_ref[...], near, preferred_element_type=F32).astype(BF16)
-        value_going_ref[0] = far_grad[key_width:]
-        value_kept_ref[0] = near_grad[key_width:]
-
-        @pl.when(step < steps + steps // 2)
-        def _():
-            key_going_ref[0, 0] = far_grad[:key_width]
-            key_going_ref[1, 0] = near_grad[:key_width]
-
-        @pl.when(step >= steps + steps // 2)
-        def _():
-            key_kept_ref[0, 0] = far_grad[:key_width]
-            key_kept_ref[1, 0] = near_grad[:key_width]
+        for x_same, value_hbm in enumerate((value_going_hbm, value_kept_hbm)):
+            block = jnp.where(odd == x_same, grad[:, own:], grad[:, :own])
+            value_ref[x_same, j] = block[key_width:]
+            key_ref[x_same, j] = block[:key_width]
+            for copy in (
+                pltpu.make_async_copy(
+                    value_ref.at[x_same, j], value_hbm.at[j], value_sems.at[x_same, j]
+                ),
+                pltpu.make_async_copy(
+                    key_ref.at[x_same, j], key_hbm.at[x_same, line], key_sems.at[x_same, j]
+                ),
+            ):
+                copy.start()
+                results.append(copy)
+    for copy in results:
+        copy.wait()
 
 
 def backward_call(
@@ -607,110 +759,59 @@
     rows, width = hat.shape
     patch_rows = context.shape[0]
     heads = w_out.shape[0]
-    groups = k.shape[0]
-    key_width = groups * HD
+    key_width = k.shape[0] * HD
     latent_rows = lk.shape[1]
-    steps = 8
-    columns = width // steps
     own = width // 16
-
-    def x_block(i, where_ref):
-        j = jnp.maximum(i - steps, 0)
-        me = where_ref[0]
-        y = ((me >> 1) & 1) ^ (1 - (j >> 2))
-        low = 1 - ((j >> 1) & 1)
-        high = 1 - (j & 1)
-        z = (me >> 2) ^ (low + 2 * high)
-        return (0, 2 * z + y)
-
-    def turn(i):
-        return jnp.maximum(i - steps, 0)
-
-    lat_width = heads + 2 * key_width
+    large = (got_own, got_other, hat, w_out, k, v, q, lk, lv, p, lat_p, context)
+    out = [
+        (rows, width // 4),
+        (rows // 2, width // 4),
+        (rows // 2, width // 4),
+        (rows // 2, width // 4),
+        (2 * key_width + 16, patch_rows),
+        (latent_rows + 16, heads + 2 * key_width),
+        (8, key_width, own),
+        (8, key_width, own),
+        (2, 4, key_width, own),
+        (2, 4, key_width, own),
+    ]
     return pl.pallas_call(
         functools.partial(backward_kernel, slot_count),
         name="attention_backward",
         grid_spec=pltpu.PrefetchScalarGridSpec(
             num_scalar_prefetch=1,
-            grid=(2 * steps,),
+            grid=(1,),
             in_specs=[
                 pl.BlockSpec(memory_space=pltpu.SMEM),
-                held(got_own.shape),
-                held(got_other.shape),
-                held(hat.shape),
                 held(inv_out.shape),
                 held((1, width)),
                 held(routes.shape),
-                pl.BlockSpec((heads, columns), lambda i, *_: (0, jnp.minimum(i, steps - 1))),
-                held(k.shape),
-                held(v.shape),
-                held(q.shape),
-                held(lk.shape),
-                held(lv.shape),
-                held(p.shape),
-                held(lat_p.shape),
                 held(inv_row.shape),
-                pl.BlockSpec((patch_rows, 2 * own), x_block),
-            ],
-            out_specs=[
-                held((rows, width // 4)),
-                held((rows // 2, width // 4)),
-                held((rows // 2, width // 4)),
-                held((rows // 2, width // 4)),
-                held((2 * key_width + 16, patch_rows)),
-                held((latent_rows + 16, lat_width)),
-                pl.BlockSpec((1, key_width, own), lambda i, *_: (turn(i), 0, 0)),
-                pl.BlockSpec((1, key_width, own), lambda i, *_: (turn(i), 0, 0)),
-                pl.BlockSpec(
-                    (2, 1, key_width, own), lambda i, *_: (0, jnp.minimum(turn(i), 3), 0, 0)
-                ),
-                pl.BlockSpec(
-                    (2, 1, key_width, own), lambda i, *_: (0, jnp.maximum(turn(i) - 4, 0), 0, 0)
-                ),
-            ],
-            scratch_shapes=[
+            ]
+            + [pl.BlockSpec(memory_space=pl.ANY)] * len(large),
+            out_specs=[pl.BlockSpec(memory_space=pl.ANY)] * len(out),
+            scratch_shapes=[pltpu.VMEM(a.shape, a.dtype) for a in large]
+            + [
                 pltpu.VMEM((rows, width), F32),
                 pltpu.VMEM((rows, width), BF16),
-                pltpu.VMEM((rows, heads), F32),
                 pltpu.VMEM((2 * key_width, patch_rows), BF16),
+            ]
+            + [pltpu.VMEM(shape, BF16) for shape in out[:6]]
+            + [
+                pltpu.VMEM((2, 8, key_width, own), BF16),
+                pltpu.VMEM((2, 8, key_width, own), BF16),
+                pltpu.SemaphoreType.DMA((len(large),)),
+                pltpu.SemaphoreType.DMA((6,)),
+                pltpu.SemaphoreType.DMA((2, 8)),
+                pltpu.SemaphoreType.DMA((2, 8)),
             ],
         ),
-        out_shape=[
-            jax.ShapeDtypeStruct((rows, width // 4), BF16),
-            jax.ShapeDtypeStruct((rows // 2, width // 4), BF16),
-            jax.ShapeDtypeStruct((rows // 2, width // 4), BF16),
-            jax.ShapeDtypeStruct((rows // 2, width // 4), BF16),
-            jax.ShapeDtypeStruct((2 * key_width + 16, patch_rows), BF16),
-            jax.ShapeDtypeStruct((latent_rows + 16, lat_width), BF16),
-            jax.ShapeDtypeStruct((8, key_width, own), BF16),
-            jax.ShapeDtypeStruct((8, key_width, own), BF16),
-            jax.ShapeDtypeStruct((2, 4, key_width, own), BF16),
-            jax.ShapeDtypeStruct((2, 4, key_width, own), BF16),
-        ],
+        out_shape=[jax.ShapeDtypeStruct(shape, BF16) for shape in out],
         cost_estimate=pl.CostEstimate(
             flops=5_000_000_000, bytes_accessed=26_000_000, transcendentals=0
         ),
         compiler_params=pltpu.CompilerParams(vmem_limit_bytes=VMEM_LIMIT),
-    )(
-        where,
-        counts,
-        got_own,
-        got_other,
-        hat,
-        inv_out,
-        gain_out.reshape(1, width),
-        routes,
-        w_out,
-        k,
-        v,
-        q,
-        lk,
-        lv,
-        p,
-        lat_p,
-        inv_row,
-        context,
-    )
+    )(where, counts, inv_out, gain_out.reshape(1, width), routes, inv_row, *large)
 
 
 def patch_kernel(
@@ -1093,6 +1194,10 @@
     )(where, kept, both, low, high, gain_ctx.reshape(1, width), pair, wk, wv)
 
 
+def add_halves(left, right):
+    return left.astype(F32) + right.astype(F32)
+
+
 def local(
     context,
     counts,
@@ -1142,9 +1247,6 @@
         context, counts, w_query, wk, wv, latents, gain_ctx, gain_lat
     )
     attn_other = swap_cores(attn_rows)
-    attn_high = swap(attn_rows, 8)
-    attn_low = swap(attn_rows, 4)
-    attn_both = swap(attn_high, 4)
     out_hat, out_inv, outgoing = branch_call(
         mp_scalar,
         attn_rows,
@@ -1195,21 +1297,35 @@
         mp_scalar, pair, pair_other, wk, wv, wk_other, wv_other, context, inv_row, gain_ctx
     )
 
+    line_low, line_high, line_both, attn_line, pair_other = lax.optimization_barrier(
+        (line_low, line_high, line_both, attn_rows, pair_other)
+    )
     got_low = swap(line_low, 4)
     got_high = swap(line_high, 8)
     got_both = swap(line_both, 12)
-
+    attn_high = swap(attn_line, 8)
+    attn_low = swap(attn_line, 4)
+    attn_both = swap(attn_high, 4)
+
+    value_got, key_got, ctx_grad, routed = lax.optimization_barrier(
+        (value_got, key_got, ctx_grad, routed)
+    )
+    key_kept = key_kept.reshape((8,) + key_kept.shape[2:])
+    key_got = key_got.reshape((8,) + key_got.shape[2:])
+    value_going = add_halves(value_kept[:4], value_got[:4]).astype(BF16)
+    key_going = add_halves(key_kept[:4], key_got[:4]).astype(BF16)
+    value_kept = add_halves(value_kept[4:], value_got[4:])
+    key_kept = add_halves(key_kept[4:], key_got[4:])
+    value_got = swap(value_going, 2)
+    key_got = swap(key_going, 1)
+
+    lat_terms, got_low, got_high, got_both, value_kept, key_kept = lax.optimization_barrier(
+        (lat_terms, got_low, got_high, got_both, value_kept, key_kept)
+    )
     lat_sum = lat_terms.astype(F32)
     for turn in (4, 8, 1):
         lat_sum = lat_sum + swap(lat_sum.astype(BF16), turn).astype(F32)
     lat_got = swap(lat_sum.astype(BF16), 2)
-
-    value_going, value_kept = halve_call(value_kept, value_got)
-    value_got = swap(value_going, 2)
-    key_going, key_kept = halve_call(
-        key_kept.reshape((8,) + key_kept.shape[2:]), key_got.reshape((8,) + key_got.shape[2:])
-    )
-    key_got = swap(key_going, 1)
 
     first_going, first_kept, second_going, second_kept = out_call(
         where,
@@ -1219,14 +1335,17 @@
     )
 
     both, low, high, kept = plane_call(value_kept, value_got, key_kept, key_got)
+    first_going, second_going, kept = lax.optimization_barrier((first_going, second_going, kept))
     both = swap(both, 12)
     low = swap(low, 4)
     high = swap(high, 8)
 
-    first_going, first_kept = halve_call(first_kept, swap(first_going, 1))
-    second_going, second_kept = halve_call(second_kept, swap(second_going, 2))
-    first = first_kept[0] + swap(first_going[0], 2).astype(F32)
-    second = second_kept[0] + swap(second_going[0], 1).astype(F32)
+    first_got = swap(first_going, 1)
+    second_got = swap(second_going, 2)
+    first = swap(add_halves(first_kept[0], first_got[0]).astype(BF16), 2)
+    second = swap(add_halves(second_kept[0], second_got[0]).astype(BF16), 1)
+    first = add_halves(first_kept[1], first_got[1]) + first.astype(F32)
+    second = add_halves(second_kept[1], second_got[1]) + second.astype(F32)
     cut = query_width // 2
     grad_w_out = jnp.concatenate([first[:cut], second], axis=0)
     share = own_width // 2

time: 207 us -> 169 us (0.82)
  Pallas kernels: 85 us -> 63.7 us
  waiting for transfers between devices: 55.1 us -> 38.5 us
    ppermute x21, waiting for transfers between devices: 51 us -> 37 us  [swap(): return lax.ppermute(array, 'dp', [(i, i ^ turn) for i in range(dp_count)])]
    pallas_call x5 -> x1, Pallas kernels: 26.4 us -> 15.1 us  [forward_call(): pl.pallas_call(forward_kernel, name='forward_attention', in_specs=[pl.Blo...]
    pallas_call x1, Pallas kernels: 24.3 us -> 16 us  [backward_call(): pl.pallas_call(functools.partial(backward_kernel, slot_count), name='atte...]
    convert_element_type x0 -> x4, other arithmetic: none -> 6.01 us  [the longest x1 2.47 us: local(): value_going = add_halves(value_kept[:4], value_got[:4]).astype(BF16)]
    ppermute x11, waiting for transfers between devices: 4.13 us -> 1.47 us  [swap_cores(): return lax.ppermute(array, 'mp', [(0, 1), (1, 0)])]
    ppermute x21, starting transfers between devices: 29.6 us -> 27 us  [swap(): return lax.ppermute(array, 'dp', [(i, i ^ turn) for i in range(dp_count)])]
    unnamed x35 -> x21, local copies, waits for them, and re-layouts: 6.27 us -> 4.97 us
  transfers between devices with their start and end apart: 34 -> 34, of which waited for: 14 -> 11; matrix products, arithmetic and copies ran while one was open for 6% -> 8% of each run, Pallas kernels for 30% -> 38%
where the time goes in v1:
time: 169 us; the launch traced here: 168 us
  Pallas kernels  63.7 us (38%)
  starting transfers between devices  44.4 us (26%)
  waiting for transfers between devices  38.5 us (23%)
  other arithmetic  14.2 us (8%)
  local copies, waits for them, and re-layouts  6.8 us (4%)
    ppermute x21, waiting for transfers between devices, swap(): return lax.ppermute(array, 'dp', [(i, i ^ turn) for i in range(dp_count)])  37 us
    ppermute x21, starting transfers between devices, swap(): return lax.ppermute(array, 'dp', [(i, i ^ turn) for i in range(dp_count)])  27 us
    pallas_call x1, Pallas kernels, backward_call(): pl.pallas_call(functools.partial(backward_kernel, slot_count), name='atte...  16 us
    pallas_call x1, Pallas kernels, forward_call(): pl.pallas_call(forward_kernel, name='forward_attention', in_specs=[pl.Blo...  15.1 us
    all_to_all x2, starting transfers between devices, exchange(): lax.all_to_all(blocks, 'dp', split_axis=0, concat_axis=0, tiled=True)  14.8 us
    pallas_call x1, Pallas kernels, patch_call(): pl.pallas_call(functools.partial(patch_kernel, width), name='patch_gradie...  9.51 us
    pallas_call x1, Pallas kernels, branch_call(): pl.pallas_call(functools.partial(branch_kernel, slot_count), name='branch...  9.33 us
    unnamed x21, local copies, waits for them, and re-layouts  4.97 us
  transfers between devices with their start and end apart: 34, of which 11 were waited for; matrix products, arithmetic and copies ran while one was open for 8% of the time, Pallas kernels for 38%

profile of v1, /device:TPU:0, one launch (start us, length us, event | category | flops | bytes accessed | tf_op | source)
XLA Modules:
  0.0 168.4 jit_solution(17618516269963987982)
XLA Ops:
  1.2 7.9 %all-to-all-start = ((bf16[16,16,2048]{2,1,0:T(8,128)(2,1)}), bf16[16,16,2048]{2,1,0:T(8,128)(2,1)}, u32[]{:S(2)}, u32[]{:S(2)}) async-start(bf16[16,16,2048]{2,1,0:T(8,128)(2,1)} %bitcast.41), calls=%async_computation | async-start | bytes 2097152 | tf_op jit(solution)/shard_map/all_to_all | solution.py:1231
  9.1 15.1 %forward_attention.1 = (bf16[128,768]{1,0:T(8,128)(2,1)}, bf16[2,1024,128]{2,1,0:T(8,128)(2,1)}, bf16[2,1024,128]{2,1,0:T(8,128)(2,1)}, f32[8,1024]{1,0:T(8,128)...) custom-call(s32[1,2]{1,0:T(1,128)} %counts_ref.3, ...), custom_call_target="tpu_custom_call" | custom-call | flops 5000000000 | bytes 24000000 | tf_op jit(solution)/shard_map/forward_attention/pallas_call | solution.py:278
  26.6 9.3 %branch_norm.1 = (f32[128,4096]{1,0:T(8,128)}, f32[128,1]{1,0:T(8,128)}, bf16[256,2048]{1,0:T(8,128)(2,1)}) custom-call(s32[1]{0:T(128)} %bitcast.1.mp_ref, bf16[128,768]{1,0:T(8,128)(2,1)} %get-tuple-element.100.own_ref.a0_ref, bf16[128,768]{1,0:T(8,128)(2,1)} %copy-done.6, bf16[64,4096]{1,0:T(8,128)(2,1)} %lat_ref.3, f32[1,4096]{1,0:T(1,128)} %bitcast.46, ...), custom_call_target="tpu_custom_call" | custom-call | flops 1610612736 | bytes 16000000 | tf_op jit(solution)/shard_map/branch_norm/pallas_call | solution.py:387
  36.2 6.8 %all-to-all-start.1 = ((bf16[16,16,2048]{2,1,0:T(8,128)(2,1)}), bf16[16,16,2048]{2,1,0:T(8,128)(2,1)}, u32[]{:S(2)}, u32[]{:S(2)}) async-start(bf16[16,16,2048]{2,1,0:T(8,128)(2,1)} %bitcast.42), calls=%async_computation.1 | async-start | bytes 2097152 | tf_op jit(solution)/shard_map/all_to_all | solution.py:1231
  44.3 16.0 %attention_backward.1 = (bf16[128,1024]{1,0:T(8,128)(2,1)}, bf16[64,1024]{1,0:T(8,128)(2,1)}, bf16[64,1024]{1,0:T(8,128)(2,1)}, bf16[64,1024]{1,0:T(8,128)(2,1)}...) custom-call(s32[2]{0:T(128)} %pad_add_fusion.where_ref, ...), custom_call_target="tpu_custom_call" | custom-call | flops 5000000000 | bytes 26000000 | tf_op jit(solution)/shard_map/attention_backward/pallas_call | solution.py:778
  60.4 1.8 %collective-permute-start.3 = (bf16[8,192,256]{2,1,0:T(8,128)(2,1)}, bf16[8,192,256]{2,1,0:T(8,128)(2,1)}, u32[]{:S(2)}, u32[]{:S(2)}) collective-permute-start(bf16[8,192,256]{2,1,0:T(8,128)(2,1)} %get-tuple-element.80), channel_id=1, source_target_pairs={{0,2},{2,0},{4,6},{6,4},{8,10},{10,8},{12,14},{14,12},{16,18},{18,... | collective-permute-start | bytes 2359304 | tf_op jit(solution)/shard_map/ppermute | solution.py:1227
  63.7 3.3 %collective-permute-start.10 = (bf16[64,1024]{1,0:T(8,128)(2,1)}, bf16[64,1024]{1,0:T(8,128)(2,1)S(1)}, u32[]{:S(2)}, u32[]{:S(2)}) collective-permute-start(bf16[64,1024]{1,0:T(8,128)(2,1)} %get-tuple-element.92), channel_id=1, source_target_pairs={{0,24},{2,26},{4,28},{6,30},{8,16},{10,18},{12,20},{14,22},{16,8},... | collective-permute-start | bytes 393224 | tf_op jit(solution)/shard_map/ppermute | solution.py:1227
  68.1 9.5 %patch_gradient.1 = bf16[1024,2048]{1,0:T(8,128)(2,1)} custom-call(s32[1]{0:T(128)} %bitcast.1.mp_ref, bf16[400,1024]{1,0:T(8,128)(2,1)} %get-tuple-element.82.own_ref, bf16[400,1024]{1,0:T(8,128)(2,1)} %copy-done.3, bf16[192,4096]{1,0:T(8,128)(2,1)} %bitcast.33, bf16[192,4096]{1,0:T(8,128)(2,1)} %bitcast.38, ...), custom_call_target="tpu_custom_call" | custom-call | flops 3300000000 | bytes 14000000 | tf_op jit(solution)/shard_map/patch_gradient/pallas_call | solution.py:870
  77.6 5.8 %collective-permute-done.3 = bf16[8,192,256]{2,1,0:T(8,128)(2,1)} collective-permute-done((bf16[8,192,256]{2,1,0:T(8,128)(2,1)}, bf16[8,192,256]{2,1,0:T(8,128)(2,1)}, u32[]{:S(2)}, u32[]{:S(2)}) %collective-permute-start.3) | collective-permute-done | bytes 786464 | tf_op jit(solution)/shard_map/ppermute | solution.py:1227
  83.5 2.4 %fusion = (bf16[4,192,256]{2,1,0:T(8,128)(2,1)S(1)}, f32[4,192,256]{2,1,0:T(8,128)}) fusion(bf16[2,4,192,256]{3,2,1,0:T(8,128)(2,1)} %collective-permute-done.4, bf16[2,4,192,256]{3,2,1,0:T(8,128)(2,1)} %get-tuple-element.95), kind=kLoop, calls=%fused_computation.8 | loop fusion | flops 1376256 | bytes 2752512 | tf_op jit(solution)/shard_map/convert_element_type | solution.py:1316
  86.0 2.5 %add_convert_fusion.1 = (bf16[4,192,256]{2,1,0:T(8,128)(2,1)S(1)}, f32[4,192,256]{2,1,0:T(8,128)}) fusion(bf16[8,192,256]{2,1,0:T(8,128)(2,1)} %collective-permute-done.3, bf16[8,192,256]{2,1,0:T(8,128)(2,1)} %get-tuple-element.93), kind=kLoop, calls=%fused_computation.3 | loop fusion | flops 1376256 | bytes 2752512 | tf_op jit(solution)/shard_map/convert_element_type | solution.py:1315
  89.1 1.7 %collective-permute-start.11 = (bf16[80,1152]{1,0:T(8,128)(2,1)S(1)}, bf16[80,1152]{1,0:T(8,128)(2,1)S(1)}, u32[]{:S(2)}, u32[]{:S(2)}) collective-permute-start(bf16[80,1152]{1,0:T(8,128)(2,1)S(1)} %copy-done.2), channel_id=1, source_target_pairs={{0,8},{2,10},{4,12},{6,14},{8,0},{10,2},{12,4},{14,6},{16,24},{18,... | collective-permute-start | bytes 552968 | tf_op jit(solution)/shard_map/ppermute | solution.py:1227
  90.8 4.9 %collective-permute-done.11 = bf16[80,1152]{1,0:T(8,128)(2,1)S(1)} collective-permute-done((bf16[80,1152]{1,0:T(8,128)(2,1)S(1)}, bf16[80,1152]{1,0:T(8,128)(2,1)S(1)}, u32[]{:S(2)}, u32[]{:S(2)}) %collective-permute-start.11) | collective-permute-done | bytes 184352 | tf_op jit(solution)/shard_map/ppermute | solution.py:1227
  95.7 2.0 %collective-permute-start.12 = (bf16[80,1152]{1,0:T(8,128)(2,1)S(1)}, bf16[80,1152]{1,0:T(8,128)(2,1)S(1)}, u32[]{:S(2)}, u32[]{:S(2)}) collective-permute-start(bf16[80,1152]{1,0:T(8,128)(2,1)S(1)} %fusion.1), channel_id=1, source_target_pairs={{0,16},{2,18},{4,20},{6,22},{8,24},{10,26},{12,28},{14,30},{16,0},... | collective-permute-start | bytes 552968 | tf_op jit(solution)/shard_map/ppermute | solution.py:1227
  101.2 9.9 %collective-permute-done.12 = bf16[80,1152]{1,0:T(8,128)(2,1)S(1)} collective-permute-done((bf16[80,1152]{1,0:T(8,128)(2,1)S(1)}, bf16[80,1152]{1,0:T(8,128)(2,1)S(1)}, u32[]{:S(2)}, u32[]{:S(2)}) %collective-permute-start.12) | collective-permute-done | bytes 184352 | tf_op jit(solution)/shard_map/ppermute | solution.py:1227
  114.5 2.6 %plane_sum.1 = (bf16[384,256]{1,0:T(8,128)(2,1)}, bf16[384,256]{1,0:T(8,128)(2,1)}, bf16[384,256]{1,0:T(8,128)(2,1)}, f32[384,256]{1,0:T(8,128)}) custom-call(f32[4,192,256]{2,1,0:T(8,128)} %get-tuple-element.107.value_ref, bf16[4,192,256]{2,1,0:T(8,128)(2,1)} %collective-permute-done.21.value_got_ref, f32[4,192,256]{2,1,0:T(8,128)} %get-tuple-element.108.key_ref, ...), custom_call_target="tpu_custom_call" | custom-call | flops 1000000 | bytes 5000000 | tf_op jit(solution)/shard_map/plane_sum/pallas_call | solution.py:1117
  119.2 1.9 %fusion.10 = (bf16[80,1152]{1,0:T(8,128)(2,1)}, f32[80,1152]{1,0:T(8,128)}) fusion(bf16[80,1152]{1,0:T(8,128)(2,1)} %collective-permute-done.13, bf16[80,1152]{1,0:T(8,128)(2,1)} %copy-done.4, bf16[80,1152]{1,0:T(8,128)(2,1)S(1)} %collective-permute-done.11, bf16[80,1152]{1,0:T(8,128)(2,1)S(1)} %copy-done.2), kind=kLoop, calls=%fused_computation.31 | loop fusion | flops 737280 | bytes 1290240 | tf_op jit(solution)/shard_map/convert_element_type | solution.py:1328
  121.1 2.6 %collective-permute-start.23 = (bf16[384,256]{1,0:T(8,128)(2,1)}, bf16[384,256]{1,0:T(8,128)(2,1)}, u32[]{:S(2)}, u32[]{:S(2)}) collective-permute-start(bf16[384,256]{1,0:T(8,128)(2,1)} %get-tuple-element.111), channel_id=1, source_target_pairs={{0,24},{2,26},{4,28},{6,30},{8,16},{10,18},{12,20},{14,22},{16,8},... | collective-permute-start | bytes 589832 | tf_op jit(solution)/shard_map/ppermute | solution.py:1227
  127.2 4.6 %output_projection_gradient.1 = (bf16[2,416,256]{2,1,0:T(8,128)(2,1)}, bf16[2,416,256]{2,1,0:T(8,128)(2,1)}, bf16[2,384,256]{2,1,0:T(8,128)(2,1)}, bf16[2,384,256]{2,1,0:T(8,128)(2,1)}) custom-call(s32[2]{0:T(128)} %pad_add_fusion.where_ref, bf16[128,768]{1,0:T(8,128)(2,1)} %get-tuple-element.100.own_ref.a0_ref, ...), custom_call_target="tpu_custom_call" | custom-call | flops 805306368 | bytes 4000000 | tf_op jit(solution)/shard_map/output_projection_gradient/pallas_call | solution.py:967
  133.0 3.7 %latent_gradients.1 = (f32[256,768]{1,0:T(8,128)}, f32[384,256]{1,0:T(8,128)}, f32[72,384]{1,0:T(8,128)}, f32[1,128]{1,0:T(1,128)}) custom-call(s32[2]{0:T(128)} %pad_add_fusion.where_ref, f32[80,1152]{1,0:T(8,128)} %get-tuple-element.125.sum_ref, bf16[80,1152]{1,0:T(8,128)(2,1)} %copy-done.7, f32[64,1152]{1,0:T(8,128)} %get-tuple-element.98.proj_ref, ...), custom_call_target="tpu_custom_call" | custom-call | flops 100000000 | bytes 3000000 | tf_op jit(solution)/shard_map/latent_gradients/pallas_call | solution.py:1061
  138.3 2.8 %collective-permute-done.25.high_ref = bf16[384,256]{1,0:T(8,128)(2,1)} collective-permute-done((bf16[384,256]{1,0:T(8,128)(2,1)}, bf16[384,256]{1,0:T(8,128)(2,1)}, u32[]{:S(2)}, u32[]{:S(2)}) %collective-permute-start.25) | collective-permute-done | bytes 196640 | tf_op jit(solution)/shard_map/ppermute | solution.py:1227
  141.0 2.9 %key_value_gradients.1 = (f32[192,256]{1,0:T(8,128)}, f32[192,256]{1,0:T(8,128)}, f32[8,256]{1,0:T(8,128)}) custom-call(s32[2]{0:T(128)} %pad_add_fusion.where_ref, f32[384,256]{1,0:T(8,128)} %get-tuple-element.110.kept_ref, bf16[384,256]{1,0:T(8,128)(2,1)} %collective-permute-done.23.both_ref, bf16[384,256]{1,0:T(8,128)(2,1)} %collective-permute-done.24.low_ref, ...), custom_call_target="tpu_custom_call" | custom-call | flops 1000000 | bytes 3000000 | tf_op jit(solution)/shard_map/key_value_gradients/pallas_call | solution.py:1177
  149.4 8.2 %collective-permute-done.26 = bf16[2,416,256]{2,1,0:T(8,128)(2,1)S(1)} collective-permute-done((bf16[2,416,256]{2,1,0:T(8,128)(2,1)}, bf16[2,416,256]{2,1,0:T(8,128)(2,1)S(1)}, u32[]{:S(2)}, u32[]{:S(2)}) %collective-permute-start.26) | collective-permute-done | bytes 426016 | tf_op jit(solution)/shard_map/ppermute | solution.py:1227
  166.1 2.3 %copy.23 = bf16[256,2048]{1,0:T(8,128)(2,1)} copy(bf16[256,2048]{1,0:T(8,128)(2,1)} %bitcast.11) | data formatting | bytes 2097152
  (96 shorter events, 37.0 us)
Async XLA Ops:
  0.6 25.3 %collective-permute-start.1 = (bf16[768,4096]{1,0:T(8,128)(2,1)}, bf16[768,4096]{1,0:T(8,128)(2,1)}, u32[]{:S(2)}, u32[]{:S(2)}) collective-permute-start(bf16[768,4096]{1,0:T(8,128)(2,1)} %w_out_hbm.1), channel_id=1, source_target_pairs={{0,1},{1,0},{2,3},{3,2},{4,5},{5,4},{6,7},{7,6},{8,9},{9,8},{10,11... | collective-permute-start | bytes 18874376 | tf_op jit(solution)/shard_map/ppermute | solution.py:30
  1.2 34.7 %all-to-all-start = ((bf16[16,16,2048]{2,1,0:T(8,128)(2,1)}), bf16[16,16,2048]{2,1,0:T(8,128)(2,1)}, u32[]{:S(2)}, u32[]{:S(2)}) async-start(bf16[16,16,2048]{2,1,0:T(8,128)(2,1)} %bitcast.41), calls=%async_computation | async-start | bytes 2097152 | tf_op jit(solution)/shard_map/all_to_all | solution.py:1231
  36.2 47.4 %all-to-all-start.1 = ((bf16[16,16,2048]{2,1,0:T(8,128)(2,1)}), bf16[16,16,2048]{2,1,0:T(8,128)(2,1)}, u32[]{:S(2)}, u32[]{:S(2)}) async-start(bf16[16,16,2048]{2,1,0:T(8,128)(2,1)} %bitcast.42), calls=%async_computation.1 | async-start | bytes 2097152 | tf_op jit(solution)/shard_map/all_to_all | solution.py:1231
  43.0 23.9 %collective-permute-start.6 = (bf16[192,4096]{1,0:T(8,128)(2,1)}, bf16[192,4096]{1,0:T(8,128)(2,1)}, u32[]{:S(2)}, u32[]{:S(2)}) collective-permute-start(bf16[192,4096]{1,0:T(8,128)(2,1)} %bitcast.32), channel_id=1, source_target_pairs={{0,1},{1,0},{2,3},{3,2},{4,5},{5,4},{6,7},{7,6},{8,9},{9,8},{10,11... | collective-permute-start | bytes 4718600 | tf_op jit(solution)/shard_map/ppermute | solution.py:30
  43.2 23.8 %collective-permute-start.7 = (bf16[192,4096]{1,0:T(8,128)(2,1)}, bf16[192,4096]{1,0:T(8,128)(2,1)}, u32[]{:S(2)}, u32[]{:S(2)}) collective-permute-start(bf16[192,4096]{1,0:T(8,128)(2,1)} %bitcast.37), channel_id=1, source_target_pairs={{0,1},{1,0},{2,3},{3,2},{4,5},{5,4},{6,7},{7,6},{8,9},{9,8},{10,11... | collective-permute-start | bytes 4718600 | tf_op jit(solution)/shard_map/ppermute | solution.py:30
  60.4 23.0 %collective-permute-start.3 = (bf16[8,192,256]{2,1,0:T(8,128)(2,1)}, bf16[8,192,256]{2,1,0:T(8,128)(2,1)}, u32[]{:S(2)}, u32[]{:S(2)}) collective-permute-start(bf16[8,192,256]{2,1,0:T(8,128)(2,1)} %get-tuple-element.80), channel_id=1, source_target_pairs={{0,2},{2,0},{4,6},{6,4},{8,10},{10,8},{12,14},{14,12},{16,18},{18,... | collective-permute-start | bytes 2359304 | tf_op jit(solution)/shard_map/ppermute | solution.py:1227
  62.2 21.3 %collective-permute-start.4 = (bf16[2,4,192,256]{3,2,1,0:T(8,128)(2,1)}, bf16[2,4,192,256]{3,2,1,0:T(8,128)(2,1)}, u32[]{:S(2)}, u32[]{:S(2)}) collective-permute-start(bf16[2,4,192,256]{3,2,1,0:T(8,128)(2,1)} %get-tuple-element.81), channel_id=1, source_target_pairs={{0,4},{2,6},{4,0},{6,2},{8,12},{10,14},{12,8},{14,10},{16,20},{18,... | collective-permute-start | bytes 2359304 | tf_op jit(solution)/shard_map/ppermute | solution.py:1227
  63.7 24.7 %collective-permute-start.10 = (bf16[64,1024]{1,0:T(8,128)(2,1)}, bf16[64,1024]{1,0:T(8,128)(2,1)S(1)}, u32[]{:S(2)}, u32[]{:S(2)}) collective-permute-start(bf16[64,1024]{1,0:T(8,128)(2,1)} %get-tuple-element.92), channel_id=1, source_target_pairs={{0,24},{2,26},{4,28},{6,30},{8,16},{10,18},{12,20},{14,22},{16,8},... | collective-permute-start | bytes 393224 | tf_op jit(solution)/shard_map/ppermute | solution.py:1227
  67.0 21.5 %collective-permute-start.8 = (bf16[64,1024]{1,0:T(8,128)(2,1)}, bf16[64,1024]{1,0:T(8,128)(2,1)}, u32[]{:S(2)}, u32[]{:S(2)}) collective-permute-start(bf16[64,1024]{1,0:T(8,128)(2,1)} %get-tuple-element.90), channel_id=1, source_target_pairs={{0,8},{2,10},{4,12},{6,14},{8,0},{10,2},{12,4},{14,6},{16,24},{18,... | collective-permute-start | bytes 393224 | tf_op jit(solution)/shard_map/ppermute | solution.py:1227
  67.0 21.5 %collective-permute-start.9 = (bf16[64,1024]{1,0:T(8,128)(2,1)}, bf16[64,1024]{1,0:T(8,128)(2,1)}, u32[]{:S(2)}, u32[]{:S(2)}) collective-permute-start(bf16[64,1024]{1,0:T(8,128)(2,1)} %get-tuple-element.91), channel_id=1, source_target_pairs={{0,16},{2,18},{4,20},{6,22},{8,24},{10,26},{12,28},{14,30},{16,0},... | collective-permute-start | bytes 393224 | tf_op jit(solution)/shard_map/ppermute | solution.py:1227
  95.7 15.4 %collective-permute-start.12 = (bf16[80,1152]{1,0:T(8,128)(2,1)S(1)}, bf16[80,1152]{1,0:T(8,128)(2,1)S(1)}, u32[]{:S(2)}, u32[]{:S(2)}) collective-permute-start(bf16[80,1152]{1,0:T(8,128)(2,1)S(1)} %fusion.1), channel_id=1, source_target_pairs={{0,16},{2,18},{4,20},{6,22},{8,24},{10,26},{12,28},{14,30},{16,0},... | collective-permute-start | bytes 552968 | tf_op jit(solution)/shard_map/ppermute | solution.py:1227
  97.7 19.4 %collective-permute-start.16 = (bf16[128,768]{1,0:T(8,128)(2,1)}, bf16[128,768]{1,0:T(8,128)(2,1)}, u32[]{:S(2)}, u32[]{:S(2)}) collective-permute-start(bf16[128,768]{1,0:T(8,128)(2,1)} %get-tuple-element.100.own_ref.a0_ref), channel_id=1, source_target_pairs={{0,16},{2,18},{4,20},{6,22},{8,24},{10,26},{12,28},{14,30},{16,0},... | collective-permute-start | bytes 589832 | tf_op jit(solution)/shard_map/ppermute | solution.py:1227
  98.7 15.3 %collective-permute-start.22 = (bf16[4,192,256]{2,1,0:T(8,128)(2,1)S(1)}, bf16[4,192,256]{2,1,0:T(8,128)(2,1)}, u32[]{:S(2)}, u32[]{:S(2)}) collective-permute-start(bf16[4,192,256]{2,1,0:T(8,128)(2,1)S(1)} %get-tuple-element.126), channel_id=1, source_target_pairs={{0,2},{2,0},{4,6},{6,4},{8,10},{10,8},{12,14},{14,12},{16,18},{18,... | collective-permute-start | bytes 1179656 | tf_op jit(solution)/shard_map/ppermute | solution.py:1227
  99.7 14.2 %collective-permute-start.21 = (bf16[4,192,256]{2,1,0:T(8,128)(2,1)S(1)}, bf16[4,192,256]{2,1,0:T(8,128)(2,1)}, u32[]{:S(2)}, u32[]{:S(2)}) collective-permute-start(bf16[4,192,256]{2,1,0:T(8,128)(2,1)S(1)} %get-tuple-element.128), channel_id=1, source_target_pairs={{0,4},{2,6},{4,0},{6,2},{8,12},{10,14},{12,8},{14,10},{16,20},{18,... | collective-permute-start | bytes 1179656 | tf_op jit(solution)/shard_map/ppermute | solution.py:1227
  114.0 9.7 %collective-permute-start.18 = (bf16[64,1024]{1,0:T(8,128)(2,1)}, bf16[64,1024]{1,0:T(8,128)(2,1)}, u32[]{:S(2)}, u32[]{:S(2)}) collective-permute-start(bf16[64,1024]{1,0:T(8,128)(2,1)} %collective-permute-done.8.d1_ref), channel_id=1, source_target_pairs={{0,1},{1,0},{2,3},{3,2},{4,5},{5,4},{6,7},{7,6},{8,9},{9,8},{10,11... | collective-permute-start | bytes 393224 | tf_op jit(solution)/shard_map/ppermute | solution.py:30
  114.0 10.6 %collective-permute-start.19 = (bf16[64,1024]{1,0:T(8,128)(2,1)}, bf16[64,1024]{1,0:T(8,128)(2,1)}, u32[]{:S(2)}, u32[]{:S(2)}) collective-permute-start(bf16[64,1024]{1,0:T(8,128)(2,1)} %collective-permute-done.9.d2_ref), channel_id=1, source_target_pairs={{0,1},{1,0},{2,3},{3,2},{4,5},{5,4},{6,7},{7,6},{8,9},{9,8},{10,11... | collective-permute-start | bytes 393224 | tf_op jit(solution)/shard_map/ppermute | solution.py:30
  118.4 8.8 %collective-permute-start.17 = (bf16[128,768]{1,0:T(8,128)(2,1)}, bf16[128,768]{1,0:T(8,128)(2,1)}, u32[]{:S(2)}, u32[]{:S(2)}) collective-permute-start(bf16[128,768]{1,0:T(8,128)(2,1)} %collective-permute-done.16.a2_ref), channel_id=1, source_target_pairs={{0,8},{2,10},{4,12},{6,14},{8,0},{10,2},{12,4},{14,6},{16,24},{18,... | collective-permute-start | bytes 589832 | tf_op jit(solution)/shard_map/ppermute | solution.py:1227
  121.1 15.6 %collective-permute-start.23 = (bf16[384,256]{1,0:T(8,128)(2,1)}, bf16[384,256]{1,0:T(8,128)(2,1)}, u32[]{:S(2)}, u32[]{:S(2)}) collective-permute-start(bf16[384,256]{1,0:T(8,128)(2,1)} %get-tuple-element.111), channel_id=1, source_target_pairs={{0,24},{2,26},{4,28},{6,30},{8,16},{10,18},{12,20},{14,22},{16,8},... | collective-permute-start | bytes 589832 | tf_op jit(solution)/shard_map/ppermute | solution.py:1227
  123.7 14.5 %collective-permute-start.24 = (bf16[384,256]{1,0:T(8,128)(2,1)}, bf16[384,256]{1,0:T(8,128)(2,1)}, u32[]{:S(2)}, u32[]{:S(2)}) collective-permute-start(bf16[384,256]{1,0:T(8,128)(2,1)} %get-tuple-element.112), channel_id=1, source_target_pairs={{0,8},{2,10},{4,12},{6,14},{8,0},{10,2},{12,4},{14,6},{16,24},{18,... | collective-permute-start | bytes 589832 | tf_op jit(solution)/shard_map/ppermute | solution.py:1227
  124.6 16.4 %collective-permute-start.25 = (bf16[384,256]{1,0:T(8,128)(2,1)}, bf16[384,256]{1,0:T(8,128)(2,1)}, u32[]{:S(2)}, u32[]{:S(2)}) collective-permute-start(bf16[384,256]{1,0:T(8,128)(2,1)} %get-tuple-element.113), channel_id=1, source_target_pairs={{0,16},{2,18},{4,20},{6,22},{8,24},{10,26},{12,28},{14,30},{16,0},... | collective-permute-start | bytes 589832 | tf_op jit(solution)/shard_map/ppermute | solution.py:1227
  131.7 16.0 %collective-permute-start.28 = (bf16[2,384,256]{2,1,0:T(8,128)(2,1)}, bf16[2,384,256]{2,1,0:T(8,128)(2,1)}, u32[]{:S(2)}, u32[]{:S(2)}) collective-permute-start(bf16[2,384,256]{2,1,0:T(8,128)(2,1)} %get-tuple-element.120), channel_id=1, source_target_pairs={{0,4},{2,6},{4,0},{6,2},{8,12},{10,14},{12,8},{14,10},{16,20},{18,... | collective-permute-start | bytes 1179656 | tf_op jit(solution)/shard_map/ppermute | solution.py:1227
  144.8 12.8 %collective-permute-start.26 = (bf16[2,416,256]{2,1,0:T(8,128)(2,1)}, bf16[2,416,256]{2,1,0:T(8,128)(2,1)S(1)}, u32[]{:S(2)}, u32[]{:S(2)}) collective-permute-start(bf16[2,416,256]{2,1,0:T(8,128)(2,1)} %get-tuple-element.118), channel_id=1, source_target_pairs={{0,2},{2,0},{4,6},{6,4},{8,10},{10,8},{12,14},{14,12},{16,18},{18,... | collective-permute-start | bytes 1277960 | tf_op jit(solution)/shard_map/ppermute | solution.py:1227
  146.3 12.7 %collective-permute-start.30 = (f32[72,384]{1,0:T(8,128)}, f32[72,384]{1,0:T(8,128)S(1)}, u32[]{:S(2)}, u32[]{:S(2)}) collective-permute-start(f32[72,384]{1,0:T(8,128)} %get-tuple-element.121), channel_id=1, source_target_pairs={{0,1},{1,0},{2,3},{3,2},{4,5},{5,4},{6,7},{7,6},{8,9},{9,8},{10,11... | collective-permute-start | bytes 331784 | tf_op jit(solution)/shard_map/ppermute | solution.py:30
  148.8 12.7 %collective-permute-start.29 = (bf16[384,256]{1,0:T(8,128)(2,1)S(1)}, bf16[384,256]{1,0:T(8,128)(2,1)S(1)}, u32[]{:S(2)}, u32[]{:S(2)}) collective-permute-start(bf16[384,256]{1,0:T(8,128)(2,1)S(1)} %fusion.4), channel_id=1, source_target_pairs={{0,2},{2,0},{4,6},{6,4},{8,10},{10,8},{12,14},{14,12},{16,18},{18,... | collective-permute-start | bytes 589832 | tf_op jit(solution)/shard_map/ppermute | solution.py:1227
  (20 other events, 146.7 us)

commit v2 on v1

--- a/solution.py
+++ b/solution.py
@@ -318,7 +318,7 @@
 
 def branch_kernel(
     slot_count,
-    mp_ref,
+    where_ref,
     own_ref,
     other_ref,
     lat_ref,
@@ -374,13 +374,13 @@
     hat_ref[...] = hat_ref[...] * inverse
     hat_copy = pltpu.make_async_copy(hat_ref, hat_hbm, hat_sem)
     hat_copy.start()
-    at = pl.ds(pl.multiple_of(mp_ref[0] * half, half), half)
+    at = pl.ds(pl.multiple_of(where_ref[1] * half, half), half)
     final = (hat_ref[:, at] * gain_ref[:, at]).astype(BF16)
     out_ref[...] = jnp.dot(table, final, preferred_element_type=F32).astype(BF16)
     hat_copy.wait()
 
 
-def branch_call(mp_index, own, other, w_own, w_other, latents, gain_out, routes, slots, slot_count):
+def branch_call(where, own, other, w_own, w_other, latents, gain_out, routes, slots, slot_count):
     width = w_own.shape[1]
     rows, heads = own.shape
     parts = 4
@@ -421,7 +421,7 @@
             flops=2 * 2 * rows * heads * width, bytes_accessed=16_000_000, transcendentals=0
         ),
         compiler_params=pltpu.CompilerParams(vmem_limit_bytes=VMEM_LIMIT),
-    )(mp_index, own, other, latents, gain_out.reshape(1, width), routes, w_own, w_other)
+    )(where, own, other, latents, gain_out.reshape(1, width), routes, w_own, w_other)
 
 
 def attention_backward(
@@ -544,6 +544,7 @@
     gain_ref,
     routes_ref,
     inv_row_ref,
+    attn_ref,
     got_own_hbm,
     got_other_hbm,
     hat_hbm,
@@ -557,11 +558,9 @@
     pl_hbm,
     x_hbm,
     line_own_hbm,
-    line_low_hbm,
     line_high_hbm,
-    line_both_hbm,
     pair_hbm,
-    lat_hbm,
+    message_hbm,
     value_going_hbm,
     value_kept_hbm,
     key_going_hbm,
@@ -582,11 +581,9 @@
     branch_ref,
     scaled_ref,
     line_own_ref,
-    line_low_ref,
     line_high_ref,
-    line_both_ref,
     pair_ref,
-    lat_ref,
+    message_ref,
     value_ref,
     key_ref,
     sems,
@@ -633,6 +630,8 @@
     slots = got_own_ref.shape[0]
     latent_rows = lk_ref.shape[1]
     key_width, own = value_ref.shape[2:]
+    lat_at = message_ref.shape[1] - (key_width * 2 + attn_ref.shape[1])
+    lat_ref = message_ref.at[:, pl.ds(lat_at, message_ref.shape[1] - lat_at)]
 
     place = slots_of(routes_ref, slot_count, False)
     table = jnp.where(
@@ -680,22 +679,31 @@
     z = where_ref[0] >> 2
     some = pl.ds(pl.multiple_of(where_ref[1] * (rows // 2), rows // 2), rows // 2)
     line_own_ref[...] = branch_ref[:, pl.ds(pl.multiple_of(z * part, part), part)]
-    for turn, ref in ((1, line_low_ref), (2, line_high_ref), (3, line_both_ref)):
-        ref[...] = branch_ref[some, pl.ds(pl.multiple_of((z ^ turn) * part, part), part)]
+    message_ref[rows // 2 :, :lat_at] = jnp.zeros_like(message_ref[rows // 2 :, :lat_at])
+    heads = attn_ref.shape[1]
+    for turn, ref, first in (
+        (1, message_ref, 0),
+        (2, line_high_ref, 0),
+        (3, line_high_ref, part + 2 * heads),
+    ):
+        ref[: rows // 2, first : first + part] = branch_ref[
+            some, pl.ds(pl.multiple_of((z ^ turn) * part, part), part)
+        ]
+    for ref in (message_ref, line_high_ref):
+        ref[: rows // 2, part : part + heads] = attn_ref[: rows // 2, :]
+        ref[: rows // 2, part + heads : part + 2 * heads] = attn_ref[rows // 2 :, :]
     results = [
         pltpu.make_async_copy(source, target, out_sems.at[i])
         for i, (source, target) in enumerate(
             (
-                (line_low_ref, line_low_hbm),
                 (line_high_ref, line_high_hbm),
-                (line_both_ref, line_both_hbm),
                 (line_own_ref, line_own_hbm),
                 (pair_ref, pair_hbm),
-                (lat_ref, lat_hbm),
+                (message_ref, message_hbm),
             )
         )
     ]
-    for copy in results[:4]:
+    for copy in results[:2]:
         copy.start()
 
     copies[3].wait()
@@ -717,7 +725,7 @@
         scaled_ref,
         lat_ref,
     )
-    for copy in results[4:]:
+    for copy in results[2:]:
         copy.start()
     copies[11].wait()
 
@@ -753,7 +761,7 @@
 
 
 def backward_call(
-    where, counts, got_own, got_other, hat, inv_out, gain_out, routes, w_out, kept, context, slot_count
+    where, counts, attn, got_own, got_other, hat, inv_out, gain_out, routes, w_out, kept, context, slot_count
 ):
     k, v, q, lk, lv, p, lat_p, inv_row = kept
     rows, width = hat.shape
@@ -765,11 +773,9 @@
     large = (got_own, got_other, hat, w_out, k, v, q, lk, lv, p, lat_p, context)
     out = [
         (rows, width // 4),
-        (rows // 2, width // 4),
-        (rows // 2, width // 4),
-        (rows // 2, width // 4),
+        (rows // 2, width // 2 + 2 * heads),
         (2 * key_width + 16, patch_rows),
-        (latent_rows + 16, heads + 2 * key_width),
+        (latent_rows + 16, width // 4 + 3 * heads + 2 * key_width),
         (8, key_width, own),
         (8, key_width, own),
         (2, 4, key_width, own),
@@ -787,6 +793,7 @@
                 held((1, width)),
                 held(routes.shape),
                 held(inv_row.shape),
+                held(attn.shape),
             ]
             + [pl.BlockSpec(memory_space=pl.ANY)] * len(large),
             out_specs=[pl.BlockSpec(memory_space=pl.ANY)] * len(out),
@@ -796,12 +803,12 @@
                 pltpu.VMEM((rows, width), BF16),
                 pltpu.VMEM((2 * key_width, patch_rows), BF16),
             ]
-            + [pltpu.VMEM(shape, BF16) for shape in out[:6]]
+            + [pltpu.VMEM(shape, BF16) for shape in out[:4]]
             + [
                 pltpu.VMEM((2, 8, key_width, own), BF16),
                 pltpu.VMEM((2, 8, key_width, own), BF16),
                 pltpu.SemaphoreType.DMA((len(large),)),
-                pltpu.SemaphoreType.DMA((6,)),
+                pltpu.SemaphoreType.DMA((4,)),
                 pltpu.SemaphoreType.DMA((2, 8)),
                 pltpu.SemaphoreType.DMA((2, 8)),
             ],
@@ -811,12 +818,12 @@
             flops=5_000_000_000, bytes_accessed=26_000_000, transcendentals=0
         ),
         compiler_params=pltpu.CompilerParams(vmem_limit_bytes=VMEM_LIMIT),
-    )(where, counts, inv_out, gain_out.reshape(1, width), routes, inv_row, *large)
+    )(where, counts, inv_out, gain_out.reshape(1, width), routes, inv_row, attn, *large)
 
 
 def patch_kernel(
     width,
-    mp_ref,
+    where_ref,
     own_ref,
     other_ref,
     wk_ref,
@@ -859,14 +866,14 @@
     ).astype(BF16)
 
 
-def patch_call(mp_index, own, other, wk, wv, wk_other, wv_other, context, inv_row, gain_ctx):
+def patch_call(where, own, other, wk, wv, wk_other, wv_other, context, inv_row, gain_ctx):
     patch_rows, width = context.shape
     half = width // 2
     steps = 4
     rows = patch_rows // steps
     key_width = wk.shape[0]
     once = pl.Buffered(1)
-    w_spec = pl.BlockSpec((key_width, half), lambda i, mp: (0, mp[0]), pipeline_mode=once)
+    w_spec = pl.BlockSpec((key_width, half), lambda i, w: (0, w[1]), pipeline_mode=once)
     return pl.pallas_call(
         functools.partial(patch_kernel, width),
         name="patch_gradient",
@@ -880,11 +887,11 @@
                 w_spec,
                 w_spec,
                 w_spec,
-                pl.BlockSpec((rows, half), lambda i, mp: (i, mp[0])),
+                pl.BlockSpec((rows, half), lambda i, w: (i, w[1])),
                 held(inv_row.shape),
-                pl.BlockSpec((1, half), lambda i, mp: (0, mp[0])),
+                pl.BlockSpec((1, half), lambda i, w: (0, w[1])),
             ],
-            out_specs=pl.BlockSpec((rows, half), lambda i, mp: (i, 0)),
+            out_specs=pl.BlockSpec((rows, half), lambda i, w: (i, 0)),
             scratch_shapes=[
                 pltpu.VMEM((patch_rows, 4 * key_width), BF16),
                 pltpu.VMEM((patch_rows, 1), F32),
@@ -897,22 +904,19 @@
             flops=3_300_000_000, bytes_accessed=14_000_000, transcendentals=0
         ),
         compiler_params=pltpu.CompilerParams(vmem_limit_bytes=VMEM_LIMIT),
-    )(mp_index, own, other, wk, wv, wk_other, wv_other, context, inv_row, gain_ctx.reshape(1, width))
+    )(where, own, other, wk, wv, wk_other, wv_other, context, inv_row, gain_ctx.reshape(1, width))
 
 
 def out_kernel(
     where_ref,
-    a0_ref,
-    a1_ref,
-    a2_ref,
-    a3_ref,
-    d0_ref,
-    d1_ref,
-    d2_ref,
-    d3_ref,
-    e1_ref,
-    e2_ref,
-    e3_ref,
+    attn_own_ref,
+    line_own_ref,
+    low_ref,
+    high_ref,
+    forwarded_ref,
+    other_low_ref,
+    other_high_ref,
+    other_forwarded_ref,
     first_going_ref,
     first_kept_ref,
     second_going_ref,
@@ -921,27 +925,36 @@
     line_ref,
     resid_ref,
 ):
-    rows, heads = a0_ref.shape
+    rows, heads = attn_own_ref.shape
     columns = line_ref.shape[1]
     own = columns // 4
     latent_rows = rows // 2
     mine = where_ref[1]
-    for i, ref in enumerate((a0_ref, a1_ref, a2_ref, a3_ref)):
-        attn_ref[i * rows : (i + 1) * rows, :] = ref[...]
-    line_ref[:rows, :] = d0_ref[...]
     half = rows // 2
-    for i, (ref, other) in enumerate(((d1_ref, e1_ref), (d2_ref, e2_ref), (d3_ref, e3_ref))):
+    attn_ref[:rows, :] = attn_own_ref[...]
+    line_ref[:rows, :] = line_own_ref[...]
+    for i, (ref, other, first) in enumerate(
+        (
+            (low_ref, other_low_ref, 0),
+            (high_ref, other_high_ref, 0),
+            (forwarded_ref, other_forwarded_ref, columns + 2 * heads),
+        )
+    ):
         at = (i + 1) * rows
-        line_ref[pl.ds(pl.multiple_of(at + mine * half, half), half), :] = ref[...]
-        line_ref[pl.ds(pl.multiple_of(at + (1 - mine) * half, half), half), :] = other[...]
+        attn_ref[at : at + half, :] = ref[:half, columns : columns + heads]
+        attn_ref[at + half : at + rows, :] = ref[:half, columns + heads : columns + 2 * heads]
+        for holder, which in ((ref, mine), (other, 1 - mine)):
+            line_ref[pl.ds(pl.multiple_of(at + which * half, half), half), :] = holder[
+                :half, first : first + columns
+            ]
     resid = jnp.zeros((latent_rows, columns), F32)
     for i in range(8):
         resid = resid + line_ref[i * latent_rows : (i + 1) * latent_rows, :].astype(F32)
     resid_ref[...] = resid
     odd = where_ref[0] & 1
     upper = (where_ref[0] >> 1) & 1
+    share = own // 2
     cut = heads // 2
-    share = own // 2
     for turn in range(4):
         x_differs, y_differs = 1 - (turn & 1), 1 - (turn >> 1)
         owner = 2 * (upper ^ y_differs) + (odd ^ x_differs)
@@ -957,20 +970,21 @@
         ref[1 - x_differs] = grad[cut:]
 
 
-def out_call(where, attn, line, line_other):
-    rows, heads = attn[0].shape
-    columns = line[0].shape[1]
+def out_call(where, attn, line, received, others):
+    rows, heads = attn.shape
+    columns = line.shape[1]
     own = columns // 4
     first = (2, heads // 2 + rows // 4, own)
     second = (2, heads // 2, own)
     shapes = [first, first, second, second]
+    operands = (attn, line, *received, *others)
     return pl.pallas_call(
         out_kernel,
         name="output_projection_gradient",
         grid_spec=pltpu.PrefetchScalarGridSpec(
             num_scalar_prefetch=1,
             grid=(1,),
-            in_specs=[held(a.shape) for a in (*attn, *line, *line_other)],
+            in_specs=[held(a.shape) for a in operands],
             out_specs=[held(shape) for shape in shapes],
             scratch_shapes=[
                 pltpu.VMEM((4 * rows, heads), BF16),
@@ -983,7 +997,7 @@
             flops=8 * rows * heads * columns, bytes_accessed=4_000_000, transcendentals=0
         ),
         compiler_params=pltpu.CompilerParams(vmem_limit_bytes=VMEM_LIMIT),
-    )(where, *attn, *line, *line_other)
+    )(where, *operands)
 
 
 def latent_kernel(
@@ -996,17 +1010,24 @@
     wq_ref,
     wk_ref,
     wv_ref,
+    routed_hbm,
     query_ref,
     pair_ref,
     message_ref,
     gain_out_ref,
+    routed_out_hbm,
     total_ref,
+    routed_ref,
+    sems,
 ):
+    arrive = pltpu.make_async_copy(routed_hbm, routed_ref, sems.at[0])
+    leave = pltpu.make_async_copy(routed_ref, routed_out_hbm, sems.at[1])
+    arrive.start()
     latent_rows, width = lat_ref.shape
     own, query_width = wq_ref.shape
     key_width = wk_ref.shape[0]
     scaling = HD ** (-0.5)
-    total_ref[...] = sum_ref[...] + got_ref[...].astype(F32)
+    total_ref[...] = sum_ref[...].astype(F32) + got_ref[...].astype(F32)
     total = total_ref[:latent_rows, :]
     low = total.astype(BF16)
     at = pl.ds(pl.multiple_of(where_ref[0] * own, own), own)
@@ -1026,6 +1047,8 @@
     )[:1]
     gain_term = gain_term + jnp.sum(wk.astype(F32) * pair[:key_width], axis=0, keepdims=True)
     gain_term = gain_term + jnp.sum(wv.astype(F32) * pair[key_width:], axis=0, keepdims=True)
+    arrive.wait()
+    leave.start()
     scaled = (total[:, :query_width] * scaling).astype(BF16)
     d_lat = dot_general(scaled, wq, 1, 1)
     d_lat = d_lat + jnp.dot(
@@ -1052,9 +1075,10 @@
         axis=0,
         keepdims=True,
     )
-
-
-def latent_call(where, sums, got, proj, latents, gain_lat, w_query, wk, wv, own):
+    leave.wait()
+
+
+def latent_call(where, sums, parts, proj, latents, gain_lat, w_query, wk, wv, own, routed):
     latent_rows, width = latents.shape
     query_width = w_query.shape[1]
     key_width = wk.shape[0]
@@ -1066,84 +1090,92 @@
             grid=(1,),
             in_specs=[
                 held(sums.shape),
-                held(got.shape),
+                *(held(part.shape) for part in parts),
                 held(proj.shape),
                 held(latents.shape),
                 held((1, width)),
                 pl.BlockSpec((own, query_width), lambda i, w: (w[0], 0)),
                 pl.BlockSpec((key_width, own), lambda i, w: (0, w[0])),
                 pl.BlockSpec((key_width, own), lambda i, w: (0, w[0])),
+                pl.BlockSpec(memory_space=pl.ANY),
             ],
             out_specs=[
                 held((own, query_width)),
                 held((2 * key_width, own)),
                 held((latent_rows + 8, own + 128)),
                 held((1, own // 2)),
+                pl.BlockSpec(memory_space=pl.ANY),
             ],
-            scratch_shapes=[pltpu.VMEM(sums.shape, F32)],
+            scratch_shapes=[
+                pltpu.VMEM(sums.shape, F32),
+                pltpu.VMEM(routed.shape, BF16),
+                pltpu.SemaphoreType.DMA((2,)),
+            ],
         ),
         out_shape=[
             jax.ShapeDtypeStruct((own, query_width), F32),
             jax.ShapeDtypeStruct((2 * key_width, own), F32),
             jax.ShapeDtypeStruct((latent_rows + 8, own + 128), F32),
             jax.ShapeDtypeStruct((1, own // 2), F32),
+            jax.ShapeDtypeStruct(routed.shape, BF16),
         ],
         cost_estimate=pl.CostEstimate(
             flops=100_000_000, bytes_accessed=3_000_000, transcendentals=0
         ),
         compiler_params=pltpu.CompilerParams(vmem_limit_bytes=VMEM_LIMIT),
-    )(where, sums, got, proj, latents, gain_lat.reshape(1, width), w_query, wk, wv)
+    )(where, sums, *parts, proj, latents, gain_lat.reshape(1, width), w_query, wk, wv, routed)
 
 
 def plane_kernel(
     value_ref,
     value_got_ref,
+    value_last_ref,
     key_ref,
     key_got_ref,
-    both_ref,
-    low_ref,
+    key_last_ref,
+    going_ref,
     high_ref,
-    kept_ref,
 ):
-    key_width = value_ref.shape[1]
-    for i, ref in enumerate((both_ref, low_ref, high_ref, kept_ref)):
-        ref[:key_width, :] = (key_ref[i] + key_got_ref[i].astype(F32)).astype(ref.dtype)
-        ref[key_width:, :] = (value_ref[i] + value_got_ref[i].astype(F32)).astype(ref.dtype)
-
-
-def plane_call(value, value_got, key, key_got):
+    key_width = value_ref.shape[-2]
+    for i, ref in enumerate((going_ref.at[0], going_ref.at[1], high_ref)):
+        for j, parts in enumerate(
+            (
+                (key_ref, key_got_ref, key_last_ref),
+                (value_ref, value_got_ref, value_last_ref),
+            )
+        ):
+            total = sum(part[i].astype(F32) for part in parts)
+            ref[j * key_width : (j + 1) * key_width, :] = total.astype(ref.dtype)
+
+
+def plane_call(value, value_got, value_last, key, key_got, key_last):
     _, key_width, own = value.shape
+    upper = pl.BlockSpec((4, key_width, own), lambda i: (1, 0, 0))
+    last = pl.BlockSpec((4, key_width, own), lambda i: (0, 0, 0))
     shape = (2 * key_width, own)
     return pl.pallas_call(
         plane_kernel,
         name="plane_sum",
-        out_shape=[jax.ShapeDtypeStruct(shape, BF16)] * 3 + [jax.ShapeDtypeStruct(shape, F32)],
-        cost_estimate=pl.CostEstimate(flops=1_000_000, bytes_accessed=5_000_000, transcendentals=0),
+        grid=(1,),
+        in_specs=[upper, upper, last] * 2,
+        out_specs=[held((2, *shape)), held(shape)],
+        out_shape=[
+            jax.ShapeDtypeStruct((2, *shape), BF16),
+            jax.ShapeDtypeStruct(shape, F32),
+        ],
+        cost_estimate=pl.CostEstimate(flops=1_000_000, bytes_accessed=3_000_000, transcendentals=0),
         compiler_params=pltpu.CompilerParams(vmem_limit_bytes=VMEM_LIMIT),
-    )(value, value_got, key, key_got)
-
-
-def halve_kernel(kept_ref, got_ref, going_ref, rest_ref):
-    half = going_ref.shape[0]
-    going_ref[...] = (kept_ref[:half].astype(F32) + got_ref[:half].astype(F32)).astype(BF16)
-    rest_ref[...] = kept_ref[half:].astype(F32) + got_ref[half:].astype(F32)
-
-
-def halve_call(kept, got):
-    shape = (kept.shape[0] // 2,) + kept.shape[1:]
-    return pl.pallas_call(
-        halve_kernel,
-        name="halve_sum",
-        out_shape=[jax.ShapeDtypeStruct(shape, BF16), jax.ShapeDtypeStruct(shape, F32)],
-        cost_estimate=pl.CostEstimate(flops=1_000_000, bytes_accessed=4_000_000, transcendentals=0),
-        compiler_params=pltpu.CompilerParams(vmem_limit_bytes=VMEM_LIMIT),
-    )(kept, got)
+    )(value, value_got, value_last, key, key_got, key_last)
 
 
 def final_kernel(
     where_ref,
-    kept_ref,
-    both_ref,
+    value_ref,
+    value_got_ref,
+    value_last_ref,
+    key_ref,
+    key_got_ref,
+    key_last_ref,
     low_ref,
     high_ref,
     gain_ref,
@@ -1155,32 +1187,36 @@
     gain_term_ref,
 ):
     key_width = wk_ref.shape[0]
-    total = (
-        kept_ref[...]
-        + both_ref[...].astype(F32)
-        + low_ref[...].astype(F32)
-        + high_ref[...].astype(F32)
-    )
-    term = jnp.sum(wk_ref[...].astype(F32) * total[:key_width], axis=0, keepdims=True)
-    term = term + jnp.sum(wv_ref[...].astype(F32) * total[key_width:], axis=0, keepdims=True)
+    term = jnp.zeros((1, wk_ref.shape[1]), F32)
+    for j, (w_ref, out_ref, parts) in enumerate(
+        (
+            (wk_ref, key_grad_ref, (key_ref, key_got_ref, key_last_ref)),
+            (wv_ref, value_grad_ref, (value_ref, value_got_ref, value_last_ref)),
+        )
+    ):
+        at = slice(j * key_width, (j + 1) * key_width)
+        total = sum(part[0].astype(F32) for part in parts)
+        total = total + low_ref[0, at, :].astype(F32) + high_ref[at, :].astype(F32)
+        term = term + jnp.sum(w_ref[...].astype(F32) * total, axis=0, keepdims=True)
+        out_ref[...] = total * gain_ref[...] + pair_ref[at, :]
     gain_term_ref[...] = jnp.broadcast_to(term, gain_term_ref.shape)
-    total = total * gain_ref[...] + pair_ref[...]
-    key_grad_ref[...] = total[:key_width]
-    value_grad_ref[...] = total[key_width:]
-
-
-def final_call(where, kept, both, low, high, gain_ctx, pair, wk, wv):
-    rows, own = kept.shape
+
+
+def final_call(where, value, value_got, value_last, key, key_got, key_last, line, gain_ctx, pair, wk, wv):
+    rows, own = pair.shape
     width = gain_ctx.shape[0]
     key_width = rows // 2
     w_spec = pl.BlockSpec((key_width, own), lambda i, w: (0, w[0]))
+    end = pl.BlockSpec((1, key_width, own), lambda i, w: (7, 0, 0))
+    last = pl.BlockSpec((1, key_width, own), lambda i, w: (3, 0, 0))
     return pl.pallas_call(
         final_kernel,
         name="key_value_gradients",
         grid_spec=pltpu.PrefetchScalarGridSpec(
             num_scalar_prefetch=1,
             grid=(1,),
-            in_specs=[held(kept.shape)] * 4
+            in_specs=[end, end, last] * 2
+            + [pl.BlockSpec((1, rows, own), lambda i, w: (1, 0, 0)), held(pair.shape)]
             + [pl.BlockSpec((1, own), lambda i, w: (0, w[0])), held(pair.shape), w_spec, w_spec],
             out_specs=[held((key_width, own)), held((key_width, own)), held((8, own))],
         ),
@@ -1191,7 +1227,87 @@
         ],
         cost_estimate=pl.CostEstimate(flops=1_000_000, bytes_accessed=3_000_000, transcendentals=0),
         compiler_params=pltpu.CompilerParams(vmem_limit_bytes=VMEM_LIMIT),
-    )(where, kept, both, low, high, gain_ctx.reshape(1, width), pair, wk, wv)
+    )(
+        where,
+        value,
+        value_got,
+        value_last,
+        key,
+        key_got,
+        key_last,
+        *line,
+        gain_ctx.reshape(1, width),
+        pair,
+        wk,
+        wv,
+    )
+
+
+def out_final_kernel(
+    where_ref,
+    first_kept_ref,
+    first_got_ref,
+    first_last_ref,
+    second_kept_ref,
+    second_got_ref,
+    second_last_ref,
+    message_ref,
+    message_got_ref,
+    lat_ref,
+    gain_ref,
+    out_ref,
+    latent_ref,
+    gain_lat_ref,
+):
+    heads, own = out_ref.shape
+    latent_rows, width = lat_ref.shape
+    share = own // 2
+    cut = heads // 2
+    first = sum(
+        part.astype(F32) for part in (first_kept_ref[0], first_got_ref[0], first_last_ref[...])
+    )
+    out_ref[:cut, :] = first[:cut]
+    out_ref[cut:, :] = sum(
+        part.astype(F32) for part in (second_kept_ref[0], second_got_ref[0], second_last_ref[...])
+    )
+    resid = first[cut:]
+    resid = jnp.concatenate([resid[:, :share], resid[:, share:]], axis=0)
+    mine = pl.ds(pl.multiple_of(where_ref[1] * share, share), share)
+    d_lat = message_ref[:, mine] + message_got_ref[:, mine]
+    lat_dot = message_ref[:latent_rows, own : own + 1] + message_got_ref[:latent_rows, own : own + 1]
+    lat = lat_ref[...].astype(F32)
+    inverse = lax.rsqrt(jnp.mean(lat * lat, axis=-1, keepdims=True) + EPSILON)
+    at = pl.ds(pl.multiple_of(where_ref[0] * own + where_ref[1] * share, share), share)
+    hat = lat_ref[:, at].astype(F32) * inverse
+    latent_ref[...] = resid + inverse * (gain_ref[:, at] * d_lat[:latent_rows] - hat * (lat_dot / width))
+    gain_lat_ref[...] = d_lat[latent_rows : latent_rows + 1]
+
+
+def out_final_call(where, parts, message, message_got, latents, gain_lat):
+    _, rows, own = parts[0].shape
+    latent_rows, width = latents.shape
+    heads = 2 * (rows - latent_rows // 2)
+    shapes = [(heads, own), (latent_rows, own // 2), (1, own // 2)]
+    return pl.pallas_call(
+        out_final_kernel,
+        name="output_gradient_sum",
+        grid_spec=pltpu.PrefetchScalarGridSpec(
+            num_scalar_prefetch=1,
+            grid=(1,),
+            in_specs=[
+                pl.BlockSpec((1, *part.shape[1:]), lambda i, w: (1, 0, 0))
+                if part.ndim == 3
+                else held(part.shape)
+                for part in parts
+            ]
+            + [held(a.shape) for a in (message, message_got, latents)]
+            + [held((1, width))],
+            out_specs=[held(shape) for shape in shapes],
+        ),
+        out_shape=[jax.ShapeDtypeStruct(shape, F32) for shape in shapes],
+        cost_estimate=pl.CostEstimate(flops=1_000_000, bytes_accessed=3_000_000, transcendentals=0),
+        compiler_params=pltpu.CompilerParams(vmem_limit_bytes=VMEM_LIMIT),
+    )(where, *parts, message, message_got, latents, gain_lat.reshape(1, width))
 
 
 def add_halves(left, right):
@@ -1235,7 +1351,6 @@
     wk = w_key.T
     wv = w_value.T
     turned_routes = routes.reshape(1, -1)
-    mp_scalar = mp_index.reshape(1)
     where = jnp.stack([dp_index, mp_index])
 
     returned = exchange(cotangent)
@@ -1246,9 +1361,10 @@
     (attn_rows, k, v, inv_row, q, lat_k, lat_v, lat_proj, p, lat_p) = forward_call(
         context, counts, w_query, wk, wv, latents, gain_ctx, gain_lat
     )
+    wk_other, wv_other, attn_rows = lax.optimization_barrier((wk_other, wv_other, attn_rows))
     attn_other = swap_cores(attn_rows)
     out_hat, out_inv, outgoing = branch_call(
-        mp_scalar,
+        where,
         attn_rows,
         attn_other,
         w_out,
@@ -1259,24 +1375,14 @@
         slots,
         slot_count,
     )
+
     routed = exchange(outgoing)
-
     returned, out_inv = lax.optimization_barrier((returned, out_inv))
     returned_other = swap_cores(returned)
-    (
-        line_own,
-        line_low,
-        line_high,
-        line_both,
-        pair,
-        lat_terms,
-        value_going,
-        value_kept,
-        key_going,
-        key_kept,
-    ) = backward_call(
+    backward = backward_call(
         where,
         counts,
+        attn_rows,
         returned,
         returned_other,
         out_hat,
@@ -1288,25 +1394,29 @@
         context,
         slot_count,
     )
+    backward = lax.optimization_barrier(backward)
+    (
+        line_own,
+        line_high,
+        pair,
+        message,
+        value_going,
+        value_kept,
+        key_going,
+        key_kept,
+    ) = backward
 
     value_got = swap(value_going, 1)
     key_got = swap(key_going, 2)
-
     pair_other = swap_cores(pair)
+
     ctx_grad = patch_call(
-        mp_scalar, pair, pair_other, wk, wv, wk_other, wv_other, context, inv_row, gain_ctx
-    )
-
-    line_low, line_high, line_both, attn_line, pair_other = lax.optimization_barrier(
-        (line_low, line_high, line_both, attn_rows, pair_other)
-    )
-    got_low = swap(line_low, 4)
+        where, pair, pair_other, wk, wv, wk_other, wv_other, context, inv_row, gain_ctx
+    )
+
+    line_high, message, pair_other = lax.optimization_barrier((line_high, message, pair_other))
     got_high = swap(line_high, 8)
-    got_both = swap(line_both, 12)
-    attn_high = swap(attn_line, 8)
-    attn_low = swap(attn_line, 4)
-    attn_both = swap(attn_high, 4)
-
+    got_low = swap(message, 4)
     value_got, key_got, ctx_grad, routed = lax.optimization_barrier(
         (value_got, key_got, ctx_grad, routed)
     )
@@ -1314,64 +1424,79 @@
     key_got = key_got.reshape((8,) + key_got.shape[2:])
     value_going = add_halves(value_kept[:4], value_got[:4]).astype(BF16)
     key_going = add_halves(key_kept[:4], key_got[:4]).astype(BF16)
-    value_kept = add_halves(value_kept[4:], value_got[4:])
-    key_kept = add_halves(key_kept[4:], key_got[4:])
-    value_got = swap(value_going, 2)
-    key_got = swap(key_going, 1)
-
-    lat_terms, got_low, got_high, got_both, value_kept, key_kept = lax.optimization_barrier(
-        (lat_terms, got_low, got_high, got_both, value_kept, key_kept)
-    )
-    lat_sum = lat_terms.astype(F32)
-    for turn in (4, 8, 1):
-        lat_sum = lat_sum + swap(lat_sum.astype(BF16), turn).astype(F32)
-    lat_got = swap(lat_sum.astype(BF16), 2)
+    value_last = swap(value_going, 2)
+    key_last = swap(key_going, 1)
+
+    got_low, got_high, value_going, key_going = lax.optimization_barrier(
+        (got_low, got_high, value_going, key_going)
+    )
+    lat_at = message.shape[1] - lat_proj.shape[1]
+    lat_sum = add_halves(message[:, lat_at:], got_low[:, lat_at:])
+    lat_got = swap(lat_sum.astype(BF16), 8)
+    forwarded = swap(got_high, 4)
+    other_low = swap_cores(got_low)
+    other_high = swap_cores(got_high)
+
+    planes = plane_call(value_kept, value_got, value_last, key_kept, key_got, key_last)
+    (going, high), lat_got, forwarded = lax.optimization_barrier((planes, lat_got, forwarded))
+    low = swap(going, 4)
+    other_forwarded = swap_cores(forwarded)
+    lat_sum = add_halves(lat_sum, lat_got)
+    lat_sum = add_halves(lat_sum, swap(lat_sum.astype(BF16), 1)).astype(BF16)
+    lat_parts = (swap(lat_sum, 2),)
 
     first_going, first_kept, second_going, second_kept = out_call(
         where,
-        (attn_rows, attn_low, attn_high, attn_both),
-        (line_own, got_low, got_high, got_both),
-        (swap_cores(got_low), swap_cores(got_high), swap_cores(got_both)),
-    )
-
-    both, low, high, kept = plane_call(value_kept, value_got, key_kept, key_got)
-    first_going, second_going, kept = lax.optimization_barrier((first_going, second_going, kept))
-    both = swap(both, 12)
-    low = swap(low, 4)
-    high = swap(high, 8)
-
+        attn_rows,
+        line_own,
+        (got_low, got_high, forwarded),
+        (other_low, other_high, other_forwarded),
+    )
+    low, lat_parts, first_going, second_going = lax.optimization_barrier(
+        (low, lat_parts, first_going, second_going)
+    )
+    high = swap(add_halves(high, low[0]).astype(BF16), 8)
     first_got = swap(first_going, 1)
     second_got = swap(second_going, 2)
-    first = swap(add_halves(first_kept[0], first_got[0]).astype(BF16), 2)
-    second = swap(add_halves(second_kept[0], second_got[0]).astype(BF16), 1)
-    first = add_halves(first_kept[1], first_got[1]) + first.astype(F32)
-    second = add_halves(second_kept[1], second_got[1]) + second.astype(F32)
-    cut = query_width // 2
-    grad_w_out = jnp.concatenate([first[:cut], second], axis=0)
+
+    grad_w_query, pair_lat, message, grad_gain_out, routed = latent_call(
+        where, lat_sum, lat_parts, lat_proj, latents, gain_lat, w_query, wk, wv, own_width, routed
+    )
+    first_got, second_got, high, message, pair_lat = lax.optimization_barrier(
+        (first_got, second_got, high, message, pair_lat)
+    )
+    first_last = swap(add_halves(first_kept[0], first_got[0]).astype(BF16), 2)
+    second_last = swap(add_halves(second_kept[0], second_got[0]).astype(BF16), 1)
+    message_got = swap_cores(message)
+
+    low, high, pair_lat, message_got = lax.optimization_barrier((low, high, pair_lat, message_got))
+    grad_key, grad_value, gain_term = final_call(
+        where,
+        value_kept,
+        value_got,
+        value_last,
+        key_kept,
+        key_got,
+        key_last,
+        (low, high),
+        gain_ctx,
+        pair_lat,
+        wk,
+        wv,
+    )
+    gain_got = swap_cores(gain_term)
+    first_last, second_last, gain_term = lax.optimization_barrier(
+        (first_last, second_last, gain_term)
+    )
+    grad_w_out, grad_latents, grad_gain_lat = out_final_call(
+        where,
+        (first_kept, first_got, first_last, second_kept, second_got, second_last),
+        message,
+        message_got,
+        latents,
+        gain_lat,
+    )
     share = own_width // 2
-    resid_sum = jnp.concatenate([first[cut:, :share], first[cut:, share:]], axis=0)
-
-    grad_w_query, pair_lat, message, grad_gain_out = latent_call(
-        where, lat_sum, lat_got, lat_proj, latents, gain_lat, w_query, wk, wv, own_width
-    )
-    message = message + swap_cores(message)
-
-    grad_key, grad_value, gain_term = final_call(
-        where, kept, both, low, high, gain_ctx, pair_lat, wk, wv
-    )
-    gain_term = gain_term + swap_cores(gain_term)
-
-    def mine_of(array, axis):
-        return lax.dynamic_slice_in_dim(
-            array, dp_index * own_width + mp_index * share, share, axis
-        )
-
-    lat_hat, lat_inv = norm_parts(latents.astype(F32))
-    mine = lax.dynamic_slice_in_dim(message, mp_index * share, share, 1)
-    lat_dot = message[:latent_rows, own_width : own_width + 1] / width
-    grad_latents = resid_sum + lat_inv * (
-        mine_of(gain_lat, 0) * mine[:latent_rows] - mine_of(lat_hat, 1) * lat_dot
-    )
     return (
         routed,
         ctx_grad,
@@ -1380,8 +1505,8 @@
         grad_value.T,
         grad_w_out,
         grad_latents,
-        lax.dynamic_slice_in_dim(gain_term, mp_index * share, share, 1)[0],
-        mine[latent_rows],
+        lax.dynamic_slice_in_dim(gain_term + gain_got, mp_index * share, share, 1)[0],
+        grad_gain_lat[0],
         grad_gain_out[0],
     )
 

time: 169 us -> 155 us (0.917)
  waiting for transfers between devices: 38.5 us -> 23.3 us
  Pallas kernels: 63.7 us -> 70.9 us
  local copies, waits for them, and re-layouts: 6.8 us -> 2.9 us
  other arithmetic: 14.2 us -> 11.3 us
    ppermute x21 -> x16, waiting for transfers between devices: 37 us -> 19.8 us  [swap(): return lax.ppermute(array, 'dp', [(i, i ^ turn) for i in range(dp_count)])]
    convert_element_type x6, other arithmetic: 3.9 us -> 7.62 us  [the longest x2 2.29 us: local(): lat_sum = add_halves(lat_sum, swap(lat_sum.astype(BF16), 1)).astype(BF16)]
    pallas_call x1 -> x2, Pallas kernels: 2.59 us -> 6.11 us  [the longest x1 3.51 us: out_final_call(): pl.pallas_call(out_final_kernel, name='output_gradient_sum', grid_spec=pl...]
    add x5 -> x1, other arithmetic: 3.5 us -> 0.69 us  [local(): gain_term + gain_got]
    unnamed x21 -> x26, local copies, waits for them, and re-layouts: 4.97 us -> 2.38 us
    ppermute x11, waiting for transfers between devices: 1.47 us -> 3.54 us  [swap_cores(): return lax.ppermute(array, 'mp', [(0, 1), (1, 0)])]
    pallas_call x1, Pallas kernels: 3.72 us -> 5.49 us  [latent_call(): pl.pallas_call(latent_kernel, name='latent_gradients', grid_spec=pltpu.Pr...]
    ppermute x21 -> x16, starting transfers between devices: 27 us -> 27.9 us  [swap(): return lax.ppermute(array, 'dp', [(i, i ^ turn) for i in range(dp_count)])]
  transfers between devices with their start and end apart: 34 -> 29, of which waited for: 11 -> 13; matrix products, arithmetic and copies ran while one was open for 8% -> 6% of each run, Pallas kernels for 38% -> 44%
where the time goes in v2:
time: 155 us; the launch traced here: 154 us
  Pallas kernels  70.9 us (46%)
  starting transfers between devices  45.1 us (29%)
  waiting for transfers between devices  23.3 us (15%)
  other arithmetic  11.3 us (7%)
  local copies, waits for them, and re-layouts  2.9 us (2%)
    ppermute x16, starting transfers between devices, swap(): return lax.ppermute(array, 'dp', [(i, i ^ turn) for i in range(dp_count)])  27.9 us
    ppermute x16, waiting for transfers between devices, swap(): return lax.ppermute(array, 'dp', [(i, i ^ turn) for i in range(dp_count)])  19.8 us
    pallas_call x1, Pallas kernels, backward_call(): pl.pallas_call(functools.partial(backward_kernel, slot_count), name='atte...  16.1 us
    pallas_call x1, Pallas kernels, forward_call(): pl.pallas_call(forward_kernel, name='forward_attention', in_specs=[pl.Blo...  15 us
    all_to_all x2, starting transfers between devices, exchange(): lax.all_to_all(blocks, 'dp', split_axis=0, concat_axis=0, tiled=True)  14.7 us
    pallas_call x1, Pallas kernels, patch_call(): pl.pallas_call(functools.partial(patch_kernel, width), name='patch_gradie...  10.2 us
    pallas_call x1, Pallas kernels, branch_call(): pl.pallas_call(functools.partial(branch_kernel, slot_count), name='branch...  9.98 us
    pallas_call x1, Pallas kernels, latent_call(): pl.pallas_call(latent_kernel, name='latent_gradients', grid_spec=pltpu.Pr...  5.49 us
  transfers between devices with their start and end apart: 29, of which 13 were waited for; matrix products, arithmetic and copies ran while one was open for 6% of the time, Pallas kernels for 44%

profile of v2, /device:TPU:0, one launch (start us, length us, event | category | flops | bytes accessed | tf_op | source)
XLA Modules:
  0.0 154.3 jit_solution(18120427390360312021)
XLA Ops:
  1.2 7.9 %all-to-all-start = ((bf16[16,16,2048]{2,1,0:T(8,128)(2,1)}), bf16[16,16,2048]{2,1,0:T(8,128)(2,1)}, u32[]{:S(2)}, u32[]{:S(2)}) async-start(bf16[16,16,2048]{2,1,0:T(8,128)(2,1)} %bitcast.41), calls=%async_computation | async-start | bytes 2097152 | tf_op jit(solution)/shard_map/all_to_all | solution.py:1347
  9.7 15.0 %forward_attention.1 = (bf16[128,768]{1,0:T(8,128)(2,1)}, bf16[2,1024,128]{2,1,0:T(8,128)(2,1)}, bf16[2,1024,128]{2,1,0:T(8,128)(2,1)}, f32[8,1024]{1,0:T(8,128)...) custom-call(s32[1,2]{1,0:T(1,128)} %counts_ref.3, ...), custom_call_target="tpu_custom_call" | custom-call | flops 5000000000 | bytes 24000000 | tf_op jit(solution)/shard_map/forward_attention/pallas_call | solution.py:278
  27.1 10.0 %branch_norm.1 = (f32[128,4096]{1,0:T(8,128)}, f32[128,1]{1,0:T(8,128)}, bf16[256,2048]{1,0:T(8,128)(2,1)}) custom-call(s32[2]{0:T(128)} %pad_add_fusion.where_ref, bf16[128,768]{1,0:T(8,128)(2,1)} %get-tuple-element.82.own_ref.attn_ref.attn_own_ref, bf16[128,768]{1,0:T(8,128)(2,1)} %copy-done.10, bf16[64,4096]{1,0:T(8,128)(2,1)} %lat_ref.5, ...), custom_call_target="tpu_custom_call" | custom-call | flops 1610612736 | bytes 16000000 | tf_op jit(solution)/shard_map/branch_norm/pallas_call | solution.py:387
  37.4 6.8 %all-to-all-start.1 = ((bf16[16,16,2048]{2,1,0:T(8,128)(2,1)}), bf16[16,16,2048]{2,1,0:T(8,128)(2,1)}, u32[]{:S(2)}, u32[]{:S(2)}) async-start(bf16[16,16,2048]{2,1,0:T(8,128)(2,1)} %bitcast.42), calls=%async_computation.1 | async-start | bytes 2097152 | tf_op jit(solution)/shard_map/all_to_all | solution.py:1347
  44.2 16.1 %attention_backward.1 = (bf16[128,1024]{1,0:T(8,128)(2,1)}, bf16[64,3584]{1,0:T(8,128)(2,1)}, bf16[400,1024]{1,0:T(8,128)(2,1)}, bf16[80,3712]{1,0:T(8,128)(2,1)...) custom-call(s32[2]{0:T(128)} %pad_add_fusion.where_ref, ...), custom_call_target="tpu_custom_call" | custom-call | flops 5000000000 | bytes 26000000 | tf_op jit(solution)/shard_map/attention_backward/pallas_call | solution.py:784
  60.5 1.9 %collective-permute-start.8 = (bf16[8,192,256]{2,1,0:T(8,128)(2,1)}, bf16[8,192,256]{2,1,0:T(8,128)(2,1)}, u32[]{:S(2)}, u32[]{:S(2)}) collective-permute-start(bf16[8,192,256]{2,1,0:T(8,128)(2,1)} %get-tuple-element.101), channel_id=1, source_target_pairs={{0,2},{2,0},{4,6},{6,4},{8,10},{10,8},{12,14},{14,12},{16,18},{18,... | collective-permute-start | bytes 2359304 | tf_op jit(solution)/shard_map/ppermute | solution.py:1343
  66.2 2.4 %collective-permute-start.7 = (bf16[64,3584]{1,0:T(8,128)(2,1)}, bf16[64,3584]{1,0:T(8,128)(2,1)}, u32[]{:S(2)}, u32[]{:S(2)}) collective-permute-start(bf16[64,3584]{1,0:T(8,128)(2,1)} %get-tuple-element.99), channel_id=1, source_target_pairs={{0,16},{2,18},{4,20},{6,22},{8,24},{10,26},{12,28},{14,30},{16,0},... | collective-permute-start | bytes 1376264 | tf_op jit(solution)/shard_map/ppermute | solution.py:1343
  68.6 10.2 %patch_gradient.1 = bf16[1024,2048]{1,0:T(8,128)(2,1)} custom-call(s32[2]{0:T(128)} %pad_add_fusion.where_ref, bf16[400,1024]{1,0:T(8,128)(2,1)} %get-tuple-element.97.own_ref, bf16[400,1024]{1,0:T(8,128)(2,1)} %copy-done.5, bf16[192,4096]{1,0:T(8,128)(2,1)} %bitcast.31, bf16[192,4096]{1,0:T(8,128)(2,1)} %bitcast.36, ...), custom_call_target="tpu_custom_call" | custom-call | flops 3300000000 | bytes 14000000 | tf_op jit(solution)/shard_map/patch_gradient/pallas_call | solution.py:877
  78.8 4.9 %collective-permute-done.8.value_got_ref = bf16[8,192,256]{2,1,0:T(8,128)(2,1)} collective-permute-done((bf16[8,192,256]{2,1,0:T(8,128)(2,1)}, bf16[8,192,256]{2,1,0:T(8,128)(2,1)}, u32[]{:S(2)}, u32[]{:S(2)}) %collective-permute-start.8) | collective-permute-done | bytes 786464 | tf_op jit(solution)/shard_map/ppermute | solution.py:1343
  90.6 1.9 %collective-permute-start.13 = (bf16[64,3584]{1,0:T(8,128)(2,1)}, bf16[64,3584]{1,0:T(8,128)(2,1)}, u32[]{:S(2)}, u32[]{:S(2)}) collective-permute-start(bf16[64,3584]{1,0:T(8,128)(2,1)} %collective-permute-done.7.high_ref), channel_id=1, source_target_pairs={{0,8},{2,10},{4,12},{6,14},{8,0},{10,2},{12,4},{14,6},{16,24},{18,... | collective-permute-start | bytes 1376264 | tf_op jit(solution)/shard_map/ppermute | solution.py:1343
  93.5 3.2 %collective-permute-start.12 = (bf16[80,1152]{1,0:T(8,128)(2,1)S(1)}, bf16[80,1152]{1,0:T(8,128)(2,1)S(1)}, u32[]{:S(2)}, u32[]{:S(2)}) collective-permute-start(bf16[80,1152]{1,0:T(8,128)(2,1)S(1)} %fusion.2), channel_id=1, source_target_pairs={{0,16},{2,18},{4,20},{6,22},{8,24},{10,26},{12,28},{14,30},{16,0},... | collective-permute-start | bytes 552968 | tf_op jit(solution)/shard_map/ppermute | solution.py:1343
  99.0 2.6 %plane_sum.1 = (bf16[2,384,256]{2,1,0:T(8,128)(2,1)}, f32[384,256]{1,0:T(8,128)}) custom-call(bf16[8,192,256]{2,1,0:T(8,128)(2,1)} %get-tuple-element.100.value_ref, bf16[8,192,256]{2,1,0:T(8,128)(2,1)} %collective-permute-done.8.value_got_ref, bf16[4,192,256]{2,1,0:T(8,128)(2,1)} %copy-done.1, bf16[8,192,256]{2,1,0:T(8,128)(2,1)} %bitcast.39, ...), custom_call_target="tpu_custom_call" | custom-call | flops 1000000 | bytes 3000000 | tf_op jit(solution)/shard_map/plane_sum/pallas_call | solution.py:1156
  101.7 3.9 %collective-permute-done.12 = bf16[80,1152]{1,0:T(8,128)(2,1)S(1)} collective-permute-done((bf16[80,1152]{1,0:T(8,128)(2,1)S(1)}, bf16[80,1152]{1,0:T(8,128)(2,1)S(1)}, u32[]{:S(2)}, u32[]{:S(2)}) %collective-permute-start.12) | collective-permute-done | bytes 184352 | tf_op jit(solution)/shard_map/ppermute | solution.py:1343
  110.0 3.6 %collective-permute-start.15 = (bf16[2,384,256]{2,1,0:T(8,128)(2,1)}, bf16[2,384,256]{2,1,0:T(8,128)(2,1)S(1)}, u32[]{:S(2)}, u32[]{:S(2)}) collective-permute-start(bf16[2,384,256]{2,1,0:T(8,128)(2,1)} %get-tuple-element.114), channel_id=1, source_target_pairs={{0,8},{2,10},{4,12},{6,14},{8,0},{10,2},{12,4},{14,6},{16,24},{18,... | collective-permute-start | bytes 1179656 | tf_op jit(solution)/shard_map/ppermute | solution.py:1343
  116.5 5.0 %output_projection_gradient.1 = (bf16[2,416,256]{2,1,0:T(8,128)(2,1)}, bf16[2,416,256]{2,1,0:T(8,128)(2,1)}, bf16[2,384,256]{2,1,0:T(8,128)(2,1)}, bf16[2,384,256]{2,1,0:T(8,128)(2,1)}) custom-call(s32[2]{0:T(128)} %pad_add_fusion.where_ref, bf16[128,768]{1,0:T(8,128)(2,1)} %get-tuple-element.82.own_ref.attn_ref.attn_own_ref, ...), custom_call_target="tpu_custom_call" | custom-call | flops 805306368 | bytes 4000000 | tf_op jit(solution)/shard_map/output_projection_gradient/pallas_call | solution.py:981
  121.7 1.9 %collective-permute-done.15.low_ref = bf16[2,384,256]{2,1,0:T(8,128)(2,1)S(1)} collective-permute-done((bf16[2,384,256]{2,1,0:T(8,128)(2,1)}, bf16[2,384,256]{2,1,0:T(8,128)(2,1)S(1)}, u32[]{:S(2)}, u32[]{:S(2)}) %collective-permute-start.15) | collective-permute-done | bytes 393248 | tf_op jit(solution)/shard_map/ppermute | solution.py:1343
  124.3 1.7 %fusion.1 = bf16[384,256]{1,0:T(8,128)(2,1)} fusion(f32[384,256]{1,0:T(8,128)} %get-tuple-element.128, bf16[2,384,256]{2,1,0:T(8,128)(2,1)S(1)} %collective-permute-done.15.low_ref), kind=kLoop, calls=%fused_computation.5 | loop fusion | flops 294912 | bytes 786432 | tf_op jit(solution)/shard_map/convert_element_type | solution.py:1458
  126.0 2.8 %collective-permute-start.22 = (bf16[384,256]{1,0:T(8,128)(2,1)}, bf16[384,256]{1,0:T(8,128)(2,1)}, u32[]{:S(2)}, u32[]{:S(2)}) collective-permute-start(bf16[384,256]{1,0:T(8,128)(2,1)} %fusion.1), channel_id=1, source_target_pairs={{0,16},{2,18},{4,20},{6,22},{8,24},{10,26},{12,28},{14,30},{16,0},... | collective-permute-start | bytes 589832 | tf_op jit(solution)/shard_map/ppermute | solution.py:1343
  128.8 5.5 %latent_gradients.1 = (f32[256,768]{1,0:T(8,128)}, f32[384,256]{1,0:T(8,128)}, f32[72,384]{1,0:T(8,128)}, f32[1,128]{1,0:T(1,128)}, bf16[256,2048]{1,0:T(8,128)(2,1)}) custom-call(s32[2]{0:T(128)} %pad_add_fusion.where_ref, bf16[80,1152]{1,0:T(8,128)(2,1)} %copy-done.6, bf16[80,1152]{1,0:T(8,128)(2,1)} %copy-done.11, ...), custom_call_target="tpu_custom_call" | custom-call | flops 100000000 | bytes 3000000 | tf_op jit(solution)/shard_map/latent_gradients/pallas_call | solution.py:1085
  134.3 3.6 %collective-permute-done.22.high_ref = bf16[384,256]{1,0:T(8,128)(2,1)} collective-permute-done((bf16[384,256]{1,0:T(8,128)(2,1)}, bf16[384,256]{1,0:T(8,128)(2,1)}, u32[]{:S(2)}, u32[]{:S(2)}) %collective-permute-start.22) | collective-permute-done | bytes 196640 | tf_op jit(solution)/shard_map/ppermute | solution.py:1343
  138.7 1.7 %collective-permute-start.24 = (bf16[416,256]{1,0:T(8,128)(2,1)}, bf16[416,256]{1,0:T(8,128)(2,1)S(1)}, u32[]{:S(2)}, u32[]{:S(2)}) collective-permute-start(bf16[416,256]{1,0:T(8,128)(2,1)} %fusion.4), channel_id=1, source_target_pairs={{0,4},{2,6},{4,0},{6,2},{8,12},{10,14},{12,8},{14,10},{16,20},{18,... | collective-permute-start | bytes 638984 | tf_op jit(solution)/shard_map/ppermute | solution.py:1343
  140.5 1.7 %fusion.5 = bf16[384,256]{1,0:T(8,128)(2,1)} fusion(bf16[2,384,256]{2,1,0:T(8,128)(2,1)} %collective-permute-done.21.second_got_ref, bf16[2,384,256]{2,1,0:T(8,128)(2,1)} %get-tuple-element.141.second_kept_ref), kind=kLoop, calls=%fused_computation.13 | loop fusion | flops 393216 | bytes 589824 | tf_op jit(solution)/shard_map/convert_element_type | solution.py:1469
  145.2 3.0 %key_value_gradients.1 = (f32[192,256]{1,0:T(8,128)}, f32[192,256]{1,0:T(8,128)}, f32[8,256]{1,0:T(8,128)}) custom-call(s32[2]{0:T(128)} %pad_add_fusion.where_ref, bf16[8,192,256]{2,1,0:T(8,128)(2,1)} %get-tuple-element.100.value_ref, bf16[8,192,256]{2,1,0:T(8,128)(2,1)} %collective-permute-done.8.value_got_ref, bf16[4,192,256]{2,1,0:T(8,128)(2,1)} %copy-done.1, ...), custom_call_target="tpu_custom_call" | custom-call | flops 1000000 | bytes 3000000 | tf_op jit(solution)/shard_map/key_value_gradients/pallas_call | solution.py:1212
  150.8 3.5 %output_gradient_sum.1 = (f32[768,256]{1,0:T(8,128)}, f32[64,128]{1,0:T(8,128)}, f32[1,128]{1,0:T(1,128)}) custom-call(s32[2]{0:T(128)} %pad_add_fusion.where_ref, bf16[2,416,256]{2,1,0:T(8,128)(2,1)} %get-tuple-element.139.first_kept_ref, bf16[2,416,256]{2,1,0:T(8,128)(2,1)} %copy-done.3, bf16[416,256]{1,0:T(8,128)(2,1)} %copy-done.8, ...), custom_call_target="tpu_custom_call" | custom-call | flops 1000000 | bytes 3000000 | tf_op jit(solution)/shard_map/output_gradient_sum/pallas_call | solution.py:1291
  (80 shorter events, 32.7 us)
Async XLA Ops:
  0.6 25.8 %collective-permute-start.3 = (bf16[768,4096]{1,0:T(8,128)(2,1)}, bf16[768,4096]{1,0:T(8,128)(2,1)}, u32[]{:S(2)}, u32[]{:S(2)}) collective-permute-start(bf16[768,4096]{1,0:T(8,128)(2,1)} %w_out_hbm.1), channel_id=1, source_target_pairs={{0,1},{1,0},{2,3},{3,2},{4,5},{5,4},{6,7},{7,6},{8,9},{9,8},{10,11... | collective-permute-start | bytes 18874376 | tf_op jit(solution)/shard_map/ppermute | solution.py:30
  1.2 36.0 %all-to-all-start = ((bf16[16,16,2048]{2,1,0:T(8,128)(2,1)}), bf16[16,16,2048]{2,1,0:T(8,128)(2,1)}, u32[]{:S(2)}, u32[]{:S(2)}) async-start(bf16[16,16,2048]{2,1,0:T(8,128)(2,1)} %bitcast.41), calls=%async_computation | async-start | bytes 2097152 | tf_op jit(solution)/shard_map/all_to_all | solution.py:1347
  9.1 15.6 %collective-permute-start = (bf16[192,4096]{1,0:T(8,128)(2,1)}, bf16[192,4096]{1,0:T(8,128)(2,1)}, u32[]{:S(2)}, u32[]{:S(2)}) collective-permute-start(bf16[192,4096]{1,0:T(8,128)(2,1)} %bitcast.29), channel_id=1, source_target_pairs={{0,1},{1,0},{2,3},{3,2},{4,5},{5,4},{6,7},{7,6},{8,9},{9,8},{10,11... | collective-permute-start | bytes 4718600 | tf_op jit(solution)/shard_map/ppermute | solution.py:30
  9.4 15.3 %collective-permute-start.1 = (bf16[192,4096]{1,0:T(8,128)(2,1)}, bf16[192,4096]{1,0:T(8,128)(2,1)}, u32[]{:S(2)}, u32[]{:S(2)}) collective-permute-start(bf16[192,4096]{1,0:T(8,128)(2,1)} %bitcast.34), channel_id=1, source_target_pairs={{0,1},{1,0},{2,3},{3,2},{4,5},{5,4},{6,7},{7,6},{8,9},{9,8},{10,11... | collective-permute-start | bytes 4718600 | tf_op jit(solution)/shard_map/ppermute | solution.py:30
  37.1 7.1 %collective-permute-start.4 = (bf16[256,2048]{1,0:T(8,128)(2,1)}, bf16[256,2048]{1,0:T(8,128)(2,1)}, u32[]{:S(2)}, u32[]{:S(2)}) collective-permute-start(bf16[256,2048]{1,0:T(8,128)(2,1)} %bitcast.3.got_own_hbm), channel_id=1, source_target_pairs={{0,1},{1,0},{2,3},{3,2},{4,5},{5,4},{6,7},{7,6},{8,9},{9,8},{10,11... | collective-permute-start | bytes 3145736 | tf_op jit(solution)/shard_map/ppermute | solution.py:30
  37.4 46.9 %all-to-all-start.1 = ((bf16[16,16,2048]{2,1,0:T(8,128)(2,1)}), bf16[16,16,2048]{2,1,0:T(8,128)(2,1)}, u32[]{:S(2)}, u32[]{:S(2)}) async-start(bf16[16,16,2048]{2,1,0:T(8,128)(2,1)} %bitcast.42), calls=%async_computation.1 | async-start | bytes 2097152 | tf_op jit(solution)/shard_map/all_to_all | solution.py:1347
  60.5 23.1 %collective-permute-start.8 = (bf16[8,192,256]{2,1,0:T(8,128)(2,1)}, bf16[8,192,256]{2,1,0:T(8,128)(2,1)}, u32[]{:S(2)}, u32[]{:S(2)}) collective-permute-start(bf16[8,192,256]{2,1,0:T(8,128)(2,1)} %get-tuple-element.101), channel_id=1, source_target_pairs={{0,2},{2,0},{4,6},{6,4},{8,10},{10,8},{12,14},{14,12},{16,18},{18,... | collective-permute-start | bytes 2359304 | tf_op jit(solution)/shard_map/ppermute | solution.py:1343
  62.4 21.9 %collective-permute-start.9 = (bf16[2,4,192,256]{3,2,1,0:T(8,128)(2,1)}, bf16[2,4,192,256]{3,2,1,0:T(8,128)(2,1)}, u32[]{:S(2)}, u32[]{:S(2)}) collective-permute-start(bf16[2,4,192,256]{3,2,1,0:T(8,128)(2,1)} %get-tuple-element.102), channel_id=1, source_target_pairs={{0,4},{2,6},{4,0},{6,2},{8,12},{10,14},{12,8},{14,10},{16,20},{18,... | collective-permute-start | bytes 2359304 | tf_op jit(solution)/shard_map/ppermute | solution.py:1343
  64.7 25.8 %collective-permute-start.6 = (bf16[80,3712]{1,0:T(8,128)(2,1)}, bf16[80,3712]{1,0:T(8,128)(2,1)}, u32[]{:S(2)}, u32[]{:S(2)}) collective-permute-start(bf16[80,3712]{1,0:T(8,128)(2,1)} %get-tuple-element.98), channel_id=1, source_target_pairs={{0,8},{2,10},{4,12},{6,14},{8,0},{10,2},{12,4},{14,6},{16,24},{18,... | collective-permute-start | bytes 1781768 | tf_op jit(solution)/shard_map/ppermute | solution.py:1343
  66.2 22.9 %collective-permute-start.7 = (bf16[64,3584]{1,0:T(8,128)(2,1)}, bf16[64,3584]{1,0:T(8,128)(2,1)}, u32[]{:S(2)}, u32[]{:S(2)}) collective-permute-start(bf16[64,3584]{1,0:T(8,128)(2,1)} %get-tuple-element.99), channel_id=1, source_target_pairs={{0,16},{2,18},{4,20},{6,22},{8,24},{10,26},{12,28},{14,30},{16,0},... | collective-permute-start | bytes 1376264 | tf_op jit(solution)/shard_map/ppermute | solution.py:1343
  85.5 11.2 %collective-permute-start.11 = (bf16[4,192,256]{2,1,0:T(8,128)(2,1)S(1)}, bf16[4,192,256]{2,1,0:T(8,128)(2,1)}, u32[]{:S(2)}, u32[]{:S(2)}) collective-permute-start(bf16[4,192,256]{2,1,0:T(8,128)(2,1)S(1)} %fusion), channel_id=1, source_target_pairs={{0,2},{2,0},{4,6},{6,4},{8,10},{10,8},{12,14},{14,12},{16,18},{18,... | collective-permute-start | bytes 1179656 | tf_op jit(solution)/shard_map/ppermute | solution.py:1343
  87.6 10.7 %collective-permute-start.10 = (bf16[4,192,256]{2,1,0:T(8,128)(2,1)S(1)}, bf16[4,192,256]{2,1,0:T(8,128)(2,1)S(1)}, u32[]{:S(2)}, u32[]{:S(2)}) collective-permute-start(bf16[4,192,256]{2,1,0:T(8,128)(2,1)S(1)} %add_convert_fusion.1), channel_id=1, source_target_pairs={{0,4},{2,6},{4,0},{6,2},{8,12},{10,14},{12,8},{14,10},{16,20},{18,... | collective-permute-start | bytes 1179656 | tf_op jit(solution)/shard_map/ppermute | solution.py:1343
  90.6 16.2 %collective-permute-start.13 = (bf16[64,3584]{1,0:T(8,128)(2,1)}, bf16[64,3584]{1,0:T(8,128)(2,1)}, u32[]{:S(2)}, u32[]{:S(2)}) collective-permute-start(bf16[64,3584]{1,0:T(8,128)(2,1)} %collective-permute-done.7.high_ref), channel_id=1, source_target_pairs={{0,8},{2,10},{4,12},{6,14},{8,0},{10,2},{12,4},{14,6},{16,24},{18,... | collective-permute-start | bytes 1376264 | tf_op jit(solution)/shard_map/ppermute | solution.py:1343
  93.5 12.1 %collective-permute-start.12 = (bf16[80,1152]{1,0:T(8,128)(2,1)S(1)}, bf16[80,1152]{1,0:T(8,128)(2,1)S(1)}, u32[]{:S(2)}, u32[]{:S(2)}) collective-permute-start(bf16[80,1152]{1,0:T(8,128)(2,1)S(1)} %fusion.2), channel_id=1, source_target_pairs={{0,16},{2,18},{4,20},{6,22},{8,24},{10,26},{12,28},{14,30},{16,0},... | collective-permute-start | bytes 552968 | tf_op jit(solution)/shard_map/ppermute | solution.py:1343
  109.5 7.0 %collective-permute-start.17 = (bf16[80,3712]{1,0:T(8,128)(2,1)}, bf16[80,3712]{1,0:T(8,128)(2,1)}, u32[]{:S(2)}, u32[]{:S(2)}) collective-permute-start(bf16[80,3712]{1,0:T(8,128)(2,1)} %collective-permute-done.6.low_ref), channel_id=1, source_target_pairs={{0,1},{1,0},{2,3},{3,2},{4,5},{5,4},{6,7},{7,6},{8,9},{9,8},{10,11... | collective-permute-start | bytes 1781768 | tf_op jit(solution)/shard_map/ppermute | solution.py:30
  109.5 7.0 %collective-permute-start.18 = (bf16[64,3584]{1,0:T(8,128)(2,1)}, bf16[64,3584]{1,0:T(8,128)(2,1)}, u32[]{:S(2)}, u32[]{:S(2)}) collective-permute-start(bf16[64,3584]{1,0:T(8,128)(2,1)} %collective-permute-done.7.high_ref), channel_id=1, source_target_pairs={{0,1},{1,0},{2,3},{3,2},{4,5},{5,4},{6,7},{7,6},{8,9},{9,8},{10,11... | collective-permute-start | bytes 1376264 | tf_op jit(solution)/shard_map/ppermute | solution.py:30
  110.0 6.5 %collective-permute-start.19 = (bf16[64,3584]{1,0:T(8,128)(2,1)}, bf16[64,3584]{1,0:T(8,128)(2,1)}, u32[]{:S(2)}, u32[]{:S(2)}) collective-permute-start(bf16[64,3584]{1,0:T(8,128)(2,1)} %collective-permute-done.13.forwarded_ref), channel_id=1, source_target_pairs={{0,1},{1,0},{2,3},{3,2},{4,5},{5,4},{6,7},{7,6},{8,9},{9,8},{10,11... | collective-permute-start | bytes 1376264 | tf_op jit(solution)/shard_map/ppermute | solution.py:30
  110.0 13.6 %collective-permute-start.15 = (bf16[2,384,256]{2,1,0:T(8,128)(2,1)}, bf16[2,384,256]{2,1,0:T(8,128)(2,1)S(1)}, u32[]{:S(2)}, u32[]{:S(2)}) collective-permute-start(bf16[2,384,256]{2,1,0:T(8,128)(2,1)} %get-tuple-element.114), channel_id=1, source_target_pairs={{0,8},{2,10},{4,12},{6,14},{8,0},{10,2},{12,4},{14,6},{16,24},{18,... | collective-permute-start | bytes 1179656 | tf_op jit(solution)/shard_map/ppermute | solution.py:1343
  114.9 6.8 %collective-permute-start.16 = (bf16[80,1152]{1,0:T(8,128)(2,1)S(1)}, bf16[80,1152]{1,0:T(8,128)(2,1)S(1)}, u32[]{:S(2)}, u32[]{:S(2)}) collective-permute-start(bf16[80,1152]{1,0:T(8,128)(2,1)S(1)} %add_convert_fusion.4.sum_ref), channel_id=1, source_target_pairs={{0,4},{2,6},{4,0},{6,2},{8,12},{10,14},{12,8},{14,10},{16,20},{18,... | collective-permute-start | bytes 552968 | tf_op jit(solution)/shard_map/ppermute | solution.py:1343
  123.6 14.3 %collective-permute-start.20 = (bf16[2,416,256]{2,1,0:T(8,128)(2,1)}, bf16[2,416,256]{2,1,0:T(8,128)(2,1)S(1)}, u32[]{:S(2)}, u32[]{:S(2)}) collective-permute-start(bf16[2,416,256]{2,1,0:T(8,128)(2,1)} %get-tuple-element.126), channel_id=1, source_target_pairs={{0,2},{2,0},{4,6},{6,4},{8,10},{10,8},{12,14},{14,12},{16,18},{18,... | collective-permute-start | bytes 1277960 | tf_op jit(solution)/shard_map/ppermute | solution.py:1343
  124.3 13.6 %collective-permute-start.21 = (bf16[2,384,256]{2,1,0:T(8,128)(2,1)}, bf16[2,384,256]{2,1,0:T(8,128)(2,1)}, u32[]{:S(2)}, u32[]{:S(2)}) collective-permute-start(bf16[2,384,256]{2,1,0:T(8,128)(2,1)} %get-tuple-element.127), channel_id=1, source_target_pairs={{0,4},{2,6},{4,0},{6,2},{8,12},{10,14},{12,8},{14,10},{16,20},{18,... | collective-permute-start | bytes 1179656 | tf_op jit(solution)/shard_map/ppermute | solution.py:1343
  126.0 11.9 %collective-permute-start.22 = (bf16[384,256]{1,0:T(8,128)(2,1)}, bf16[384,256]{1,0:T(8,128)(2,1)}, u32[]{:S(2)}, u32[]{:S(2)}) collective-permute-start(bf16[384,256]{1,0:T(8,128)(2,1)} %fusion.1), channel_id=1, source_target_pairs={{0,16},{2,18},{4,20},{6,22},{8,24},{10,26},{12,28},{14,30},{16,0},... | collective-permute-start | bytes 589832 | tf_op jit(solution)/shard_map/ppermute | solution.py:1343
  138.7 9.6 %collective-permute-start.24 = (bf16[416,256]{1,0:T(8,128)(2,1)}, bf16[416,256]{1,0:T(8,128)(2,1)S(1)}, u32[]{:S(2)}, u32[]{:S(2)}) collective-permute-start(bf16[416,256]{1,0:T(8,128)(2,1)} %fusion.4), channel_id=1, source_target_pairs={{0,4},{2,6},{4,0},{6,2},{8,12},{10,14},{12,8},{14,10},{16,20},{18,... | collective-permute-start | bytes 638984 | tf_op jit(solution)/shard_map/ppermute | solution.py:1343
  142.2 6.1 %collective-permute-start.25 = (bf16[384,256]{1,0:T(8,128)(2,1)}, bf16[384,256]{1,0:T(8,128)(2,1)S(1)}, u32[]{:S(2)}, u32[]{:S(2)}) collective-permute-start(bf16[384,256]{1,0:T(8,128)(2,1)} %fusion.5), channel_id=1, source_target_pairs={{0,2},{2,0},{4,6},{6,4},{8,10},{10,8},{12,14},{14,12},{16,18},{18,... | collective-permute-start | bytes 589832 | tf_op jit(solution)/shard_map/ppermute | solution.py:1343
  (18 other events, 88.3 us)

commit v3 on v2

--- a/solution.py
+++ b/solution.py
@@ -54,8 +54,8 @@
 
 def forward_kernel(
     counts_ref,
-    gain_ctx_ref,
-    gain_lat_ref,
+    gain_ctx_hbm,
+    gain_lat_hbm,
     lat_hbm,
     wk_hbm,
     wv_hbm,
@@ -71,6 +71,8 @@
     lat_proj_hbm,
     p_hbm,
     pl_hbm,
+    gain_ctx_ref,
+    gain_lat_ref,
     lat_ref,
     wk_ref,
     wv_ref,
@@ -93,7 +95,7 @@
     out_sems,
 ):
     patch_rows, width = x_ref.shape
-    chunks = sems.shape[0] - 4
+    chunks = sems.shape[0] - 6
     rows = patch_rows // chunks
     groups = k_ref.shape[0]
     latent_rows = lat_ref.shape[0]
@@ -114,7 +116,11 @@
             ((lat_hbm, lat_ref), (wk_hbm, wk_ref), (wv_hbm, wv_ref), (wq_hbm, wq_ref))
         )
     ]
-    for copy in weights[:3]:
+    gains = [
+        fetch(gain_ctx_hbm, gain_ctx_ref, chunks + 4),
+        fetch(gain_lat_hbm, gain_lat_ref, chunks + 5),
+    ]
+    for copy in (*gains, *weights[:3]):
         copy.start()
     blocks = [fetch_rows(i) for i in range(chunks)]
     for copy in blocks + weights[3:]:
@@ -137,7 +143,8 @@
     ):
         results[name] = pltpu.make_async_copy(source, target, out_sems.at[i])
 
-    weights[0].wait()
+    for copy in (*gains, weights[0]):
+        copy.wait()
     lat = lat_ref[...].astype(F32)
     lat_inverse = lax.rsqrt(jnp.mean(lat * lat, axis=-1, keepdims=True) + EPSILON)
     lat_normed = lat * lat_inverse * gain_lat_ref[...]
@@ -280,19 +287,20 @@
         name="forward_attention",
         in_specs=[
             pl.BlockSpec(memory_space=pltpu.SMEM),
-            pl.BlockSpec(memory_space=pltpu.VMEM),
-            pl.BlockSpec(memory_space=pltpu.VMEM),
+            pl.BlockSpec(memory_space=pl.ANY),
+            pl.BlockSpec(memory_space=pl.ANY),
         ]
         + [pl.BlockSpec(memory_space=pl.ANY)] * len(large),
         out_specs=[pl.BlockSpec(memory_space=pl.ANY)] * len(out),
         out_shape=[jax.ShapeDtypeStruct(shape, dtype) for shape, dtype in out],
-        scratch_shapes=[pltpu.VMEM(a.shape, a.dtype) for a in large]
+        scratch_shapes=[pltpu.VMEM((1, width), F32)] * 2
+        + [pltpu.VMEM(a.shape, a.dtype) for a in large]
         + [pltpu.VMEM(shape, dtype) for shape, dtype in out]
         + [
             pltpu.VMEM((latent_rows, width), BF16),
             pltpu.VMEM((patch_rows // chunks + latent_rows, width), BF16),
             pltpu.VMEM((2 * key_width, width), BF16),
-            pltpu.SemaphoreType.DMA((chunks + 4,)),
+            pltpu.SemaphoreType.DMA((chunks + 6,)),
             pltpu.SemaphoreType.DMA((len(out) + 1,)),
         ],
         cost_estimate=pl.CostEstimate(
@@ -318,27 +326,49 @@
 
 def branch_kernel(
     slot_count,
-    where_ref,
+    own_hbm,
+    other_hbm,
+    lat_hbm,
+    gain_hbm,
+    routes_hbm,
+    w_own_hbm,
+    w_other_hbm,
+    hat_hbm,
+    inv_hbm,
+    out_hbm,
     own_ref,
     other_ref,
     lat_ref,
     gain_ref,
     routes_ref,
-    w_own_hbm,
-    w_other_hbm,
-    hat_hbm,
-    inv_ref,
-    out_ref,
     w_own_ref,
     w_other_ref,
     hat_ref,
+    low_ref,
+    inv_ref,
+    out_ref,
     sems,
-    hat_sem,
+    out_sems,
+    small_sems,
 ):
     rows, width = hat_ref.shape
     slots, half = out_ref.shape
     parts = sems.shape[1]
     size = width // parts
+    small = [
+        pltpu.make_async_copy(source, target, small_sems.at[i])
+        for i, (source, target) in enumerate(
+            (
+                (routes_hbm, routes_ref),
+                (own_hbm, own_ref),
+                (other_hbm, other_ref),
+                (lat_hbm, lat_ref),
+                (gain_hbm, gain_ref),
+            )
+        )
+    ]
+    for copy in small:
+        copy.start()
     copies = []
     for part in range(parts):
         at = pl.ds(part * size, size)
@@ -350,7 +380,10 @@
             )
     for copy in copies:
         copy.start()
+    small[0].wait()
     place = slots_of(routes_ref, slot_count, True)
+    for copy in small[1:]:
+        copy.wait()
     table = jnp.where(
         lax.broadcasted_iota(jnp.int32, (slots, rows), 0) == place, 1.0, 0.0
     ).astype(BF16)
@@ -371,49 +404,52 @@
             squares = squares + piece * piece
     inverse = lax.rsqrt(jnp.sum(squares, axis=-1, keepdims=True) / width + EPSILON)
     inv_ref[...] = inverse
-    hat_ref[...] = hat_ref[...] * inverse
-    hat_copy = pltpu.make_async_copy(hat_ref, hat_hbm, hat_sem)
-    hat_copy.start()
-    at = pl.ds(pl.multiple_of(where_ref[1] * half, half), half)
-    final = (hat_ref[:, at] * gain_ref[:, at]).astype(BF16)
+    low_ref[...] = (hat_ref[...] * inverse).astype(BF16)
+    results = [
+        pltpu.make_async_copy(source, target, out_sems.at[i])
+        for i, (source, target) in enumerate(
+            ((low_ref, hat_hbm), (inv_ref, inv_hbm), (out_ref, out_hbm))
+        )
+    ]
+    for copy in results[:2]:
+        copy.start()
+    at = pl.ds(pl.multiple_of(lax.axis_index("mp") * half, half), half)
+    final = (hat_ref[:, at] * inverse * gain_ref[:, at]).astype(BF16)
     out_ref[...] = jnp.dot(table, final, preferred_element_type=F32).astype(BF16)
-    hat_copy.wait()
-
-
-def branch_call(where, own, other, w_own, w_other, latents, gain_out, routes, slots, slot_count):
+    results[2].start()
+    for copy in results:
+        copy.wait()
+
+
+def branch_call(own, other, w_own, w_other, latents, gain_out, routes, slots, slot_count):
     width = w_own.shape[1]
     rows, heads = own.shape
     parts = 4
     return pl.pallas_call(
         functools.partial(branch_kernel, slot_count),
         name="branch_norm",
-        grid_spec=pltpu.PrefetchScalarGridSpec(
-            num_scalar_prefetch=1,
-            grid=(1,),
-            in_specs=[
-                held((rows, heads)),
-                held((rows, heads)),
-                held(latents.shape),
-                held((1, width)),
-                held((1, rows)),
-                pl.BlockSpec(memory_space=pl.ANY),
-                pl.BlockSpec(memory_space=pl.ANY),
-            ],
-            out_specs=[
-                pl.BlockSpec(memory_space=pl.ANY),
-                held((rows, 1)),
-                held((slots, width // 2)),
-            ],
+        **dict(
+            in_specs=[pl.BlockSpec(memory_space=pl.ANY)] * 7,
+            out_specs=[pl.BlockSpec(memory_space=pl.ANY)] * 3,
             scratch_shapes=[
+                pltpu.VMEM((rows, heads), BF16),
+                pltpu.VMEM((rows, heads), BF16),
+                pltpu.VMEM(latents.shape, BF16),
+                pltpu.VMEM((1, width), F32),
+                pltpu.VMEM((1, rows), jnp.int32),
                 pltpu.VMEM(w_own.shape, BF16),
                 pltpu.VMEM(w_other.shape, BF16),
                 pltpu.VMEM((rows, width), F32),
+                pltpu.VMEM((rows, width), BF16),
+                pltpu.VMEM((rows, 1), F32),
+                pltpu.VMEM((slots, width // 2), BF16),
                 pltpu.SemaphoreType.DMA((2, parts)),
-                pltpu.SemaphoreType.DMA,
+                pltpu.SemaphoreType.DMA((3,)),
+                pltpu.SemaphoreType.DMA((5,)),
             ],
         ),
         out_shape=[
-            jax.ShapeDtypeStruct((rows, width), F32),
+            jax.ShapeDtypeStruct((rows, width), BF16),
             jax.ShapeDtypeStruct((rows, 1), F32),
             jax.ShapeDtypeStruct((slots, width // 2), BF16),
         ],
@@ -421,7 +457,7 @@
             flops=2 * 2 * rows * heads * width, bytes_accessed=16_000_000, transcendentals=0
         ),
         compiler_params=pltpu.CompilerParams(vmem_limit_bytes=VMEM_LIMIT),
-    )(where, own, other, latents, gain_out.reshape(1, width), routes, w_own, w_other)
+    )(own, other, latents, gain_out.reshape(1, width), routes, w_own, w_other)
 
 
 def attention_backward(
@@ -538,13 +574,12 @@
 
 def backward_kernel(
     slot_count,
-    where_ref,
     counts_ref,
-    inv_out_ref,
-    gain_ref,
-    routes_ref,
-    inv_row_ref,
-    attn_ref,
+    inv_out_hbm,
+    gain_hbm,
+    routes_hbm,
+    inv_row_hbm,
+    attn_hbm,
     got_own_hbm,
     got_other_hbm,
     hat_hbm,
@@ -561,10 +596,16 @@
     line_high_hbm,
     pair_hbm,
     message_hbm,
+    lat_hbm,
     value_going_hbm,
     value_kept_hbm,
     key_going_hbm,
     key_kept_hbm,
+    inv_out_ref,
+    gain_ref,
+    routes_ref,
+    inv_row_ref,
+    attn_ref,
     got_own_ref,
     got_other_ref,
     hat_ref,
@@ -584,13 +625,29 @@
     line_high_ref,
     pair_ref,
     message_ref,
+    lat_ref,
     value_ref,
     key_ref,
     sems,
     out_sems,
     value_sems,
     key_sems,
+    small_sems,
 ):
+    small = [
+        pltpu.make_async_copy(source, target, small_sems.at[i])
+        for i, (source, target) in enumerate(
+            (
+                (routes_hbm, routes_ref),
+                (inv_out_hbm, inv_out_ref),
+                (gain_hbm, gain_ref),
+                (inv_row_hbm, inv_row_ref),
+                (attn_hbm, attn_ref),
+            )
+        )
+    ]
+    for copy in small:
+        copy.start()
     sources = (
         got_own_hbm,
         got_other_hbm,
@@ -625,15 +682,17 @@
     ]
     for copy in copies[:4]:
         copy.start()
+    me, core = lax.axis_index("dp"), lax.axis_index("mp")
     rows, width = hat_ref.shape
     half = width // 2
     slots = got_own_ref.shape[0]
     latent_rows = lk_ref.shape[1]
     key_width, own = value_ref.shape[2:]
-    lat_at = message_ref.shape[1] - (key_width * 2 + attn_ref.shape[1])
-    lat_ref = message_ref.at[:, pl.ds(lat_at, message_ref.shape[1] - lat_at)]
-
+
+    small[0].wait()
     place = slots_of(routes_ref, slot_count, False)
+    for copy in small[1:]:
+        copy.wait()
     table = jnp.where(
         lax.broadcasted_iota(jnp.int32, (rows, slots), 1) == place, 1.0, 0.0
     ).astype(BF16)
@@ -643,13 +702,13 @@
         copy.wait()
     for copy in copies[4:]:
         copy.start()
-    for got_ref, which in ((got_own_ref, where_ref[1]), (got_other_ref, 1 - where_ref[1])):
+    for got_ref, which in ((got_own_ref, core), (got_other_ref, 1 - core)):
         for c in range(half // chunk):
             at = pl.ds(pl.multiple_of(which * half + c * chunk, chunk), chunk)
             d_final = jnp.dot(
                 table, got_ref[:, c * chunk : (c + 1) * chunk], preferred_element_type=F32
             )
-            product = d_final * hat_ref[:, at]
+            product = d_final * hat_ref[:, at].astype(F32)
             total = total + jnp.sum(product * gain_ref[:, at], axis=-1, keepdims=True)
             d_final_ref[:, at] = d_final
     total = total / width
@@ -659,7 +718,7 @@
     for c in range(width // chunk):
         at = slice(c * chunk, (c + 1) * chunk)
         d_final = d_final_ref[:, at]
-        hat = hat_ref[:, at]
+        hat = hat_ref[:, at].astype(F32)
         term = jnp.sum(d_final * hat, axis=0, keepdims=True)
         high = term.astype(BF16).astype(F32)
         highs.append(high)
@@ -676,10 +735,9 @@
     lat_ref[latent_rows : latent_rows + 16, :part] = jnp.concatenate(
         lines + [jnp.zeros((8, part), F32)], axis=0
     ).astype(BF16)
-    z = where_ref[0] >> 2
-    some = pl.ds(pl.multiple_of(where_ref[1] * (rows // 2), rows // 2), rows // 2)
+    z = me >> 2
+    some = pl.ds(pl.multiple_of(core * (rows // 2), rows // 2), rows // 2)
     line_own_ref[...] = branch_ref[:, pl.ds(pl.multiple_of(z * part, part), part)]
-    message_ref[rows // 2 :, :lat_at] = jnp.zeros_like(message_ref[rows // 2 :, :lat_at])
     heads = attn_ref.shape[1]
     for turn, ref, first in (
         (1, message_ref, 0),
@@ -697,13 +755,14 @@
         for i, (source, target) in enumerate(
             (
                 (line_high_ref, line_high_hbm),
+                (message_ref, message_hbm),
                 (line_own_ref, line_own_hbm),
                 (pair_ref, pair_hbm),
-                (message_ref, message_hbm),
+                (lat_ref, lat_hbm),
             )
         )
     ]
-    for copy in results[:2]:
+    for copy in results[:3]:
         copy.start()
 
     copies[3].wait()
@@ -725,11 +784,10 @@
         scaled_ref,
         lat_ref,
     )
-    for copy in results[2:]:
+    for copy in results[3:]:
         copy.start()
     copies[11].wait()
 
-    me = where_ref[0]
     odd = me & 1
     for j in range(8):
         y = ((me >> 1) & 1) ^ (1 - (j >> 2))
@@ -761,7 +819,7 @@
 
 
 def backward_call(
-    where, counts, attn, got_own, got_other, hat, inv_out, gain_out, routes, w_out, kept, context, slot_count
+    counts, attn, got_own, got_other, hat, inv_out, gain_out, routes, w_out, kept, context, slot_count
 ):
     k, v, q, lk, lv, p, lat_p, inv_row = kept
     rows, width = hat.shape
@@ -771,11 +829,13 @@
     latent_rows = lk.shape[1]
     own = width // 16
     large = (got_own, got_other, hat, w_out, k, v, q, lk, lv, p, lat_p, context)
+    small = (inv_out, gain_out.reshape(1, width), routes, inv_row, attn)
     out = [
         (rows, width // 4),
         (rows // 2, width // 2 + 2 * heads),
         (2 * key_width + 16, patch_rows),
-        (latent_rows + 16, width // 4 + 3 * heads + 2 * key_width),
+        (rows // 2, width // 4 + 2 * heads),
+        (latent_rows + 16, heads + 2 * key_width),
         (8, key_width, own),
         (8, key_width, own),
         (2, 4, key_width, own),
@@ -784,33 +844,27 @@
     return pl.pallas_call(
         functools.partial(backward_kernel, slot_count),
         name="attention_backward",
-        grid_spec=pltpu.PrefetchScalarGridSpec(
-            num_scalar_prefetch=1,
-            grid=(1,),
+        **dict(
             in_specs=[
                 pl.BlockSpec(memory_space=pltpu.SMEM),
-                held(inv_out.shape),
-                held((1, width)),
-                held(routes.shape),
-                held(inv_row.shape),
-                held(attn.shape),
             ]
-            + [pl.BlockSpec(memory_space=pl.ANY)] * len(large),
+            + [pl.BlockSpec(memory_space=pl.ANY)] * (5 + len(large)),
             out_specs=[pl.BlockSpec(memory_space=pl.ANY)] * len(out),
-            scratch_shapes=[pltpu.VMEM(a.shape, a.dtype) for a in large]
+            scratch_shapes=[pltpu.VMEM(a.shape, a.dtype) for a in (*small, *large)]
             + [
                 pltpu.VMEM((rows, width), F32),
                 pltpu.VMEM((rows, width), BF16),
                 pltpu.VMEM((2 * key_width, patch_rows), BF16),
             ]
-            + [pltpu.VMEM(shape, BF16) for shape in out[:4]]
+            + [pltpu.VMEM(shape, BF16) for shape in out[:5]]
             + [
                 pltpu.VMEM((2, 8, key_width, own), BF16),
                 pltpu.VMEM((2, 8, key_width, own), BF16),
                 pltpu.SemaphoreType.DMA((len(large),)),
-                pltpu.SemaphoreType.DMA((4,)),
+                pltpu.SemaphoreType.DMA((5,)),
                 pltpu.SemaphoreType.DMA((2, 8)),
                 pltpu.SemaphoreType.DMA((2, 8)),
+                pltpu.SemaphoreType.DMA((5,)),
             ],
         ),
         out_shape=[jax.ShapeDtypeStruct(shape, BF16) for shape in out],
@@ -818,7 +872,7 @@
             flops=5_000_000_000, bytes_accessed=26_000_000, transcendentals=0
         ),
         compiler_params=pltpu.CompilerParams(vmem_limit_bytes=VMEM_LIMIT),
-    )(where, counts, inv_out, gain_out.reshape(1, width), routes, inv_row, attn, *large)
+    )(counts, *small, *large)
 
 
 def patch_kernel(
@@ -933,16 +987,16 @@
     half = rows // 2
     attn_ref[:rows, :] = attn_own_ref[...]
     line_ref[:rows, :] = line_own_ref[...]
-    for i, (ref, other, first) in enumerate(
+    for i, (ref, other, first, attn_at) in enumerate(
         (
-            (low_ref, other_low_ref, 0),
-            (high_ref, other_high_ref, 0),
-            (forwarded_ref, other_forwarded_ref, columns + 2 * heads),
+            (low_ref, other_low_ref, 0, columns),
+            (high_ref, other_high_ref, 0, columns),
+            (forwarded_ref, other_forwarded_ref, 2 * heads, 0),
         )
     ):
         at = (i + 1) * rows
-        attn_ref[at : at + half, :] = ref[:half, columns : columns + heads]
-        attn_ref[at + half : at + rows, :] = ref[:half, columns + heads : columns + 2 * heads]
+        attn_ref[at : at + half, :] = ref[:half, attn_at : attn_at + heads]
+        attn_ref[at + half : at + rows, :] = ref[:half, attn_at + heads : attn_at + 2 * heads]
         for holder, which in ((ref, mine), (other, 1 - mine)):
             line_ref[pl.ds(pl.multiple_of(at + which * half, half), half), :] = holder[
                 :half, first : first + columns
@@ -1003,7 +1057,9 @@
 def latent_kernel(
     where_ref,
     sum_ref,
-    got_ref,
+    across_ref,
+    along_ref,
+    corner_ref,
     proj_ref,
     lat_ref,
     gain_ref,
@@ -1027,7 +1083,9 @@
     own, query_width = wq_ref.shape
     key_width = wk_ref.shape[0]
     scaling = HD ** (-0.5)
-    total_ref[...] = sum_ref[...].astype(F32) + got_ref[...].astype(F32)
+    total_ref[...] = sum(
+        ref[...].astype(F32) for ref in (sum_ref, across_ref, along_ref, corner_ref)
+    )
     total = total_ref[:latent_rows, :]
     low = total.astype(BF16)
     at = pl.ds(pl.multiple_of(where_ref[0] * own, own), own)
@@ -1253,11 +1311,14 @@
     second_last_ref,
     message_ref,
     message_got_ref,
+    term_ref,
+    term_got_ref,
     lat_ref,
     gain_ref,
     out_ref,
     latent_ref,
     gain_lat_ref,
+    gain_ctx_ref,
 ):
     heads, own = out_ref.shape
     latent_rows, width = lat_ref.shape
@@ -1281,13 +1342,14 @@
     hat = lat_ref[:, at].astype(F32) * inverse
     latent_ref[...] = resid + inverse * (gain_ref[:, at] * d_lat[:latent_rows] - hat * (lat_dot / width))
     gain_lat_ref[...] = d_lat[latent_rows : latent_rows + 1]
-
-
-def out_final_call(where, parts, message, message_got, latents, gain_lat):
+    gain_ctx_ref[...] = term_ref[:1, mine] + term_got_ref[:1, mine]
+
+
+def out_final_call(where, parts, message, message_got, term, term_got, latents, gain_lat):
     _, rows, own = parts[0].shape
     latent_rows, width = latents.shape
     heads = 2 * (rows - latent_rows // 2)
-    shapes = [(heads, own), (latent_rows, own // 2), (1, own // 2)]
+    shapes = [(heads, own), (latent_rows, own // 2), (1, own // 2), (1, own // 2)]
     return pl.pallas_call(
         out_final_kernel,
         name="output_gradient_sum",
@@ -1300,14 +1362,23 @@
                 else held(part.shape)
                 for part in parts
             ]
-            + [held(a.shape) for a in (message, message_got, latents)]
+            + [held(a.shape) for a in (message, message_got, term, term_got, latents)]
             + [held((1, width))],
             out_specs=[held(shape) for shape in shapes],
         ),
         out_shape=[jax.ShapeDtypeStruct(shape, F32) for shape in shapes],
         cost_estimate=pl.CostEstimate(flops=1_000_000, bytes_accessed=3_000_000, transcendentals=0),
         compiler_params=pltpu.CompilerParams(vmem_limit_bytes=VMEM_LIMIT),
-    )(where, *parts, message, message_got, latents, gain_lat.reshape(1, width))
+    )(
+        where,
+        *parts,
+        message,
+        message_got,
+        term,
+        term_got,
+        latents,
+        gain_lat.reshape(1, width),
+    )
 
 
 def add_halves(left, right):
@@ -1364,7 +1435,6 @@
     wk_other, wv_other, attn_rows = lax.optimization_barrier((wk_other, wv_other, attn_rows))
     attn_other = swap_cores(attn_rows)
     out_hat, out_inv, outgoing = branch_call(
-        where,
         attn_rows,
         attn_other,
         w_out,
@@ -1380,7 +1450,6 @@
     returned, out_inv = lax.optimization_barrier((returned, out_inv))
     returned_other = swap_cores(returned)
     backward = backward_call(
-        where,
         counts,
         attn_rows,
         returned,
@@ -1400,6 +1469,7 @@
         line_high,
         pair,
         message,
+        lat_terms,
         value_going,
         value_kept,
         key_going,
@@ -1410,15 +1480,22 @@
     key_got = swap(key_going, 2)
     pair_other = swap_cores(pair)
 
+    line_high, message, lat_terms, pair_other = lax.optimization_barrier(
+        (line_high, message, lat_terms, pair_other)
+    )
+    lat_got = swap(lat_terms, 4)
+    got_high = swap(line_high, 8)
+    got_low = swap(message, 4)
+
     ctx_grad = patch_call(
         where, pair, pair_other, wk, wv, wk_other, wv_other, context, inv_row, gain_ctx
     )
 
-    line_high, message, pair_other = lax.optimization_barrier((line_high, message, pair_other))
-    got_high = swap(line_high, 8)
-    got_low = swap(message, 4)
-    value_got, key_got, ctx_grad, routed = lax.optimization_barrier(
-        (value_got, key_got, ctx_grad, routed)
+    lat_got, ctx_grad = lax.optimization_barrier((lat_got, ctx_grad))
+    lat_sum = add_halves(lat_terms, lat_got)
+    lat_low = lat_sum.astype(BF16)
+    value_got, key_got, ctx_grad, routed, lat_low = lax.optimization_barrier(
+        (value_got, key_got, ctx_grad, routed, lat_low)
     )
     key_kept = key_kept.reshape((8,) + key_kept.shape[2:])
     key_got = key_got.reshape((8,) + key_got.shape[2:])
@@ -1427,13 +1504,11 @@
     value_last = swap(value_going, 2)
     key_last = swap(key_going, 1)
 
-    got_low, got_high, value_going, key_going = lax.optimization_barrier(
-        (got_low, got_high, value_going, key_going)
-    )
-    lat_at = message.shape[1] - lat_proj.shape[1]
-    lat_sum = add_halves(message[:, lat_at:], got_low[:, lat_at:])
-    lat_got = swap(lat_sum.astype(BF16), 8)
-    forwarded = swap(got_high, 4)
+    got_low, got_high, value_going, key_going, lat_low = lax.optimization_barrier(
+        (got_low, got_high, value_going, key_going, lat_low)
+    )
+    lat_got = swap(lat_low, 8)
+    forwarded = swap(got_high[:, width // 4 :], 4)
     other_low = swap_cores(got_low)
     other_high = swap_cores(got_high)
 
@@ -1441,9 +1516,8 @@
     (going, high), lat_got, forwarded = lax.optimization_barrier((planes, lat_got, forwarded))
     low = swap(going, 4)
     other_forwarded = swap_cores(forwarded)
-    lat_sum = add_halves(lat_sum, lat_got)
-    lat_sum = add_halves(lat_sum, swap(lat_sum.astype(BF16), 1)).astype(BF16)
-    lat_parts = (swap(lat_sum, 2),)
+    lat_sum = add_halves(lat_sum, lat_got).astype(BF16)
+    lat_parts = (swap(lat_sum, 1), swap(lat_sum, 2), swap(lat_sum, 3))
 
     first_going, first_kept, second_going, second_kept = out_call(
         where,
@@ -1452,10 +1526,12 @@
         (got_low, got_high, forwarded),
         (other_low, other_high, other_forwarded),
     )
-    low, lat_parts, first_going, second_going = lax.optimization_barrier(
-        (low, lat_parts, first_going, second_going)
-    )
-    high = swap(add_halves(high, low[0]).astype(BF16), 8)
+    low, first_going, second_going = lax.optimization_barrier((low, first_going, second_going))
+    high = add_halves(high, low[0]).astype(BF16)
+    high, lat_parts, first_going, second_going = lax.optimization_barrier(
+        (high, lat_parts, first_going, second_going)
+    )
+    high = swap(high, 8)
     first_got = swap(first_going, 1)
     second_got = swap(second_going, 2)
 
@@ -1469,7 +1545,6 @@
     second_last = swap(add_halves(second_kept[0], second_got[0]).astype(BF16), 1)
     message_got = swap_cores(message)
 
-    low, high, pair_lat, message_got = lax.optimization_barrier((low, high, pair_lat, message_got))
     grad_key, grad_value, gain_term = final_call(
         where,
         value_kept,
@@ -1488,15 +1563,16 @@
     first_last, second_last, gain_term = lax.optimization_barrier(
         (first_last, second_last, gain_term)
     )
-    grad_w_out, grad_latents, grad_gain_lat = out_final_call(
+    grad_w_out, grad_latents, grad_gain_lat, grad_gain_ctx = out_final_call(
         where,
         (first_kept, first_got, first_last, second_kept, second_got, second_last),
         message,
         message_got,
+        gain_term,
+        gain_got,
         latents,
         gain_lat,
     )
-    share = own_width // 2
     return (
         routed,
         ctx_grad,
@@ -1505,7 +1581,7 @@
         grad_value.T,
         grad_w_out,
         grad_latents,
-        lax.dynamic_slice_in_dim(gain_term + gain_got, mp_index * share, share, 1)[0],
+        grad_gain_ctx[0],
         grad_gain_lat[0],
         grad_gain_out[0],
     )

time: 155 us -> 148 us (0.955)
  waiting for transfers between devices: 23.3 us -> 19.8 us
  starting transfers between devices: 45.1 us -> 41.8 us
  local copies, waits for them, and re-layouts: 2.9 us -> 5.95 us
  Pallas kernels: 70.9 us -> 68.3 us
    ppermute x16 -> x18, starting transfers between devices: 27.9 us -> 24.7 us  [swap(): return lax.ppermute(array, 'dp', [(i, i ^ turn) for i in range(dp_count)])]
    unnamed x26 -> x30, local copies, waits for them, and re-layouts: 2.38 us -> 4.96 us
    ppermute x11, waiting for transfers between devices: 3.54 us -> 1.47 us  [swap_cores(): return lax.ppermute(array, 'mp', [(0, 1), (1, 0)])]
    ppermute x16 -> x18, waiting for transfers between devices: 19.8 us -> 18.3 us  [swap(): return lax.ppermute(array, 'dp', [(i, i ^ turn) for i in range(dp_count)])]
    convert_element_type x4 -> x3, other arithmetic: 5.06 us -> 4.58 us  [the longest x1 1.86 us: local(): high = add_halves(high, low[0]).astype(BF16)]
  transfers between devices with their start and end apart: 29 -> 31, of which waited for: 13 -> 12; matrix products, arithmetic and copies ran while one was open for 6% -> 7% of each run, Pallas kernels for 44% -> 44%
where the time goes in v3:
time: 148 us; the launch traced here: 147 us
  Pallas kernels  68.3 us (46%)
  starting transfers between devices  41.8 us (28%)
  waiting for transfers between devices  19.8 us (13%)
  other arithmetic  10.1 us (7%)
  local copies, waits for them, and re-layouts  5.95 us (4%)
    ppermute x18, starting transfers between devices, swap(): return lax.ppermute(array, 'dp', [(i, i ^ turn) for i in range(dp_count)])  24.7 us
    ppermute x18, waiting for transfers between devices, swap(): return lax.ppermute(array, 'dp', [(i, i ^ turn) for i in range(dp_count)])  18.3 us
    pallas_call x1, Pallas kernels, backward_call(): pl.pallas_call(functools.partial(backward_kernel, slot_count), name='atte...  15 us
    pallas_call x1, Pallas kernels, forward_call(): pl.pallas_call(forward_kernel, name='forward_attention', in_specs=[pl.Blo...  14.9 us
    all_to_all x2, starting transfers between devices, exchange(): lax.all_to_all(blocks, 'dp', split_axis=0, concat_axis=0, tiled=True)  14.7 us
    pallas_call x1, Pallas kernels, patch_call(): pl.pallas_call(functools.partial(patch_kernel, width), name='patch_gradie...  10.2 us
    pallas_call x1, Pallas kernels, branch_call(): pl.pallas_call(functools.partial(branch_kernel, slot_count), name='branch...  8.74 us
    pallas_call x1, Pallas kernels, latent_call(): pl.pallas_call(latent_kernel, name='latent_gradients', grid_spec=pltpu.Pr...  5.64 us
  transfers between devices with their start and end apart: 31, of which 12 were waited for; matrix products, arithmetic and copies ran while one was open for 7% of the time, Pallas kernels for 44%

profile of v3, /device:TPU:0, one launch (start us, length us, event | category | flops | bytes accessed | tf_op | source)
XLA Modules:
  0.0 146.8 jit_solution(5997523859335149237)
XLA Ops:
  1.2 7.9 %all-to-all-start = ((bf16[16,16,2048]{2,1,0:T(8,128)(2,1)}), bf16[16,16,2048]{2,1,0:T(8,128)(2,1)}, u32[]{:S(2)}, u32[]{:S(2)}) async-start(bf16[16,16,2048]{2,1,0:T(8,128)(2,1)} %bitcast.40), calls=%async_computation | async-start | bytes 2097152 | tf_op jit(solution)/shard_map/all_to_all | solution.py:1418
  9.7 14.9 %forward_attention.1 = (bf16[128,768]{1,0:T(8,128)(2,1)}, bf16[2,1024,128]{2,1,0:T(8,128)(2,1)}, bf16[2,1024,128]{2,1,0:T(8,128)(2,1)}, f32[8,1024]{1,0:T(8,128)...) custom-call(s32[1,2]{1,0:T(1,128)} %counts_ref.3, ...), custom_call_target="tpu_custom_call" | custom-call | flops 5000000000 | bytes 24000000 | tf_op jit(solution)/shard_map/forward_attention/pallas_call | solution.py:285
  27.1 8.7 %branch_norm.1 = (bf16[128,4096]{1,0:T(8,128)(2,1)}, f32[128,1]{1,0:T(8,128)}, bf16[256,2048]{1,0:T(8,128)(2,1)}) custom-call(bf16[128,768]{1,0:T(8,128)(2,1)} %get-tuple-element.91.own_hbm.attn_hbm.attn_own_ref, bf16[128,768]{1,0:T(8,128)(2,1)} %copy-done.10, bf16[64,4096]{1,0:T(8,128)(2,1)} %lat_ref.3, f32[1,4096]{1,0:T(1,128)} %bitcast.48, ...), custom_call_target="tpu_custom_call" | custom-call | flops 1610612736 | bytes 16000000 | tf_op jit(solution)/shard_map/branch_norm/pallas_call | solution.py:428
  36.1 6.8 %all-to-all-start.1 = ((bf16[16,16,2048]{2,1,0:T(8,128)(2,1)}), bf16[16,16,2048]{2,1,0:T(8,128)(2,1)}, u32[]{:S(2)}, u32[]{:S(2)}) async-start(bf16[16,16,2048]{2,1,0:T(8,128)(2,1)} %bitcast.41), calls=%async_computation.1 | async-start | bytes 2097152 | tf_op jit(solution)/shard_map/all_to_all | solution.py:1418
  42.9 15.0 %attention_backward.1 = (bf16[128,1024]{1,0:T(8,128)(2,1)}, bf16[64,3584]{1,0:T(8,128)(2,1)}, bf16[400,1024]{1,0:T(8,128)(2,1)}, bf16[64,2560]{1,0:T(8,128)(2,1)...) custom-call(s32[1,2]{1,0:T(1,128)} %counts_ref.3, ...), custom_call_target="tpu_custom_call" | custom-call | flops 5000000000 | bytes 26000000 | tf_op jit(solution)/shard_map/attention_backward/pallas_call | solution.py:844
  58.1 1.9 %collective-permute-start.7 = (bf16[8,192,256]{2,1,0:T(8,128)(2,1)}, bf16[8,192,256]{2,1,0:T(8,128)(2,1)}, u32[]{:S(2)}, u32[]{:S(2)}) collective-permute-start(bf16[8,192,256]{2,1,0:T(8,128)(2,1)} %get-tuple-element.114), channel_id=1, source_target_pairs={{0,2},{2,0},{4,6},{6,4},{8,10},{10,8},{12,14},{14,12},{16,18},{18,... | collective-permute-start | bytes 2359304 | tf_op jit(solution)/shard_map/ppermute | solution.py:1414
  64.4 2.4 %collective-permute-start.12 = (bf16[64,3584]{1,0:T(8,128)(2,1)}, bf16[64,3584]{1,0:T(8,128)(2,1)}, u32[]{:S(2)}, u32[]{:S(2)}) collective-permute-start(bf16[64,3584]{1,0:T(8,128)(2,1)} %get-tuple-element.124), channel_id=1, source_target_pairs={{0,16},{2,18},{4,20},{6,22},{8,24},{10,26},{12,28},{14,30},{16,0},... | collective-permute-start | bytes 1376264 | tf_op jit(solution)/shard_map/ppermute | solution.py:1414
  67.3 10.2 %patch_gradient.1 = bf16[1024,2048]{1,0:T(8,128)(2,1)} custom-call(s32[2]{0:T(128)} %pad_add_fusion.where_ref, bf16[400,1024]{1,0:T(8,128)(2,1)} %get-tuple-element.107.own_ref, bf16[400,1024]{1,0:T(8,128)(2,1)} %copy-done.5, bf16[192,4096]{1,0:T(8,128)(2,1)} %bitcast.30, bf16[192,4096]{1,0:T(8,128)(2,1)} %bitcast.35, ...), custom_call_target="tpu_custom_call" | custom-call | flops 3300000000 | bytes 14000000 | tf_op jit(solution)/shard_map/patch_gradient/pallas_call | solution.py:931
  77.6 1.6 %fusion.2 = bf16[80,1152]{1,0:T(8,128)(2,1)} fusion(bf16[80,1152]{1,0:T(8,128)(2,1)} %collective-permute-done.6, bf16[80,1152]{1,0:T(8,128)(2,1)S(1)} %copy-done.6), kind=kLoop, calls=%fused_computation.9 | loop fusion | flops 368640 | bytes 552960 | tf_op jit(solution)/shard_map/convert_element_type | solution.py:1496
  79.2 2.0 %collective-permute-done.7.value_got_ref = bf16[8,192,256]{2,1,0:T(8,128)(2,1)} collective-permute-done((bf16[8,192,256]{2,1,0:T(8,128)(2,1)}, bf16[8,192,256]{2,1,0:T(8,128)(2,1)}, u32[]{:S(2)}, u32[]{:S(2)}) %collective-permute-start.7) | collective-permute-done | bytes 786464 | tf_op jit(solution)/shard_map/ppermute | solution.py:1414
  86.7 2.1 %collective-permute-done.12.high_ref = bf16[64,3584]{1,0:T(8,128)(2,1)} collective-permute-done((bf16[64,3584]{1,0:T(8,128)(2,1)}, bf16[64,3584]{1,0:T(8,128)(2,1)}, u32[]{:S(2)}, u32[]{:S(2)}) %collective-permute-start.12) | collective-permute-done | bytes 458784 | tf_op jit(solution)/shard_map/ppermute | solution.py:1414
  89.9 3.6 %collective-permute-start.13 = (bf16[80,1152]{1,0:T(8,128)(2,1)}, bf16[80,1152]{1,0:T(8,128)(2,1)}, u32[]{:S(2)}, u32[]{:S(2)}) collective-permute-start(bf16[80,1152]{1,0:T(8,128)(2,1)} %fusion.2), channel_id=1, source_target_pairs={{0,16},{2,18},{4,20},{6,22},{8,24},{10,26},{12,28},{14,30},{16,0},... | collective-permute-start | bytes 552968 | tf_op jit(solution)/shard_map/ppermute | solution.py:1414
  96.6 2.6 %plane_sum.1 = (bf16[2,384,256]{2,1,0:T(8,128)(2,1)}, f32[384,256]{1,0:T(8,128)}) custom-call(bf16[8,192,256]{2,1,0:T(8,128)(2,1)} %get-tuple-element.113.value_ref, bf16[8,192,256]{2,1,0:T(8,128)(2,1)} %collective-permute-done.7.value_got_ref, bf16[4,192,256]{2,1,0:T(8,128)(2,1)} %copy-done.1, bf16[8,192,256]{2,1,0:T(8,128)(2,1)} %bitcast.38, ...), custom_call_target="tpu_custom_call" | custom-call | flops 1000000 | bytes 3000000 | tf_op jit(solution)/shard_map/plane_sum/pallas_call | solution.py:1214
  100.6 2.2 %collective-permute-done.14.forwarded_ref = bf16[64,2560]{1,0:T(8,128)(2,1)} collective-permute-done((bf16[64,2560]{1,0:T(8,128)(2,1)S(1)}, bf16[64,2560]{1,0:T(8,128)(2,1)}, u32[]{:S(2)}, u32[]{:S(2)}) %collective-permute-start.14) | collective-permute-done | bytes 327712 | tf_op jit(solution)/shard_map/ppermute | solution.py:1414
  102.8 2.5 %collective-permute-start.15 = (bf16[2,384,256]{2,1,0:T(8,128)(2,1)}, bf16[2,384,256]{2,1,0:T(8,128)(2,1)S(1)}, u32[]{:S(2)}, u32[]{:S(2)}) collective-permute-start(bf16[2,384,256]{2,1,0:T(8,128)(2,1)} %get-tuple-element.130), channel_id=1, source_target_pairs={{0,8},{2,10},{4,12},{6,14},{8,0},{10,2},{12,4},{14,6},{16,24},{18,... | collective-permute-start | bytes 1179656 | tf_op jit(solution)/shard_map/ppermute | solution.py:1414
  107.5 2.5 %collective-permute-start.21 = (bf16[80,1152]{1,0:T(8,128)(2,1)S(1)}, bf16[80,1152]{1,0:T(8,128)(2,1)}, u32[]{:S(2)}, u32[]{:S(2)}) collective-permute-start(bf16[80,1152]{1,0:T(8,128)(2,1)S(1)} %add_convert_fusion.4.sum_ref), channel_id=1, source_target_pairs={{0,6},{2,4},{4,2},{6,0},{8,14},{10,12},{12,10},{14,8},{16,22},{18,... | collective-permute-start | bytes 552968 | tf_op jit(solution)/shard_map/ppermute | solution.py:1414
  110.0 4.7 %output_projection_gradient.1 = (bf16[2,416,256]{2,1,0:T(8,128)(2,1)}, bf16[2,416,256]{2,1,0:T(8,128)(2,1)}, bf16[2,384,256]{2,1,0:T(8,128)(2,1)}, bf16[2,384,256]{2,1,0:T(8,128)(2,1)}) custom-call(s32[2]{0:T(128)} %pad_add_fusion.where_ref, bf16[128,768]{1,0:T(8,128)(2,1)} %get-tuple-element.91.own_hbm.attn_hbm.attn_own_ref, ...), custom_call_target="tpu_custom_call" | custom-call | flops 805306368 | bytes 4000000 | tf_op jit(solution)/shard_map/output_projection_gradient/pallas_call | solution.py:1035
  115.3 1.9 %fusion.1 = bf16[384,256]{1,0:T(8,128)(2,1)} fusion(f32[384,256]{1,0:T(8,128)} %get-tuple-element.129, bf16[2,384,256]{2,1,0:T(8,128)(2,1)S(1)} %collective-permute-done.15.low_ref), kind=kLoop, calls=%fused_computation.5 | loop fusion | flops 294912 | bytes 786432 | tf_op jit(solution)/shard_map/convert_element_type | solution.py:1530
  122.0 5.6 %latent_gradients.1 = (f32[256,768]{1,0:T(8,128)}, f32[384,256]{1,0:T(8,128)}, f32[72,384]{1,0:T(8,128)}, f32[1,128]{1,0:T(1,128)}, bf16[256,2048]{1,0:T(8,128)(2,1)}) custom-call(s32[2]{0:T(128)} %pad_add_fusion.where_ref, bf16[80,1152]{1,0:T(8,128)(2,1)} %copy-done.7, bf16[80,1152]{1,0:T(8,128)(2,1)} %copy-done.11, bf16[80,1152]{1,0:T(8,128)(2,1)} %copy-done.12, ...), custom_call_target="tpu_custom_call" | custom-call | flops 100000000 | bytes 3000000 | tf_op jit(solution)/shard_map/latent_gradients/pallas_call | solution.py:1143
  127.6 4.6 %collective-permute-done.24.high_ref = bf16[384,256]{1,0:T(8,128)(2,1)} collective-permute-done((bf16[384,256]{1,0:T(8,128)(2,1)}, bf16[384,256]{1,0:T(8,128)(2,1)}, u32[]{:S(2)}, u32[]{:S(2)}) %collective-permute-start.24) | collective-permute-done | bytes 196640 | tf_op jit(solution)/shard_map/ppermute | solution.py:1414
  133.6 1.7 %fusion.4 = bf16[384,256]{1,0:T(8,128)(2,1)} fusion(bf16[2,384,256]{2,1,0:T(8,128)(2,1)} %collective-permute-done.23.second_got_ref, bf16[2,384,256]{2,1,0:T(8,128)(2,1)} %get-tuple-element.158.second_kept_ref), kind=kLoop, calls=%fused_computation.11 | loop fusion | flops 393216 | bytes 589824 | tf_op jit(solution)/shard_map/convert_element_type | solution.py:1545
  135.4 1.5 %collective-permute-start.26 = (bf16[384,256]{1,0:T(8,128)(2,1)}, bf16[384,256]{1,0:T(8,128)(2,1)S(1)}, u32[]{:S(2)}, u32[]{:S(2)}) collective-permute-start(bf16[384,256]{1,0:T(8,128)(2,1)} %fusion.4), channel_id=1, source_target_pairs={{0,2},{2,0},{4,6},{6,4},{8,10},{10,8},{12,14},{14,12},{16,18},{18,... | collective-permute-start | bytes 589832 | tf_op jit(solution)/shard_map/ppermute | solution.py:1414
  136.9 3.0 %key_value_gradients.1 = (f32[192,256]{1,0:T(8,128)}, f32[192,256]{1,0:T(8,128)}, f32[8,256]{1,0:T(8,128)}) custom-call(s32[2]{0:T(128)} %pad_add_fusion.where_ref, bf16[8,192,256]{2,1,0:T(8,128)(2,1)} %get-tuple-element.113.value_ref, bf16[8,192,256]{2,1,0:T(8,128)(2,1)} %collective-permute-done.7.value_got_ref, bf16[4,192,256]{2,1,0:T(8,128)(2,1)} %copy-done.1, ...), custom_call_target="tpu_custom_call" | custom-call | flops 1000000 | bytes 3000000 | tf_op jit(solution)/shard_map/key_value_gradients/pallas_call | solution.py:1270
  143.3 3.5 %output_gradient_sum.1 = (f32[768,256]{1,0:T(8,128)}, f32[64,128]{1,0:T(8,128)}, f32[1,128]{1,0:T(1,128)}, f32[1,128]{1,0:T(1,128)}) custom-call(s32[2]{0:T(128)} %pad_add_fusion.where_ref, bf16[2,416,256]{2,1,0:T(8,128)(2,1)} %get-tuple-element.156.first_kept_ref, bf16[2,416,256]{2,1,0:T(8,128)(2,1)} %copy-done.3, bf16[416,256]{1,0:T(8,128)(2,1)} %copy-done.8, ...), custom_call_target="tpu_custom_call" | custom-call | flops 1000000 | bytes 3000000 | tf_op jit(solution)/shard_map/output_gradient_sum/pallas_call | solution.py:1353
  (86 shorter events, 32.4 us)
Async XLA Ops:
  0.6 25.7 %collective-permute-start.3 = (bf16[768,4096]{1,0:T(8,128)(2,1)}, bf16[768,4096]{1,0:T(8,128)(2,1)}, u32[]{:S(2)}, u32[]{:S(2)}) collective-permute-start(bf16[768,4096]{1,0:T(8,128)(2,1)} %w_out_hbm.1), channel_id=1, source_target_pairs={{0,1},{1,0},{2,3},{3,2},{4,5},{5,4},{6,7},{7,6},{8,9},{9,8},{10,11... | collective-permute-start | bytes 18874376 | tf_op jit(solution)/shard_map/ppermute | solution.py:30
  1.2 34.6 %all-to-all-start = ((bf16[16,16,2048]{2,1,0:T(8,128)(2,1)}), bf16[16,16,2048]{2,1,0:T(8,128)(2,1)}, u32[]{:S(2)}, u32[]{:S(2)}) async-start(bf16[16,16,2048]{2,1,0:T(8,128)(2,1)} %bitcast.40), calls=%async_computation | async-start | bytes 2097152 | tf_op jit(solution)/shard_map/all_to_all | solution.py:1418
  9.1 15.5 %collective-permute-start = (bf16[192,4096]{1,0:T(8,128)(2,1)}, bf16[192,4096]{1,0:T(8,128)(2,1)}, u32[]{:S(2)}, u32[]{:S(2)}) collective-permute-start(bf16[192,4096]{1,0:T(8,128)(2,1)} %bitcast.28), channel_id=1, source_target_pairs={{0,1},{1,0},{2,3},{3,2},{4,5},{5,4},{6,7},{7,6},{8,9},{9,8},{10,11... | collective-permute-start | bytes 4718600 | tf_op jit(solution)/shard_map/ppermute | solution.py:30
  9.4 15.3 %collective-permute-start.1 = (bf16[192,4096]{1,0:T(8,128)(2,1)}, bf16[192,4096]{1,0:T(8,128)(2,1)}, u32[]{:S(2)}, u32[]{:S(2)}) collective-permute-start(bf16[192,4096]{1,0:T(8,128)(2,1)} %bitcast.33), channel_id=1, source_target_pairs={{0,1},{1,0},{2,3},{3,2},{4,5},{5,4},{6,7},{7,6},{8,9},{9,8},{10,11... | collective-permute-start | bytes 4718600 | tf_op jit(solution)/shard_map/ppermute | solution.py:30
  36.1 46.6 %all-to-all-start.1 = ((bf16[16,16,2048]{2,1,0:T(8,128)(2,1)}), bf16[16,16,2048]{2,1,0:T(8,128)(2,1)}, u32[]{:S(2)}, u32[]{:S(2)}) async-start(bf16[16,16,2048]{2,1,0:T(8,128)(2,1)} %bitcast.41), calls=%async_computation.1 | async-start | bytes 2097152 | tf_op jit(solution)/shard_map/all_to_all | solution.py:1418
  58.1 23.1 %collective-permute-start.7 = (bf16[8,192,256]{2,1,0:T(8,128)(2,1)}, bf16[8,192,256]{2,1,0:T(8,128)(2,1)}, u32[]{:S(2)}, u32[]{:S(2)}) collective-permute-start(bf16[8,192,256]{2,1,0:T(8,128)(2,1)} %get-tuple-element.114), channel_id=1, source_target_pairs={{0,2},{2,0},{4,6},{6,4},{8,10},{10,8},{12,14},{14,12},{16,18},{18,... | collective-permute-start | bytes 2359304 | tf_op jit(solution)/shard_map/ppermute | solution.py:1414
  59.9 22.7 %collective-permute-start.8 = (bf16[2,4,192,256]{3,2,1,0:T(8,128)(2,1)}, bf16[2,4,192,256]{3,2,1,0:T(8,128)(2,1)}, u32[]{:S(2)}, u32[]{:S(2)}) collective-permute-start(bf16[2,4,192,256]{3,2,1,0:T(8,128)(2,1)} %get-tuple-element.115), channel_id=1, source_target_pairs={{0,4},{2,6},{4,0},{6,2},{8,12},{10,14},{12,8},{14,10},{16,20},{18,... | collective-permute-start | bytes 2359304 | tf_op jit(solution)/shard_map/ppermute | solution.py:1414
  62.9 14.6 %collective-permute-start.6 = (bf16[80,1152]{1,0:T(8,128)(2,1)}, bf16[80,1152]{1,0:T(8,128)(2,1)}, u32[]{:S(2)}, u32[]{:S(2)}) collective-permute-start(bf16[80,1152]{1,0:T(8,128)(2,1)} %get-tuple-element.108), channel_id=1, source_target_pairs={{0,8},{2,10},{4,12},{6,14},{8,0},{10,2},{12,4},{14,6},{16,24},{18,... | collective-permute-start | bytes 552968 | tf_op jit(solution)/shard_map/ppermute | solution.py:1414
  64.4 24.4 %collective-permute-start.12 = (bf16[64,3584]{1,0:T(8,128)(2,1)}, bf16[64,3584]{1,0:T(8,128)(2,1)}, u32[]{:S(2)}, u32[]{:S(2)}) collective-permute-start(bf16[64,3584]{1,0:T(8,128)(2,1)} %get-tuple-element.124), channel_id=1, source_target_pairs={{0,16},{2,18},{4,20},{6,22},{8,24},{10,26},{12,28},{14,30},{16,0},... | collective-permute-start | bytes 1376264 | tf_op jit(solution)/shard_map/ppermute | solution.py:1414
  66.8 20.0 %collective-permute-start.11 = (bf16[64,2560]{1,0:T(8,128)(2,1)}, bf16[64,2560]{1,0:T(8,128)(2,1)}, u32[]{:S(2)}, u32[]{:S(2)}) collective-permute-start(bf16[64,2560]{1,0:T(8,128)(2,1)} %get-tuple-element.123), channel_id=1, source_target_pairs={{0,8},{2,10},{4,12},{6,14},{8,0},{10,2},{12,4},{14,6},{16,24},{18,... | collective-permute-start | bytes 983048 | tf_op jit(solution)/shard_map/ppermute | solution.py:1414
  83.9 10.9 %collective-permute-start.10 = (bf16[4,192,256]{2,1,0:T(8,128)(2,1)S(1)}, bf16[4,192,256]{2,1,0:T(8,128)(2,1)}, u32[]{:S(2)}, u32[]{:S(2)}) collective-permute-start(bf16[4,192,256]{2,1,0:T(8,128)(2,1)S(1)} %fusion), channel_id=1, source_target_pairs={{0,2},{2,0},{4,6},{6,4},{8,10},{10,8},{12,14},{14,12},{16,18},{18,... | collective-permute-start | bytes 1179656 | tf_op jit(solution)/shard_map/ppermute | solution.py:1414
  85.3 10.6 %collective-permute-start.9 = (bf16[4,192,256]{2,1,0:T(8,128)(2,1)S(1)}, bf16[4,192,256]{2,1,0:T(8,128)(2,1)S(1)}, u32[]{:S(2)}, u32[]{:S(2)}) collective-permute-start(bf16[4,192,256]{2,1,0:T(8,128)(2,1)S(1)} %add_convert_fusion.1), channel_id=1, source_target_pairs={{0,4},{2,6},{4,0},{6,2},{8,12},{10,14},{12,8},{14,10},{16,20},{18,... | collective-permute-start | bytes 1179656 | tf_op jit(solution)/shard_map/ppermute | solution.py:1414
  89.8 13.0 %collective-permute-start.14 = (bf16[64,2560]{1,0:T(8,128)(2,1)S(1)}, bf16[64,2560]{1,0:T(8,128)(2,1)}, u32[]{:S(2)}, u32[]{:S(2)}) collective-permute-start(bf16[64,2560]{1,0:T(8,128)(2,1)S(1)} %slice.36), channel_id=1, source_target_pairs={{0,8},{2,10},{4,12},{6,14},{8,0},{10,2},{12,4},{14,6},{16,24},{18,... | collective-permute-start | bytes 983048 | tf_op jit(solution)/shard_map/ppermute | solution.py:1414
  89.9 10.7 %collective-permute-start.13 = (bf16[80,1152]{1,0:T(8,128)(2,1)}, bf16[80,1152]{1,0:T(8,128)(2,1)}, u32[]{:S(2)}, u32[]{:S(2)}) collective-permute-start(bf16[80,1152]{1,0:T(8,128)(2,1)} %fusion.2), channel_id=1, source_target_pairs={{0,16},{2,18},{4,20},{6,22},{8,24},{10,26},{12,28},{14,30},{16,0},... | collective-permute-start | bytes 552968 | tf_op jit(solution)/shard_map/ppermute | solution.py:1414
  93.5 14.0 %collective-permute-start.17 = (bf16[64,3584]{1,0:T(8,128)(2,1)}, bf16[64,3584]{1,0:T(8,128)(2,1)}, u32[]{:S(2)}, u32[]{:S(2)}) collective-permute-start(bf16[64,3584]{1,0:T(8,128)(2,1)} %collective-permute-done.12.high_ref), channel_id=1, source_target_pairs={{0,1},{1,0},{2,3},{3,2},{4,5},{5,4},{6,7},{7,6},{8,9},{9,8},{10,11... | collective-permute-start | bytes 1376264 | tf_op jit(solution)/shard_map/ppermute | solution.py:30
  94.8 11.7 %collective-permute-start.16 = (bf16[64,2560]{1,0:T(8,128)(2,1)}, bf16[64,2560]{1,0:T(8,128)(2,1)}, u32[]{:S(2)}, u32[]{:S(2)}) collective-permute-start(bf16[64,2560]{1,0:T(8,128)(2,1)} %collective-permute-done.11.low_ref), channel_id=1, source_target_pairs={{0,1},{1,0},{2,3},{3,2},{4,5},{5,4},{6,7},{7,6},{8,9},{9,8},{10,11... | collective-permute-start | bytes 983048 | tf_op jit(solution)/shard_map/ppermute | solution.py:30
  102.8 12.5 %collective-permute-start.15 = (bf16[2,384,256]{2,1,0:T(8,128)(2,1)}, bf16[2,384,256]{2,1,0:T(8,128)(2,1)S(1)}, u32[]{:S(2)}, u32[]{:S(2)}) collective-permute-start(bf16[2,384,256]{2,1,0:T(8,128)(2,1)} %get-tuple-element.130), channel_id=1, source_target_pairs={{0,8},{2,10},{4,12},{6,14},{8,0},{10,2},{12,4},{14,6},{16,24},{18,... | collective-permute-start | bytes 1179656 | tf_op jit(solution)/shard_map/ppermute | solution.py:1414
  106.4 10.8 %collective-permute-start.19 = (bf16[80,1152]{1,0:T(8,128)(2,1)S(1)}, bf16[80,1152]{1,0:T(8,128)(2,1)S(1)}, u32[]{:S(2)}, u32[]{:S(2)}) collective-permute-start(bf16[80,1152]{1,0:T(8,128)(2,1)S(1)} %add_convert_fusion.4.sum_ref), channel_id=1, source_target_pairs={{0,2},{2,0},{4,6},{6,4},{8,10},{10,8},{12,14},{14,12},{16,18},{18,... | collective-permute-start | bytes 552968 | tf_op jit(solution)/shard_map/ppermute | solution.py:1414
  106.5 10.8 %collective-permute-start.20 = (bf16[80,1152]{1,0:T(8,128)(2,1)S(1)}, bf16[80,1152]{1,0:T(8,128)(2,1)S(1)}, u32[]{:S(2)}, u32[]{:S(2)}) collective-permute-start(bf16[80,1152]{1,0:T(8,128)(2,1)S(1)} %add_convert_fusion.4.sum_ref), channel_id=1, source_target_pairs={{0,4},{2,6},{4,0},{6,2},{8,12},{10,14},{12,8},{14,10},{16,20},{18,... | collective-permute-start | bytes 552968 | tf_op jit(solution)/shard_map/ppermute | solution.py:1414
  107.5 11.0 %collective-permute-start.21 = (bf16[80,1152]{1,0:T(8,128)(2,1)S(1)}, bf16[80,1152]{1,0:T(8,128)(2,1)}, u32[]{:S(2)}, u32[]{:S(2)}) collective-permute-start(bf16[80,1152]{1,0:T(8,128)(2,1)S(1)} %add_convert_fusion.4.sum_ref), channel_id=1, source_target_pairs={{0,6},{2,4},{4,2},{6,0},{8,14},{10,12},{12,10},{14,8},{16,22},{18,... | collective-permute-start | bytes 552968 | tf_op jit(solution)/shard_map/ppermute | solution.py:1414
  118.5 13.7 %collective-permute-start.22 = (bf16[2,416,256]{2,1,0:T(8,128)(2,1)}, bf16[2,416,256]{2,1,0:T(8,128)(2,1)S(1)}, u32[]{:S(2)}, u32[]{:S(2)}) collective-permute-start(bf16[2,416,256]{2,1,0:T(8,128)(2,1)} %get-tuple-element.147), channel_id=1, source_target_pairs={{0,2},{2,0},{4,6},{6,4},{8,10},{10,8},{12,14},{14,12},{16,18},{18,... | collective-permute-start | bytes 1277960 | tf_op jit(solution)/shard_map/ppermute | solution.py:1414
  119.6 12.6 %collective-permute-start.23 = (bf16[2,384,256]{2,1,0:T(8,128)(2,1)}, bf16[2,384,256]{2,1,0:T(8,128)(2,1)}, u32[]{:S(2)}, u32[]{:S(2)}) collective-permute-start(bf16[2,384,256]{2,1,0:T(8,128)(2,1)} %get-tuple-element.148), channel_id=1, source_target_pairs={{0,4},{2,6},{4,0},{6,2},{8,12},{10,14},{12,8},{14,10},{16,20},{18,... | collective-permute-start | bytes 1179656 | tf_op jit(solution)/shard_map/ppermute | solution.py:1414
  120.8 11.4 %collective-permute-start.24 = (bf16[384,256]{1,0:T(8,128)(2,1)}, bf16[384,256]{1,0:T(8,128)(2,1)}, u32[]{:S(2)}, u32[]{:S(2)}) collective-permute-start(bf16[384,256]{1,0:T(8,128)(2,1)} %fusion.1), channel_id=1, source_target_pairs={{0,16},{2,18},{4,20},{6,22},{8,24},{10,26},{12,28},{14,30},{16,0},... | collective-permute-start | bytes 589832 | tf_op jit(solution)/shard_map/ppermute | solution.py:1414
  133.1 8.8 %collective-permute-start.25 = (bf16[416,256]{1,0:T(8,128)(2,1)}, bf16[416,256]{1,0:T(8,128)(2,1)S(1)}, u32[]{:S(2)}, u32[]{:S(2)}) collective-permute-start(bf16[416,256]{1,0:T(8,128)(2,1)} %fusion.3), channel_id=1, source_target_pairs={{0,4},{2,6},{4,0},{6,2},{8,12},{10,14},{12,8},{14,10},{16,20},{18,... | collective-permute-start | bytes 638984 | tf_op jit(solution)/shard_map/ppermute | solution.py:1414
  (22 other events, 111.4 us)

commit v4 on v3

--- a/solution.py
+++ b/solution.py
@@ -971,9 +971,11 @@
     other_low_ref,
     other_high_ref,
     other_forwarded_ref,
-    first_going_ref,
+    first_onward_ref,
+    first_last_ref,
     first_kept_ref,
-    second_going_ref,
+    second_onward_ref,
+    second_last_ref,
     second_kept_ref,
     attn_ref,
     line_ref,
@@ -1017,20 +1019,22 @@
         mine_at = pl.ds(pl.multiple_of(owner * own + mine * share, share), share)
         part = resid_ref[:, mine_at]
         part = jnp.concatenate([part[: latent_rows // 2], part[latent_rows // 2 :]], axis=1)
-        ref = first_going_ref if x_differs else first_kept_ref
-        ref[1 - y_differs, :cut, :] = grad[:cut]
-        ref[1 - y_differs, cut:, :] = part.astype(BF16)
-        ref = second_going_ref if y_differs else second_kept_ref
-        ref[1 - x_differs] = grad[cut:]
+        ends = 1 - y_differs
+        ref = (first_onward_ref, first_last_ref)[ends] if x_differs else first_kept_ref.at[ends]
+        ref[:cut, :] = grad[:cut]
+        ref[cut:, :] = part.astype(BF16)
+        ends = 1 - x_differs
+        ref = (second_onward_ref, second_last_ref)[ends] if y_differs else second_kept_ref.at[ends]
+        ref[...] = grad[cut:]
 
 
 def out_call(where, attn, line, received, others):
     rows, heads = attn.shape
     columns = line.shape[1]
     own = columns // 4
-    first = (2, heads // 2 + rows // 4, own)
-    second = (2, heads // 2, own)
-    shapes = [first, first, second, second]
+    first = (heads // 2 + rows // 4, own)
+    second = (heads // 2, own)
+    shapes = [first, first, (2, *first), second, second, (2, *second)]
     operands = (attn, line, *received, *others)
     return pl.pallas_call(
         out_kernel,
@@ -1325,11 +1329,11 @@
     share = own // 2
     cut = heads // 2
     first = sum(
-        part.astype(F32) for part in (first_kept_ref[0], first_got_ref[0], first_last_ref[...])
+        part.astype(F32) for part in (first_kept_ref[0], first_got_ref[...], first_last_ref[...])
     )
     out_ref[:cut, :] = first[:cut]
     out_ref[cut:, :] = sum(
-        part.astype(F32) for part in (second_kept_ref[0], second_got_ref[0], second_last_ref[...])
+        part.astype(F32) for part in (second_kept_ref[0], second_got_ref[...], second_last_ref[...])
     )
     resid = first[cut:]
     resid = jnp.concatenate([resid[:, :share], resid[:, share:]], axis=0)
@@ -1513,36 +1517,39 @@
     other_high = swap_cores(got_high)
 
     planes = plane_call(value_kept, value_got, value_last, key_kept, key_got, key_last)
-    (going, high), lat_got, forwarded = lax.optimization_barrier((planes, lat_got, forwarded))
-    low = swap(going, 4)
+    low = swap(planes[0], 4)
+    (_, high), lat_got, forwarded = lax.optimization_barrier((planes, lat_got, forwarded))
     other_forwarded = swap_cores(forwarded)
     lat_sum = add_halves(lat_sum, lat_got).astype(BF16)
     lat_parts = (swap(lat_sum, 1), swap(lat_sum, 2), swap(lat_sum, 3))
 
-    first_going, first_kept, second_going, second_kept = out_call(
+    first_onward, first_end, first_kept, second_onward, second_end, second_kept = out_call(
         where,
         attn_rows,
         line_own,
         (got_low, got_high, forwarded),
         (other_low, other_high, other_forwarded),
     )
-    low, first_going, second_going = lax.optimization_barrier((low, first_going, second_going))
+    low, first_onward, second_onward, first_end, second_end = lax.optimization_barrier(
+        (low, first_onward, second_onward, first_end, second_end)
+    )
     high = add_halves(high, low[0]).astype(BF16)
-    high, lat_parts, first_going, second_going = lax.optimization_barrier(
-        (high, lat_parts, first_going, second_going)
-    )
+    high, lat_parts = lax.optimization_barrier((high, lat_parts))
     high = swap(high, 8)
-    first_got = swap(first_going, 1)
-    second_got = swap(second_going, 2)
+    first_onward = swap(first_onward, 1)
+    second_onward = swap(second_onward, 2)
+    first_end = swap(first_end, 1)
+    second_end = swap(second_end, 2)
 
     grad_w_query, pair_lat, message, grad_gain_out, routed = latent_call(
         where, lat_sum, lat_parts, lat_proj, latents, gain_lat, w_query, wk, wv, own_width, routed
     )
-    first_got, second_got, high, message, pair_lat = lax.optimization_barrier(
-        (first_got, second_got, high, message, pair_lat)
-    )
-    first_last = swap(add_halves(first_kept[0], first_got[0]).astype(BF16), 2)
-    second_last = swap(add_halves(second_kept[0], second_got[0]).astype(BF16), 1)
+    first_onward, second_onward, message, pair_lat = lax.optimization_barrier(
+        (first_onward, second_onward, message, pair_lat)
+    )
+    high, pair_lat = lax.optimization_barrier((high, pair_lat))
+    first_last = swap(add_halves(first_kept[0], first_onward).astype(BF16), 2)
+    second_last = swap(add_halves(second_kept[0], second_onward).astype(BF16), 1)
     message_got = swap_cores(message)
 
     grad_key, grad_value, gain_term = final_call(
@@ -1565,7 +1572,7 @@
     )
     grad_w_out, grad_latents, grad_gain_lat, grad_gain_ctx = out_final_call(
         where,
-        (first_kept, first_got, first_last, second_kept, second_got, second_last),
+        (first_kept, first_end, first_last, second_kept, second_end, second_last),
         message,
         message_got,
         gain_term,

time: 148 us -> 143 us (0.966)
  waiting for transfers between devices: 19.8 us -> 15.8 us
  starting transfers between devices: 41.8 us -> 43.3 us
    ppermute x18 -> x20, waiting for transfers between devices: 18.3 us -> 14.3 us  [swap(): return lax.ppermute(array, 'dp', [(i, i ^ turn) for i in range(dp_count)])]
    ppermute x18 -> x20, starting transfers between devices: 24.7 us -> 26.7 us  [swap(): return lax.ppermute(array, 'dp', [(i, i ^ turn) for i in range(dp_count)])]
    unnamed x30 -> x28, local copies, waits for them, and re-layouts: 4.96 us -> 3.53 us
  transfers between devices with their start and end apart: 31 -> 33, of which waited for: 12 -> 11; matrix products, arithmetic and copies ran while one was open for 7% -> 7% of each run, Pallas kernels for 44% -> 46%
where the time goes in v4:
time: 143 us; the launch traced here: 142 us
  Pallas kernels  68.3 us (48%)
  starting transfers between devices  43.3 us (30%)
  waiting for transfers between devices  15.8 us (11%)
  other arithmetic  9.44 us (7%)
  local copies, waits for them, and re-layouts  4.53 us (3%)
    ppermute x20, starting transfers between devices, swap(): return lax.ppermute(array, 'dp', [(i, i ^ turn) for i in range(dp_count)])  26.7 us
    pallas_call x1, Pallas kernels, backward_call(): pl.pallas_call(functools.partial(backward_kernel, slot_count), name='atte...  15 us
    pallas_call x1, Pallas kernels, forward_call(): pl.pallas_call(forward_kernel, name='forward_attention', in_specs=[pl.Blo...  15 us
    all_to_all x2, starting transfers between devices, exchange(): lax.all_to_all(blocks, 'dp', split_axis=0, concat_axis=0, tiled=True)  14.7 us
    ppermute x20, waiting for transfers between devices, swap(): return lax.ppermute(array, 'dp', [(i, i ^ turn) for i in range(dp_count)])  14.3 us
    pallas_call x1, Pallas kernels, patch_call(): pl.pallas_call(functools.partial(patch_kernel, width), name='patch_gradie...  10.2 us
    pallas_call x1, Pallas kernels, branch_call(): pl.pallas_call(functools.partial(branch_kernel, slot_count), name='branch...  8.75 us
    pallas_call x1, Pallas kernels, latent_call(): pl.pallas_call(latent_kernel, name='latent_gradients', grid_spec=pltpu.Pr...  5.66 us
  transfers between devices with their start and end apart: 33, of which 11 were waited for; matrix products, arithmetic and copies ran while one was open for 7% of the time, Pallas kernels for 46%

profile of v4, /device:TPU:0, one launch (start us, length us, event | category | flops | bytes accessed | tf_op | source)
XLA Modules:
  0.0 142.2 jit_solution(9198535146935232914)
XLA Ops:
  1.2 7.9 %all-to-all-start = ((bf16[16,16,2048]{2,1,0:T(8,128)(2,1)}), bf16[16,16,2048]{2,1,0:T(8,128)(2,1)}, u32[]{:S(2)}, u32[]{:S(2)}) async-start(bf16[16,16,2048]{2,1,0:T(8,128)(2,1)} %bitcast.42), calls=%async_computation | async-start | bytes 2097152 | tf_op jit(solution)/shard_map/all_to_all | solution.py:1422
  9.7 15.0 %forward_attention.1 = (bf16[128,768]{1,0:T(8,128)(2,1)}, bf16[2,1024,128]{2,1,0:T(8,128)(2,1)}, bf16[2,1024,128]{2,1,0:T(8,128)(2,1)}, f32[8,1024]{1,0:T(8,128)...) custom-call(s32[1,2]{1,0:T(1,128)} %counts_ref.3, ...), custom_call_target="tpu_custom_call" | custom-call | flops 5000000000 | bytes 24000000 | tf_op jit(solution)/shard_map/forward_attention/pallas_call | solution.py:285
  27.1 8.8 %branch_norm.1 = (bf16[128,4096]{1,0:T(8,128)(2,1)}, f32[128,1]{1,0:T(8,128)}, bf16[256,2048]{1,0:T(8,128)(2,1)}) custom-call(bf16[128,768]{1,0:T(8,128)(2,1)} %get-tuple-element.93.own_hbm.attn_hbm.attn_own_ref, bf16[128,768]{1,0:T(8,128)(2,1)} %copy-done.9, bf16[64,4096]{1,0:T(8,128)(2,1)} %lat_ref.3, f32[1,4096]{1,0:T(1,128)} %bitcast.50, ...), custom_call_target="tpu_custom_call" | custom-call | flops 1610612736 | bytes 16000000 | tf_op jit(solution)/shard_map/branch_norm/pallas_call | solution.py:428
  36.1 6.8 %all-to-all-start.1 = ((bf16[16,16,2048]{2,1,0:T(8,128)(2,1)}), bf16[16,16,2048]{2,1,0:T(8,128)(2,1)}, u32[]{:S(2)}, u32[]{:S(2)}) async-start(bf16[16,16,2048]{2,1,0:T(8,128)(2,1)} %bitcast.43), calls=%async_computation.1 | async-start | bytes 2097152 | tf_op jit(solution)/shard_map/all_to_all | solution.py:1422
  42.9 15.0 %attention_backward.1 = (bf16[128,1024]{1,0:T(8,128)(2,1)}, bf16[64,3584]{1,0:T(8,128)(2,1)}, bf16[400,1024]{1,0:T(8,128)(2,1)}, bf16[64,2560]{1,0:T(8,128)(2,1)...) custom-call(s32[1,2]{1,0:T(1,128)} %counts_ref.3, ...), custom_call_target="tpu_custom_call" | custom-call | flops 5000000000 | bytes 26000000 | tf_op jit(solution)/shard_map/attention_backward/pallas_call | solution.py:844
  58.1 1.9 %collective-permute-start.7 = (bf16[8,192,256]{2,1,0:T(8,128)(2,1)}, bf16[8,192,256]{2,1,0:T(8,128)(2,1)}, u32[]{:S(2)}, u32[]{:S(2)}) collective-permute-start(bf16[8,192,256]{2,1,0:T(8,128)(2,1)} %get-tuple-element.116), channel_id=1, source_target_pairs={{0,2},{2,0},{4,6},{6,4},{8,10},{10,8},{12,14},{14,12},{16,18},{18,... | collective-permute-start | bytes 2359304 | tf_op jit(solution)/shard_map/ppermute | solution.py:1418
  64.4 2.4 %collective-permute-start.12 = (bf16[64,3584]{1,0:T(8,128)(2,1)}, bf16[64,3584]{1,0:T(8,128)(2,1)}, u32[]{:S(2)}, u32[]{:S(2)}) collective-permute-start(bf16[64,3584]{1,0:T(8,128)(2,1)} %get-tuple-element.126), channel_id=1, source_target_pairs={{0,16},{2,18},{4,20},{6,22},{8,24},{10,26},{12,28},{14,30},{16,0},... | collective-permute-start | bytes 1376264 | tf_op jit(solution)/shard_map/ppermute | solution.py:1418
  67.4 10.2 %patch_gradient.1 = bf16[1024,2048]{1,0:T(8,128)(2,1)} custom-call(s32[2]{0:T(128)} %pad_add_fusion.where_ref, bf16[400,1024]{1,0:T(8,128)(2,1)} %get-tuple-element.109.own_ref, bf16[400,1024]{1,0:T(8,128)(2,1)} %copy-done.4, bf16[192,4096]{1,0:T(8,128)(2,1)} %bitcast.32, bf16[192,4096]{1,0:T(8,128)(2,1)} %bitcast.37, ...), custom_call_target="tpu_custom_call" | custom-call | flops 3300000000 | bytes 14000000 | tf_op jit(solution)/shard_map/patch_gradient/pallas_call | solution.py:931
  77.6 1.6 %fusion.4 = bf16[80,1152]{1,0:T(8,128)(2,1)} fusion(bf16[80,1152]{1,0:T(8,128)(2,1)} %collective-permute-done.6, bf16[80,1152]{1,0:T(8,128)(2,1)S(1)} %copy-done.5), kind=kLoop, calls=%fused_computation.11 | loop fusion | flops 368640 | bytes 552960 | tf_op jit(solution)/shard_map/convert_element_type | solution.py:1500
  79.2 2.0 %collective-permute-done.7.value_got_ref = bf16[8,192,256]{2,1,0:T(8,128)(2,1)} collective-permute-done((bf16[8,192,256]{2,1,0:T(8,128)(2,1)}, bf16[8,192,256]{2,1,0:T(8,128)(2,1)}, u32[]{:S(2)}, u32[]{:S(2)}) %collective-permute-start.7) | collective-permute-done | bytes 786464 | tf_op jit(solution)/shard_map/ppermute | solution.py:1418
  86.8 2.1 %collective-permute-done.12.high_ref = bf16[64,3584]{1,0:T(8,128)(2,1)} collective-permute-done((bf16[64,3584]{1,0:T(8,128)(2,1)}, bf16[64,3584]{1,0:T(8,128)(2,1)}, u32[]{:S(2)}, u32[]{:S(2)}) %collective-permute-start.12) | collective-permute-done | bytes 458784 | tf_op jit(solution)/shard_map/ppermute | solution.py:1418
  89.9 3.6 %collective-permute-start.13 = (bf16[80,1152]{1,0:T(8,128)(2,1)}, bf16[80,1152]{1,0:T(8,128)(2,1)}, u32[]{:S(2)}, u32[]{:S(2)}) collective-permute-start(bf16[80,1152]{1,0:T(8,128)(2,1)} %fusion.4), channel_id=1, source_target_pairs={{0,16},{2,18},{4,20},{6,22},{8,24},{10,26},{12,28},{14,30},{16,0},... | collective-permute-start | bytes 552968 | tf_op jit(solution)/shard_map/ppermute | solution.py:1418
  96.7 2.6 %plane_sum.1 = (bf16[2,384,256]{2,1,0:T(8,128)(2,1)}, f32[384,256]{1,0:T(8,128)}) custom-call(bf16[8,192,256]{2,1,0:T(8,128)(2,1)} %get-tuple-element.115.value_ref, bf16[8,192,256]{2,1,0:T(8,128)(2,1)} %collective-permute-done.7.value_got_ref, bf16[4,192,256]{2,1,0:T(8,128)(2,1)} %copy-done.1, bf16[8,192,256]{2,1,0:T(8,128)(2,1)} %bitcast.40, ...), custom_call_target="tpu_custom_call" | custom-call | flops 1000000 | bytes 3000000 | tf_op jit(solution)/shard_map/plane_sum/pallas_call | solution.py:1218
  101.3 2.7 %collective-permute-done.14.forwarded_ref = bf16[64,2560]{1,0:T(8,128)(2,1)} collective-permute-done((bf16[64,2560]{1,0:T(8,128)(2,1)S(1)}, bf16[64,2560]{1,0:T(8,128)(2,1)}, u32[]{:S(2)}, u32[]{:S(2)}) %collective-permute-start.14) | collective-permute-done | bytes 327712 | tf_op jit(solution)/shard_map/ppermute | solution.py:1418
  105.1 1.7 %collective-permute-start.19 = (bf16[80,1152]{1,0:T(8,128)(2,1)S(1)}, bf16[80,1152]{1,0:T(8,128)(2,1)S(1)}, u32[]{:S(2)}, u32[]{:S(2)}) collective-permute-start(bf16[80,1152]{1,0:T(8,128)(2,1)S(1)} %add_convert_fusion.2.sum_ref), channel_id=1, source_target_pairs={{0,2},{2,0},{4,6},{6,4},{8,10},{10,8},{12,14},{14,12},{16,18},{18,... | collective-permute-start | bytes 552968 | tf_op jit(solution)/shard_map/ppermute | solution.py:1418
  106.8 1.5 %collective-permute-start.20 = (bf16[80,1152]{1,0:T(8,128)(2,1)S(1)}, bf16[80,1152]{1,0:T(8,128)(2,1)S(1)}, u32[]{:S(2)}, u32[]{:S(2)}) collective-permute-start(bf16[80,1152]{1,0:T(8,128)(2,1)S(1)} %add_convert_fusion.2.sum_ref), channel_id=1, source_target_pairs={{0,4},{2,6},{4,0},{6,2},{8,12},{10,14},{12,8},{14,10},{16,20},{18,... | collective-permute-start | bytes 552968 | tf_op jit(solution)/shard_map/ppermute | solution.py:1418
  108.7 4.6 %output_projection_gradient.1 = (bf16[416,256]{1,0:T(8,128)(2,1)}, bf16[416,256]{1,0:T(8,128)(2,1)}, bf16[2,416,256]{2,1,0:T(8,128)(2,1)}, bf16[384,256]{1,0:T(8...) custom-call(s32[2]{0:T(128)} %pad_add_fusion.where_ref, ...), custom_call_target="tpu_custom_call" | custom-call | flops 805306368 | bytes 4000000 | tf_op jit(solution)/shard_map/output_projection_gradient/pallas_call | solution.py:1039
  113.3 1.7 %collective-permute-start.23 = (bf16[416,256]{1,0:T(8,128)(2,1)}, bf16[416,256]{1,0:T(8,128)(2,1)}, u32[]{:S(2)}, u32[]{:S(2)}) collective-permute-start(bf16[416,256]{1,0:T(8,128)(2,1)} %get-tuple-element.149), channel_id=1, source_target_pairs={{0,2},{2,0},{4,6},{6,4},{8,10},{10,8},{12,14},{14,12},{16,18},{18,... | collective-permute-start | bytes 638984 | tf_op jit(solution)/shard_map/ppermute | solution.py:1418
  115.0 1.5 %collective-permute-start.24 = (bf16[384,256]{1,0:T(8,128)(2,1)}, bf16[384,256]{1,0:T(8,128)(2,1)}, u32[]{:S(2)}, u32[]{:S(2)}) collective-permute-start(bf16[384,256]{1,0:T(8,128)(2,1)} %get-tuple-element.150), channel_id=1, source_target_pairs={{0,4},{2,6},{4,0},{6,2},{8,12},{10,14},{12,8},{14,10},{16,20},{18,... | collective-permute-start | bytes 589832 | tf_op jit(solution)/shard_map/ppermute | solution.py:1418
  116.5 1.7 %fusion.3 = bf16[384,256]{1,0:T(8,128)(2,1)} fusion(f32[384,256]{1,0:T(8,128)} %get-tuple-element.131, bf16[2,384,256]{2,1,0:T(8,128)(2,1)S(1)} %collective-permute-done.15.low_ref), kind=kLoop, calls=%fused_computation.8 | loop fusion | flops 294912 | bytes 786432 | tf_op jit(solution)/shard_map/convert_element_type | solution.py:1536
  120.4 5.7 %latent_gradients.1 = (f32[256,768]{1,0:T(8,128)}, f32[384,256]{1,0:T(8,128)}, f32[72,384]{1,0:T(8,128)}, f32[1,128]{1,0:T(1,128)}, bf16[256,2048]{1,0:T(8,128)(2,1)}) custom-call(s32[2]{0:T(128)} %pad_add_fusion.where_ref, bf16[80,1152]{1,0:T(8,128)(2,1)} %copy-done.6, bf16[80,1152]{1,0:T(8,128)(2,1)} %copy-done.10, bf16[80,1152]{1,0:T(8,128)(2,1)} %copy-done.11, ...), custom_call_target="tpu_custom_call" | custom-call | flops 100000000 | bytes 3000000 | tf_op jit(solution)/shard_map/latent_gradients/pallas_call | solution.py:1147
  131.5 3.0 %key_value_gradients.1 = (f32[192,256]{1,0:T(8,128)}, f32[192,256]{1,0:T(8,128)}, f32[8,256]{1,0:T(8,128)}) custom-call(s32[2]{0:T(128)} %pad_add_fusion.where_ref, bf16[8,192,256]{2,1,0:T(8,128)(2,1)} %get-tuple-element.115.value_ref, bf16[8,192,256]{2,1,0:T(8,128)(2,1)} %collective-permute-done.7.value_got_ref, bf16[4,192,256]{2,1,0:T(8,128)(2,1)} %copy-done.1, ...), custom_call_target="tpu_custom_call" | custom-call | flops 1000000 | bytes 3000000 | tf_op jit(solution)/shard_map/key_value_gradients/pallas_call | solution.py:1274
  135.1 2.3 %collective-permute-done.28.second_got_ref = bf16[384,256]{1,0:T(8,128)(2,1)} collective-permute-done((bf16[384,256]{1,0:T(8,128)(2,1)}, bf16[384,256]{1,0:T(8,128)(2,1)}, u32[]{:S(2)}, u32[]{:S(2)}) %collective-permute-start.28) | collective-permute-done | bytes 196640 | tf_op jit(solution)/shard_map/ppermute | solution.py:1418
  138.7 3.5 %output_gradient_sum.1 = (f32[768,256]{1,0:T(8,128)}, f32[64,128]{1,0:T(8,128)}, f32[1,128]{1,0:T(1,128)}, f32[1,128]{1,0:T(1,128)}) custom-call(s32[2]{0:T(128)} %pad_add_fusion.where_ref, bf16[2,416,256]{2,1,0:T(8,128)(2,1)} %get-tuple-element.158.first_kept_ref, bf16[416,256]{1,0:T(8,128)(2,1)} %collective-permute-done.25.first_got_ref, ...), custom_call_target="tpu_custom_call" | custom-call | flops 1000000 | bytes 3000000 | tf_op jit(solution)/shard_map/output_gradient_sum/pallas_call | solution.py:1357
  (88 shorter events, 31.6 us)
Async XLA Ops:
  0.6 25.7 %collective-permute-start.3 = (bf16[768,4096]{1,0:T(8,128)(2,1)}, bf16[768,4096]{1,0:T(8,128)(2,1)}, u32[]{:S(2)}, u32[]{:S(2)}) collective-permute-start(bf16[768,4096]{1,0:T(8,128)(2,1)} %w_out_hbm.1), channel_id=1, source_target_pairs={{0,1},{1,0},{2,3},{3,2},{4,5},{5,4},{6,7},{7,6},{8,9},{9,8},{10,11... | collective-permute-start | bytes 18874376 | tf_op jit(solution)/shard_map/ppermute | solution.py:30
  1.2 34.7 %all-to-all-start = ((bf16[16,16,2048]{2,1,0:T(8,128)(2,1)}), bf16[16,16,2048]{2,1,0:T(8,128)(2,1)}, u32[]{:S(2)}, u32[]{:S(2)}) async-start(bf16[16,16,2048]{2,1,0:T(8,128)(2,1)} %bitcast.42), calls=%async_computation | async-start | bytes 2097152 | tf_op jit(solution)/shard_map/all_to_all | solution.py:1422
  9.1 15.5 %collective-permute-start = (bf16[192,4096]{1,0:T(8,128)(2,1)}, bf16[192,4096]{1,0:T(8,128)(2,1)}, u32[]{:S(2)}, u32[]{:S(2)}) collective-permute-start(bf16[192,4096]{1,0:T(8,128)(2,1)} %bitcast.30), channel_id=1, source_target_pairs={{0,1},{1,0},{2,3},{3,2},{4,5},{5,4},{6,7},{7,6},{8,9},{9,8},{10,11... | collective-permute-start | bytes 4718600 | tf_op jit(solution)/shard_map/ppermute | solution.py:30
  9.4 15.3 %collective-permute-start.1 = (bf16[192,4096]{1,0:T(8,128)(2,1)}, bf16[192,4096]{1,0:T(8,128)(2,1)}, u32[]{:S(2)}, u32[]{:S(2)}) collective-permute-start(bf16[192,4096]{1,0:T(8,128)(2,1)} %bitcast.35), channel_id=1, source_target_pairs={{0,1},{1,0},{2,3},{3,2},{4,5},{5,4},{6,7},{7,6},{8,9},{9,8},{10,11... | collective-permute-start | bytes 4718600 | tf_op jit(solution)/shard_map/ppermute | solution.py:30
  36.1 46.6 %all-to-all-start.1 = ((bf16[16,16,2048]{2,1,0:T(8,128)(2,1)}), bf16[16,16,2048]{2,1,0:T(8,128)(2,1)}, u32[]{:S(2)}, u32[]{:S(2)}) async-start(bf16[16,16,2048]{2,1,0:T(8,128)(2,1)} %bitcast.43), calls=%async_computation.1 | async-start | bytes 2097152 | tf_op jit(solution)/shard_map/all_to_all | solution.py:1422
  58.1 23.1 %collective-permute-start.7 = (bf16[8,192,256]{2,1,0:T(8,128)(2,1)}, bf16[8,192,256]{2,1,0:T(8,128)(2,1)}, u32[]{:S(2)}, u32[]{:S(2)}) collective-permute-start(bf16[8,192,256]{2,1,0:T(8,128)(2,1)} %get-tuple-element.116), channel_id=1, source_target_pairs={{0,2},{2,0},{4,6},{6,4},{8,10},{10,8},{12,14},{14,12},{16,18},{18,... | collective-permute-start | bytes 2359304 | tf_op jit(solution)/shard_map/ppermute | solution.py:1418
  60.0 22.7 %collective-permute-start.8 = (bf16[2,4,192,256]{3,2,1,0:T(8,128)(2,1)}, bf16[2,4,192,256]{3,2,1,0:T(8,128)(2,1)}, u32[]{:S(2)}, u32[]{:S(2)}) collective-permute-start(bf16[2,4,192,256]{3,2,1,0:T(8,128)(2,1)} %get-tuple-element.117), channel_id=1, source_target_pairs={{0,4},{2,6},{4,0},{6,2},{8,12},{10,14},{12,8},{14,10},{16,20},{18,... | collective-permute-start | bytes 2359304 | tf_op jit(solution)/shard_map/ppermute | solution.py:1418
  63.0 14.6 %collective-permute-start.6 = (bf16[80,1152]{1,0:T(8,128)(2,1)}, bf16[80,1152]{1,0:T(8,128)(2,1)}, u32[]{:S(2)}, u32[]{:S(2)}) collective-permute-start(bf16[80,1152]{1,0:T(8,128)(2,1)} %get-tuple-element.110), channel_id=1, source_target_pairs={{0,8},{2,10},{4,12},{6,14},{8,0},{10,2},{12,4},{14,6},{16,24},{18,... | collective-permute-start | bytes 552968 | tf_op jit(solution)/shard_map/ppermute | solution.py:1418
  64.4 24.4 %collective-permute-start.12 = (bf16[64,3584]{1,0:T(8,128)(2,1)}, bf16[64,3584]{1,0:T(8,128)(2,1)}, u32[]{:S(2)}, u32[]{:S(2)}) collective-permute-start(bf16[64,3584]{1,0:T(8,128)(2,1)} %get-tuple-element.126), channel_id=1, source_target_pairs={{0,16},{2,18},{4,20},{6,22},{8,24},{10,26},{12,28},{14,30},{16,0},... | collective-permute-start | bytes 1376264 | tf_op jit(solution)/shard_map/ppermute | solution.py:1418
  66.8 20.0 %collective-permute-start.11 = (bf16[64,2560]{1,0:T(8,128)(2,1)}, bf16[64,2560]{1,0:T(8,128)(2,1)}, u32[]{:S(2)}, u32[]{:S(2)}) collective-permute-start(bf16[64,2560]{1,0:T(8,128)(2,1)} %get-tuple-element.125), channel_id=1, source_target_pairs={{0,8},{2,10},{4,12},{6,14},{8,0},{10,2},{12,4},{14,6},{16,24},{18,... | collective-permute-start | bytes 983048 | tf_op jit(solution)/shard_map/ppermute | solution.py:1418
  83.9 11.0 %collective-permute-start.10 = (bf16[4,192,256]{2,1,0:T(8,128)(2,1)S(1)}, bf16[4,192,256]{2,1,0:T(8,128)(2,1)}, u32[]{:S(2)}, u32[]{:S(2)}) collective-permute-start(bf16[4,192,256]{2,1,0:T(8,128)(2,1)S(1)} %fusion.1), channel_id=1, source_target_pairs={{0,2},{2,0},{4,6},{6,4},{8,10},{10,8},{12,14},{14,12},{16,18},{18,... | collective-permute-start | bytes 1179656 | tf_op jit(solution)/shard_map/ppermute | solution.py:1418
  85.4 10.6 %collective-permute-start.9 = (bf16[4,192,256]{2,1,0:T(8,128)(2,1)S(1)}, bf16[4,192,256]{2,1,0:T(8,128)(2,1)S(1)}, u32[]{:S(2)}, u32[]{:S(2)}) collective-permute-start(bf16[4,192,256]{2,1,0:T(8,128)(2,1)S(1)} %add_convert_fusion.1), channel_id=1, source_target_pairs={{0,4},{2,6},{4,0},{6,2},{8,12},{10,14},{12,8},{14,10},{16,20},{18,... | collective-permute-start | bytes 1179656 | tf_op jit(solution)/shard_map/ppermute | solution.py:1418
  89.9 14.1 %collective-permute-start.14 = (bf16[64,2560]{1,0:T(8,128)(2,1)S(1)}, bf16[64,2560]{1,0:T(8,128)(2,1)}, u32[]{:S(2)}, u32[]{:S(2)}) collective-permute-start(bf16[64,2560]{1,0:T(8,128)(2,1)S(1)} %slice.30), channel_id=1, source_target_pairs={{0,8},{2,10},{4,12},{6,14},{8,0},{10,2},{12,4},{14,6},{16,24},{18,... | collective-permute-start | bytes 983048 | tf_op jit(solution)/shard_map/ppermute | solution.py:1418
  89.9 11.4 %collective-permute-start.13 = (bf16[80,1152]{1,0:T(8,128)(2,1)}, bf16[80,1152]{1,0:T(8,128)(2,1)}, u32[]{:S(2)}, u32[]{:S(2)}) collective-permute-start(bf16[80,1152]{1,0:T(8,128)(2,1)} %fusion.4), channel_id=1, source_target_pairs={{0,16},{2,18},{4,20},{6,22},{8,24},{10,26},{12,28},{14,30},{16,0},... | collective-permute-start | bytes 552968 | tf_op jit(solution)/shard_map/ppermute | solution.py:1418
  93.6 14.8 %collective-permute-start.17 = (bf16[64,3584]{1,0:T(8,128)(2,1)}, bf16[64,3584]{1,0:T(8,128)(2,1)}, u32[]{:S(2)}, u32[]{:S(2)}) collective-permute-start(bf16[64,3584]{1,0:T(8,128)(2,1)} %collective-permute-done.12.high_ref), channel_id=1, source_target_pairs={{0,1},{1,0},{2,3},{3,2},{4,5},{5,4},{6,7},{7,6},{8,9},{9,8},{10,11... | collective-permute-start | bytes 1376264 | tf_op jit(solution)/shard_map/ppermute | solution.py:30
  94.9 12.0 %collective-permute-start.16 = (bf16[64,2560]{1,0:T(8,128)(2,1)}, bf16[64,2560]{1,0:T(8,128)(2,1)}, u32[]{:S(2)}, u32[]{:S(2)}) collective-permute-start(bf16[64,2560]{1,0:T(8,128)(2,1)} %collective-permute-done.11.low_ref), channel_id=1, source_target_pairs={{0,1},{1,0},{2,3},{3,2},{4,5},{5,4},{6,7},{7,6},{8,9},{9,8},{10,11... | collective-permute-start | bytes 983048 | tf_op jit(solution)/shard_map/ppermute | solution.py:30
  99.3 14.0 %collective-permute-start.15 = (bf16[2,384,256]{2,1,0:T(8,128)(2,1)}, bf16[2,384,256]{2,1,0:T(8,128)(2,1)S(1)}, u32[]{:S(2)}, u32[]{:S(2)}) collective-permute-start(bf16[2,384,256]{2,1,0:T(8,128)(2,1)} %get-tuple-element.123), channel_id=1, source_target_pairs={{0,8},{2,10},{4,12},{6,14},{8,0},{10,2},{12,4},{14,6},{16,24},{18,... | collective-permute-start | bytes 1179656 | tf_op jit(solution)/shard_map/ppermute | solution.py:1418
  105.1 13.2 %collective-permute-start.19 = (bf16[80,1152]{1,0:T(8,128)(2,1)S(1)}, bf16[80,1152]{1,0:T(8,128)(2,1)S(1)}, u32[]{:S(2)}, u32[]{:S(2)}) collective-permute-start(bf16[80,1152]{1,0:T(8,128)(2,1)S(1)} %add_convert_fusion.2.sum_ref), channel_id=1, source_target_pairs={{0,2},{2,0},{4,6},{6,4},{8,10},{10,8},{12,14},{14,12},{16,18},{18,... | collective-permute-start | bytes 552968 | tf_op jit(solution)/shard_map/ppermute | solution.py:1418
  106.8 11.4 %collective-permute-start.20 = (bf16[80,1152]{1,0:T(8,128)(2,1)S(1)}, bf16[80,1152]{1,0:T(8,128)(2,1)S(1)}, u32[]{:S(2)}, u32[]{:S(2)}) collective-permute-start(bf16[80,1152]{1,0:T(8,128)(2,1)S(1)} %add_convert_fusion.2.sum_ref), channel_id=1, source_target_pairs={{0,4},{2,6},{4,0},{6,2},{8,12},{10,14},{12,8},{14,10},{16,20},{18,... | collective-permute-start | bytes 552968 | tf_op jit(solution)/shard_map/ppermute | solution.py:1418
  108.4 9.9 %collective-permute-start.21 = (bf16[80,1152]{1,0:T(8,128)(2,1)S(1)}, bf16[80,1152]{1,0:T(8,128)(2,1)}, u32[]{:S(2)}, u32[]{:S(2)}) collective-permute-start(bf16[80,1152]{1,0:T(8,128)(2,1)S(1)} %add_convert_fusion.2.sum_ref), channel_id=1, source_target_pairs={{0,6},{2,4},{4,2},{6,0},{8,14},{10,12},{12,10},{14,8},{16,22},{18,... | collective-permute-start | bytes 552968 | tf_op jit(solution)/shard_map/ppermute | solution.py:1418
  113.3 12.8 %collective-permute-start.23 = (bf16[416,256]{1,0:T(8,128)(2,1)}, bf16[416,256]{1,0:T(8,128)(2,1)}, u32[]{:S(2)}, u32[]{:S(2)}) collective-permute-start(bf16[416,256]{1,0:T(8,128)(2,1)} %get-tuple-element.149), channel_id=1, source_target_pairs={{0,2},{2,0},{4,6},{6,4},{8,10},{10,8},{12,14},{14,12},{16,18},{18,... | collective-permute-start | bytes 638984 | tf_op jit(solution)/shard_map/ppermute | solution.py:1418
  115.0 11.1 %collective-permute-start.24 = (bf16[384,256]{1,0:T(8,128)(2,1)}, bf16[384,256]{1,0:T(8,128)(2,1)}, u32[]{:S(2)}, u32[]{:S(2)}) collective-permute-start(bf16[384,256]{1,0:T(8,128)(2,1)} %get-tuple-element.150), channel_id=1, source_target_pairs={{0,4},{2,6},{4,0},{6,2},{8,12},{10,14},{12,8},{14,10},{16,20},{18,... | collective-permute-start | bytes 589832 | tf_op jit(solution)/shard_map/ppermute | solution.py:1418
  118.3 13.2 %collective-permute-start.22 = (bf16[384,256]{1,0:T(8,128)(2,1)}, bf16[384,256]{1,0:T(8,128)(2,1)}, u32[]{:S(2)}, u32[]{:S(2)}) collective-permute-start(bf16[384,256]{1,0:T(8,128)(2,1)} %fusion.3), channel_id=1, source_target_pairs={{0,16},{2,18},{4,20},{6,22},{8,24},{10,26},{12,28},{14,30},{16,0},... | collective-permute-start | bytes 589832 | tf_op jit(solution)/shard_map/ppermute | solution.py:1418
  119.5 18.0 %collective-permute-start.25 = (bf16[416,256]{1,0:T(8,128)(2,1)}, bf16[416,256]{1,0:T(8,128)(2,1)}, u32[]{:S(2)}, u32[]{:S(2)}) collective-permute-start(bf16[416,256]{1,0:T(8,128)(2,1)} %get-tuple-element.159), channel_id=1, source_target_pairs={{0,2},{2,0},{4,6},{6,4},{8,10},{10,8},{12,14},{14,12},{16,18},{18,... | collective-permute-start | bytes 638984 | tf_op jit(solution)/shard_map/ppermute | solution.py:1418
  (23 other events, 129.4 us)

commit v5 on v4

--- a/solution.py
+++ b/solution.py
@@ -424,7 +424,7 @@
 def branch_call(own, other, w_own, w_other, latents, gain_out, routes, slots, slot_count):
     width = w_own.shape[1]
     rows, heads = own.shape
-    parts = 4
+    parts = 2
     return pl.pallas_call(
         functools.partial(branch_kernel, slot_count),
         name="branch_norm",
@@ -697,7 +697,7 @@
         lax.broadcasted_iota(jnp.int32, (rows, slots), 1) == place, 1.0, 0.0
     ).astype(BF16)
     total = jnp.zeros((rows, 1), F32)
-    chunk = 512
+    chunk = 1024
     for copy in copies[:3]:
         copy.wait()
     for copy in copies[4:]:
@@ -710,14 +710,14 @@
             )
             product = d_final * hat_ref[:, at].astype(F32)
             total = total + jnp.sum(product * gain_ref[:, at], axis=-1, keepdims=True)
-            d_final_ref[:, at] = d_final
+            d_final_ref[:, at] = d_final.astype(BF16)
     total = total / width
     lat_ref[latent_rows:, :] = jnp.zeros_like(lat_ref[latent_rows:, :])
     highs, lows = [], []
     part = width // 4
     for c in range(width // chunk):
         at = slice(c * chunk, (c + 1) * chunk)
-        d_final = d_final_ref[:, at]
+        d_final = d_final_ref[:, at].astype(F32)
         hat = hat_ref[:, at].astype(F32)
         term = jnp.sum(d_final * hat, axis=0, keepdims=True)
         high = term.astype(BF16).astype(F32)
@@ -852,7 +852,7 @@
             out_specs=[pl.BlockSpec(memory_space=pl.ANY)] * len(out),
             scratch_shapes=[pltpu.VMEM(a.shape, a.dtype) for a in (*small, *large)]
             + [
-                pltpu.VMEM((rows, width), F32),
+                pltpu.VMEM((rows, width), BF16),
                 pltpu.VMEM((rows, width), BF16),
                 pltpu.VMEM((2 * key_width, patch_rows), BF16),
             ]
@@ -1011,6 +1011,7 @@
     upper = (where_ref[0] >> 1) & 1
     share = own // 2
     cut = heads // 2
+    extra = latent_rows // 4
     for turn in range(4):
         x_differs, y_differs = 1 - (turn & 1), 1 - (turn >> 1)
         owner = 2 * (upper ^ y_differs) + (odd ^ x_differs)
@@ -1022,19 +1023,19 @@
         ends = 1 - y_differs
         ref = (first_onward_ref, first_last_ref)[ends] if x_differs else first_kept_ref.at[ends]
         ref[:cut, :] = grad[:cut]
-        ref[cut:, :] = part.astype(BF16)
+        ref[cut:, :] = part[:extra].astype(BF16)
         ends = 1 - x_differs
         ref = (second_onward_ref, second_last_ref)[ends] if y_differs else second_kept_ref.at[ends]
-        ref[...] = grad[cut:]
+        ref[:cut, :] = grad[cut:]
+        ref[cut:, :] = part[extra:].astype(BF16)
 
 
 def out_call(where, attn, line, received, others):
     rows, heads = attn.shape
     columns = line.shape[1]
     own = columns // 4
-    first = (heads // 2 + rows // 4, own)
-    second = (heads // 2, own)
-    shapes = [first, first, (2, *first), second, second, (2, *second)]
+    block = (heads // 2 + rows // 8, own)
+    shapes = [block, block, (2, *block)] * 2
     operands = (attn, line, *received, *others)
     return pl.pallas_call(
         out_kernel,
@@ -1328,14 +1329,16 @@
     latent_rows, width = lat_ref.shape
     share = own // 2
     cut = heads // 2
-    first = sum(
-        part.astype(F32) for part in (first_kept_ref[0], first_got_ref[...], first_last_ref[...])
+    first, second = (
+        sum(part.astype(F32) for part in parts)
+        for parts in (
+            (first_kept_ref[0], first_got_ref[...], first_last_ref[...]),
+            (second_kept_ref[0], second_got_ref[...], second_last_ref[...]),
+        )
     )
     out_ref[:cut, :] = first[:cut]
-    out_ref[cut:, :] = sum(
-        part.astype(F32) for part in (second_kept_ref[0], second_got_ref[...], second_last_ref[...])
-    )
-    resid = first[cut:]
+    out_ref[cut:, :] = second[:cut]
+    resid = jnp.concatenate([first[cut:], second[cut:]], axis=0)
     resid = jnp.concatenate([resid[:, :share], resid[:, share:]], axis=0)
     mine = pl.ds(pl.multiple_of(where_ref[1] * share, share), share)
     d_lat = message_ref[:, mine] + message_got_ref[:, mine]
@@ -1352,7 +1355,7 @@
 def out_final_call(where, parts, message, message_got, term, term_got, latents, gain_lat):
     _, rows, own = parts[0].shape
     latent_rows, width = latents.shape
-    heads = 2 * (rows - latent_rows // 2)
+    heads = 2 * (rows - latent_rows // 4)
     shapes = [(heads, own), (latent_rows, own // 2), (1, own // 2), (1, own // 2)]
     return pl.pallas_call(
         out_final_kernel,
@@ -1544,8 +1547,10 @@
     grad_w_query, pair_lat, message, grad_gain_out, routed = latent_call(
         where, lat_sum, lat_parts, lat_proj, latents, gain_lat, w_query, wk, wv, own_width, routed
     )
-    first_onward, second_onward, message, pair_lat = lax.optimization_barrier(
-        (first_onward, second_onward, message, pair_lat)
+    first_onward, second_onward, first_end, second_end, message, pair_lat = (
+        lax.optimization_barrier(
+            (first_onward, second_onward, first_end, second_end, message, pair_lat)
+        )
     )
     high, pair_lat = lax.optimization_barrier((high, pair_lat))
     first_last = swap(add_halves(first_kept[0], first_onward).astype(BF16), 2)

time: 143 us -> 142 us (level)
    unnamed x28 -> x30, local copies, waits for them, and re-layouts: 3.53 us -> 3.66 us
  transfers between devices with their start and end apart: 33 -> 33, of which waited for: 11 -> 9; matrix products, arithmetic and copies ran while one was open for 7% -> 8% of each run, Pallas kernels for 46% -> 45%
where the time goes in v5:
time: 142 us; the launch traced here: 141 us
  Pallas kernels  67.6 us (48%)
  starting transfers between devices  43.6 us (31%)
  waiting for transfers between devices  14.5 us (10%)
  other arithmetic  10 us (7%)
  local copies, waits for them, and re-layouts  4.65 us (3%)
    ppermute x20, starting transfers between devices, swap(): return lax.ppermute(array, 'dp', [(i, i ^ turn) for i in range(dp_count)])  26.6 us
    pallas_call x1, Pallas kernels, backward_call(): pl.pallas_call(functools.partial(backward_kernel, slot_count), name='atte...  15 us
    pallas_call x1, Pallas kernels, forward_call(): pl.pallas_call(forward_kernel, name='forward_attention', in_specs=[pl.Blo...  14.9 us
    all_to_all x2, starting transfers between devices, exchange(): lax.all_to_all(blocks, 'dp', split_axis=0, concat_axis=0, tiled=True)  14.7 us
    ppermute x20, waiting for transfers between devices, swap(): return lax.ppermute(array, 'dp', [(i, i ^ turn) for i in range(dp_count)])  13 us
    pallas_call x1, Pallas kernels, patch_call(): pl.pallas_call(functools.partial(patch_kernel, width), name='patch_gradie...  10.2 us
    pallas_call x1, Pallas kernels, branch_call(): pl.pallas_call(functools.partial(branch_kernel, slot_count), name='branch...  7.96 us
    pallas_call x1, Pallas kernels, latent_call(): pl.pallas_call(latent_kernel, name='latent_gradients', grid_spec=pltpu.Pr...  5.65 us
  transfers between devices with their start and end apart: 33, of which 9 were waited for; matrix products, arithmetic and copies ran while one was open for 8% of the time, Pallas kernels for 45%

profile of v5, /device:TPU:0, one launch (start us, length us, event | category | flops | bytes accessed | tf_op | source)
XLA Modules:
  0.0 141.2 jit_solution(8858052268120378350)
XLA Ops:
  1.2 7.9 %all-to-all-start = ((bf16[16,16,2048]{2,1,0:T(8,128)(2,1)}), bf16[16,16,2048]{2,1,0:T(8,128)(2,1)}, u32[]{:S(2)}, u32[]{:S(2)}) async-start(bf16[16,16,2048]{2,1,0:T(8,128)(2,1)} %bitcast.42), calls=%async_computation | async-start | bytes 2097152 | tf_op jit(solution)/shard_map/all_to_all | solution.py:1425
  9.7 14.9 %forward_attention.1 = (bf16[128,768]{1,0:T(8,128)(2,1)}, bf16[2,1024,128]{2,1,0:T(8,128)(2,1)}, bf16[2,1024,128]{2,1,0:T(8,128)(2,1)}, f32[8,1024]{1,0:T(8,128)...) custom-call(s32[1,2]{1,0:T(1,128)} %counts_ref.3, ...), custom_call_target="tpu_custom_call" | custom-call | flops 5000000000 | bytes 24000000 | tf_op jit(solution)/shard_map/forward_attention/pallas_call | solution.py:285
  27.1 8.0 %branch_norm.1 = (bf16[128,4096]{1,0:T(8,128)(2,1)}, f32[128,1]{1,0:T(8,128)}, bf16[256,2048]{1,0:T(8,128)(2,1)}) custom-call(bf16[128,768]{1,0:T(8,128)(2,1)} %get-tuple-element.95.own_hbm.attn_hbm.attn_own_ref, bf16[128,768]{1,0:T(8,128)(2,1)} %copy-done.10, bf16[64,4096]{1,0:T(8,128)(2,1)} %lat_ref.3, f32[1,4096]{1,0:T(1,128)} %bitcast.50, ...), custom_call_target="tpu_custom_call" | custom-call | flops 1610612736 | bytes 16000000 | tf_op jit(solution)/shard_map/branch_norm/pallas_call | solution.py:428
  35.3 6.8 %all-to-all-start.1 = ((bf16[16,16,2048]{2,1,0:T(8,128)(2,1)}), bf16[16,16,2048]{2,1,0:T(8,128)(2,1)}, u32[]{:S(2)}, u32[]{:S(2)}) async-start(bf16[16,16,2048]{2,1,0:T(8,128)(2,1)} %bitcast.43), calls=%async_computation.1 | async-start | bytes 2097152 | tf_op jit(solution)/shard_map/all_to_all | solution.py:1425
  42.1 15.0 %attention_backward.1 = (bf16[128,1024]{1,0:T(8,128)(2,1)}, bf16[64,3584]{1,0:T(8,128)(2,1)}, bf16[400,1024]{1,0:T(8,128)(2,1)}, bf16[64,2560]{1,0:T(8,128)(2,1)...) custom-call(s32[1,2]{1,0:T(1,128)} %counts_ref.3, ...), custom_call_target="tpu_custom_call" | custom-call | flops 5000000000 | bytes 26000000 | tf_op jit(solution)/shard_map/attention_backward/pallas_call | solution.py:844
  57.2 1.9 %collective-permute-start.7 = (bf16[8,192,256]{2,1,0:T(8,128)(2,1)}, bf16[8,192,256]{2,1,0:T(8,128)(2,1)}, u32[]{:S(2)}, u32[]{:S(2)}) collective-permute-start(bf16[8,192,256]{2,1,0:T(8,128)(2,1)} %get-tuple-element.118), channel_id=1, source_target_pairs={{0,2},{2,0},{4,6},{6,4},{8,10},{10,8},{12,14},{14,12},{16,18},{18,... | collective-permute-start | bytes 2359304 | tf_op jit(solution)/shard_map/ppermute | solution.py:1421
  63.6 2.4 %collective-permute-start.12 = (bf16[64,3584]{1,0:T(8,128)(2,1)}, bf16[64,3584]{1,0:T(8,128)(2,1)}, u32[]{:S(2)}, u32[]{:S(2)}) collective-permute-start(bf16[64,3584]{1,0:T(8,128)(2,1)} %get-tuple-element.128), channel_id=1, source_target_pairs={{0,16},{2,18},{4,20},{6,22},{8,24},{10,26},{12,28},{14,30},{16,0},... | collective-permute-start | bytes 1376264 | tf_op jit(solution)/shard_map/ppermute | solution.py:1421
  66.5 10.2 %patch_gradient.1 = bf16[1024,2048]{1,0:T(8,128)(2,1)} custom-call(s32[2]{0:T(128)} %pad_add_fusion.where_ref, bf16[400,1024]{1,0:T(8,128)(2,1)} %get-tuple-element.111.own_ref, bf16[400,1024]{1,0:T(8,128)(2,1)} %copy-done.5, bf16[192,4096]{1,0:T(8,128)(2,1)} %bitcast.32, bf16[192,4096]{1,0:T(8,128)(2,1)} %bitcast.37, ...), custom_call_target="tpu_custom_call" | custom-call | flops 3300000000 | bytes 14000000 | tf_op jit(solution)/shard_map/patch_gradient/pallas_call | solution.py:931
  76.7 1.6 %fusion.4 = bf16[80,1152]{1,0:T(8,128)(2,1)} fusion(bf16[80,1152]{1,0:T(8,128)(2,1)} %collective-permute-done.6, bf16[80,1152]{1,0:T(8,128)(2,1)S(1)} %copy-done.6), kind=kLoop, calls=%fused_computation.11 | loop fusion | flops 368640 | bytes 552960 | tf_op jit(solution)/shard_map/convert_element_type | solution.py:1503
  78.4 2.0 %collective-permute-done.7.value_got_ref = bf16[8,192,256]{2,1,0:T(8,128)(2,1)} collective-permute-done((bf16[8,192,256]{2,1,0:T(8,128)(2,1)}, bf16[8,192,256]{2,1,0:T(8,128)(2,1)}, u32[]{:S(2)}, u32[]{:S(2)}) %collective-permute-start.7) | collective-permute-done | bytes 786464 | tf_op jit(solution)/shard_map/ppermute | solution.py:1421
  85.9 2.1 %collective-permute-done.12.high_ref = bf16[64,3584]{1,0:T(8,128)(2,1)} collective-permute-done((bf16[64,3584]{1,0:T(8,128)(2,1)}, bf16[64,3584]{1,0:T(8,128)(2,1)}, u32[]{:S(2)}, u32[]{:S(2)}) %collective-permute-start.12) | collective-permute-done | bytes 458784 | tf_op jit(solution)/shard_map/ppermute | solution.py:1421
  89.1 3.6 %collective-permute-start.13 = (bf16[80,1152]{1,0:T(8,128)(2,1)}, bf16[80,1152]{1,0:T(8,128)(2,1)}, u32[]{:S(2)}, u32[]{:S(2)}) collective-permute-start(bf16[80,1152]{1,0:T(8,128)(2,1)} %fusion.4), channel_id=1, source_target_pairs={{0,16},{2,18},{4,20},{6,22},{8,24},{10,26},{12,28},{14,30},{16,0},... | collective-permute-start | bytes 552968 | tf_op jit(solution)/shard_map/ppermute | solution.py:1421
  95.8 2.6 %plane_sum.1 = (bf16[2,384,256]{2,1,0:T(8,128)(2,1)}, f32[384,256]{1,0:T(8,128)}) custom-call(bf16[8,192,256]{2,1,0:T(8,128)(2,1)} %get-tuple-element.117.value_ref, bf16[8,192,256]{2,1,0:T(8,128)(2,1)} %collective-permute-done.7.value_got_ref, bf16[4,192,256]{2,1,0:T(8,128)(2,1)} %copy-done.1, bf16[8,192,256]{2,1,0:T(8,128)(2,1)} %bitcast.40, ...), custom_call_target="tpu_custom_call" | custom-call | flops 1000000 | bytes 3000000 | tf_op jit(solution)/shard_map/plane_sum/pallas_call | solution.py:1219
  100.5 2.7 %collective-permute-done.14.forwarded_ref = bf16[64,2560]{1,0:T(8,128)(2,1)} collective-permute-done((bf16[64,2560]{1,0:T(8,128)(2,1)S(1)}, bf16[64,2560]{1,0:T(8,128)(2,1)}, u32[]{:S(2)}, u32[]{:S(2)}) %collective-permute-start.14) | collective-permute-done | bytes 327712 | tf_op jit(solution)/shard_map/ppermute | solution.py:1421
  104.3 1.7 %collective-permute-start.19 = (bf16[80,1152]{1,0:T(8,128)(2,1)S(1)}, bf16[80,1152]{1,0:T(8,128)(2,1)S(1)}, u32[]{:S(2)}, u32[]{:S(2)}) collective-permute-start(bf16[80,1152]{1,0:T(8,128)(2,1)S(1)} %add_convert_fusion.2.sum_ref), channel_id=1, source_target_pairs={{0,2},{2,0},{4,6},{6,4},{8,10},{10,8},{12,14},{14,12},{16,18},{18,... | collective-permute-start | bytes 552968 | tf_op jit(solution)/shard_map/ppermute | solution.py:1421
  107.9 4.7 %output_projection_gradient.1 = (bf16[400,256]{1,0:T(8,128)(2,1)}, bf16[400,256]{1,0:T(8,128)(2,1)}, bf16[2,400,256]{2,1,0:T(8,128)(2,1)}, bf16[400,256]{1,0:T(8...) custom-call(s32[2]{0:T(128)} %pad_add_fusion.where_ref, ...), custom_call_target="tpu_custom_call" | custom-call | flops 805306368 | bytes 4000000 | tf_op jit(solution)/shard_map/output_projection_gradient/pallas_call | solution.py:1040
  112.6 1.7 %collective-permute-start.23 = (bf16[400,256]{1,0:T(8,128)(2,1)}, bf16[400,256]{1,0:T(8,128)(2,1)}, u32[]{:S(2)}, u32[]{:S(2)}) collective-permute-start(bf16[400,256]{1,0:T(8,128)(2,1)} %get-tuple-element.151), channel_id=1, source_target_pairs={{0,2},{2,0},{4,6},{6,4},{8,10},{10,8},{12,14},{14,12},{16,18},{18,... | collective-permute-start | bytes 614408 | tf_op jit(solution)/shard_map/ppermute | solution.py:1421
  116.7 1.7 %collective-permute-start.26 = (bf16[400,256]{1,0:T(8,128)(2,1)}, bf16[400,256]{1,0:T(8,128)(2,1)}, u32[]{:S(2)}, u32[]{:S(2)}) collective-permute-start(bf16[400,256]{1,0:T(8,128)(2,1)} %get-tuple-element.154), channel_id=1, source_target_pairs={{0,4},{2,6},{4,0},{6,2},{8,12},{10,14},{12,8},{14,10},{16,20},{18,... | collective-permute-start | bytes 614408 | tf_op jit(solution)/shard_map/ppermute | solution.py:1421
  118.4 1.7 %fusion.3 = bf16[384,256]{1,0:T(8,128)(2,1)} fusion(f32[384,256]{1,0:T(8,128)} %get-tuple-element.133, bf16[2,384,256]{2,1,0:T(8,128)(2,1)S(1)} %collective-permute-done.15.low_ref), kind=kLoop, calls=%fused_computation.8 | loop fusion | flops 294912 | bytes 786432 | tf_op jit(solution)/shard_map/convert_element_type | solution.py:1539
  121.4 5.6 %latent_gradients.1 = (f32[256,768]{1,0:T(8,128)}, f32[384,256]{1,0:T(8,128)}, f32[72,384]{1,0:T(8,128)}, f32[1,128]{1,0:T(1,128)}, bf16[256,2048]{1,0:T(8,128)(2,1)}) custom-call(s32[2]{0:T(128)} %pad_add_fusion.where_ref, bf16[80,1152]{1,0:T(8,128)(2,1)} %copy-done.7, bf16[80,1152]{1,0:T(8,128)(2,1)} %copy-done.11, bf16[80,1152]{1,0:T(8,128)(2,1)} %copy-done.12, ...), custom_call_target="tpu_custom_call" | custom-call | flops 100000000 | bytes 3000000 | tf_op jit(solution)/shard_map/latent_gradients/pallas_call | solution.py:1148
  127.1 1.7 %fusion = bf16[400,256]{1,0:T(8,128)(2,1)} fusion(bf16[400,256]{1,0:T(8,128)(2,1)} %collective-permute-done.24, bf16[2,400,256]{2,1,0:T(8,128)(2,1)S(1)} %copy-done.3), kind=kLoop, calls=%fused_computation.3 | loop fusion | flops 409600 | bytes 614400 | tf_op jit(solution)/shard_map/convert_element_type | solution.py:1557
  131.3 3.0 %key_value_gradients.1 = (f32[192,256]{1,0:T(8,128)}, f32[192,256]{1,0:T(8,128)}, f32[8,256]{1,0:T(8,128)}) custom-call(s32[2]{0:T(128)} %pad_add_fusion.where_ref, bf16[8,192,256]{2,1,0:T(8,128)(2,1)} %get-tuple-element.117.value_ref, bf16[8,192,256]{2,1,0:T(8,128)(2,1)} %collective-permute-done.7.value_got_ref, bf16[4,192,256]{2,1,0:T(8,128)(2,1)} %copy-done.1, ...), custom_call_target="tpu_custom_call" | custom-call | flops 1000000 | bytes 3000000 | tf_op jit(solution)/shard_map/key_value_gradients/pallas_call | solution.py:1275
  134.8 1.5 %collective-permute-done.27.first_last_ref = bf16[400,256]{1,0:T(8,128)(2,1)S(1)} collective-permute-done((bf16[400,256]{1,0:T(8,128)(2,1)S(1)}, bf16[400,256]{1,0:T(8,128)(2,1)S(1)}, u32[]{:S(2)}, u32[]{:S(2)}) %collective-permute-start.27) | collective-permute-done | bytes 204832 | tf_op jit(solution)/shard_map/ppermute | solution.py:1421
  137.7 3.5 %output_gradient_sum.1 = (f32[768,256]{1,0:T(8,128)}, f32[64,128]{1,0:T(8,128)}, f32[1,128]{1,0:T(1,128)}, f32[1,128]{1,0:T(1,128)}) custom-call(s32[2]{0:T(128)} %pad_add_fusion.where_ref, bf16[2,400,256]{2,1,0:T(8,128)(2,1)} %get-tuple-element.162.first_kept_ref, bf16[400,256]{1,0:T(8,128)(2,1)} %collective-permute-done.25.first_got_ref, ...), custom_call_target="tpu_custom_call" | custom-call | flops 1000000 | bytes 3000000 | tf_op jit(solution)/shard_map/output_gradient_sum/pallas_call | solution.py:1360
  (90 shorter events, 31.7 us)
Async XLA Ops:
  0.6 25.7 %collective-permute-start.3 = (bf16[768,4096]{1,0:T(8,128)(2,1)}, bf16[768,4096]{1,0:T(8,128)(2,1)}, u32[]{:S(2)}, u32[]{:S(2)}) collective-permute-start(bf16[768,4096]{1,0:T(8,128)(2,1)} %w_out_hbm.1), channel_id=1, source_target_pairs={{0,1},{1,0},{2,3},{3,2},{4,5},{5,4},{6,7},{7,6},{8,9},{9,8},{10,11... | collective-permute-start | bytes 18874376 | tf_op jit(solution)/shard_map/ppermute | solution.py:30
  1.2 33.9 %all-to-all-start = ((bf16[16,16,2048]{2,1,0:T(8,128)(2,1)}), bf16[16,16,2048]{2,1,0:T(8,128)(2,1)}, u32[]{:S(2)}, u32[]{:S(2)}) async-start(bf16[16,16,2048]{2,1,0:T(8,128)(2,1)} %bitcast.42), calls=%async_computation | async-start | bytes 2097152 | tf_op jit(solution)/shard_map/all_to_all | solution.py:1425
  9.1 15.5 %collective-permute-start = (bf16[192,4096]{1,0:T(8,128)(2,1)}, bf16[192,4096]{1,0:T(8,128)(2,1)}, u32[]{:S(2)}, u32[]{:S(2)}) collective-permute-start(bf16[192,4096]{1,0:T(8,128)(2,1)} %bitcast.30), channel_id=1, source_target_pairs={{0,1},{1,0},{2,3},{3,2},{4,5},{5,4},{6,7},{7,6},{8,9},{9,8},{10,11... | collective-permute-start | bytes 4718600 | tf_op jit(solution)/shard_map/ppermute | solution.py:30
  9.4 15.3 %collective-permute-start.1 = (bf16[192,4096]{1,0:T(8,128)(2,1)}, bf16[192,4096]{1,0:T(8,128)(2,1)}, u32[]{:S(2)}, u32[]{:S(2)}) collective-permute-start(bf16[192,4096]{1,0:T(8,128)(2,1)} %bitcast.35), channel_id=1, source_target_pairs={{0,1},{1,0},{2,3},{3,2},{4,5},{5,4},{6,7},{7,6},{8,9},{9,8},{10,11... | collective-permute-start | bytes 4718600 | tf_op jit(solution)/shard_map/ppermute | solution.py:30
  35.3 46.5 %all-to-all-start.1 = ((bf16[16,16,2048]{2,1,0:T(8,128)(2,1)}), bf16[16,16,2048]{2,1,0:T(8,128)(2,1)}, u32[]{:S(2)}, u32[]{:S(2)}) async-start(bf16[16,16,2048]{2,1,0:T(8,128)(2,1)} %bitcast.43), calls=%async_computation.1 | async-start | bytes 2097152 | tf_op jit(solution)/shard_map/all_to_all | solution.py:1425
  57.2 23.1 %collective-permute-start.7 = (bf16[8,192,256]{2,1,0:T(8,128)(2,1)}, bf16[8,192,256]{2,1,0:T(8,128)(2,1)}, u32[]{:S(2)}, u32[]{:S(2)}) collective-permute-start(bf16[8,192,256]{2,1,0:T(8,128)(2,1)} %get-tuple-element.118), channel_id=1, source_target_pairs={{0,2},{2,0},{4,6},{6,4},{8,10},{10,8},{12,14},{14,12},{16,18},{18,... | collective-permute-start | bytes 2359304 | tf_op jit(solution)/shard_map/ppermute | solution.py:1421
  59.1 22.7 %collective-permute-start.8 = (bf16[2,4,192,256]{3,2,1,0:T(8,128)(2,1)}, bf16[2,4,192,256]{3,2,1,0:T(8,128)(2,1)}, u32[]{:S(2)}, u32[]{:S(2)}) collective-permute-start(bf16[2,4,192,256]{3,2,1,0:T(8,128)(2,1)} %get-tuple-element.119), channel_id=1, source_target_pairs={{0,4},{2,6},{4,0},{6,2},{8,12},{10,14},{12,8},{14,10},{16,20},{18,... | collective-permute-start | bytes 2359304 | tf_op jit(solution)/shard_map/ppermute | solution.py:1421
  62.1 14.6 %collective-permute-start.6 = (bf16[80,1152]{1,0:T(8,128)(2,1)}, bf16[80,1152]{1,0:T(8,128)(2,1)}, u32[]{:S(2)}, u32[]{:S(2)}) collective-permute-start(bf16[80,1152]{1,0:T(8,128)(2,1)} %get-tuple-element.112), channel_id=1, source_target_pairs={{0,8},{2,10},{4,12},{6,14},{8,0},{10,2},{12,4},{14,6},{16,24},{18,... | collective-permute-start | bytes 552968 | tf_op jit(solution)/shard_map/ppermute | solution.py:1421
  63.6 24.5 %collective-permute-start.12 = (bf16[64,3584]{1,0:T(8,128)(2,1)}, bf16[64,3584]{1,0:T(8,128)(2,1)}, u32[]{:S(2)}, u32[]{:S(2)}) collective-permute-start(bf16[64,3584]{1,0:T(8,128)(2,1)} %get-tuple-element.128), channel_id=1, source_target_pairs={{0,16},{2,18},{4,20},{6,22},{8,24},{10,26},{12,28},{14,30},{16,0},... | collective-permute-start | bytes 1376264 | tf_op jit(solution)/shard_map/ppermute | solution.py:1421
  66.0 20.0 %collective-permute-start.11 = (bf16[64,2560]{1,0:T(8,128)(2,1)}, bf16[64,2560]{1,0:T(8,128)(2,1)}, u32[]{:S(2)}, u32[]{:S(2)}) collective-permute-start(bf16[64,2560]{1,0:T(8,128)(2,1)} %get-tuple-element.127), channel_id=1, source_target_pairs={{0,8},{2,10},{4,12},{6,14},{8,0},{10,2},{12,4},{14,6},{16,24},{18,... | collective-permute-start | bytes 983048 | tf_op jit(solution)/shard_map/ppermute | solution.py:1421
  83.1 10.9 %collective-permute-start.10 = (bf16[4,192,256]{2,1,0:T(8,128)(2,1)S(1)}, bf16[4,192,256]{2,1,0:T(8,128)(2,1)}, u32[]{:S(2)}, u32[]{:S(2)}) collective-permute-start(bf16[4,192,256]{2,1,0:T(8,128)(2,1)S(1)} %fusion.2), channel_id=1, source_target_pairs={{0,2},{2,0},{4,6},{6,4},{8,10},{10,8},{12,14},{14,12},{16,18},{18,... | collective-permute-start | bytes 1179656 | tf_op jit(solution)/shard_map/ppermute | solution.py:1421
  84.5 10.6 %collective-permute-start.9 = (bf16[4,192,256]{2,1,0:T(8,128)(2,1)S(1)}, bf16[4,192,256]{2,1,0:T(8,128)(2,1)S(1)}, u32[]{:S(2)}, u32[]{:S(2)}) collective-permute-start(bf16[4,192,256]{2,1,0:T(8,128)(2,1)S(1)} %add_convert_fusion.1), channel_id=1, source_target_pairs={{0,4},{2,6},{4,0},{6,2},{8,12},{10,14},{12,8},{14,10},{16,20},{18,... | collective-permute-start | bytes 1179656 | tf_op jit(solution)/shard_map/ppermute | solution.py:1421
  89.1 14.2 %collective-permute-start.14 = (bf16[64,2560]{1,0:T(8,128)(2,1)S(1)}, bf16[64,2560]{1,0:T(8,128)(2,1)}, u32[]{:S(2)}, u32[]{:S(2)}) collective-permute-start(bf16[64,2560]{1,0:T(8,128)(2,1)S(1)} %slice.30), channel_id=1, source_target_pairs={{0,8},{2,10},{4,12},{6,14},{8,0},{10,2},{12,4},{14,6},{16,24},{18,... | collective-permute-start | bytes 983048 | tf_op jit(solution)/shard_map/ppermute | solution.py:1421
  89.1 11.4 %collective-permute-start.13 = (bf16[80,1152]{1,0:T(8,128)(2,1)}, bf16[80,1152]{1,0:T(8,128)(2,1)}, u32[]{:S(2)}, u32[]{:S(2)}) collective-permute-start(bf16[80,1152]{1,0:T(8,128)(2,1)} %fusion.4), channel_id=1, source_target_pairs={{0,16},{2,18},{4,20},{6,22},{8,24},{10,26},{12,28},{14,30},{16,0},... | collective-permute-start | bytes 552968 | tf_op jit(solution)/shard_map/ppermute | solution.py:1421
  92.7 14.8 %collective-permute-start.17 = (bf16[64,3584]{1,0:T(8,128)(2,1)}, bf16[64,3584]{1,0:T(8,128)(2,1)}, u32[]{:S(2)}, u32[]{:S(2)}) collective-permute-start(bf16[64,3584]{1,0:T(8,128)(2,1)} %collective-permute-done.12.high_ref), channel_id=1, source_target_pairs={{0,1},{1,0},{2,3},{3,2},{4,5},{5,4},{6,7},{7,6},{8,9},{9,8},{10,11... | collective-permute-start | bytes 1376264 | tf_op jit(solution)/shard_map/ppermute | solution.py:30
  94.0 12.0 %collective-permute-start.16 = (bf16[64,2560]{1,0:T(8,128)(2,1)}, bf16[64,2560]{1,0:T(8,128)(2,1)}, u32[]{:S(2)}, u32[]{:S(2)}) collective-permute-start(bf16[64,2560]{1,0:T(8,128)(2,1)} %collective-permute-done.11.low_ref), channel_id=1, source_target_pairs={{0,1},{1,0},{2,3},{3,2},{4,5},{5,4},{6,7},{7,6},{8,9},{9,8},{10,11... | collective-permute-start | bytes 983048 | tf_op jit(solution)/shard_map/ppermute | solution.py:30
  98.4 14.2 %collective-permute-start.15 = (bf16[2,384,256]{2,1,0:T(8,128)(2,1)}, bf16[2,384,256]{2,1,0:T(8,128)(2,1)S(1)}, u32[]{:S(2)}, u32[]{:S(2)}) collective-permute-start(bf16[2,384,256]{2,1,0:T(8,128)(2,1)} %get-tuple-element.125), channel_id=1, source_target_pairs={{0,8},{2,10},{4,12},{6,14},{8,0},{10,2},{12,4},{14,6},{16,24},{18,... | collective-permute-start | bytes 1179656 | tf_op jit(solution)/shard_map/ppermute | solution.py:1421
  104.3 11.5 %collective-permute-start.19 = (bf16[80,1152]{1,0:T(8,128)(2,1)S(1)}, bf16[80,1152]{1,0:T(8,128)(2,1)S(1)}, u32[]{:S(2)}, u32[]{:S(2)}) collective-permute-start(bf16[80,1152]{1,0:T(8,128)(2,1)S(1)} %add_convert_fusion.2.sum_ref), channel_id=1, source_target_pairs={{0,2},{2,0},{4,6},{6,4},{8,10},{10,8},{12,14},{14,12},{16,18},{18,... | collective-permute-start | bytes 552968 | tf_op jit(solution)/shard_map/ppermute | solution.py:1421
  106.0 10.7 %collective-permute-start.20 = (bf16[80,1152]{1,0:T(8,128)(2,1)S(1)}, bf16[80,1152]{1,0:T(8,128)(2,1)S(1)}, u32[]{:S(2)}, u32[]{:S(2)}) collective-permute-start(bf16[80,1152]{1,0:T(8,128)(2,1)S(1)} %add_convert_fusion.2.sum_ref), channel_id=1, source_target_pairs={{0,4},{2,6},{4,0},{6,2},{8,12},{10,14},{12,8},{14,10},{16,20},{18,... | collective-permute-start | bytes 552968 | tf_op jit(solution)/shard_map/ppermute | solution.py:1421
  107.5 12.6 %collective-permute-start.21 = (bf16[80,1152]{1,0:T(8,128)(2,1)S(1)}, bf16[80,1152]{1,0:T(8,128)(2,1)}, u32[]{:S(2)}, u32[]{:S(2)}) collective-permute-start(bf16[80,1152]{1,0:T(8,128)(2,1)S(1)} %add_convert_fusion.2.sum_ref), channel_id=1, source_target_pairs={{0,6},{2,4},{4,2},{6,0},{8,14},{10,12},{12,10},{14,8},{16,22},{18,... | collective-permute-start | bytes 552968 | tf_op jit(solution)/shard_map/ppermute | solution.py:1421
  112.6 14.4 %collective-permute-start.23 = (bf16[400,256]{1,0:T(8,128)(2,1)}, bf16[400,256]{1,0:T(8,128)(2,1)}, u32[]{:S(2)}, u32[]{:S(2)}) collective-permute-start(bf16[400,256]{1,0:T(8,128)(2,1)} %get-tuple-element.151), channel_id=1, source_target_pairs={{0,2},{2,0},{4,6},{6,4},{8,10},{10,8},{12,14},{14,12},{16,18},{18,... | collective-permute-start | bytes 614408 | tf_op jit(solution)/shard_map/ppermute | solution.py:1421
  114.3 12.7 %collective-permute-start.24 = (bf16[400,256]{1,0:T(8,128)(2,1)}, bf16[400,256]{1,0:T(8,128)(2,1)}, u32[]{:S(2)}, u32[]{:S(2)}) collective-permute-start(bf16[400,256]{1,0:T(8,128)(2,1)} %get-tuple-element.152), channel_id=1, source_target_pairs={{0,4},{2,6},{4,0},{6,2},{8,12},{10,14},{12,8},{14,10},{16,20},{18,... | collective-permute-start | bytes 614408 | tf_op jit(solution)/shard_map/ppermute | solution.py:1421
  115.8 11.2 %collective-permute-start.25 = (bf16[400,256]{1,0:T(8,128)(2,1)}, bf16[400,256]{1,0:T(8,128)(2,1)}, u32[]{:S(2)}, u32[]{:S(2)}) collective-permute-start(bf16[400,256]{1,0:T(8,128)(2,1)} %get-tuple-element.153), channel_id=1, source_target_pairs={{0,2},{2,0},{4,6},{6,4},{8,10},{10,8},{12,14},{14,12},{16,18},{18,... | collective-permute-start | bytes 614408 | tf_op jit(solution)/shard_map/ppermute | solution.py:1421
  120.1 11.2 %collective-permute-start.22 = (bf16[384,256]{1,0:T(8,128)(2,1)}, bf16[384,256]{1,0:T(8,128)(2,1)}, u32[]{:S(2)}, u32[]{:S(2)}) collective-permute-start(bf16[384,256]{1,0:T(8,128)(2,1)} %fusion.3), channel_id=1, source_target_pairs={{0,16},{2,18},{4,20},{6,22},{8,24},{10,26},{12,28},{14,30},{16,0},... | collective-permute-start | bytes 589832 | tf_op jit(solution)/shard_map/ppermute | solution.py:1421
  (24 other events, 138.5 us)

commit v6 on v5

--- a/solution.py
+++ b/solution.py
@@ -1076,6 +1076,7 @@
     pair_ref,
     message_ref,
     gain_out_ref,
+    terms_ref,
     routed_out_hbm,
     total_ref,
     routed_ref,
@@ -1112,6 +1113,14 @@
     gain_term = gain_term + jnp.sum(wv.astype(F32) * pair[key_width:], axis=0, keepdims=True)
     arrive.wait()
     leave.start()
+    share = own // 2
+    own_at = pl.ds(
+        pl.multiple_of(where_ref[0] * own + where_ref[1] * share, share), share
+    )
+    terms_ref[:latent_rows, :] = inverse * gain_ref[:, own_at]
+    terms_ref[latent_rows:, :] = (
+        inverse * inverse / width * lat_ref[:, own_at].astype(F32)
+    )
     scaled = (total[:, :query_width] * scaling).astype(BF16)
     d_lat = dot_general(scaled, wq, 1, 1)
     d_lat = d_lat + jnp.dot(
@@ -1167,6 +1176,7 @@
                 held((2 * key_width, own)),
                 held((latent_rows + 8, own + 128)),
                 held((1, own // 2)),
+                held((2 * latent_rows, own // 2)),
                 pl.BlockSpec(memory_space=pl.ANY),
             ],
             scratch_shapes=[
@@ -1180,6 +1190,7 @@
             jax.ShapeDtypeStruct((2 * key_width, own), F32),
             jax.ShapeDtypeStruct((latent_rows + 8, own + 128), F32),
             jax.ShapeDtypeStruct((1, own // 2), F32),
+            jax.ShapeDtypeStruct((2 * latent_rows, own // 2), F32),
             jax.ShapeDtypeStruct(routed.shape, BF16),
         ],
         cost_estimate=pl.CostEstimate(
@@ -1318,15 +1329,14 @@
     message_got_ref,
     term_ref,
     term_got_ref,
-    lat_ref,
-    gain_ref,
+    terms_ref,
     out_ref,
     latent_ref,
     gain_lat_ref,
     gain_ctx_ref,
 ):
     heads, own = out_ref.shape
-    latent_rows, width = lat_ref.shape
+    latent_rows = latent_ref.shape[0]
     share = own // 2
     cut = heads // 2
     first, second = (
@@ -1343,18 +1353,18 @@
     mine = pl.ds(pl.multiple_of(where_ref[1] * share, share), share)
     d_lat = message_ref[:, mine] + message_got_ref[:, mine]
     lat_dot = message_ref[:latent_rows, own : own + 1] + message_got_ref[:latent_rows, own : own + 1]
-    lat = lat_ref[...].astype(F32)
-    inverse = lax.rsqrt(jnp.mean(lat * lat, axis=-1, keepdims=True) + EPSILON)
-    at = pl.ds(pl.multiple_of(where_ref[0] * own + where_ref[1] * share, share), share)
-    hat = lat_ref[:, at].astype(F32) * inverse
-    latent_ref[...] = resid + inverse * (gain_ref[:, at] * d_lat[:latent_rows] - hat * (lat_dot / width))
+    latent_ref[...] = (
+        resid
+        + terms_ref[:latent_rows, :] * d_lat[:latent_rows]
+        - terms_ref[latent_rows:, :] * lat_dot
+    )
     gain_lat_ref[...] = d_lat[latent_rows : latent_rows + 1]
     gain_ctx_ref[...] = term_ref[:1, mine] + term_got_ref[:1, mine]
 
 
-def out_final_call(where, parts, message, message_got, term, term_got, latents, gain_lat):
+def out_final_call(where, parts, message, message_got, term, term_got, terms):
     _, rows, own = parts[0].shape
-    latent_rows, width = latents.shape
+    latent_rows = terms.shape[0] // 2
     heads = 2 * (rows - latent_rows // 4)
     shapes = [(heads, own), (latent_rows, own // 2), (1, own // 2), (1, own // 2)]
     return pl.pallas_call(
@@ -1369,8 +1379,7 @@
                 else held(part.shape)
                 for part in parts
             ]
-            + [held(a.shape) for a in (message, message_got, term, term_got, latents)]
-            + [held((1, width))],
+            + [held(a.shape) for a in (message, message_got, term, term_got, terms)],
             out_specs=[held(shape) for shape in shapes],
         ),
         out_shape=[jax.ShapeDtypeStruct(shape, F32) for shape in shapes],
@@ -1383,8 +1392,7 @@
         message_got,
         term,
         term_got,
-        latents,
-        gain_lat.reshape(1, width),
+        terms,
     )
 
 
@@ -1544,7 +1552,7 @@
     first_end = swap(first_end, 1)
     second_end = swap(second_end, 2)
 
-    grad_w_query, pair_lat, message, grad_gain_out, routed = latent_call(
+    grad_w_query, pair_lat, message, grad_gain_out, terms, routed = latent_call(
         where, lat_sum, lat_parts, lat_proj, latents, gain_lat, w_query, wk, wv, own_width, routed
     )
     first_onward, second_onward, first_end, second_end, message, pair_lat = (
@@ -1582,8 +1590,7 @@
         message_got,
         gain_term,
         gain_got,
-        latents,
-        gain_lat,
+        terms,
     )
     return (
         routed,

time: 142 us -> 141 us (level)
  transfers between devices with their start and end apart: 33 -> 33, of which waited for: 9 -> 9; matrix products, arithmetic and copies ran while one was open for 8% -> 8% of each run, Pallas kernels for 45% -> 46%
where the time goes in v6:
time: 141 us; the launch traced here: 140 us
  Pallas kernels  67.2 us (48%)
  starting transfers between devices  43.6 us (31%)
  waiting for transfers between devices  14.5 us (10%)
  other arithmetic  10 us (7%)
  local copies, waits for them, and re-layouts  4.05 us (3%)
    ppermute x20, starting transfers between devices, swap(): return lax.ppermute(array, 'dp', [(i, i ^ turn) for i in range(dp_count)])  26.6 us
    pallas_call x1, Pallas kernels, backward_call(): pl.pallas_call(functools.partial(backward_kernel, slot_count), name='atte...  15 us
    pallas_call x1, Pallas kernels, forward_call(): pl.pallas_call(forward_kernel, name='forward_attention', in_specs=[pl.Blo...  14.9 us
    all_to_all x2, starting transfers between devices, exchange(): lax.all_to_all(blocks, 'dp', split_axis=0, concat_axis=0, tiled=True)  14.7 us
    ppermute x20, waiting for transfers between devices, swap(): return lax.ppermute(array, 'dp', [(i, i ^ turn) for i in range(dp_count)])  13 us
    pallas_call x1, Pallas kernels, patch_call(): pl.pallas_call(functools.partial(patch_kernel, width), name='patch_gradie...  10.2 us
    pallas_call x1, Pallas kernels, branch_call(): pl.pallas_call(functools.partial(branch_kernel, slot_count), name='branch...  7.96 us
    pallas_call x1, Pallas kernels, latent_call(): pl.pallas_call(latent_kernel, name='latent_gradients', grid_spec=pltpu.Pr...  5.67 us
  transfers between devices with their start and end apart: 33, of which 9 were waited for; matrix products, arithmetic and copies ran while one was open for 8% of the time, Pallas kernels for 46%

profile of v6, /device:TPU:0, one launch (start us, length us, event | category | flops | bytes accessed | tf_op | source)
XLA Modules:
  0.0 140.3 jit_solution(856530623558397986)
XLA Ops:
  1.2 7.9 %all-to-all-start = ((bf16[16,16,2048]{2,1,0:T(8,128)(2,1)}), bf16[16,16,2048]{2,1,0:T(8,128)(2,1)}, u32[]{:S(2)}, u32[]{:S(2)}) async-start(bf16[16,16,2048]{2,1,0:T(8,128)(2,1)} %bitcast.42), calls=%async_computation | async-start | bytes 2097152 | tf_op jit(solution)/shard_map/all_to_all | solution.py:1433
  9.7 14.9 %forward_attention.1 = (bf16[128,768]{1,0:T(8,128)(2,1)}, bf16[2,1024,128]{2,1,0:T(8,128)(2,1)}, bf16[2,1024,128]{2,1,0:T(8,128)(2,1)}, f32[8,1024]{1,0:T(8,128)...) custom-call(s32[1,2]{1,0:T(1,128)} %counts_ref.3, ...), custom_call_target="tpu_custom_call" | custom-call | flops 5000000000 | bytes 24000000 | tf_op jit(solution)/shard_map/forward_attention/pallas_call | solution.py:285
  27.1 8.0 %branch_norm.1 = (bf16[128,4096]{1,0:T(8,128)(2,1)}, f32[128,1]{1,0:T(8,128)}, bf16[256,2048]{1,0:T(8,128)(2,1)}) custom-call(bf16[128,768]{1,0:T(8,128)(2,1)} %get-tuple-element.96.own_hbm.attn_hbm.attn_own_ref, bf16[128,768]{1,0:T(8,128)(2,1)} %copy-done.10, bf16[64,4096]{1,0:T(8,128)(2,1)} %lat_ref.1, f32[1,4096]{1,0:T(1,128)} %bitcast.47, ...), custom_call_target="tpu_custom_call" | custom-call | flops 1610612736 | bytes 16000000 | tf_op jit(solution)/shard_map/branch_norm/pallas_call | solution.py:428
  35.3 6.8 %all-to-all-start.1 = ((bf16[16,16,2048]{2,1,0:T(8,128)(2,1)}), bf16[16,16,2048]{2,1,0:T(8,128)(2,1)}, u32[]{:S(2)}, u32[]{:S(2)}) async-start(bf16[16,16,2048]{2,1,0:T(8,128)(2,1)} %bitcast.43), calls=%async_computation.1 | async-start | bytes 2097152 | tf_op jit(solution)/shard_map/all_to_all | solution.py:1433
  42.1 15.0 %attention_backward.1 = (bf16[128,1024]{1,0:T(8,128)(2,1)}, bf16[64,3584]{1,0:T(8,128)(2,1)}, bf16[400,1024]{1,0:T(8,128)(2,1)}, bf16[64,2560]{1,0:T(8,128)(2,1)...) custom-call(s32[1,2]{1,0:T(1,128)} %counts_ref.3, ...), custom_call_target="tpu_custom_call" | custom-call | flops 5000000000 | bytes 26000000 | tf_op jit(solution)/shard_map/attention_backward/pallas_call | solution.py:844
  57.2 1.9 %collective-permute-start.7 = (bf16[8,192,256]{2,1,0:T(8,128)(2,1)}, bf16[8,192,256]{2,1,0:T(8,128)(2,1)}, u32[]{:S(2)}, u32[]{:S(2)}) collective-permute-start(bf16[8,192,256]{2,1,0:T(8,128)(2,1)} %get-tuple-element.119), channel_id=1, source_target_pairs={{0,2},{2,0},{4,6},{6,4},{8,10},{10,8},{12,14},{14,12},{16,18},{18,... | collective-permute-start | bytes 2359304 | tf_op jit(solution)/shard_map/ppermute | solution.py:1429
  63.6 2.4 %collective-permute-start.12 = (bf16[64,3584]{1,0:T(8,128)(2,1)}, bf16[64,3584]{1,0:T(8,128)(2,1)}, u32[]{:S(2)}, u32[]{:S(2)}) collective-permute-start(bf16[64,3584]{1,0:T(8,128)(2,1)} %get-tuple-element.129), channel_id=1, source_target_pairs={{0,16},{2,18},{4,20},{6,22},{8,24},{10,26},{12,28},{14,30},{16,0},... | collective-permute-start | bytes 1376264 | tf_op jit(solution)/shard_map/ppermute | solution.py:1429
  66.5 10.2 %patch_gradient.1 = bf16[1024,2048]{1,0:T(8,128)(2,1)} custom-call(s32[2]{0:T(128)} %pad_add_fusion.where_ref, bf16[400,1024]{1,0:T(8,128)(2,1)} %get-tuple-element.112.own_ref, bf16[400,1024]{1,0:T(8,128)(2,1)} %copy-done.5, bf16[192,4096]{1,0:T(8,128)(2,1)} %bitcast.32, bf16[192,4096]{1,0:T(8,128)(2,1)} %bitcast.37, ...), custom_call_target="tpu_custom_call" | custom-call | flops 3300000000 | bytes 14000000 | tf_op jit(solution)/shard_map/patch_gradient/pallas_call | solution.py:931
  76.7 1.6 %fusion.4 = bf16[80,1152]{1,0:T(8,128)(2,1)} fusion(bf16[80,1152]{1,0:T(8,128)(2,1)} %collective-permute-done.6, bf16[80,1152]{1,0:T(8,128)(2,1)S(1)} %copy-done.6), kind=kLoop, calls=%fused_computation.11 | loop fusion | flops 368640 | bytes 552960 | tf_op jit(solution)/shard_map/convert_element_type | solution.py:1511
  78.4 2.0 %collective-permute-done.7.value_got_ref = bf16[8,192,256]{2,1,0:T(8,128)(2,1)} collective-permute-done((bf16[8,192,256]{2,1,0:T(8,128)(2,1)}, bf16[8,192,256]{2,1,0:T(8,128)(2,1)}, u32[]{:S(2)}, u32[]{:S(2)}) %collective-permute-start.7) | collective-permute-done | bytes 786464 | tf_op jit(solution)/shard_map/ppermute | solution.py:1429
  85.9 2.1 %collective-permute-done.12.high_ref = bf16[64,3584]{1,0:T(8,128)(2,1)} collective-permute-done((bf16[64,3584]{1,0:T(8,128)(2,1)}, bf16[64,3584]{1,0:T(8,128)(2,1)}, u32[]{:S(2)}, u32[]{:S(2)}) %collective-permute-start.12) | collective-permute-done | bytes 458784 | tf_op jit(solution)/shard_map/ppermute | solution.py:1429
  89.1 3.6 %collective-permute-start.13 = (bf16[80,1152]{1,0:T(8,128)(2,1)}, bf16[80,1152]{1,0:T(8,128)(2,1)}, u32[]{:S(2)}, u32[]{:S(2)}) collective-permute-start(bf16[80,1152]{1,0:T(8,128)(2,1)} %fusion.4), channel_id=1, source_target_pairs={{0,16},{2,18},{4,20},{6,22},{8,24},{10,26},{12,28},{14,30},{16,0},... | collective-permute-start | bytes 552968 | tf_op jit(solution)/shard_map/ppermute | solution.py:1429
  95.8 2.6 %plane_sum.1 = (bf16[2,384,256]{2,1,0:T(8,128)(2,1)}, f32[384,256]{1,0:T(8,128)}) custom-call(bf16[8,192,256]{2,1,0:T(8,128)(2,1)} %get-tuple-element.118.value_ref, bf16[8,192,256]{2,1,0:T(8,128)(2,1)} %collective-permute-done.7.value_got_ref, bf16[4,192,256]{2,1,0:T(8,128)(2,1)} %copy-done.1, bf16[8,192,256]{2,1,0:T(8,128)(2,1)} %bitcast.40, ...), custom_call_target="tpu_custom_call" | custom-call | flops 1000000 | bytes 3000000 | tf_op jit(solution)/shard_map/plane_sum/pallas_call | solution.py:1230
  100.5 2.7 %collective-permute-done.14.forwarded_ref = bf16[64,2560]{1,0:T(8,128)(2,1)} collective-permute-done((bf16[64,2560]{1,0:T(8,128)(2,1)S(1)}, bf16[64,2560]{1,0:T(8,128)(2,1)}, u32[]{:S(2)}, u32[]{:S(2)}) %collective-permute-start.14) | collective-permute-done | bytes 327712 | tf_op jit(solution)/shard_map/ppermute | solution.py:1429
  104.3 1.7 %collective-permute-start.19 = (bf16[80,1152]{1,0:T(8,128)(2,1)S(1)}, bf16[80,1152]{1,0:T(8,128)(2,1)S(1)}, u32[]{:S(2)}, u32[]{:S(2)}) collective-permute-start(bf16[80,1152]{1,0:T(8,128)(2,1)S(1)} %add_convert_fusion.2.sum_ref), channel_id=1, source_target_pairs={{0,2},{2,0},{4,6},{6,4},{8,10},{10,8},{12,14},{14,12},{16,18},{18,... | collective-permute-start | bytes 552968 | tf_op jit(solution)/shard_map/ppermute | solution.py:1429
  107.9 4.7 %output_projection_gradient.1 = (bf16[400,256]{1,0:T(8,128)(2,1)}, bf16[400,256]{1,0:T(8,128)(2,1)}, bf16[2,400,256]{2,1,0:T(8,128)(2,1)}, bf16[400,256]{1,0:T(8...) custom-call(s32[2]{0:T(128)} %pad_add_fusion.where_ref, ...), custom_call_target="tpu_custom_call" | custom-call | flops 805306368 | bytes 4000000 | tf_op jit(solution)/shard_map/output_projection_gradient/pallas_call | solution.py:1040
  112.6 1.7 %collective-permute-start.23 = (bf16[400,256]{1,0:T(8,128)(2,1)}, bf16[400,256]{1,0:T(8,128)(2,1)}, u32[]{:S(2)}, u32[]{:S(2)}) collective-permute-start(bf16[400,256]{1,0:T(8,128)(2,1)} %get-tuple-element.152), channel_id=1, source_target_pairs={{0,2},{2,0},{4,6},{6,4},{8,10},{10,8},{12,14},{14,12},{16,18},{18,... | collective-permute-start | bytes 614408 | tf_op jit(solution)/shard_map/ppermute | solution.py:1429
  116.7 1.7 %collective-permute-start.26 = (bf16[400,256]{1,0:T(8,128)(2,1)}, bf16[400,256]{1,0:T(8,128)(2,1)}, u32[]{:S(2)}, u32[]{:S(2)}) collective-permute-start(bf16[400,256]{1,0:T(8,128)(2,1)} %get-tuple-element.155), channel_id=1, source_target_pairs={{0,4},{2,6},{4,0},{6,2},{8,12},{10,14},{12,8},{14,10},{16,20},{18,... | collective-permute-start | bytes 614408 | tf_op jit(solution)/shard_map/ppermute | solution.py:1429
  118.4 1.7 %fusion.3 = bf16[384,256]{1,0:T(8,128)(2,1)} fusion(f32[384,256]{1,0:T(8,128)} %get-tuple-element.134, bf16[2,384,256]{2,1,0:T(8,128)(2,1)S(1)} %collective-permute-done.15.low_ref), kind=kLoop, calls=%fused_computation.8 | loop fusion | flops 294912 | bytes 786432 | tf_op jit(solution)/shard_map/convert_element_type | solution.py:1547
  121.4 5.7 %latent_gradients.1 = (f32[256,768]{1,0:T(8,128)}, f32[384,256]{1,0:T(8,128)}, f32[72,384]{1,0:T(8,128)}, f32[1,128]{1,0:T(1,128)}, f32[128,128]{1,0:T(8,128)}, /*index=5*/bf16[256,2048]{1,0:T(8,128)(2,1)}) custom-call(s32[2]{0:T(128)} %pad_add_fusion.where_ref, bf16[80,1152]{1,0:T(8,128)(2,1)} %copy-done.7, bf16[80,1152]{1,0:T(8,128)(2,1)} %copy-done.11, ...), custom_call_target="tpu_custom_call" | custom-call | flops 100000000 | bytes 3000000 | tf_op jit(solution)/shard_map/latent_gradients/pallas_call | solution.py:1157
  127.1 1.7 %fusion = bf16[400,256]{1,0:T(8,128)(2,1)} fusion(bf16[400,256]{1,0:T(8,128)(2,1)} %collective-permute-done.24, bf16[2,400,256]{2,1,0:T(8,128)(2,1)S(1)} %copy-done.3), kind=kLoop, calls=%fused_computation.3 | loop fusion | flops 409600 | bytes 614400 | tf_op jit(solution)/shard_map/convert_element_type | solution.py:1565
  131.3 3.0 %key_value_gradients.1 = (f32[192,256]{1,0:T(8,128)}, f32[192,256]{1,0:T(8,128)}, f32[8,256]{1,0:T(8,128)}) custom-call(s32[2]{0:T(128)} %pad_add_fusion.where_ref, bf16[8,192,256]{2,1,0:T(8,128)(2,1)} %get-tuple-element.118.value_ref, bf16[8,192,256]{2,1,0:T(8,128)(2,1)} %collective-permute-done.7.value_got_ref, bf16[4,192,256]{2,1,0:T(8,128)(2,1)} %copy-done.1, ...), custom_call_target="tpu_custom_call" | custom-call | flops 1000000 | bytes 3000000 | tf_op jit(solution)/shard_map/key_value_gradients/pallas_call | solution.py:1286
  134.8 1.5 %collective-permute-done.27.first_last_ref = bf16[400,256]{1,0:T(8,128)(2,1)S(1)} collective-permute-done((bf16[400,256]{1,0:T(8,128)(2,1)S(1)}, bf16[400,256]{1,0:T(8,128)(2,1)S(1)}, u32[]{:S(2)}, u32[]{:S(2)}) %collective-permute-start.27) | collective-permute-done | bytes 204832 | tf_op jit(solution)/shard_map/ppermute | solution.py:1429
  137.1 3.2 %output_gradient_sum.1 = (f32[768,256]{1,0:T(8,128)}, f32[64,128]{1,0:T(8,128)}, f32[1,128]{1,0:T(1,128)}, f32[1,128]{1,0:T(1,128)}) custom-call(s32[2]{0:T(128)} %pad_add_fusion.where_ref, bf16[2,400,256]{2,1,0:T(8,128)(2,1)} %get-tuple-element.163.first_kept_ref, bf16[400,256]{1,0:T(8,128)(2,1)} %collective-permute-done.25.first_got_ref, ...), custom_call_target="tpu_custom_call" | custom-call | flops 1000000 | bytes 3000000 | tf_op jit(solution)/shard_map/output_gradient_sum/pallas_call | solution.py:1370
  (90 shorter events, 31.1 us)
Async XLA Ops:
  0.6 25.7 %collective-permute-start.3 = (bf16[768,4096]{1,0:T(8,128)(2,1)}, bf16[768,4096]{1,0:T(8,128)(2,1)}, u32[]{:S(2)}, u32[]{:S(2)}) collective-permute-start(bf16[768,4096]{1,0:T(8,128)(2,1)} %w_out_hbm.1), channel_id=1, source_target_pairs={{0,1},{1,0},{2,3},{3,2},{4,5},{5,4},{6,7},{7,6},{8,9},{9,8},{10,11... | collective-permute-start | bytes 18874376 | tf_op jit(solution)/shard_map/ppermute | solution.py:30
  1.2 33.9 %all-to-all-start = ((bf16[16,16,2048]{2,1,0:T(8,128)(2,1)}), bf16[16,16,2048]{2,1,0:T(8,128)(2,1)}, u32[]{:S(2)}, u32[]{:S(2)}) async-start(bf16[16,16,2048]{2,1,0:T(8,128)(2,1)} %bitcast.42), calls=%async_computation | async-start | bytes 2097152 | tf_op jit(solution)/shard_map/all_to_all | solution.py:1433
  9.1 15.5 %collective-permute-start = (bf16[192,4096]{1,0:T(8,128)(2,1)}, bf16[192,4096]{1,0:T(8,128)(2,1)}, u32[]{:S(2)}, u32[]{:S(2)}) collective-permute-start(bf16[192,4096]{1,0:T(8,128)(2,1)} %bitcast.30), channel_id=1, source_target_pairs={{0,1},{1,0},{2,3},{3,2},{4,5},{5,4},{6,7},{7,6},{8,9},{9,8},{10,11... | collective-permute-start | bytes 4718600 | tf_op jit(solution)/shard_map/ppermute | solution.py:30
  9.4 15.3 %collective-permute-start.1 = (bf16[192,4096]{1,0:T(8,128)(2,1)}, bf16[192,4096]{1,0:T(8,128)(2,1)}, u32[]{:S(2)}, u32[]{:S(2)}) collective-permute-start(bf16[192,4096]{1,0:T(8,128)(2,1)} %bitcast.35), channel_id=1, source_target_pairs={{0,1},{1,0},{2,3},{3,2},{4,5},{5,4},{6,7},{7,6},{8,9},{9,8},{10,11... | collective-permute-start | bytes 4718600 | tf_op jit(solution)/shard_map/ppermute | solution.py:30
  35.3 46.5 %all-to-all-start.1 = ((bf16[16,16,2048]{2,1,0:T(8,128)(2,1)}), bf16[16,16,2048]{2,1,0:T(8,128)(2,1)}, u32[]{:S(2)}, u32[]{:S(2)}) async-start(bf16[16,16,2048]{2,1,0:T(8,128)(2,1)} %bitcast.43), calls=%async_computation.1 | async-start | bytes 2097152 | tf_op jit(solution)/shard_map/all_to_all | solution.py:1433
  57.2 23.1 %collective-permute-start.7 = (bf16[8,192,256]{2,1,0:T(8,128)(2,1)}, bf16[8,192,256]{2,1,0:T(8,128)(2,1)}, u32[]{:S(2)}, u32[]{:S(2)}) collective-permute-start(bf16[8,192,256]{2,1,0:T(8,128)(2,1)} %get-tuple-element.119), channel_id=1, source_target_pairs={{0,2},{2,0},{4,6},{6,4},{8,10},{10,8},{12,14},{14,12},{16,18},{18,... | collective-permute-start | bytes 2359304 | tf_op jit(solution)/shard_map/ppermute | solution.py:1429
  59.1 22.7 %collective-permute-start.8 = (bf16[2,4,192,256]{3,2,1,0:T(8,128)(2,1)}, bf16[2,4,192,256]{3,2,1,0:T(8,128)(2,1)}, u32[]{:S(2)}, u32[]{:S(2)}) collective-permute-start(bf16[2,4,192,256]{3,2,1,0:T(8,128)(2,1)} %get-tuple-element.120), channel_id=1, source_target_pairs={{0,4},{2,6},{4,0},{6,2},{8,12},{10,14},{12,8},{14,10},{16,20},{18,... | collective-permute-start | bytes 2359304 | tf_op jit(solution)/shard_map/ppermute | solution.py:1429
  62.1 14.6 %collective-permute-start.6 = (bf16[80,1152]{1,0:T(8,128)(2,1)}, bf16[80,1152]{1,0:T(8,128)(2,1)}, u32[]{:S(2)}, u32[]{:S(2)}) collective-permute-start(bf16[80,1152]{1,0:T(8,128)(2,1)} %get-tuple-element.113), channel_id=1, source_target_pairs={{0,8},{2,10},{4,12},{6,14},{8,0},{10,2},{12,4},{14,6},{16,24},{18,... | collective-permute-start | bytes 552968 | tf_op jit(solution)/shard_map/ppermute | solution.py:1429
  63.6 24.5 %collective-permute-start.12 = (bf16[64,3584]{1,0:T(8,128)(2,1)}, bf16[64,3584]{1,0:T(8,128)(2,1)}, u32[]{:S(2)}, u32[]{:S(2)}) collective-permute-start(bf16[64,3584]{1,0:T(8,128)(2,1)} %get-tuple-element.129), channel_id=1, source_target_pairs={{0,16},{2,18},{4,20},{6,22},{8,24},{10,26},{12,28},{14,30},{16,0},... | collective-permute-start | bytes 1376264 | tf_op jit(solution)/shard_map/ppermute | solution.py:1429
  66.0 20.0 %collective-permute-start.11 = (bf16[64,2560]{1,0:T(8,128)(2,1)}, bf16[64,2560]{1,0:T(8,128)(2,1)}, u32[]{:S(2)}, u32[]{:S(2)}) collective-permute-start(bf16[64,2560]{1,0:T(8,128)(2,1)} %get-tuple-element.128), channel_id=1, source_target_pairs={{0,8},{2,10},{4,12},{6,14},{8,0},{10,2},{12,4},{14,6},{16,24},{18,... | collective-permute-start | bytes 983048 | tf_op jit(solution)/shard_map/ppermute | solution.py:1429
  83.1 10.9 %collective-permute-start.10 = (bf16[4,192,256]{2,1,0:T(8,128)(2,1)S(1)}, bf16[4,192,256]{2,1,0:T(8,128)(2,1)}, u32[]{:S(2)}, u32[]{:S(2)}) collective-permute-start(bf16[4,192,256]{2,1,0:T(8,128)(2,1)S(1)} %fusion.2), channel_id=1, source_target_pairs={{0,2},{2,0},{4,6},{6,4},{8,10},{10,8},{12,14},{14,12},{16,18},{18,... | collective-permute-start | bytes 1179656 | tf_op jit(solution)/shard_map/ppermute | solution.py:1429
  84.5 10.6 %collective-permute-start.9 = (bf16[4,192,256]{2,1,0:T(8,128)(2,1)S(1)}, bf16[4,192,256]{2,1,0:T(8,128)(2,1)S(1)}, u32[]{:S(2)}, u32[]{:S(2)}) collective-permute-start(bf16[4,192,256]{2,1,0:T(8,128)(2,1)S(1)} %add_convert_fusion.1), channel_id=1, source_target_pairs={{0,4},{2,6},{4,0},{6,2},{8,12},{10,14},{12,8},{14,10},{16,20},{18,... | collective-permute-start | bytes 1179656 | tf_op jit(solution)/shard_map/ppermute | solution.py:1429
  89.1 14.2 %collective-permute-start.14 = (bf16[64,2560]{1,0:T(8,128)(2,1)S(1)}, bf16[64,2560]{1,0:T(8,128)(2,1)}, u32[]{:S(2)}, u32[]{:S(2)}) collective-permute-start(bf16[64,2560]{1,0:T(8,128)(2,1)S(1)} %slice.30), channel_id=1, source_target_pairs={{0,8},{2,10},{4,12},{6,14},{8,0},{10,2},{12,4},{14,6},{16,24},{18,... | collective-permute-start | bytes 983048 | tf_op jit(solution)/shard_map/ppermute | solution.py:1429
  89.1 11.4 %collective-permute-start.13 = (bf16[80,1152]{1,0:T(8,128)(2,1)}, bf16[80,1152]{1,0:T(8,128)(2,1)}, u32[]{:S(2)}, u32[]{:S(2)}) collective-permute-start(bf16[80,1152]{1,0:T(8,128)(2,1)} %fusion.4), channel_id=1, source_target_pairs={{0,16},{2,18},{4,20},{6,22},{8,24},{10,26},{12,28},{14,30},{16,0},... | collective-permute-start | bytes 552968 | tf_op jit(solution)/shard_map/ppermute | solution.py:1429
  92.7 14.8 %collective-permute-start.17 = (bf16[64,3584]{1,0:T(8,128)(2,1)}, bf16[64,3584]{1,0:T(8,128)(2,1)}, u32[]{:S(2)}, u32[]{:S(2)}) collective-permute-start(bf16[64,3584]{1,0:T(8,128)(2,1)} %collective-permute-done.12.high_ref), channel_id=1, source_target_pairs={{0,1},{1,0},{2,3},{3,2},{4,5},{5,4},{6,7},{7,6},{8,9},{9,8},{10,11... | collective-permute-start | bytes 1376264 | tf_op jit(solution)/shard_map/ppermute | solution.py:30
  94.0 12.0 %collective-permute-start.16 = (bf16[64,2560]{1,0:T(8,128)(2,1)}, bf16[64,2560]{1,0:T(8,128)(2,1)}, u32[]{:S(2)}, u32[]{:S(2)}) collective-permute-start(bf16[64,2560]{1,0:T(8,128)(2,1)} %collective-permute-done.11.low_ref), channel_id=1, source_target_pairs={{0,1},{1,0},{2,3},{3,2},{4,5},{5,4},{6,7},{7,6},{8,9},{9,8},{10,11... | collective-permute-start | bytes 983048 | tf_op jit(solution)/shard_map/ppermute | solution.py:30
  98.4 14.2 %collective-permute-start.15 = (bf16[2,384,256]{2,1,0:T(8,128)(2,1)}, bf16[2,384,256]{2,1,0:T(8,128)(2,1)S(1)}, u32[]{:S(2)}, u32[]{:S(2)}) collective-permute-start(bf16[2,384,256]{2,1,0:T(8,128)(2,1)} %get-tuple-element.126), channel_id=1, source_target_pairs={{0,8},{2,10},{4,12},{6,14},{8,0},{10,2},{12,4},{14,6},{16,24},{18,... | collective-permute-start | bytes 1179656 | tf_op jit(solution)/shard_map/ppermute | solution.py:1429
  104.3 11.5 %collective-permute-start.19 = (bf16[80,1152]{1,0:T(8,128)(2,1)S(1)}, bf16[80,1152]{1,0:T(8,128)(2,1)S(1)}, u32[]{:S(2)}, u32[]{:S(2)}) collective-permute-start(bf16[80,1152]{1,0:T(8,128)(2,1)S(1)} %add_convert_fusion.2.sum_ref), channel_id=1, source_target_pairs={{0,2},{2,0},{4,6},{6,4},{8,10},{10,8},{12,14},{14,12},{16,18},{18,... | collective-permute-start | bytes 552968 | tf_op jit(solution)/shard_map/ppermute | solution.py:1429
  106.0 10.7 %collective-permute-start.20 = (bf16[80,1152]{1,0:T(8,128)(2,1)S(1)}, bf16[80,1152]{1,0:T(8,128)(2,1)S(1)}, u32[]{:S(2)}, u32[]{:S(2)}) collective-permute-start(bf16[80,1152]{1,0:T(8,128)(2,1)S(1)} %add_convert_fusion.2.sum_ref), channel_id=1, source_target_pairs={{0,4},{2,6},{4,0},{6,2},{8,12},{10,14},{12,8},{14,10},{16,20},{18,... | collective-permute-start | bytes 552968 | tf_op jit(solution)/shard_map/ppermute | solution.py:1429
  107.5 12.6 %collective-permute-start.21 = (bf16[80,1152]{1,0:T(8,128)(2,1)S(1)}, bf16[80,1152]{1,0:T(8,128)(2,1)}, u32[]{:S(2)}, u32[]{:S(2)}) collective-permute-start(bf16[80,1152]{1,0:T(8,128)(2,1)S(1)} %add_convert_fusion.2.sum_ref), channel_id=1, source_target_pairs={{0,6},{2,4},{4,2},{6,0},{8,14},{10,12},{12,10},{14,8},{16,22},{18,... | collective-permute-start | bytes 552968 | tf_op jit(solution)/shard_map/ppermute | solution.py:1429
  112.6 14.4 %collective-permute-start.23 = (bf16[400,256]{1,0:T(8,128)(2,1)}, bf16[400,256]{1,0:T(8,128)(2,1)}, u32[]{:S(2)}, u32[]{:S(2)}) collective-permute-start(bf16[400,256]{1,0:T(8,128)(2,1)} %get-tuple-element.152), channel_id=1, source_target_pairs={{0,2},{2,0},{4,6},{6,4},{8,10},{10,8},{12,14},{14,12},{16,18},{18,... | collective-permute-start | bytes 614408 | tf_op jit(solution)/shard_map/ppermute | solution.py:1429
  114.3 12.7 %collective-permute-start.24 = (bf16[400,256]{1,0:T(8,128)(2,1)}, bf16[400,256]{1,0:T(8,128)(2,1)}, u32[]{:S(2)}, u32[]{:S(2)}) collective-permute-start(bf16[400,256]{1,0:T(8,128)(2,1)} %get-tuple-element.153), channel_id=1, source_target_pairs={{0,4},{2,6},{4,0},{6,2},{8,12},{10,14},{12,8},{14,10},{16,20},{18,... | collective-permute-start | bytes 614408 | tf_op jit(solution)/shard_map/ppermute | solution.py:1429
  115.8 11.2 %collective-permute-start.25 = (bf16[400,256]{1,0:T(8,128)(2,1)}, bf16[400,256]{1,0:T(8,128)(2,1)}, u32[]{:S(2)}, u32[]{:S(2)}) collective-permute-start(bf16[400,256]{1,0:T(8,128)(2,1)} %get-tuple-element.154), channel_id=1, source_target_pairs={{0,2},{2,0},{4,6},{6,4},{8,10},{10,8},{12,14},{14,12},{16,18},{18,... | collective-permute-start | bytes 614408 | tf_op jit(solution)/shard_map/ppermute | solution.py:1429
  120.1 11.2 %collective-permute-start.22 = (bf16[384,256]{1,0:T(8,128)(2,1)}, bf16[384,256]{1,0:T(8,128)(2,1)}, u32[]{:S(2)}, u32[]{:S(2)}) collective-permute-start(bf16[384,256]{1,0:T(8,128)(2,1)} %fusion.3), channel_id=1, source_target_pairs={{0,16},{2,18},{4,20},{6,22},{8,24},{10,26},{12,28},{14,30},{16,0},... | collective-permute-start | bytes 589832 | tf_op jit(solution)/shard_map/ppermute | solution.py:1429
  (24 other events, 138.6 us)
